TPU v7x, 256 devices: a whole 4x4x8 slice. The times are simulated.
256 devices in a mesh: uly: 16 (over z, y_hi), blk: 16 (over x, y_lo, core).
Axes of the slice: x: 4, y: 4 (y_hi: 2, y_lo: 2; y = y_hi * 2 + y_lo), z: 8, core: 2. Of those that a mesh axis runs over, the one named last changes fastest.
Arguments:
- queries: bfloat16 [32768, 1024], P(('blk', 'uly')), may hold values from -6 to 6
- keys: bfloat16 [32768, 1024], P(('blk', 'uly')), may hold values from -6 to 6
- values: bfloat16 [32768, 1024], P(('blk', 'uly')), may hold values from -6 to 6
- lengths: int32 [64], replicated, may hold values from 1 to 1024, 32768 in all
- conv_weight: float32 [31, 1024], P(None, 'uly'), may hold values from -8 to 8
- norm_gain: float32 [1024], P('uly'), may hold values from 0.1 to 1.9
- cotangent: bfloat16 [1024, 32768], P('uly', 'blk'), may hold values from -6 to 6
Outputs:
- conv_out: bfloat16 [1024, 32768], P('uly', 'blk')
- grad_queries: bfloat16 [1024, 32768], P('uly', 'blk')
- grad_keys: bfloat16 [1024, 32768], P('uly', 'blk')
- grad_values: bfloat16 [1024, 32768], P('uly', 'blk')
Inputs may be any that keep to these rules, and one draw needn't show every extreme that they name: `lengths`: utterances follow one another and cover the 32768 frames; one utterance has exactly 1024 frames.
All inputs are finite; a program needn't handle non-finite values.
Results may differ from a plain program's by a relative error of at most 0.03.
Values may be sent and summed in bfloat16 or wider, within the bound.
A program may use at most 64 MiB of HBM per device.

v0:
```python
import jax
import jax.numpy as jnp
from jax import lax
from jax.sharding import PartitionSpec as P

KERNEL = 31
HEAD_DIM = 64


def extended(block, sides, width):
    for axis, dim in sides:
        count = lax.axis_size(axis)
        forward = [(i, i + 1) for i in range(count - 1)]
        backward = [(target, source) for source, target in forward]
        low = lax.ppermute(
            lax.slice_in_dim(block, block.shape[dim] - width, None, axis=dim), axis, forward
        )
        high = lax.ppermute(lax.slice_in_dim(block, 0, width, axis=dim), axis, backward)
        block = jnp.concatenate([low, block, high], axis=dim)
    return block


def passed_along(block, axis, distance):
    devices = range(lax.axis_size(axis))
    route = [(i - distance, i) for i in devices if i - distance in devices]
    return lax.ppermute(block, axis, route)


def segment_ids(lengths, frames, frame_total):
    starts = jnp.cumsum(lengths) - lengths
    seg_ids = jnp.sum((starts[None, :] <= frames[:, None]).astype(jnp.int32), axis=1) - 1
    inside = (frames >= 0) & (frames < frame_total)
    return jnp.where(inside, seg_ids, -1)


def rows_at(values_in, row_start, row_count):
    return lax.dynamic_slice_in_dim(values_in, row_start, row_count, 0)


def masked_scores(query_rows, key_rows, query_seg, key_seg):
    scores = HEAD_DIM ** (-0.5) * jnp.einsum(
        "rhe,she->hrs", query_rows, key_rows, preferred_element_type=jnp.float32
    )
    same_seg = (query_seg[:, None] == key_seg[None, :])[None]
    return (scores, same_seg)


def weights_of(scores, same_seg, row_top, row_total):
    return jnp.where(same_seg, jnp.exp(scores - row_top), 0.0) / row_total


def on_device(queries, keys, values, lengths, conv_weight, norm_gain, cotangent):
    local_q, local_k, local_v = (
        lax.all_to_all(queries, "uly", split_axis=1, concat_axis=0, tiled=True),
        lax.all_to_all(keys, "uly", split_axis=1, concat_axis=0, tiled=True),
        lax.all_to_all(values, "uly", split_axis=1, concat_axis=0, tiled=True),
    )
    block_rows, channels = local_q.shape
    heads_here = channels // HEAD_DIM
    maxlen = block_rows // 2
    rows_q = min(512, block_rows)
    window = rows_q + 2 * maxlen
    conv_half = KERNEL // 2
    block_count = block_rows // rows_q
    score_scale = HEAD_DIM ** (-0.5)
    frame_total = lax.axis_size("blk") * block_rows
    first_frame = lax.axis_index("blk") * block_rows
    seg_ext = segment_ids(
        lengths,
        first_frame - maxlen + jnp.arange(block_rows + 2 * maxlen, dtype=jnp.int32),
        frame_total,
    )
    seg_own = seg_ext[maxlen : maxlen + block_rows]
    seg_conv = seg_ext[maxlen - conv_half : maxlen + block_rows + conv_half]
    near_pairs = extended(jnp.concatenate([local_k, local_v], axis=1), (("blk", 0),), maxlen)
    k_ext = near_pairs[:, :channels].reshape(-1, heads_here, HEAD_DIM)
    v_ext = near_pairs[:, channels:].reshape(-1, heads_here, HEAD_DIM)
    q_heads = local_q.reshape(block_rows, heads_here, HEAD_DIM)
    starts = jnp.arange(block_count, dtype=jnp.int32) * rows_q

    def forward_block(row_start):
        scores, same_seg = masked_scores(
            rows_at(q_heads, row_start, rows_q),
            rows_at(k_ext, row_start, window),
            rows_at(seg_own, row_start, rows_q),
            rows_at(seg_ext, row_start, window),
        )
        row_top = jnp.max(jnp.where(same_seg, scores, -1e30), axis=2, keepdims=True)
        shifted_exp = jnp.where(same_seg, jnp.exp(scores - row_top), 0.0)
        row_total = jnp.sum(shifted_exp, axis=2, keepdims=True)
        weights_bf = (shifted_exp / row_total).astype(jnp.bfloat16)
        attended = jnp.einsum(
            "hrs,she->rhe",
            weights_bf,
            rows_at(v_ext, row_start, window),
            preferred_element_type=jnp.float32,
        )
        return (attended.astype(jnp.bfloat16), row_top[:, :, 0].T, row_total[:, :, 0].T)

    attended, row_tops, row_totals = lax.map(forward_block, starts)
    attended = attended.reshape(block_rows, channels)
    row_tops = row_tops.reshape(block_rows, heads_here)
    row_totals = row_totals.reshape(block_rows, heads_here)
    attended_ext = extended(attended, (("blk", 0),), conv_half)
    conv_sum = jnp.zeros((block_rows, channels), jnp.float32)
    for tap_index in range(KERNEL):
        same_seg = (seg_conv[tap_index : tap_index + block_rows] == seg_own)[:, None]
        conv_sum = conv_sum + conv_weight[tap_index][None, :] * jnp.where(
            same_seg, attended_ext[tap_index : tap_index + block_rows].astype(jnp.float32), 0.0
        )
    grouped = conv_sum.reshape(block_rows, heads_here, HEAD_DIM)
    spread = jnp.sqrt(jnp.mean(grouped * grouped, axis=2, keepdims=True) + 1e-05)
    normed = grouped / spread
    pre_act = normed.reshape(block_rows, channels) * norm_gain[None, :]
    sigmoid_gate = jax.nn.sigmoid(pre_act)
    conv_out = (pre_act * sigmoid_gate).astype(jnp.bfloat16)
    grad_pre = (
        cotangent.astype(jnp.float32).T * sigmoid_gate * (1.0 + pre_act * (1.0 - sigmoid_gate))
    )
    weighted = (grad_pre * norm_gain[None, :]).reshape(block_rows, heads_here, HEAD_DIM)
    grad_conv = (
        (weighted - normed * jnp.mean(weighted * normed, axis=2, keepdims=True)) / spread
    ).reshape(block_rows, channels)
    grad_ext = extended(grad_conv, (("blk", 0),), conv_half)
    grad_sum = jnp.zeros((block_rows, channels), jnp.float32)
    for tap_index in range(KERNEL):
        offset = 2 * conv_half - tap_index
        same_seg = (seg_conv[offset : offset + block_rows] == seg_own)[:, None]
        grad_sum = grad_sum + conv_weight[tap_index][None, :] * jnp.where(
            same_seg, grad_ext[offset : offset + block_rows], 0.0
        )
    grad_attended = grad_sum.astype(jnp.bfloat16)
    row_delta = jnp.sum(
        (grad_attended.astype(jnp.float32) * attended.astype(jnp.float32)).reshape(
            block_rows, heads_here, HEAD_DIM
        ),
        axis=2,
    )
    grad_heads = grad_attended.reshape(block_rows, heads_here, HEAD_DIM)

    def tile_grads(row_start):
        query_rows = rows_at(q_heads, row_start, rows_q)
        key_rows = rows_at(k_ext, row_start, window)
        value_rows = rows_at(v_ext, row_start, window)
        grad_rows = rows_at(grad_heads, row_start, rows_q)
        scores, same_seg = masked_scores(
            query_rows,
            key_rows,
            rows_at(seg_own, row_start, rows_q),
            rows_at(seg_ext, row_start, window),
        )
        probs = weights_of(
            scores,
            same_seg,
            rows_at(row_tops, row_start, rows_q).T[:, :, None],
            rows_at(row_totals, row_start, rows_q).T[:, :, None],
        )
        grad_p = jnp.einsum(
            "rhe,she->hrs", grad_rows, value_rows, preferred_element_type=jnp.float32
        )
        grad_s = (probs * (grad_p - rows_at(row_delta, row_start, rows_q).T[:, :, None])).astype(
            jnp.bfloat16
        )
        grad_q = (
            score_scale
            * jnp.einsum("hrs,she->rhe", grad_s, key_rows, preferred_element_type=jnp.float32)
        ).astype(jnp.bfloat16)
        return (probs, grad_s, grad_q, query_rows, grad_rows)

    def backward_block(running, row_start):
        probs, grad_s, grad_q, query_rows, grad_rows = tile_grads(row_start)
        key_term = score_scale * jnp.einsum(
            "hrs,rhe->she", grad_s, query_rows, preferred_element_type=jnp.float32
        )
        value_term = jnp.einsum(
            "hrs,rhe->she",
            probs.astype(jnp.bfloat16),
            grad_rows,
            preferred_element_type=jnp.float32,
        )
        key_value = jnp.concatenate(
            [key_term.reshape(window, channels), value_term.reshape(window, channels)], axis=1
        )
        running = lax.dynamic_update_slice_in_dim(
            running, rows_at(running, row_start, window) + key_value, row_start, 0
        )
        return (running, grad_q)

    ext_terms, grad_q = lax.scan(
        backward_block, jnp.zeros((block_rows + 2 * maxlen, 2 * channels), jnp.float32), starts
    )
    received = []
    for rim_part, direction in ((ext_terms[:maxlen], -1), (ext_terms[maxlen + block_rows :], 1)):
        received.append(
            passed_along(rim_part.astype(jnp.bfloat16), "blk", direction).astype(rim_part.dtype)
        )
    key_grads = ext_terms[maxlen : maxlen + block_rows] + jnp.concatenate(
        [received[1], received[0]], axis=0
    )
    grad_queries = grad_q.reshape(block_rows, channels)
    grad_keys = key_grads[:, :channels].astype(jnp.bfloat16)
    grad_values = key_grads[:, channels:].astype(jnp.bfloat16)
    return (conv_out.T, grad_queries.T, grad_keys.T, grad_values.T)


def solution(mesh):
    in_specs = (
        P(("blk", "uly"), None),
        P(("blk", "uly"), None),
        P(("blk", "uly"), None),
        P(),
        P(None, "uly"),
        P("uly"),
        P("uly", "blk"),
    )
    out_specs = (P("uly", "blk"), P("uly", "blk"), P("uly", "blk"), P("uly", "blk"))
    return jax.shard_map(
        on_device, mesh=mesh, in_specs=in_specs, out_specs=out_specs, check_vma=False
    )
```

profile of v0, /device:TPU:9, one launch (start us, length us, event | category | flops | bytes accessed | tf_op | source)
XLA Modules:
  0.0 218.2 jit_solution(5368850095118419733)
XLA Ops:
  0.6 1.8 copy.35
  2.4 10.0 %all-to-all-start = ((bf16[128,16,64]{0,2,1:T(8,128)(2,1)}), bf16[128,16,64]{0,2,1:T(8,128)(2,1)S(1)}, u32[]{:S(2)}, u32[]{:S(2)}) async-start(bf16[128,16,64]{0,2,1:T(8,128)(2,1)} %bitcast.28), calls=%async_computation | async-start | bytes 524288 | tf_op jit(solution)/shard_map/all_to_all | solution.py:55
  15.4 1.8 copy.37
  17.4 7.1 %all-to-all-done = bf16[128,16,64]{0,2,1:T(8,128)(2,1)S(1)} async-done(((bf16[128,16,64]{0,2,1:T(8,128)(2,1)}), bf16[128,16,64]{0,2,1:T(8,128)(2,1)S(1)}, u32[]{:S(2)}, u32[]{:S(2)}) %all-to-all-start) | async-done | bytes 262176 | tf_op jit(solution)/shard_map/all_to_all | solution.py:55
  24.5 3.5 %all-to-all-start.1 = ((bf16[128,16,64]{0,2,1:T(8,128)(2,1)}), bf16[128,16,64]{0,2,1:T(8,128)(2,1)S(1)}, u32[]{:S(2)}, u32[]{:S(2)}) async-start(bf16[128,16,64]{0,2,1:T(8,128)(2,1)} %bitcast.30), calls=%async_computation.1 | async-start | bytes 524288 | tf_op jit(solution)/shard_map/all_to_all | solution.py:56
  29.0 1.8 copy.39
  30.8 8.3 %all-to-all-done.1 = bf16[128,16,64]{0,2,1:T(8,128)(2,1)S(1)} async-done(((bf16[128,16,64]{0,2,1:T(8,128)(2,1)}), bf16[128,16,64]{0,2,1:T(8,128)(2,1)S(1)}, u32[]{:S(2)}, u32[]{:S(2)}) %all-to-all-start.1) | async-done | bytes 262176 | tf_op jit(solution)/shard_map/all_to_all | solution.py:56
  39.1 3.5 %all-to-all-start.2 = ((bf16[128,16,64]{0,2,1:T(8,128)(2,1)}), bf16[128,16,64]{0,2,1:T(8,128)(2,1)S(1)}, u32[]{:S(2)}, u32[]{:S(2)}) async-start(bf16[128,16,64]{0,2,1:T(8,128)(2,1)} %bitcast.33), calls=%async_computation.2 | async-start | bytes 524288 | tf_op jit(solution)/shard_map/all_to_all | solution.py:54
  42.7 7.6 %collective-permute-start = (bf16[1024,128]{0,1:T(8,128)(2,1)S(1)}, bf16[1024,128]{0,1:T(8,128)(2,1)S(1)}, u32[]{:S(2)}, u32[]{:S(2)}) collective-permute-start(bf16[1024,128]{0,1:T(8,128)(2,1)S(1)} %get-tuple-element.210), channel_id=1, source_target_pairs={{0,1},{1,2},{2,3},{3,4},{4,5},{5,6},{6,7},{7,8},{8,9},{9,10},{10,1... | collective-permute-start | bytes 786440 | tf_op jit(solution)/shard_map/ppermute | solution.py:15
  50.3 1.9 collective-permute-start.1
  54.8 4.1 %collective-permute-done.1 = bf16[1024,128]{0,1:T(8,128)(2,1)S(1)} collective-permute-done((bf16[1024,128]{0,1:T(8,128)(2,1)S(1)}, bf16[1024,128]{0,1:T(8,128)(2,1)S(1)}, u32[]{:S(2)}, u32[]{:S(2)}) %collective-permute-start.1) | collective-permute-done | bytes 262176 | tf_op jit(solution)/shard_map/ppermute | solution.py:18
  60.1 39.3 %while.26 = (s32[]{:T(128)}, bf16[4,512,1,64]{1,3,2,0:T(8,128)(2,1)S(1)}, f32[4,512,1]{1,2,0:T(1,128)S(1)}, f32[4,512,1]{1,2,0:T(1,128)S(1)}, s32[4]{0:T(128)S(1...) while((s32[]{:T(128)}, ...), condition=%wide.region_5.6_spmd, body=%wide.region_2.5_spmd.sunk | while | flops 352615424 | bytes 16597232 | solution.py:100
  64.0 2.2 fusion.219
  67.4 2.5 %fusion.221 = bf16[4,512,1,64]{1,3,2,0:T(8,128)(2,1)S(1)} fusion(bf16[4,512,1,64]{1,3,2,0:T(8,128)(2,1)S(1)} %get-tuple-element.442, s32[]{:T(128)S(6)} %copy.59, f32[512,2560]{1,0:T(8,128)S(1)} %get-tuple-element.408, f32[512]{0:T(512)S(1)} %fusion.220, f32[512]{0:T(512)S(1)} %get-tuple-element.409, s32[2560]{0:T(1024)S(1)} %dynamic_slice.123, ...), kind=kOutput, calls=%fused_computation.9.clone.1 | convolution fusion | flops 174358528 | bytes 5654536 | tf_op jit(solution)/shard_map/while/body/eval_jaxpr/hrs,she->rhe/dot_general | solution.py:92
  73.9 2.2 fusion.219
  77.2 2.5 %fusion.221 = bf16[4,512,1,64]{1,3,2,0:T(8,128)(2,1)S(1)} fusion(bf16[4,512,1,64]{1,3,2,0:T(8,128)(2,1)S(1)} %get-tuple-element.442, s32[]{:T(128)S(6)} %copy.59, f32[512,2560]{1,0:T(8,128)S(1)} %get-tuple-element.408, f32[512]{0:T(512)S(1)} %fusion.220, f32[512]{0:T(512)S(1)} %get-tuple-element.409, s32[2560]{0:T(1024)S(1)} %dynamic_slice.123, ...), kind=kOutput, calls=%fused_computation.9.clone.1 | convolution fusion | flops 174358528 | bytes 5654536 | tf_op jit(solution)/shard_map/while/body/eval_jaxpr/hrs,she->rhe/dot_general | solution.py:92
  83.7 2.2 fusion.219
  87.0 2.5 %fusion.221 = bf16[4,512,1,64]{1,3,2,0:T(8,128)(2,1)S(1)} fusion(bf16[4,512,1,64]{1,3,2,0:T(8,128)(2,1)S(1)} %get-tuple-element.442, s32[]{:T(128)S(6)} %copy.59, f32[512,2560]{1,0:T(8,128)S(1)} %get-tuple-element.408, f32[512]{0:T(512)S(1)} %fusion.220, f32[512]{0:T(512)S(1)} %get-tuple-element.409, s32[2560]{0:T(1024)S(1)} %dynamic_slice.123, ...), kind=kOutput, calls=%fused_computation.9.clone.1 | convolution fusion | flops 174358528 | bytes 5654536 | tf_op jit(solution)/shard_map/while/body/eval_jaxpr/hrs,she->rhe/dot_general | solution.py:92
  93.5 2.2 fusion.219
  96.9 2.5 %fusion.221 = bf16[4,512,1,64]{1,3,2,0:T(8,128)(2,1)S(1)} fusion(bf16[4,512,1,64]{1,3,2,0:T(8,128)(2,1)S(1)} %get-tuple-element.442, s32[]{:T(128)S(6)} %copy.59, f32[512,2560]{1,0:T(8,128)S(1)} %get-tuple-element.408, f32[512]{0:T(512)S(1)} %fusion.220, f32[512]{0:T(512)S(1)} %get-tuple-element.409, s32[2560]{0:T(1024)S(1)} %dynamic_slice.123, ...), kind=kOutput, calls=%fused_computation.9.clone.1 | convolution fusion | flops 174358528 | bytes 5654536 | tf_op jit(solution)/shard_map/while/body/eval_jaxpr/hrs,she->rhe/dot_general | solution.py:92
  99.7 2.7 %collective-permute-start.3 = (bf16[15,64]{0,1:T(8,128)(2,1)S(1)}, bf16[15,64]{0,1:T(8,128)(2,1)S(1)}, u32[]{:S(2)}, u32[]{:S(2)}) collective-permute-start(bf16[15,64]{0,1:T(8,128)(2,1)S(1)} %get-tuple-element.213), channel_id=1, source_target_pairs={{1,0},{2,1},{3,2},{4,3},{5,4},{6,5},{7,6},{8,7},{9,8},{10,9},{11,1... | collective-permute-start | bytes 5768 | tf_op jit(solution)/shard_map/ppermute | solution.py:18
  102.5 3.8 %collective-permute-start.2 = (bf16[15,64]{0,1:T(8,128)(2,1)S(1)}, bf16[15,64]{0,1:T(8,128)(2,1)S(1)}, u32[]{:S(2)}, u32[]{:S(2)}) collective-permute-start(bf16[15,64]{0,1:T(8,128)(2,1)S(1)} %get-tuple-element.212), channel_id=1, source_target_pairs={{0,1},{1,2},{2,3},{3,4},{4,5},{5,6},{6,7},{7,8},{8,9},{9,10},{10,1... | collective-permute-start | bytes 5768 | tf_op jit(solution)/shard_map/ppermute | solution.py:15
  107.1 4.4 %multiply_reduce_fusion.1 = (f32[2048]{0:T(1024)S(1)}, f32[2048,64]{0,1:T(8,128)S(1)}) fusion(bf16[2063,64]{0,1:T(8,128)(2,1)S(1)} %constant_dynamic-update-slice_fusion.2, pred[2048]{0:T(1024)(128)(4,1)S(1)} %get-tuple-element.234, f32[64]{0:T(128)S(1)} %get-tuple-element.252, pred[2048]{0:T(1024)(128)(4,1)S(1)} %get-tuple-element.235, ...), kind=kLoop, calls=%fused_computation.272 | loop fusion | flops 22149120 | bytes 4798080 | tf_op jit(solution)/shard_map/reduce_sum | solution.py:112
  113.0 2.4 %collective-permute-start.4 = (f32[15,64]{0,1:T(8,128)S(1)}, f32[15,64]{0,1:T(8,128)S(1)}, u32[]{:S(2)}, u32[]{:S(2)}) collective-permute-start(f32[15,64]{0,1:T(8,128)S(1)} %get-tuple-element.208), channel_id=1, source_target_pairs={{1,0},{2,1},{3,2},{4,3},{5,4},{6,5},{7,6},{8,7},{9,8},{10,9},{11,1... | collective-permute-start | bytes 11528 | tf_op jit(solution)/shard_map/ppermute | solution.py:18
  115.4 4.8 %collective-permute-start.5 = (f32[15,64]{0,1:T(8,128)S(1)}, f32[15,64]{0,1:T(8,128)S(1)}, u32[]{:S(2)}, u32[]{:S(2)}) collective-permute-start(f32[15,64]{0,1:T(8,128)S(1)} %get-tuple-element.209), channel_id=1, source_target_pairs={{0,1},{1,2},{2,3},{3,4},{4,5},{5,6},{6,7},{7,8},{8,9},{9,10},{10,1... | collective-permute-start | bytes 11528 | tf_op jit(solution)/shard_map/ppermute | solution.py:15
  121.1 6.6 %fusion.55 = (f32[2048]{0:T(1024)S(1)}, bf16[2048,64]{0,1:T(8,128)(2,1)}) fusion(bf16[2048,64]{0,1:T(8,128)(2,1)S(1)} %bitcast.234, f32[2048,64]{0,1:T(8,128)S(1)} %get-tuple-element.204, f32[15,64]{0,1:T(8,128)S(1)} %collective-permute-done.5, pred[2048]{0:T(1024)(128)(4,1)S(1)} %get-tuple-element.233, f32[64]{0:T(128)S(1)} %get-tuple-element.252, ...), kind=kLoop, calls=%fused_computation.117 | loop fusion | flops 16513024 | bytes 1133824 | tf_op jit(solution)/shard_map/reduce_sum | solution.py:133
  128.6 74.8 %while.27 = (s32[]{:T(128)}, f32[4096,128]{0,1:T(8,128)S(1)}, bf16[4,512,1,64]{1,3,2,0:T(8,128)(2,1)}, s32[4]{0:T(128)S(1)}, bf16[2048,1,64]{0,2,1:T(8,128)(2,1)...) while((s32[]{:T(128)}, f32[4096,128]{0,1:T(8,128)S(1)}, ...), condition=%wide.region_10.11_spmd, body=%wide.region_9.10_spmd.sunk | while | flops 851542016 | bytes 32823588 | solution.py:189
  133.0 2.7 %select_divide_fusion.2 = f32[512,2560]{1,0:T(8,128)S(1)} fusion(f32[512]{0:T(512)S(1)} %bitcast.242, f32[512]{0:T(512)S(1)} %bitcast.243, s32[2560]{0:T(1024)S(1)} %dynamic_slice.136, s32[512]{0:T(512)S(1)} %dynamic_slice.137, bf16[4096,1,64]{0,2,1:T(8,128)(2,1)} %get-tuple-element.510, s32[]{:T(128)S(6)} %select_n.617, ...), kind=kOutput, calls=%fused_computation.22.clone.1 | convolution fusion | flops 174325760 | bytes 5652488 | tf_op jit(solution)/shard_map/while/body/eval_jaxpr/rhe,she->hrs/dot_general | solution.py:41
  135.7 1.5 convolution_bitcast_fusion.2
  137.2 2.1 multiply_convert_fusion.3
  139.3 2.5 %fusion.233 = bf16[4,512,1,64]{1,3,2,0:T(8,128)(2,1)} fusion(bf16[4,512,1,64]{1,3,2,0:T(8,128)(2,1)} %get-tuple-element.488, s32[]{:T(128)S(6)} %copy.71, bf16[512,2560]{1,0:T(8,128)(2,1)S(1)} %multiply_convert_fusion.3, bf16[4096,1,64]{0,2,1:T(8,128)(2,1)} %get-tuple-element.510, s32[]{:T(128)S(6)} %select_n.617), kind=kOutput, calls=%fused_computation.31.clone.1 | convolution fusion | flops 167837696 | bytes 3014664 | tf_op jit(solution)/shard_map/while/body/eval_jaxpr/hrs,she->rhe/dot_general | solution.py:166
  143.8 4.8 %dynamic_update_slice.28 = f32[4096,128]{0,1:T(8,128)S(1)} dynamic-update-slice(f32[4096,128]{0,1:T(8,128)S(1)} %get-tuple-element.487, f32[2560,128]{0,1:T(8,128)S(1)} %maximum_add_fusion.2, s32[]{:T(128)S(6)} %select_n.617, s32[]{:T(128)} %constant.47.clone.1..sunk.1) | dynamic-update-slice | bytes 2621444 | tf_op jit(solution)/shard_map/while/body/eval_jaxpr/dynamic_update_slice | solution.py:184
  153.0 2.7 %select_divide_fusion.2 = f32[512,2560]{1,0:T(8,128)S(1)} fusion(f32[512]{0:T(512)S(1)} %bitcast.242, f32[512]{0:T(512)S(1)} %bitcast.243, s32[2560]{0:T(1024)S(1)} %dynamic_slice.136, s32[512]{0:T(512)S(1)} %dynamic_slice.137, bf16[4096,1,64]{0,2,1:T(8,128)(2,1)} %get-tuple-element.510, s32[]{:T(128)S(6)} %select_n.617, ...), kind=kOutput, calls=%fused_computation.22.clone.1 | convolution fusion | flops 174325760 | bytes 5652488 | tf_op jit(solution)/shard_map/while/body/eval_jaxpr/rhe,she->hrs/dot_general | solution.py:41
  155.7 1.5 convolution_bitcast_fusion.2
  157.2 2.1 multiply_convert_fusion.3
  159.3 2.5 %fusion.233 = bf16[4,512,1,64]{1,3,2,0:T(8,128)(2,1)} fusion(bf16[4,512,1,64]{1,3,2,0:T(8,128)(2,1)} %get-tuple-element.488, s32[]{:T(128)S(6)} %copy.71, bf16[512,2560]{1,0:T(8,128)(2,1)S(1)} %multiply_convert_fusion.3, bf16[4096,1,64]{0,2,1:T(8,128)(2,1)} %get-tuple-element.510, s32[]{:T(128)S(6)} %select_n.617), kind=kOutput, calls=%fused_computation.31.clone.1 | convolution fusion | flops 167837696 | bytes 3014664 | tf_op jit(solution)/shard_map/while/body/eval_jaxpr/hrs,she->rhe/dot_general | solution.py:166
  163.8 4.0 %dynamic_update_slice.28 = f32[4096,128]{0,1:T(8,128)S(1)} dynamic-update-slice(f32[4096,128]{0,1:T(8,128)S(1)} %get-tuple-element.487, f32[2560,128]{0,1:T(8,128)S(1)} %maximum_add_fusion.2, s32[]{:T(128)S(6)} %select_n.617, s32[]{:T(128)} %constant.47.clone.1..sunk.1) | dynamic-update-slice | bytes 2621444 | tf_op jit(solution)/shard_map/while/body/eval_jaxpr/dynamic_update_slice | solution.py:184
  172.2 2.7 %select_divide_fusion.2 = f32[512,2560]{1,0:T(8,128)S(1)} fusion(f32[512]{0:T(512)S(1)} %bitcast.242, f32[512]{0:T(512)S(1)} %bitcast.243, s32[2560]{0:T(1024)S(1)} %dynamic_slice.136, s32[512]{0:T(512)S(1)} %dynamic_slice.137, bf16[4096,1,64]{0,2,1:T(8,128)(2,1)} %get-tuple-element.510, s32[]{:T(128)S(6)} %select_n.617, ...), kind=kOutput, calls=%fused_computation.22.clone.1 | convolution fusion | flops 174325760 | bytes 5652488 | tf_op jit(solution)/shard_map/while/body/eval_jaxpr/rhe,she->hrs/dot_general | solution.py:41
  176.4 2.1 multiply_convert_fusion.3
  178.5 2.5 %fusion.233 = bf16[4,512,1,64]{1,3,2,0:T(8,128)(2,1)} fusion(bf16[4,512,1,64]{1,3,2,0:T(8,128)(2,1)} %get-tuple-element.488, s32[]{:T(128)S(6)} %copy.71, bf16[512,2560]{1,0:T(8,128)(2,1)S(1)} %multiply_convert_fusion.3, bf16[4096,1,64]{0,2,1:T(8,128)(2,1)} %get-tuple-element.510, s32[]{:T(128)S(6)} %select_n.617), kind=kOutput, calls=%fused_computation.31.clone.1 | convolution fusion | flops 167837696 | bytes 3014664 | tf_op jit(solution)/shard_map/while/body/eval_jaxpr/hrs,she->rhe/dot_general | solution.py:166
  182.9 3.2 %dynamic_update_slice.28 = f32[4096,128]{0,1:T(8,128)S(1)} dynamic-update-slice(f32[4096,128]{0,1:T(8,128)S(1)} %get-tuple-element.487, f32[2560,128]{0,1:T(8,128)S(1)} %maximum_add_fusion.2, s32[]{:T(128)S(6)} %select_n.617, s32[]{:T(128)} %constant.47.clone.1..sunk.1) | dynamic-update-slice | bytes 2621444 | tf_op jit(solution)/shard_map/while/body/eval_jaxpr/dynamic_update_slice | solution.py:184
  190.6 2.7 %select_divide_fusion.2 = f32[512,2560]{1,0:T(8,128)S(1)} fusion(f32[512]{0:T(512)S(1)} %bitcast.242, f32[512]{0:T(512)S(1)} %bitcast.243, s32[2560]{0:T(1024)S(1)} %dynamic_slice.136, s32[512]{0:T(512)S(1)} %dynamic_slice.137, bf16[4096,1,64]{0,2,1:T(8,128)(2,1)} %get-tuple-element.510, s32[]{:T(128)S(6)} %select_n.617, ...), kind=kOutput, calls=%fused_computation.22.clone.1 | convolution fusion | flops 174325760 | bytes 5652488 | tf_op jit(solution)/shard_map/while/body/eval_jaxpr/rhe,she->hrs/dot_general | solution.py:41
  194.7 2.0 multiply_convert_fusion.3
  196.8 2.5 %fusion.233 = bf16[4,512,1,64]{1,3,2,0:T(8,128)(2,1)} fusion(bf16[4,512,1,64]{1,3,2,0:T(8,128)(2,1)} %get-tuple-element.488, s32[]{:T(128)S(6)} %copy.71, bf16[512,2560]{1,0:T(8,128)(2,1)S(1)} %multiply_convert_fusion.3, bf16[4096,1,64]{0,2,1:T(8,128)(2,1)} %get-tuple-element.510, s32[]{:T(128)S(6)} %select_n.617), kind=kOutput, calls=%fused_computation.31.clone.1 | convolution fusion | flops 167837696 | bytes 3014664 | tf_op jit(solution)/shard_map/while/body/eval_jaxpr/hrs,she->rhe/dot_general | solution.py:166
  201.2 2.2 %dynamic_update_slice.28 = f32[4096,128]{0,1:T(8,128)S(1)} dynamic-update-slice(f32[4096,128]{0,1:T(8,128)S(1)} %get-tuple-element.487, f32[2560,128]{0,1:T(8,128)S(1)} %maximum_add_fusion.2, s32[]{:T(128)S(6)} %select_n.617, s32[]{:T(128)} %constant.47.clone.1..sunk.1) | dynamic-update-slice | bytes 2621444 | tf_op jit(solution)/shard_map/while/body/eval_jaxpr/dynamic_update_slice | solution.py:184
  203.6 5.1 %collective-permute-start.6 = (bf16[1024,128]{0,1:T(8,128)(2,1)S(1)}, bf16[1024,128]{0,1:T(8,128)(2,1)S(1)}, u32[]{:S(2)}, u32[]{:S(2)}) collective-permute-start(bf16[1024,128]{0,1:T(8,128)(2,1)S(1)} %get-tuple-element.200), channel_id=1, source_target_pairs={{0,1},{1,2},{2,3},{3,4},{4,5},{5,6},{6,7},{7,8},{8,9},{9,10},{10,1... | collective-permute-start | bytes 786440 | tf_op jit(solution)/shard_map/ppermute | solution.py:26
  208.7 1.9 collective-permute-start.7
  212.5 4.7 %collective-permute-done.7 = bf16[1024,128]{0,1:T(8,128)(2,1)S(1)} collective-permute-done((bf16[1024,128]{0,1:T(8,128)(2,1)S(1)}, bf16[1024,128]{0,1:T(8,128)(2,1)S(1)}, u32[]{:S(2)}, u32[]{:S(2)}) %collective-permute-start.7) | collective-permute-done | bytes 262176 | tf_op jit(solution)/shard_map/ppermute | solution.py:26
  (104 shorter events, 37.4 us)
Async XLA Ops:
  2.4 22.0 %all-to-all-start = ((bf16[128,16,64]{0,2,1:T(8,128)(2,1)}), bf16[128,16,64]{0,2,1:T(8,128)(2,1)S(1)}, u32[]{:S(2)}, u32[]{:S(2)}) async-start(bf16[128,16,64]{0,2,1:T(8,128)(2,1)} %bitcast.28), calls=%async_computation | async-start | bytes 524288 | tf_op jit(solution)/shard_map/all_to_all | solution.py:55
  24.5 14.6 %all-to-all-start.1 = ((bf16[128,16,64]{0,2,1:T(8,128)(2,1)}), bf16[128,16,64]{0,2,1:T(8,128)(2,1)S(1)}, u32[]{:S(2)}, u32[]{:S(2)}) async-start(bf16[128,16,64]{0,2,1:T(8,128)(2,1)} %bitcast.30), calls=%async_computation.1 | async-start | bytes 524288 | tf_op jit(solution)/shard_map/all_to_all | solution.py:56
  39.1 14.7 %all-to-all-start.2 = ((bf16[128,16,64]{0,2,1:T(8,128)(2,1)}), bf16[128,16,64]{0,2,1:T(8,128)(2,1)S(1)}, u32[]{:S(2)}, u32[]{:S(2)}) async-start(bf16[128,16,64]{0,2,1:T(8,128)(2,1)} %bitcast.33), calls=%async_computation.2 | async-start | bytes 524288 | tf_op jit(solution)/shard_map/all_to_all | solution.py:54
  42.7 12.1 %collective-permute-start = (bf16[1024,128]{0,1:T(8,128)(2,1)S(1)}, bf16[1024,128]{0,1:T(8,128)(2,1)S(1)}, u32[]{:S(2)}, u32[]{:S(2)}) collective-permute-start(bf16[1024,128]{0,1:T(8,128)(2,1)S(1)} %get-tuple-element.210), channel_id=1, source_target_pairs={{0,1},{1,2},{2,3},{3,4},{4,5},{5,6},{6,7},{7,8},{8,9},{9,10},{10,1... | collective-permute-start | bytes 786440 | tf_op jit(solution)/shard_map/ppermute | solution.py:15
  50.3 8.6 %collective-permute-start.1 = (bf16[1024,128]{0,1:T(8,128)(2,1)S(1)}, bf16[1024,128]{0,1:T(8,128)(2,1)S(1)}, u32[]{:S(2)}, u32[]{:S(2)}) collective-permute-start(bf16[1024,128]{0,1:T(8,128)(2,1)S(1)} %get-tuple-element.211), channel_id=1, source_target_pairs={{1,0},{2,1},{3,2},{4,3},{5,4},{6,5},{7,6},{8,7},{9,8},{10,9},{11,1... | collective-permute-start | bytes 786440 | tf_op jit(solution)/shard_map/ppermute | solution.py:18
  99.4 12.1 %copy-start = (bf16[64,2048]{1,0:T(8,128)(2,1)S(1)}, bf16[64,2048]{1,0:T(8,128)(2,1)}, u32[]{:S(2)}) copy-start(bf16[64,2048]{1,0:T(8,128)(2,1)} %param.17) | copy-start | bytes 786436
  99.4 12.1 %copy-start.1 = (f32[64]{0:T(128)S(1)}, f32[64]{0:T(128)}, u32[]{:S(2)}) copy-start(f32[64]{0:T(128)} %param.16) | copy-start | bytes 772
  99.7 6.5 %collective-permute-start.3 = (bf16[15,64]{0,1:T(8,128)(2,1)S(1)}, bf16[15,64]{0,1:T(8,128)(2,1)S(1)}, u32[]{:S(2)}, u32[]{:S(2)}) collective-permute-start(bf16[15,64]{0,1:T(8,128)(2,1)S(1)} %get-tuple-element.213), channel_id=1, source_target_pairs={{1,0},{2,1},{3,2},{4,3},{5,4},{6,5},{7,6},{8,7},{9,8},{10,9},{11,1... | collective-permute-start | bytes 5768 | tf_op jit(solution)/shard_map/ppermute | solution.py:18
  102.5 4.6 %collective-permute-start.2 = (bf16[15,64]{0,1:T(8,128)(2,1)S(1)}, bf16[15,64]{0,1:T(8,128)(2,1)S(1)}, u32[]{:S(2)}, u32[]{:S(2)}) collective-permute-start(bf16[15,64]{0,1:T(8,128)(2,1)S(1)} %get-tuple-element.212), channel_id=1, source_target_pairs={{0,1},{1,2},{2,3},{3,4},{4,5},{5,6},{6,7},{7,8},{8,9},{9,10},{10,1... | collective-permute-start | bytes 5768 | tf_op jit(solution)/shard_map/ppermute | solution.py:15
  113.0 7.2 %collective-permute-start.4 = (f32[15,64]{0,1:T(8,128)S(1)}, f32[15,64]{0,1:T(8,128)S(1)}, u32[]{:S(2)}, u32[]{:S(2)}) collective-permute-start(f32[15,64]{0,1:T(8,128)S(1)} %get-tuple-element.208), channel_id=1, source_target_pairs={{1,0},{2,1},{3,2},{4,3},{5,4},{6,5},{7,6},{8,7},{9,8},{10,9},{11,1... | collective-permute-start | bytes 11528 | tf_op jit(solution)/shard_map/ppermute | solution.py:18
  115.4 5.7 %collective-permute-start.5 = (f32[15,64]{0,1:T(8,128)S(1)}, f32[15,64]{0,1:T(8,128)S(1)}, u32[]{:S(2)}, u32[]{:S(2)}) collective-permute-start(f32[15,64]{0,1:T(8,128)S(1)} %get-tuple-element.209), channel_id=1, source_target_pairs={{0,1},{1,2},{2,3},{3,4},{4,5},{5,6},{6,7},{7,8},{8,9},{9,10},{10,1... | collective-permute-start | bytes 11528 | tf_op jit(solution)/shard_map/ppermute | solution.py:15
  203.6 9.0 %collective-permute-start.6 = (bf16[1024,128]{0,1:T(8,128)(2,1)S(1)}, bf16[1024,128]{0,1:T(8,128)(2,1)S(1)}, u32[]{:S(2)}, u32[]{:S(2)}) collective-permute-start(bf16[1024,128]{0,1:T(8,128)(2,1)S(1)} %get-tuple-element.200), channel_id=1, source_target_pairs={{0,1},{1,2},{2,3},{3,4},{4,5},{5,6},{6,7},{7,8},{8,9},{9,10},{10,1... | collective-permute-start | bytes 786440 | tf_op jit(solution)/shard_map/ppermute | solution.py:26
  208.7 8.6 %collective-permute-start.7 = (bf16[1024,128]{0,1:T(8,128)(2,1)S(1)}, bf16[1024,128]{0,1:T(8,128)(2,1)S(1)}, u32[]{:S(2)}, u32[]{:S(2)}) collective-permute-start(bf16[1024,128]{0,1:T(8,128)(2,1)S(1)} %get-tuple-element.201), channel_id=1, source_target_pairs={{1,0},{2,1},{3,2},{4,3},{5,4},{6,5},{7,6},{8,7},{9,8},{10,9},{11,1... | collective-permute-start | bytes 786440 | tf_op jit(solution)/shard_map/ppermute | solution.py:26
where the time goes:
time: 221 us; the launch traced here: 218 us
  matrix products  59.6 us (27%)
  starting transfers between devices  47.3 us (21%)
  local copies, waits for them, and re-layouts  35.5 us (16%)
  waiting for transfers between devices  27.3 us (12%)
  loops' own time  27.1 us (12%)
  other arithmetic  20.5 us (9%)
    dot_general x8, matrix products, masked_scores(): jnp.einsum('rhe,she->hrs', query_rows, key_rows, preferred_element_type=j...  19.4 us
    ppermute x3, starting transfers between devices, extended(): lax.ppermute(lax.slice_in_dim(block, block.shape[dim] - width, None, axis...  16.2 us
    dynamic_update_slice x4, local copies, waits for them, and re-layouts, backward_block(): lax.dynamic_update_slice_in_dim(running, rows_at(running, row_start, wind...  14.3 us
    another operation x1, loops' own time, on_device(): lax.scan(backward_block, jnp.zeros((block_rows + 2 * maxlen, 2 * channels...  14 us
    another operation x1, loops' own time, on_device(): attended, row_tops, row_totals = lax.map(forward_block, starts)  13.1 us
    dot_general x4, matrix products, tile_grads(): jnp.einsum('hrs,she->rhe', grad_s, key_rows, preferred_element_type=jnp.f...  10.1 us
    all_to_all x1, starting transfers between devices, on_device(): lax.all_to_all(keys, 'uly', split_axis=1, concat_axis=0, tiled=True)  10 us
    dot_general x4, matrix products, forward_block(): jnp.einsum('hrs,she->rhe', weights_bf, rows_at(v_ext, row_start, window),...  9.89 us
  transfers between devices with their start and end apart: 11, of which 7 were waited for; matrix products, arithmetic and copies ran while one was open for 5% of the time, Pallas kernels for 0%

commit v1 on v0

--- a/solution.py
+++ b/solution.py
@@ -50,10 +50,15 @@
 
 
 def on_device(queries, keys, values, lengths, conv_weight, norm_gain, cotangent):
+    rows_in, width = queries.shape
+    heads_total = width // HEAD_DIM
+    stacked = jnp.stack(
+        [a.reshape(rows_in, heads_total, HEAD_DIM) for a in (queries, keys, values)], axis=2
+    ).reshape(rows_in, heads_total * 3 * HEAD_DIM)
+    local_qkv = lax.all_to_all(stacked, "uly", split_axis=1, concat_axis=0, tiled=True)
+    local_qkv = local_qkv.reshape(local_qkv.shape[0], -1, 3, HEAD_DIM)
     local_q, local_k, local_v = (
-        lax.all_to_all(queries, "uly", split_axis=1, concat_axis=0, tiled=True),
-        lax.all_to_all(keys, "uly", split_axis=1, concat_axis=0, tiled=True),
-        lax.all_to_all(values, "uly", split_axis=1, concat_axis=0, tiled=True),
+        local_qkv[:, :, i].reshape(local_qkv.shape[0], -1) for i in range(3)
     )
     block_rows, channels = local_q.shape
     heads_here = channels // HEAD_DIM

time: 221 us -> 213 us (0.964)
  starting transfers between devices: 47.3 us -> 39.5 us
  waiting for transfers between devices: 27.3 us -> 34.3 us
  local copies, waits for them, and re-layouts: 35.5 us -> 32.1 us
  loops' own time: 27.1 us -> 24.6 us
    all_to_all x3 -> x1, starting transfers between devices: 17.1 us -> 10 us  [on_device(): lax.all_to_all(stacked, 'uly', split_axis=1, concat_axis=0, tiled=True)]
    all_to_all x3 -> x1, waiting for transfers between devices: 16.8 us -> 21.4 us  [on_device(): lax.all_to_all(stacked, 'uly', split_axis=1, concat_axis=0, tiled=True)]
    another operation x1, loops' own time: 14 us -> 11.6 us  [on_device(): lax.scan(backward_block, jnp.zeros((block_rows + 2 * maxlen, 2 * channels...]
    unnamed x11 -> x14, local copies, waits for them, and re-layouts: 6.24 us -> 4.21 us
  transfers between devices with their start and end apart: 11 -> 9, of which waited for: 7 -> 6; matrix products, arithmetic and copies ran while one was open for 5% -> 1% of each run, Pallas kernels for 0% -> 0%
where the time goes in v1:
time: 213 us; the launch traced here: 211 us
  matrix products  59.6 us (28%)
  starting transfers between devices  39.5 us (19%)
  waiting for transfers between devices  34.3 us (16%)
  local copies, waits for them, and re-layouts  32.1 us (15%)
  loops' own time  24.6 us (12%)
  other arithmetic  20 us (9%)
    all_to_all x1, waiting for transfers between devices, on_device(): lax.all_to_all(stacked, 'uly', split_axis=1, concat_axis=0, tiled=True)  21.4 us
    dot_general x8, matrix products, masked_scores(): jnp.einsum('rhe,she->hrs', query_rows, key_rows, preferred_element_type=j...  19.4 us
    ppermute x3, starting transfers between devices, extended(): lax.ppermute(lax.slice_in_dim(block, block.shape[dim] - width, None, axis...  16.7 us
    dynamic_update_slice x4, local copies, waits for them, and re-layouts, backward_block(): lax.dynamic_update_slice_in_dim(running, rows_at(running, row_start, wind...  14.3 us
    another operation x1, loops' own time, on_device(): attended, row_tops, row_totals = lax.map(forward_block, starts)  13.1 us
    another operation x1, loops' own time, on_device(): lax.scan(backward_block, jnp.zeros((block_rows + 2 * maxlen, 2 * channels...  11.6 us
    dot_general x4, matrix products, tile_grads(): jnp.einsum('hrs,she->rhe', grad_s, key_rows, preferred_element_type=jnp.f...  10.1 us
    all_to_all x1, starting transfers between devices, on_device(): lax.all_to_all(stacked, 'uly', split_axis=1, concat_axis=0, tiled=True)  10 us
  transfers between devices with their start and end apart: 9, of which 6 were waited for; matrix products, arithmetic and copies ran while one was open for 1% of the time, Pallas kernels for 0%

profile of v1, /device:TPU:9, one launch (start us, length us, event | category | flops | bytes accessed | tf_op | source)
XLA Modules:
  0.0 211.1 jit_solution(8937579358551004443)
XLA Ops:
  5.1 10.0 %all-to-all-start = ((bf16[128,16,192]{0,2,1:T(8,128)(2,1)}), bf16[128,16,192]{0,2,1:T(8,128)(2,1)S(1)}, u32[]{:S(2)}, u32[]{:S(2)}) async-start(bf16[128,16,192]{0,2,1:T(8,128)(2,1)} %bitcast.31), calls=%async_computation | async-start | bytes 1572864 | tf_op jit(solution)/shard_map/all_to_all | solution.py:58
  16.0 21.4 %all-to-all-done = bf16[128,16,192]{0,2,1:T(8,128)(2,1)S(1)} async-done(((bf16[128,16,192]{0,2,1:T(8,128)(2,1)}), bf16[128,16,192]{0,2,1:T(8,128)(2,1)S(1)}, u32[]{:S(2)}, u32[]{:S(2)}) %all-to-all-start) | async-done | bytes 786464 | tf_op jit(solution)/shard_map/all_to_all | solution.py:58
  39.1 6.9 %collective-permute-start = (bf16[1024,128]{0,1:T(8,128)(2,1)S(1)}, bf16[1024,128]{0,1:T(8,128)(2,1)S(1)}, u32[]{:S(2)}, u32[]{:S(2)}) collective-permute-start(bf16[1024,128]{0,1:T(8,128)(2,1)S(1)} %get-tuple-element.213), channel_id=1, source_target_pairs={{0,1},{1,2},{2,3},{3,4},{4,5},{5,6},{6,7},{7,8},{8,9},{9,10},{10,1... | collective-permute-start | bytes 786440 | tf_op jit(solution)/shard_map/ppermute | solution.py:15
  46.0 1.9 collective-permute-start.1
  49.3 5.3 %collective-permute-done.1 = bf16[1024,128]{0,1:T(8,128)(2,1)S(1)} collective-permute-done((bf16[1024,128]{0,1:T(8,128)(2,1)S(1)}, bf16[1024,128]{0,1:T(8,128)(2,1)S(1)}, u32[]{:S(2)}, u32[]{:S(2)}) %collective-permute-start.1) | collective-permute-done | bytes 262176 | tf_op jit(solution)/shard_map/ppermute | solution.py:18
  55.7 39.3 %while.26 = (s32[]{:T(128)}, bf16[4,512,1,64]{1,3,2,0:T(8,128)(2,1)S(1)}, f32[4,512,1]{1,2,0:T(1,128)S(1)}, f32[4,512,1]{1,2,0:T(1,128)S(1)}, s32[4]{0:T(128)S(1...) while((s32[]{:T(128)}, ...), condition=%wide.region_5.6_spmd, body=%wide.region_2.5_spmd.sunk | while | flops 352615424 | bytes 16597232 | solution.py:105
  59.7 2.2 %fusion.217 = (f32[512]{0:T(512)S(1)}, f32[512,2560]{1,0:T(8,128)S(1)}) fusion(s32[2560]{0:T(1024)S(1)} %dynamic_slice.123, s32[512]{0:T(512)S(1)} %dynamic_slice.124, bf16[4096,1,64]{0,2,1:T(8,128)(2,1)} %get-tuple-element.467, s32[]{:T(128)S(6)} %select_n.613, bf16[2048,1,64]{0,2,1:T(8,128)(2,1)} %get-tuple-element.466, s32[]{:T(128)S(6)} %select_n.614), kind=kOutput, calls=%fused_computation.2.clone.1 | convolution fusion | flops 173014528 | bytes 5650440 | tf_op jit(solution)/shard_map/while/body/eval_jaxpr/rhe,she->hrs/dot_general | solution.py:41
  63.0 2.5 %fusion.219 = bf16[4,512,1,64]{1,3,2,0:T(8,128)(2,1)S(1)} fusion(bf16[4,512,1,64]{1,3,2,0:T(8,128)(2,1)S(1)} %get-tuple-element.445, s32[]{:T(128)S(6)} %copy.42, f32[512,2560]{1,0:T(8,128)S(1)} %get-tuple-element.411, f32[512]{0:T(512)S(1)} %fusion.218, f32[512]{0:T(512)S(1)} %get-tuple-element.412, s32[2560]{0:T(1024)S(1)} %dynamic_slice.123, ...), kind=kOutput, calls=%fused_computation.9.clone.1 | convolution fusion | flops 174358528 | bytes 5654536 | tf_op jit(solution)/shard_map/while/body/eval_jaxpr/hrs,she->rhe/dot_general | solution.py:97
  69.5 2.2 %fusion.217 = (f32[512]{0:T(512)S(1)}, f32[512,2560]{1,0:T(8,128)S(1)}) fusion(s32[2560]{0:T(1024)S(1)} %dynamic_slice.123, s32[512]{0:T(512)S(1)} %dynamic_slice.124, bf16[4096,1,64]{0,2,1:T(8,128)(2,1)} %get-tuple-element.467, s32[]{:T(128)S(6)} %select_n.613, bf16[2048,1,64]{0,2,1:T(8,128)(2,1)} %get-tuple-element.466, s32[]{:T(128)S(6)} %select_n.614), kind=kOutput, calls=%fused_computation.2.clone.1 | convolution fusion | flops 173014528 | bytes 5650440 | tf_op jit(solution)/shard_map/while/body/eval_jaxpr/rhe,she->hrs/dot_general | solution.py:41
  72.9 2.5 %fusion.219 = bf16[4,512,1,64]{1,3,2,0:T(8,128)(2,1)S(1)} fusion(bf16[4,512,1,64]{1,3,2,0:T(8,128)(2,1)S(1)} %get-tuple-element.445, s32[]{:T(128)S(6)} %copy.42, f32[512,2560]{1,0:T(8,128)S(1)} %get-tuple-element.411, f32[512]{0:T(512)S(1)} %fusion.218, f32[512]{0:T(512)S(1)} %get-tuple-element.412, s32[2560]{0:T(1024)S(1)} %dynamic_slice.123, ...), kind=kOutput, calls=%fused_computation.9.clone.1 | convolution fusion | flops 174358528 | bytes 5654536 | tf_op jit(solution)/shard_map/while/body/eval_jaxpr/hrs,she->rhe/dot_general | solution.py:97
  79.4 2.2 %fusion.217 = (f32[512]{0:T(512)S(1)}, f32[512,2560]{1,0:T(8,128)S(1)}) fusion(s32[2560]{0:T(1024)S(1)} %dynamic_slice.123, s32[512]{0:T(512)S(1)} %dynamic_slice.124, bf16[4096,1,64]{0,2,1:T(8,128)(2,1)} %get-tuple-element.467, s32[]{:T(128)S(6)} %select_n.613, bf16[2048,1,64]{0,2,1:T(8,128)(2,1)} %get-tuple-element.466, s32[]{:T(128)S(6)} %select_n.614), kind=kOutput, calls=%fused_computation.2.clone.1 | convolution fusion | flops 173014528 | bytes 5650440 | tf_op jit(solution)/shard_map/while/body/eval_jaxpr/rhe,she->hrs/dot_general | solution.py:41
  82.7 2.5 %fusion.219 = bf16[4,512,1,64]{1,3,2,0:T(8,128)(2,1)S(1)} fusion(bf16[4,512,1,64]{1,3,2,0:T(8,128)(2,1)S(1)} %get-tuple-element.445, s32[]{:T(128)S(6)} %copy.42, f32[512,2560]{1,0:T(8,128)S(1)} %get-tuple-element.411, f32[512]{0:T(512)S(1)} %fusion.218, f32[512]{0:T(512)S(1)} %get-tuple-element.412, s32[2560]{0:T(1024)S(1)} %dynamic_slice.123, ...), kind=kOutput, calls=%fused_computation.9.clone.1 | convolution fusion | flops 174358528 | bytes 5654536 | tf_op jit(solution)/shard_map/while/body/eval_jaxpr/hrs,she->rhe/dot_general | solution.py:97
  89.2 2.2 %fusion.217 = (f32[512]{0:T(512)S(1)}, f32[512,2560]{1,0:T(8,128)S(1)}) fusion(s32[2560]{0:T(1024)S(1)} %dynamic_slice.123, s32[512]{0:T(512)S(1)} %dynamic_slice.124, bf16[4096,1,64]{0,2,1:T(8,128)(2,1)} %get-tuple-element.467, s32[]{:T(128)S(6)} %select_n.613, bf16[2048,1,64]{0,2,1:T(8,128)(2,1)} %get-tuple-element.466, s32[]{:T(128)S(6)} %select_n.614), kind=kOutput, calls=%fused_computation.2.clone.1 | convolution fusion | flops 173014528 | bytes 5650440 | tf_op jit(solution)/shard_map/while/body/eval_jaxpr/rhe,she->hrs/dot_general | solution.py:41
  92.5 2.5 %fusion.219 = bf16[4,512,1,64]{1,3,2,0:T(8,128)(2,1)S(1)} fusion(bf16[4,512,1,64]{1,3,2,0:T(8,128)(2,1)S(1)} %get-tuple-element.445, s32[]{:T(128)S(6)} %copy.42, f32[512,2560]{1,0:T(8,128)S(1)} %get-tuple-element.411, f32[512]{0:T(512)S(1)} %fusion.218, f32[512]{0:T(512)S(1)} %get-tuple-element.412, s32[2560]{0:T(1024)S(1)} %dynamic_slice.123, ...), kind=kOutput, calls=%fused_computation.9.clone.1 | convolution fusion | flops 174358528 | bytes 5654536 | tf_op jit(solution)/shard_map/while/body/eval_jaxpr/hrs,she->rhe/dot_general | solution.py:97
  95.4 1.9 collective-permute-start.3
  97.4 4.5 %collective-permute-start.2 = (bf16[15,64]{0,1:T(8,128)(2,1)S(1)}, bf16[15,64]{0,1:T(8,128)(2,1)S(1)}, u32[]{:S(2)}, u32[]{:S(2)}) collective-permute-start(bf16[15,64]{0,1:T(8,128)(2,1)S(1)} %get-tuple-element.215), channel_id=1, source_target_pairs={{0,1},{1,2},{2,3},{3,4},{4,5},{5,6},{6,7},{7,8},{8,9},{9,10},{10,1... | collective-permute-start | bytes 5768 | tf_op jit(solution)/shard_map/ppermute | solution.py:15
  102.7 4.4 %multiply_reduce_fusion.1 = (f32[2048]{0:T(1024)S(1)}, f32[2048,64]{0,1:T(8,128)S(1)}) fusion(bf16[2063,64]{0,1:T(8,128)(2,1)S(1)} %constant_dynamic-update-slice_fusion.2, pred[2048]{0:T(1024)(128)(4,1)S(1)} %get-tuple-element.237, f32[64]{0:T(128)S(1)} %get-tuple-element.255, pred[2048]{0:T(1024)(128)(4,1)S(1)} %get-tuple-element.238, ...), kind=kLoop, calls=%fused_computation.275 | loop fusion | flops 22149120 | bytes 4798080 | tf_op jit(solution)/shard_map/reduce_sum | solution.py:117
  108.7 1.9 collective-permute-start.4
  110.6 5.3 %collective-permute-start.5 = (f32[15,64]{0,1:T(8,128)S(1)}, f32[15,64]{0,1:T(8,128)S(1)}, u32[]{:S(2)}, u32[]{:S(2)}) collective-permute-start(f32[15,64]{0,1:T(8,128)S(1)} %get-tuple-element.212), channel_id=1, source_target_pairs={{0,1},{1,2},{2,3},{3,4},{4,5},{5,6},{6,7},{7,8},{8,9},{9,10},{10,1... | collective-permute-start | bytes 11528 | tf_op jit(solution)/shard_map/ppermute | solution.py:15
  116.7 6.6 %fusion.55 = (f32[2048]{0:T(1024)S(1)}, bf16[2048,64]{0,1:T(8,128)(2,1)}) fusion(bf16[2048,64]{0,1:T(8,128)(2,1)S(1)} %bitcast.229, f32[2048,64]{0,1:T(8,128)S(1)} %get-tuple-element.207, f32[15,64]{0,1:T(8,128)S(1)} %collective-permute-done.5, pred[2048]{0:T(1024)(128)(4,1)S(1)} %get-tuple-element.236, f32[64]{0:T(128)S(1)} %get-tuple-element.255, ...), kind=kLoop, calls=%fused_computation.118 | loop fusion | flops 16513024 | bytes 1133824 | tf_op jit(solution)/shard_map/reduce_sum | solution.py:138
  124.3 72.0 %while.27 = (s32[]{:T(128)}, f32[4096,128]{0,1:T(8,128)S(1)}, bf16[4,512,1,64]{1,3,2,0:T(8,128)(2,1)}, s32[4]{0:T(128)S(1)}, bf16[2048,1,64]{0,2,1:T(8,128)(2,1)...) while((s32[]{:T(128)}, f32[4096,128]{0,1:T(8,128)S(1)}, ...), condition=%wide.region_10.11_spmd, body=%wide.region_9.10_spmd.sunk | while | flops 851542016 | bytes 32823588 | solution.py:194
  128.0 2.7 %select_divide_fusion.2 = f32[512,2560]{1,0:T(8,128)S(1)} fusion(f32[512]{0:T(512)S(1)} %bitcast.240, f32[512]{0:T(512)S(1)} %bitcast.241, s32[2560]{0:T(1024)S(1)} %dynamic_slice.136, s32[512]{0:T(512)S(1)} %dynamic_slice.137, bf16[4096,1,64]{0,2,1:T(8,128)(2,1)} %get-tuple-element.513, s32[]{:T(128)S(6)} %select_n.617, ...), kind=kOutput, calls=%fused_computation.22.clone.1 | convolution fusion | flops 174325760 | bytes 5652488 | tf_op jit(solution)/shard_map/while/body/eval_jaxpr/rhe,she->hrs/dot_general | solution.py:41
  130.7 1.5 convolution_bitcast_fusion.2
  132.2 2.1 multiply_convert_fusion.3
  134.3 2.5 %fusion.231 = bf16[4,512,1,64]{1,3,2,0:T(8,128)(2,1)} fusion(bf16[4,512,1,64]{1,3,2,0:T(8,128)(2,1)} %get-tuple-element.491, s32[]{:T(128)S(6)} %copy.54, bf16[512,2560]{1,0:T(8,128)(2,1)S(1)} %multiply_convert_fusion.3, bf16[4096,1,64]{0,2,1:T(8,128)(2,1)} %get-tuple-element.513, s32[]{:T(128)S(6)} %select_n.617), kind=kOutput, calls=%fused_computation.31.clone.1 | convolution fusion | flops 167837696 | bytes 3014664 | tf_op jit(solution)/shard_map/while/body/eval_jaxpr/hrs,she->rhe/dot_general | solution.py:171
  136.8 1.5 fusion.230
  138.7 4.8 %dynamic_update_slice.28 = f32[4096,128]{0,1:T(8,128)S(1)} dynamic-update-slice(f32[4096,128]{0,1:T(8,128)S(1)} %get-tuple-element.490, f32[2560,128]{0,1:T(8,128)S(1)} %maximum_add_fusion.2, s32[]{:T(128)S(6)} %select_n.617, s32[]{:T(128)} %constant.47.clone.1..sunk.1) | dynamic-update-slice | bytes 2621444 | tf_op jit(solution)/shard_map/while/body/eval_jaxpr/dynamic_update_slice | solution.py:189
  147.3 2.7 %select_divide_fusion.2 = f32[512,2560]{1,0:T(8,128)S(1)} fusion(f32[512]{0:T(512)S(1)} %bitcast.240, f32[512]{0:T(512)S(1)} %bitcast.241, s32[2560]{0:T(1024)S(1)} %dynamic_slice.136, s32[512]{0:T(512)S(1)} %dynamic_slice.137, bf16[4096,1,64]{0,2,1:T(8,128)(2,1)} %get-tuple-element.513, s32[]{:T(128)S(6)} %select_n.617, ...), kind=kOutput, calls=%fused_computation.22.clone.1 | convolution fusion | flops 174325760 | bytes 5652488 | tf_op jit(solution)/shard_map/while/body/eval_jaxpr/rhe,she->hrs/dot_general | solution.py:41
  150.0 1.5 convolution_bitcast_fusion.2
  151.5 2.1 multiply_convert_fusion.3
  153.6 2.5 %fusion.231 = bf16[4,512,1,64]{1,3,2,0:T(8,128)(2,1)} fusion(bf16[4,512,1,64]{1,3,2,0:T(8,128)(2,1)} %get-tuple-element.491, s32[]{:T(128)S(6)} %copy.54, bf16[512,2560]{1,0:T(8,128)(2,1)S(1)} %multiply_convert_fusion.3, bf16[4096,1,64]{0,2,1:T(8,128)(2,1)} %get-tuple-element.513, s32[]{:T(128)S(6)} %select_n.617), kind=kOutput, calls=%fused_computation.31.clone.1 | convolution fusion | flops 167837696 | bytes 3014664 | tf_op jit(solution)/shard_map/while/body/eval_jaxpr/hrs,she->rhe/dot_general | solution.py:171
  156.1 1.5 fusion.230
  158.0 4.0 %dynamic_update_slice.28 = f32[4096,128]{0,1:T(8,128)S(1)} dynamic-update-slice(f32[4096,128]{0,1:T(8,128)S(1)} %get-tuple-element.490, f32[2560,128]{0,1:T(8,128)S(1)} %maximum_add_fusion.2, s32[]{:T(128)S(6)} %select_n.617, s32[]{:T(128)} %constant.47.clone.1..sunk.1) | dynamic-update-slice | bytes 2621444 | tf_op jit(solution)/shard_map/while/body/eval_jaxpr/dynamic_update_slice | solution.py:189
  165.8 2.7 %select_divide_fusion.2 = f32[512,2560]{1,0:T(8,128)S(1)} fusion(f32[512]{0:T(512)S(1)} %bitcast.240, f32[512]{0:T(512)S(1)} %bitcast.241, s32[2560]{0:T(1024)S(1)} %dynamic_slice.136, s32[512]{0:T(512)S(1)} %dynamic_slice.137, bf16[4096,1,64]{0,2,1:T(8,128)(2,1)} %get-tuple-element.513, s32[]{:T(128)S(6)} %select_n.617, ...), kind=kOutput, calls=%fused_computation.22.clone.1 | convolution fusion | flops 174325760 | bytes 5652488 | tf_op jit(solution)/shard_map/while/body/eval_jaxpr/rhe,she->hrs/dot_general | solution.py:41
  168.5 1.5 convolution_bitcast_fusion.2
  170.0 2.1 multiply_convert_fusion.3
  172.1 2.5 %fusion.231 = bf16[4,512,1,64]{1,3,2,0:T(8,128)(2,1)} fusion(bf16[4,512,1,64]{1,3,2,0:T(8,128)(2,1)} %get-tuple-element.491, s32[]{:T(128)S(6)} %copy.54, bf16[512,2560]{1,0:T(8,128)(2,1)S(1)} %multiply_convert_fusion.3, bf16[4096,1,64]{0,2,1:T(8,128)(2,1)} %get-tuple-element.513, s32[]{:T(128)S(6)} %select_n.617), kind=kOutput, calls=%fused_computation.31.clone.1 | convolution fusion | flops 167837696 | bytes 3014664 | tf_op jit(solution)/shard_map/while/body/eval_jaxpr/hrs,she->rhe/dot_general | solution.py:171
  174.6 1.5 fusion.230
  176.6 3.2 %dynamic_update_slice.28 = f32[4096,128]{0,1:T(8,128)S(1)} dynamic-update-slice(f32[4096,128]{0,1:T(8,128)S(1)} %get-tuple-element.490, f32[2560,128]{0,1:T(8,128)S(1)} %maximum_add_fusion.2, s32[]{:T(128)S(6)} %select_n.617, s32[]{:T(128)} %constant.47.clone.1..sunk.1) | dynamic-update-slice | bytes 2621444 | tf_op jit(solution)/shard_map/while/body/eval_jaxpr/dynamic_update_slice | solution.py:189
  183.5 2.7 %select_divide_fusion.2 = f32[512,2560]{1,0:T(8,128)S(1)} fusion(f32[512]{0:T(512)S(1)} %bitcast.240, f32[512]{0:T(512)S(1)} %bitcast.241, s32[2560]{0:T(1024)S(1)} %dynamic_slice.136, s32[512]{0:T(512)S(1)} %dynamic_slice.137, bf16[4096,1,64]{0,2,1:T(8,128)(2,1)} %get-tuple-element.513, s32[]{:T(128)S(6)} %select_n.617, ...), kind=kOutput, calls=%fused_computation.22.clone.1 | convolution fusion | flops 174325760 | bytes 5652488 | tf_op jit(solution)/shard_map/while/body/eval_jaxpr/rhe,she->hrs/dot_general | solution.py:41
  186.2 1.5 convolution_bitcast_fusion.2
  187.6 2.0 multiply_convert_fusion.3
  189.7 2.5 %fusion.231 = bf16[4,512,1,64]{1,3,2,0:T(8,128)(2,1)} fusion(bf16[4,512,1,64]{1,3,2,0:T(8,128)(2,1)} %get-tuple-element.491, s32[]{:T(128)S(6)} %copy.54, bf16[512,2560]{1,0:T(8,128)(2,1)S(1)} %multiply_convert_fusion.3, bf16[4096,1,64]{0,2,1:T(8,128)(2,1)} %get-tuple-element.513, s32[]{:T(128)S(6)} %select_n.617), kind=kOutput, calls=%fused_computation.31.clone.1 | convolution fusion | flops 167837696 | bytes 3014664 | tf_op jit(solution)/shard_map/while/body/eval_jaxpr/hrs,she->rhe/dot_general | solution.py:171
  192.2 1.5 fusion.230
  194.1 2.2 %dynamic_update_slice.28 = f32[4096,128]{0,1:T(8,128)S(1)} dynamic-update-slice(f32[4096,128]{0,1:T(8,128)S(1)} %get-tuple-element.490, f32[2560,128]{0,1:T(8,128)S(1)} %maximum_add_fusion.2, s32[]{:T(128)S(6)} %select_n.617, s32[]{:T(128)} %constant.47.clone.1..sunk.1) | dynamic-update-slice | bytes 2621444 | tf_op jit(solution)/shard_map/while/body/eval_jaxpr/dynamic_update_slice | solution.py:189
  196.5 5.1 %collective-permute-start.6 = (bf16[1024,128]{0,1:T(8,128)(2,1)S(1)}, bf16[1024,128]{0,1:T(8,128)(2,1)S(1)}, u32[]{:S(2)}, u32[]{:S(2)}) collective-permute-start(bf16[1024,128]{0,1:T(8,128)(2,1)S(1)} %get-tuple-element.200), channel_id=1, source_target_pairs={{0,1},{1,2},{2,3},{3,4},{4,5},{5,6},{6,7},{7,8},{8,9},{9,10},{10,1... | collective-permute-start | bytes 786440 | tf_op jit(solution)/shard_map/ppermute | solution.py:26
  201.6 1.9 collective-permute-start.7
  205.5 4.7 %collective-permute-done.7 = bf16[1024,128]{0,1:T(8,128)(2,1)S(1)} collective-permute-done((bf16[1024,128]{0,1:T(8,128)(2,1)S(1)}, bf16[1024,128]{0,1:T(8,128)(2,1)S(1)}, u32[]{:S(2)}, u32[]{:S(2)}) %collective-permute-start.7) | collective-permute-done | bytes 262176 | tf_op jit(solution)/shard_map/ppermute | solution.py:26
  (105 shorter events, 29.7 us)
Async XLA Ops:
  0.6 14.5 %copy-start.3 = (s32[64]{0:T(128)S(1)}, s32[64]{0:T(128)}, u32[]{:S(2)}) copy-start(s32[64]{0:T(128)} %param.14) | copy-start | bytes 772
  0.6 15.0 %copy-start.1 = (f32[31,64]{1,0:T(8,128)S(1)}, f32[31,64]{1,0:T(8,128)}, u32[]{:S(2)}) copy-start(f32[31,64]{1,0:T(8,128)} %param.15) | copy-start | bytes 23812
  5.1 32.3 %all-to-all-start = ((bf16[128,16,192]{0,2,1:T(8,128)(2,1)}), bf16[128,16,192]{0,2,1:T(8,128)(2,1)S(1)}, u32[]{:S(2)}, u32[]{:S(2)}) async-start(bf16[128,16,192]{0,2,1:T(8,128)(2,1)} %bitcast.31), calls=%async_computation | async-start | bytes 1572864 | tf_op jit(solution)/shard_map/all_to_all | solution.py:58
  39.1 10.2 %collective-permute-start = (bf16[1024,128]{0,1:T(8,128)(2,1)S(1)}, bf16[1024,128]{0,1:T(8,128)(2,1)S(1)}, u32[]{:S(2)}, u32[]{:S(2)}) collective-permute-start(bf16[1024,128]{0,1:T(8,128)(2,1)S(1)} %get-tuple-element.213), channel_id=1, source_target_pairs={{0,1},{1,2},{2,3},{3,4},{4,5},{5,6},{6,7},{7,8},{8,9},{9,10},{10,1... | collective-permute-start | bytes 786440 | tf_op jit(solution)/shard_map/ppermute | solution.py:15
  46.0 8.6 %collective-permute-start.1 = (bf16[1024,128]{0,1:T(8,128)(2,1)S(1)}, bf16[1024,128]{0,1:T(8,128)(2,1)S(1)}, u32[]{:S(2)}, u32[]{:S(2)}) collective-permute-start(bf16[1024,128]{0,1:T(8,128)(2,1)S(1)} %get-tuple-element.214), channel_id=1, source_target_pairs={{1,0},{2,1},{3,2},{4,3},{5,4},{6,5},{7,6},{8,7},{9,8},{10,9},{11,1... | collective-permute-start | bytes 786440 | tf_op jit(solution)/shard_map/ppermute | solution.py:18
  95.0 12.1 %copy-start = (bf16[64,2048]{1,0:T(8,128)(2,1)S(1)}, bf16[64,2048]{1,0:T(8,128)(2,1)}, u32[]{:S(2)}) copy-start(bf16[64,2048]{1,0:T(8,128)(2,1)} %param.17) | copy-start | bytes 786436
  95.0 12.1 %copy-start.2 = (f32[64]{0:T(128)S(1)}, f32[64]{0:T(128)}, u32[]{:S(2)}) copy-start(f32[64]{0:T(128)} %param.16) | copy-start | bytes 772
  95.4 6.5 %collective-permute-start.3 = (bf16[15,64]{0,1:T(8,128)(2,1)S(1)}, bf16[15,64]{0,1:T(8,128)(2,1)S(1)}, u32[]{:S(2)}, u32[]{:S(2)}) collective-permute-start(bf16[15,64]{0,1:T(8,128)(2,1)S(1)} %get-tuple-element.216), channel_id=1, source_target_pairs={{1,0},{2,1},{3,2},{4,3},{5,4},{6,5},{7,6},{8,7},{9,8},{10,9},{11,1... | collective-permute-start | bytes 5768 | tf_op jit(solution)/shard_map/ppermute | solution.py:18
  97.4 5.4 %collective-permute-start.2 = (bf16[15,64]{0,1:T(8,128)(2,1)S(1)}, bf16[15,64]{0,1:T(8,128)(2,1)S(1)}, u32[]{:S(2)}, u32[]{:S(2)}) collective-permute-start(bf16[15,64]{0,1:T(8,128)(2,1)S(1)} %get-tuple-element.215), channel_id=1, source_target_pairs={{0,1},{1,2},{2,3},{3,4},{4,5},{5,6},{6,7},{7,8},{8,9},{9,10},{10,1... | collective-permute-start | bytes 5768 | tf_op jit(solution)/shard_map/ppermute | solution.py:15
  108.7 7.2 %collective-permute-start.4 = (f32[15,64]{0,1:T(8,128)S(1)}, f32[15,64]{0,1:T(8,128)S(1)}, u32[]{:S(2)}, u32[]{:S(2)}) collective-permute-start(f32[15,64]{0,1:T(8,128)S(1)} %get-tuple-element.211), channel_id=1, source_target_pairs={{1,0},{2,1},{3,2},{4,3},{5,4},{6,5},{7,6},{8,7},{9,8},{10,9},{11,1... | collective-permute-start | bytes 11528 | tf_op jit(solution)/shard_map/ppermute | solution.py:18
  110.6 6.1 %collective-permute-start.5 = (f32[15,64]{0,1:T(8,128)S(1)}, f32[15,64]{0,1:T(8,128)S(1)}, u32[]{:S(2)}, u32[]{:S(2)}) collective-permute-start(f32[15,64]{0,1:T(8,128)S(1)} %get-tuple-element.212), channel_id=1, source_target_pairs={{0,1},{1,2},{2,3},{3,4},{4,5},{5,6},{6,7},{7,8},{8,9},{9,10},{10,1... | collective-permute-start | bytes 11528 | tf_op jit(solution)/shard_map/ppermute | solution.py:15
  196.5 9.0 %collective-permute-start.6 = (bf16[1024,128]{0,1:T(8,128)(2,1)S(1)}, bf16[1024,128]{0,1:T(8,128)(2,1)S(1)}, u32[]{:S(2)}, u32[]{:S(2)}) collective-permute-start(bf16[1024,128]{0,1:T(8,128)(2,1)S(1)} %get-tuple-element.200), channel_id=1, source_target_pairs={{0,1},{1,2},{2,3},{3,4},{4,5},{5,6},{6,7},{7,8},{8,9},{9,10},{10,1... | collective-permute-start | bytes 786440 | tf_op jit(solution)/shard_map/ppermute | solution.py:26
  201.6 8.6 %collective-permute-start.7 = (bf16[1024,128]{0,1:T(8,128)(2,1)S(1)}, bf16[1024,128]{0,1:T(8,128)(2,1)S(1)}, u32[]{:S(2)}, u32[]{:S(2)}) collective-permute-start(bf16[1024,128]{0,1:T(8,128)(2,1)S(1)} %get-tuple-element.201), channel_id=1, source_target_pairs={{1,0},{2,1},{3,2},{4,3},{5,4},{6,5},{7,6},{8,7},{9,8},{10,9},{11,1... | collective-permute-start | bytes 786440 | tf_op jit(solution)/shard_map/ppermute | solution.py:26

commit v2 on v1

--- a/solution.py
+++ b/solution.py
@@ -1,6 +1,9 @@
 import jax
 import jax.numpy as jnp
+import functools
 from jax import lax
+from jax.experimental import pallas as pl
+from jax.experimental.pallas import tpu as pltpu
 from jax.sharding import PartitionSpec as P
 
 KERNEL = 31
@@ -47,6 +50,118 @@
 
 def weights_of(scores, same_seg, row_top, row_total):
     return jnp.where(same_seg, jnp.exp(scores - row_top), 0.0) / row_total
+
+
+TILE_Q = 256
+TILE_K = 256
+NT = (((1,), (1,)), ((), ()))
+TN = (((0,), (0,)), ((), ()))
+
+
+def forward_kernel(lo_ref, hi_ref, q_ref, k_ref, v_ref, qseg_ref, kseg_ref, o_ref, m_ref, l_ref):
+    scale = HEAD_DIM ** (-0.5)
+
+    def q_body(i, carry):
+        r0 = pl.multiple_of(i * TILE_Q, TILE_Q)
+        q = q_ref[pl.ds(r0, TILE_Q), :]
+        qs = qseg_ref[pl.ds(r0, TILE_Q), :]
+
+        def k_body(j, c):
+            m, l, acc = c
+            c0 = pl.multiple_of(j * TILE_K, TILE_K)
+            k = k_ref[pl.ds(c0, TILE_K), :]
+            v = v_ref[pl.ds(c0, TILE_K), :]
+            ks = kseg_ref[:, pl.ds(c0, TILE_K)]
+            s = scale * lax.dot_general(q, k, NT, preferred_element_type=jnp.float32)
+            mask = qs == ks
+            m_new = jnp.maximum(m, jnp.max(jnp.where(mask, s, -1e30), axis=1, keepdims=True))
+            alpha = jnp.exp(m - m_new)
+            p = jnp.where(mask, jnp.exp(s - m_new), 0.0)
+            l = alpha * l + jnp.sum(p, axis=1, keepdims=True)
+            acc = alpha * acc + jnp.dot(
+                p.astype(jnp.bfloat16), v, preferred_element_type=jnp.float32
+            )
+            return (m_new, l, acc)
+
+        init = (
+            jnp.full((TILE_Q, 1), -1e30, jnp.float32),
+            jnp.zeros((TILE_Q, 1), jnp.float32),
+            jnp.zeros((TILE_Q, HEAD_DIM), jnp.float32),
+        )
+        m, l, acc = lax.fori_loop(lo_ref[i], hi_ref[i], k_body, init)
+        o_ref[pl.ds(r0, TILE_Q), :] = (acc / l).astype(o_ref.dtype)
+        m_ref[pl.ds(r0, TILE_Q), :] = m
+        l_ref[pl.ds(r0, TILE_Q), :] = l
+        return carry
+
+    lax.fori_loop(0, q_ref.shape[0] // TILE_Q, q_body, 0)
+
+
+def backward_kernel(
+    lo_ref, hi_ref, q_ref, k_ref, v_ref, do_ref, qseg_ref, kseg_ref, m_ref, il_ref, d_ref,
+    dq_ref, dk_ref, dv_ref,
+):
+    scale = HEAD_DIM ** (-0.5)
+    dk_ref[...] = jnp.zeros_like(dk_ref)
+    dv_ref[...] = jnp.zeros_like(dv_ref)
+
+    def q_body(i, carry):
+        r0 = pl.multiple_of(i * TILE_Q, TILE_Q)
+        q = q_ref[pl.ds(r0, TILE_Q), :]
+        do = do_ref[pl.ds(r0, TILE_Q), :]
+        qs = qseg_ref[pl.ds(r0, TILE_Q), :]
+        m = m_ref[pl.ds(r0, TILE_Q), :]
+        il = il_ref[pl.ds(r0, TILE_Q), :]
+        dlt = d_ref[pl.ds(r0, TILE_Q), :]
+
+        def k_body(j, dq):
+            c0 = pl.multiple_of(j * TILE_K, TILE_K)
+            k = k_ref[pl.ds(c0, TILE_K), :]
+            v = v_ref[pl.ds(c0, TILE_K), :]
+            ks = kseg_ref[:, pl.ds(c0, TILE_K)]
+            s = scale * lax.dot_general(q, k, NT, preferred_element_type=jnp.float32)
+            mask = qs == ks
+            p = jnp.where(mask, jnp.exp(s - m) * il, 0.0)
+            dp = lax.dot_general(do, v, NT, preferred_element_type=jnp.float32)
+            ds = (p * (dp - dlt)).astype(jnp.bfloat16)
+            dk_ref[pl.ds(c0, TILE_K), :] += lax.dot_general(
+                ds, q, TN, preferred_element_type=jnp.float32
+            )
+            dv_ref[pl.ds(c0, TILE_K), :] += lax.dot_general(
+                p.astype(jnp.bfloat16), do, TN, preferred_element_type=jnp.float32
+            )
+            return dq + jnp.dot(ds, k, preferred_element_type=jnp.float32)
+
+        dq = lax.fori_loop(
+            lo_ref[i], hi_ref[i], k_body, jnp.zeros((TILE_Q, HEAD_DIM), jnp.float32)
+        )
+        dq_ref[pl.ds(r0, TILE_Q), :] = (scale * dq).astype(dq_ref.dtype)
+        return carry
+
+    lax.fori_loop(0, q_ref.shape[0] // TILE_Q, q_body, 0)
+    dk_ref[...] = scale * dk_ref[...]
+
+
+def vmem_call(kernel, n_smem, n_vmem, out_shape):
+    return pl.pallas_call(
+        kernel,
+        out_shape=out_shape,
+        in_specs=[pl.BlockSpec(memory_space=pltpu.SMEM)] * n_smem
+        + [pl.BlockSpec(memory_space=pltpu.VMEM)] * n_vmem,
+        out_specs=[pl.BlockSpec(memory_space=pltpu.VMEM)] * len(out_shape),
+    )
+
+
+def tile_ranges(lengths, seg_own, base, ext_rows):
+    ends = jnp.cumsum(lengths)
+    starts = ends - lengths
+    first = seg_own[::TILE_Q]
+    last = seg_own[TILE_Q - 1 :: TILE_Q]
+    lo = (starts[first] - base) // TILE_K
+    hi = (ends[last] - base + TILE_K - 1) // TILE_K
+    lo = jnp.clip(lo, 0, ext_rows // TILE_K).astype(jnp.int32)
+    hi = jnp.clip(hi, lo, ext_rows // TILE_K).astype(jnp.int32)
+    return (lo, hi)
 
 
 def on_device(queries, keys, values, lengths, conv_weight, norm_gain, cotangent):
@@ -83,29 +198,22 @@
     q_heads = local_q.reshape(block_rows, heads_here, HEAD_DIM)
     starts = jnp.arange(block_count, dtype=jnp.int32) * rows_q
 
-    def forward_block(row_start):
-        scores, same_seg = masked_scores(
-            rows_at(q_heads, row_start, rows_q),
-            rows_at(k_ext, row_start, window),
-            rows_at(seg_own, row_start, rows_q),
-            rows_at(seg_ext, row_start, window),
-        )
-        row_top = jnp.max(jnp.where(same_seg, scores, -1e30), axis=2, keepdims=True)
-        shifted_exp = jnp.where(same_seg, jnp.exp(scores - row_top), 0.0)
-        row_total = jnp.sum(shifted_exp, axis=2, keepdims=True)
-        weights_bf = (shifted_exp / row_total).astype(jnp.bfloat16)
-        attended = jnp.einsum(
-            "hrs,she->rhe",
-            weights_bf,
-            rows_at(v_ext, row_start, window),
-            preferred_element_type=jnp.float32,
-        )
-        return (attended.astype(jnp.bfloat16), row_top[:, :, 0].T, row_total[:, :, 0].T)
-
-    attended, row_tops, row_totals = lax.map(forward_block, starts)
-    attended = attended.reshape(block_rows, channels)
-    row_tops = row_tops.reshape(block_rows, heads_here)
-    row_totals = row_totals.reshape(block_rows, heads_here)
+    assert heads_here == 1
+    lo_t, hi_t = tile_ranges(lengths, seg_own, first_frame - maxlen, block_rows + 2 * maxlen)
+    qseg_col = seg_own[:, None].astype(jnp.int32)
+    kseg_row = seg_ext[None, :].astype(jnp.int32)
+    k_flat = k_ext.reshape(-1, HEAD_DIM)
+    v_flat = v_ext.reshape(-1, HEAD_DIM)
+    attended, row_tops, row_totals = vmem_call(
+        forward_kernel,
+        2,
+        5,
+        (
+            jax.ShapeDtypeStruct((block_rows, HEAD_DIM), jnp.bfloat16),
+            jax.ShapeDtypeStruct((block_rows, 1), jnp.float32),
+            jax.ShapeDtypeStruct((block_rows, 1), jnp.float32),
+        ),
+    )(lo_t, hi_t, local_q, k_flat, v_flat, qseg_col, kseg_row)
     attended_ext = extended(attended, (("blk", 0),), conv_half)
     conv_sum = jnp.zeros((block_rows, channels), jnp.float32)
     for tap_index in range(KERNEL):
@@ -143,57 +251,29 @@
     )
     grad_heads = grad_attended.reshape(block_rows, heads_here, HEAD_DIM)
 
-    def tile_grads(row_start):
-        query_rows = rows_at(q_heads, row_start, rows_q)
-        key_rows = rows_at(k_ext, row_start, window)
-        value_rows = rows_at(v_ext, row_start, window)
-        grad_rows = rows_at(grad_heads, row_start, rows_q)
-        scores, same_seg = masked_scores(
-            query_rows,
-            key_rows,
-            rows_at(seg_own, row_start, rows_q),
-            rows_at(seg_ext, row_start, window),
-        )
-        probs = weights_of(
-            scores,
-            same_seg,
-            rows_at(row_tops, row_start, rows_q).T[:, :, None],
-            rows_at(row_totals, row_start, rows_q).T[:, :, None],
-        )
-        grad_p = jnp.einsum(
-            "rhe,she->hrs", grad_rows, value_rows, preferred_element_type=jnp.float32
-        )
-        grad_s = (probs * (grad_p - rows_at(row_delta, row_start, rows_q).T[:, :, None])).astype(
-            jnp.bfloat16
-        )
-        grad_q = (
-            score_scale
-            * jnp.einsum("hrs,she->rhe", grad_s, key_rows, preferred_element_type=jnp.float32)
-        ).astype(jnp.bfloat16)
-        return (probs, grad_s, grad_q, query_rows, grad_rows)
-
-    def backward_block(running, row_start):
-        probs, grad_s, grad_q, query_rows, grad_rows = tile_grads(row_start)
-        key_term = score_scale * jnp.einsum(
-            "hrs,rhe->she", grad_s, query_rows, preferred_element_type=jnp.float32
-        )
-        value_term = jnp.einsum(
-            "hrs,rhe->she",
-            probs.astype(jnp.bfloat16),
-            grad_rows,
-            preferred_element_type=jnp.float32,
-        )
-        key_value = jnp.concatenate(
-            [key_term.reshape(window, channels), value_term.reshape(window, channels)], axis=1
-        )
-        running = lax.dynamic_update_slice_in_dim(
-            running, rows_at(running, row_start, window) + key_value, row_start, 0
-        )
-        return (running, grad_q)
-
-    ext_terms, grad_q = lax.scan(
-        backward_block, jnp.zeros((block_rows + 2 * maxlen, 2 * channels), jnp.float32), starts
-    )
+    grad_q, dk_ext, dv_ext = vmem_call(
+        backward_kernel,
+        2,
+        9,
+        (
+            jax.ShapeDtypeStruct((block_rows, HEAD_DIM), jnp.bfloat16),
+            jax.ShapeDtypeStruct((block_rows + 2 * maxlen, HEAD_DIM), jnp.float32),
+            jax.ShapeDtypeStruct((block_rows + 2 * maxlen, HEAD_DIM), jnp.float32),
+        ),
+    )(
+        lo_t,
+        hi_t,
+        local_q,
+        k_flat,
+        v_flat,
+        grad_attended,
+        qseg_col,
+        kseg_row,
+        row_tops,
+        1.0 / row_totals,
+        row_delta,
+    )
+    ext_terms = jnp.concatenate([dk_ext, dv_ext], axis=1)
     received = []
     for rim_part, direction in ((ext_terms[:maxlen], -1), (ext_terms[maxlen + block_rows :], 1)):
         received.append(

time: 213 us -> 190 us (0.89)
  matrix products: 59.6 us -> 0 us
  Pallas kernels: 0 us -> 57.6 us
  loops' own time: 24.6 us -> 0 us
  other arithmetic: 20 us -> 43.9 us
  local copies, waits for them, and re-layouts: 32.1 us -> 20.8 us
  waiting for transfers between devices: 34.3 us -> 27.4 us
    dot_general x28 -> x0, matrix products: 59.6 us -> none  [the longest x8 19.4 us: masked_scores(): jnp.einsum('rhe,she->hrs', query_rows, key_rows, preferred_element_type=j...]
    pallas_call x0 -> x2, Pallas kernels: none -> 57.6 us  [the longest x1 31.4 us: on_device(): vmem_call(backward_kernel, 2, 9, (jax.ShapeDtypeStruct((block_rows, HEAD_...]
    another operation x2 -> x0, loops' own time: 24.6 us -> none  [the longest x1 13.1 us: on_device(): attended, row_tops, row_totals = lax.map(forward_block, starts)]
    dynamic_update_slice x8 -> x0, local copies, waits for them, and re-layouts: 14.3 us -> none  [the longest x4 14.3 us: backward_block(): lax.dynamic_update_slice_in_dim(running, rows_at(running, row_start, wind...]
    reduce_sum x1, other arithmetic: 4.37 us -> 18.1 us  [on_device(): jnp.mean(grouped * grouped, axis=2, keepdims=True) + 1e-05]
    reduce_sum x1, other arithmetic: 6.61 us -> 15.3 us  [on_device(): jnp.sum((grad_attended.astype(jnp.float32) * attended.astype(jnp.float32)...]
    dynamic_slice x32 -> x0, local copies, waits for them, and re-layouts: 6.51 us -> none  [the longest x8 4.66 us: on_device(): attended, row_tops, row_totals = lax.map(forward_block, starts)]
    unnamed x14 -> x77, local copies, waits for them, and re-layouts: 4.21 us -> 9.74 us
  transfers between devices with their start and end apart: 9 -> 9, of which waited for: 6 -> 4; matrix products, arithmetic and copies ran while one was open for 1% -> 6% of each run, Pallas kernels for 0% -> 0%
where the time goes in v2:
time: 190 us; the launch traced here: 189 us
  Pallas kernels  57.6 us (30%)
  other arithmetic  43.9 us (23%)
  starting transfers between devices  37.5 us (20%)
  waiting for transfers between devices  27.4 us (14%)
  local copies, waits for them, and re-layouts  20.8 us (11%)
    pallas_call x1, Pallas kernels, on_device(): vmem_call(backward_kernel, 2, 9, (jax.ShapeDtypeStruct((block_rows, HEAD_...  31.4 us
    pallas_call x1, Pallas kernels, on_device(): vmem_call(forward_kernel, 2, 5, (jax.ShapeDtypeStruct((block_rows, HEAD_D...  26.2 us
    reduce_sum x1, other arithmetic, on_device(): jnp.mean(grouped * grouped, axis=2, keepdims=True) + 1e-05  18.1 us
    all_to_all x1, waiting for transfers between devices, on_device(): lax.all_to_all(stacked, 'uly', split_axis=1, concat_axis=0, tiled=True)  18 us
    ppermute x3, starting transfers between devices, extended(): lax.ppermute(lax.slice_in_dim(block, block.shape[dim] - width, None, axis...  16.5 us
    reduce_sum x1, other arithmetic, on_device(): jnp.sum((grad_attended.astype(jnp.float32) * attended.astype(jnp.float32)...  15.3 us
    all_to_all x1, starting transfers between devices, on_device(): lax.all_to_all(stacked, 'uly', split_axis=1, concat_axis=0, tiled=True)  10 us
    unnamed x77, local copies, waits for them, and re-layouts  9.74 us
  transfers between devices with their start and end apart: 9, of which 4 were waited for; matrix products, arithmetic and copies ran while one was open for 6% of the time, Pallas kernels for 0%

profile of v2, /device:TPU:9, one launch (start us, length us, event | category | flops | bytes accessed | tf_op | source)
XLA Modules:
  0.0 188.5 jit_solution(14193947067202844600)
XLA Ops:
  0.6 1.1 copy.52
  1.8 1.1 copy.53
  2.9 1.1 copy.54
  4.1 0.9 copy.55
  5.1 10.0 %all-to-all-start = ((bf16[128,16,192]{0,2,1:T(8,128)(2,1)}), bf16[128,16,192]{0,2,1:T(8,128)(2,1)S(1)}, u32[]{:S(2)}, u32[]{:S(2)}) async-start(bf16[128,16,192]{0,2,1:T(8,128)(2,1)} %bitcast.5), calls=%async_computation | async-start | bytes 1572864 | tf_op jit(solution)/shard_map/all_to_all | solution.py:173
  15.9 0.6 slice_bitcast_fusion.32
  16.6 0.6 gather_fusion.1
  17.3 0.6 gather_fusion
  17.9 0.6 slice_bitcast_fusion.31
  18.7 0.6 and_select_fusion.kseg_ref
  19.4 18.0 %all-to-all-done = bf16[128,16,192]{0,2,1:T(8,128)(2,1)S(1)} async-done(((bf16[128,16,192]{0,2,1:T(8,128)(2,1)}), bf16[128,16,192]{0,2,1:T(8,128)(2,1)S(1)}, u32[]{:S(2)}, u32[]{:S(2)}) %all-to-all-start) | async-done | bytes 786464 | tf_op jit(solution)/shard_map/all_to_all | solution.py:173
  37.4 0.5 copy.56
  37.9 0.3 reshape.152
  38.6 0.3 copy.70
  38.9 1.0 fusion.156
  39.9 6.9 %collective-permute-start = (bf16[1024,128]{1,0:T(8,128)(2,1)}, bf16[1024,128]{1,0:T(8,128)(2,1)S(1)}, u32[]{:S(2)}, u32[]{:S(2)}) collective-permute-start(bf16[1024,128]{1,0:T(8,128)(2,1)} %get-tuple-element.46), channel_id=1, source_target_pairs={{0,1},{1,2},{2,3},{3,4},{4,5},{5,6},{6,7},{7,8},{8,9},{9,10},{10,1... | collective-permute-start | bytes 786440 | tf_op jit(solution)/shard_map/ppermute | solution.py:18
  46.8 1.9 %collective-permute-start.1 = (bf16[1024,128]{1,0:T(8,128)(2,1)S(1)}, bf16[1024,128]{1,0:T(8,128)(2,1)S(1)}, u32[]{:S(2)}, u32[]{:S(2)}) collective-permute-start(bf16[1024,128]{1,0:T(8,128)(2,1)S(1)} %get-tuple-element.47), channel_id=1, source_target_pairs={{1,0},{2,1},{3,2},{4,3},{5,4},{6,5},{7,6},{8,7},{9,8},{10,9},{11,1... | collective-permute-start | bytes 786440 | tf_op jit(solution)/shard_map/ppermute | solution.py:21
  48.7 0.5 maximum_minimum_fusion
  49.2 1.3 copy.60.qseg_ref
  50.9 1.0 copy.68
  51.9 3.5 %collective-permute-done.1 = bf16[1024,128]{1,0:T(8,128)(2,1)S(1)} collective-permute-done((bf16[1024,128]{1,0:T(8,128)(2,1)S(1)}, bf16[1024,128]{1,0:T(8,128)(2,1)S(1)}, u32[]{:S(2)}, u32[]{:S(2)}) %collective-permute-start.1) | collective-permute-done | bytes 262176 | tf_op jit(solution)/shard_map/ppermute | solution.py:21
  55.4 0.3 pad_maximum_fusion.2
  55.6 1.7 fusion.163
  57.6 26.2 %shard_map.102 = (bf16[2048,64]{1,0:T(8,128)(2,1)}, f32[2048,1]{1,0:T(8,128)}, f32[2048,1]{1,0:T(8,128)}) custom-call(s32[8]{0:T(128)} %get-tuple-element.37.lo_ref, s32[8]{0:T(128)} %get-tuple-element.36.hi_ref, bf16[2048,64]{1,0:T(8,128)(2,1)} %bitcast.97, bf16[4096,64]{1,0:T(8,128)(2,1)} %get-tuple-element.45.k_ref, ...), custom_call_target="tpu_custom_call" | custom-call | tf_op jit(solution)/shard_map/pallas_call | solution.py:207
  83.8 0.7 fusion.165
  84.5 1.9 %collective-permute-start.3 = (bf16[15,64]{1,0:T(8,128)(2,1)S(1)}, bf16[15,64]{1,0:T(8,128)(2,1)S(1)}, u32[]{:S(2)}, u32[]{:S(2)}) collective-permute-start(bf16[15,64]{1,0:T(8,128)(2,1)S(1)} %get-tuple-element.54), channel_id=1, source_target_pairs={{1,0},{2,1},{3,2},{4,3},{5,4},{6,5},{7,6},{8,7},{9,8},{10,9},{11,1... | collective-permute-start | bytes 5768 | tf_op jit(solution)/shard_map/ppermute | solution.py:21
  86.4 1.1 constant_dynamic-update-slice_fusion.1
  87.5 4.5 %collective-permute-start.2 = (bf16[15,64]{1,0:T(8,128)(2,1)S(1)}, bf16[15,64]{1,0:T(8,128)(2,1)S(1)}, u32[]{:S(2)}, u32[]{:S(2)}) collective-permute-start(bf16[15,64]{1,0:T(8,128)(2,1)S(1)} %get-tuple-element.53), channel_id=1, source_target_pairs={{0,1},{1,2},{2,3},{3,4},{4,5},{5,6},{6,7},{7,8},{8,9},{9,10},{10,1... | collective-permute-start | bytes 5768 | tf_op jit(solution)/shard_map/ppermute | solution.py:18
  92.0 0.7 collective-permute-done.2
  93.0 18.1 %multiply_reduce_fusion.1 = (f32[2048]{0:T(1024)S(1)}, f32[2048,64]{1,0:T(8,128)S(1)}) fusion(bf16[2063,64]{1,0:T(8,128)(2,1)S(1)} %constant_dynamic-update-slice_fusion, pred[2048]{0:T(1024)(128)(4,1)S(1)} %get-tuple-element.75, f32[64]{0:T(128)S(1)} %copy-done.29, pred[2048]{0:T(1024)(128)(4,1)S(1)} %get-tuple-element.76, f32[64]{0:T(128)S(1)} %copy-done.30, ...), kind=kLoop, calls=%fused_computation.219 | loop fusion | flops 22149120 | bytes 4798080 | tf_op jit(solution)/shard_map/reduce_sum | solution.py:225
  111.1 0.8 multiply_reduce_fusion
  112.0 0.9 subtract_divide_fusion
  112.9 1.9 %collective-permute-start.4 = (f32[15,64]{1,0:T(8,128)S(1)}, f32[15,64]{1,0:T(8,128)S(1)}, u32[]{:S(2)}, u32[]{:S(2)}) collective-permute-start(f32[15,64]{1,0:T(8,128)S(1)} %get-tuple-element.42), channel_id=1, source_target_pairs={{1,0},{2,1},{3,2},{4,3},{5,4},{6,5},{7,6},{8,7},{9,8},{10,9},{11,1... | collective-permute-start | bytes 11528 | tf_op jit(solution)/shard_map/ppermute | solution.py:21
  114.8 5.1 %collective-permute-start.5 = (f32[15,64]{1,0:T(8,128)S(1)}, f32[15,64]{1,0:T(8,128)S(1)}, u32[]{:S(2)}, u32[]{:S(2)}) collective-permute-start(f32[15,64]{1,0:T(8,128)S(1)} %get-tuple-element.43), channel_id=1, source_target_pairs={{0,1},{1,2},{2,3},{3,4},{4,5},{5,6},{6,7},{7,8},{8,9},{9,10},{10,1... | collective-permute-start | bytes 11528 | tf_op jit(solution)/shard_map/ppermute | solution.py:18
  119.9 1.1 broadcast_divide_fusion.il_ref
  121.1 15.3 %fusion.16 = (f32[2048]{0:T(1024)S(1)}, bf16[2048,64]{1,0:T(8,128)(2,1)}) fusion(bf16[2048,64]{1,0:T(8,128)(2,1)S(1)} %copy-done.1, f32[2048,64]{1,0:T(8,128)S(1)} %get-tuple-element.38, f32[15,64]{1,0:T(8,128)S(1)} %collective-permute-done.5, pred[2048]{0:T(1024)(128)(4,1)S(1)} %get-tuple-element.74, f32[64]{0:T(128)S(1)} %copy-done.29, ...), kind=kLoop, calls=%fused_computation.65 | loop fusion | flops 16513024 | bytes 1133824 | tf_op jit(solution)/shard_map/reduce_sum | solution.py:246
  136.4 1.3 copy.63.d_ref
  137.7 31.4 %shard_map.103 = (bf16[2048,64]{1,0:T(8,128)(2,1)}, f32[4096,64]{1,0:T(8,128)}, f32[4096,64]{1,0:T(8,128)}) custom-call(s32[8]{0:T(128)} %get-tuple-element.37.lo_ref, s32[8]{0:T(128)} %get-tuple-element.36.hi_ref, bf16[2048,64]{1,0:T(8,128)(2,1)} %bitcast.98, bf16[4096,64]{1,0:T(8,128)(2,1)} %get-tuple-element.45.k_ref, ...), custom_call_target="tpu_custom_call" | custom-call | tf_op jit(solution)/shard_map/pallas_call | solution.py:254
  169.1 2.7 %maximum_convert_fusion = bf16[4096,128]{1,0:T(8,128)(2,1)S(1)} fusion(f32[4096,64]{1,0:T(8,128)} %get-tuple-element.15, f32[4096,64]{1,0:T(8,128)} %get-tuple-element.14), kind=kLoop, calls=%fused_computation.44 | loop fusion | flops 2097152 | bytes 3145728 | tf_op jit(solution)/shard_map/convert.5
  171.9 0.8 fusion.161
  172.7 3.3 %collective-permute-start.6 = (bf16[1024,128]{1,0:T(8,128)(2,1)}, bf16[1024,128]{1,0:T(8,128)(2,1)S(1)}, u32[]{:S(2)}, u32[]{:S(2)}) collective-permute-start(bf16[1024,128]{1,0:T(8,128)(2,1)} %get-tuple-element.40), channel_id=1, source_target_pairs={{0,1},{1,2},{2,3},{3,4},{4,5},{5,6},{6,7},{7,8},{8,9},{9,10},{10,1... | collective-permute-start | bytes 786440 | tf_op jit(solution)/shard_map/ppermute | solution.py:29
  176.0 1.9 %collective-permute-start.7 = (bf16[1024,128]{1,0:T(8,128)(2,1)}, bf16[1024,128]{1,0:T(8,128)(2,1)}, u32[]{:S(2)}, u32[]{:S(2)}) collective-permute-start(bf16[1024,128]{1,0:T(8,128)(2,1)} %get-tuple-element.41), channel_id=1, source_target_pairs={{1,0},{2,1},{3,2},{4,3},{5,4},{6,5},{7,6},{8,7},{9,8},{10,9},{11,1... | collective-permute-start | bytes 786440 | tf_op jit(solution)/shard_map/ppermute | solution.py:29
  177.9 0.9 copy.64
  178.8 0.9 copy.65
  179.7 5.2 %collective-permute-done.7 = bf16[1024,128]{1,0:T(8,128)(2,1)} collective-permute-done((bf16[1024,128]{1,0:T(8,128)(2,1)}, bf16[1024,128]{1,0:T(8,128)(2,1)}, u32[]{:S(2)}, u32[]{:S(2)}) %collective-permute-start.7) | collective-permute-done | bytes 262176 | tf_op jit(solution)/shard_map/ppermute | solution.py:29
  184.9 1.6 fusion.19
  186.7 0.9 copy.67
  187.6 0.9 copy.66
  (97 shorter events, 2.1 us)
Async XLA Ops:
  4.0 11.1 %copy-start.32 = (s32[64]{0:T(128)S(1)}, s32[64]{0:T(128)}, u32[]{:S(2)}) copy-start(s32[64]{0:T(128)} %param.10) | copy-start | bytes 772
  4.1 11.8 %copy-start.5 = (f32[31,64]{1,0:T(8,128)S(1)}, f32[31,64]{1,0:T(8,128)}, u32[]{:S(2)}) copy-start(f32[31,64]{1,0:T(8,128)} %param.11) | copy-start | bytes 23812
  5.1 32.3 %all-to-all-start = ((bf16[128,16,192]{0,2,1:T(8,128)(2,1)}), bf16[128,16,192]{0,2,1:T(8,128)(2,1)S(1)}, u32[]{:S(2)}, u32[]{:S(2)}) async-start(bf16[128,16,192]{0,2,1:T(8,128)(2,1)} %bitcast.5), calls=%async_computation | async-start | bytes 1572864 | tf_op jit(solution)/shard_map/all_to_all | solution.py:173
  38.3 12.2 %copy-start.4 = (bf16[64,2048]{1,0:T(8,128)(2,1)S(1)}, bf16[64,2048]{1,0:T(8,128)(2,1)}, u32[]{:S(2)}) copy-start(bf16[64,2048]{1,0:T(8,128)(2,1)} %param.13) | copy-start | bytes 786436
  39.9 12.0 %collective-permute-start = (bf16[1024,128]{1,0:T(8,128)(2,1)}, bf16[1024,128]{1,0:T(8,128)(2,1)S(1)}, u32[]{:S(2)}, u32[]{:S(2)}) collective-permute-start(bf16[1024,128]{1,0:T(8,128)(2,1)} %get-tuple-element.46), channel_id=1, source_target_pairs={{0,1},{1,2},{2,3},{3,4},{4,5},{5,6},{6,7},{7,8},{8,9},{9,10},{10,1... | collective-permute-start | bytes 786440 | tf_op jit(solution)/shard_map/ppermute | solution.py:18
  46.8 8.6 %collective-permute-start.1 = (bf16[1024,128]{1,0:T(8,128)(2,1)S(1)}, bf16[1024,128]{1,0:T(8,128)(2,1)S(1)}, u32[]{:S(2)}, u32[]{:S(2)}) collective-permute-start(bf16[1024,128]{1,0:T(8,128)(2,1)S(1)} %get-tuple-element.47), channel_id=1, source_target_pairs={{1,0},{2,1},{3,2},{4,3},{5,4},{6,5},{7,6},{8,7},{9,8},{10,9},{11,1... | collective-permute-start | bytes 786440 | tf_op jit(solution)/shard_map/ppermute | solution.py:21
  57.4 35.4 %copy-start.6 = (f32[64]{0:T(128)S(1)}, f32[64]{0:T(128)}, u32[]{:S(2)}) copy-start(f32[64]{0:T(128)} %get-tuple-element.61) | copy-start | bytes 772
  57.4 35.4 %copy-start.7 = (f32[64]{0:T(128)S(1)}, f32[64]{0:T(128)}, u32[]{:S(2)}) copy-start(f32[64]{0:T(128)} %get-tuple-element.62) | copy-start | bytes 772
  57.4 35.4 %copy-start.8 = (f32[64]{0:T(128)S(1)}, f32[64]{0:T(128)}, u32[]{:S(2)}) copy-start(f32[64]{0:T(128)} %get-tuple-element.63) | copy-start | bytes 772
  57.4 35.4 %copy-start.9 = (f32[64]{0:T(128)S(1)}, f32[64]{0:T(128)}, u32[]{:S(2)}) copy-start(f32[64]{0:T(128)} %get-tuple-element.64) | copy-start | bytes 772
  57.4 35.4 %copy-start.10 = (f32[64]{0:T(128)S(1)}, f32[64]{0:T(128)}, u32[]{:S(2)}) copy-start(f32[64]{0:T(128)} %get-tuple-element.65) | copy-start | bytes 772
  57.4 35.4 %copy-start.11 = (f32[64]{0:T(128)S(1)}, f32[64]{0:T(128)}, u32[]{:S(2)}) copy-start(f32[64]{0:T(128)} %get-tuple-element.66) | copy-start | bytes 772
  57.4 35.4 %copy-start.12 = (f32[64]{0:T(128)S(1)}, f32[64]{0:T(128)}, u32[]{:S(2)}) copy-start(f32[64]{0:T(128)} %get-tuple-element.67) | copy-start | bytes 772
  57.4 35.4 %copy-start.13 = (f32[64]{0:T(128)S(1)}, f32[64]{0:T(128)}, u32[]{:S(2)}) copy-start(f32[64]{0:T(128)} %get-tuple-element.68) | copy-start | bytes 772
  57.4 35.4 %copy-start.14 = (f32[64]{0:T(128)S(1)}, f32[64]{0:T(128)}, u32[]{:S(2)}) copy-start(f32[64]{0:T(128)} %get-tuple-element.69) | copy-start | bytes 772
  57.4 35.4 %copy-start.15 = (f32[64]{0:T(128)S(1)}, f32[64]{0:T(128)}, u32[]{:S(2)}) copy-start(f32[64]{0:T(128)} %get-tuple-element.70) | copy-start | bytes 772
  57.5 35.4 %copy-start.16 = (f32[64]{0:T(128)S(1)}, f32[64]{0:T(128)}, u32[]{:S(2)}) copy-start(f32[64]{0:T(128)} %get-tuple-element.71) | copy-start | bytes 772
  57.5 35.4 %copy-start.17 = (f32[64]{0:T(128)S(1)}, f32[64]{0:T(128)}, u32[]{:S(2)}) copy-start(f32[64]{0:T(128)} %get-tuple-element.72) | copy-start | bytes 772
  57.5 35.4 %copy-start.18 = (f32[64]{0:T(128)S(1)}, f32[64]{0:T(128)}, u32[]{:S(2)}) copy-start(f32[64]{0:T(128)} %get-tuple-element.73) | copy-start | bytes 772
  57.5 35.4 %copy-start.19 = (f32[64]{0:T(128)S(1)}, f32[64]{0:T(128)}, u32[]{:S(2)}) copy-start(f32[64]{0:T(128)} %get-tuple-element.83) | copy-start | bytes 772
  57.5 35.4 %copy-start.20 = (f32[64]{0:T(128)S(1)}, f32[64]{0:T(128)}, u32[]{:S(2)}) copy-start(f32[64]{0:T(128)} %get-tuple-element.84) | copy-start | bytes 772
  57.5 35.4 %copy-start.21 = (f32[64]{0:T(128)S(1)}, f32[64]{0:T(128)}, u32[]{:S(2)}) copy-start(f32[64]{0:T(128)} %get-tuple-element.85) | copy-start | bytes 772
  57.5 35.4 %copy-start.22 = (f32[64]{0:T(128)S(1)}, f32[64]{0:T(128)}, u32[]{:S(2)}) copy-start(f32[64]{0:T(128)} %get-tuple-element.86) | copy-start | bytes 772
  57.5 35.4 %copy-start.23 = (f32[64]{0:T(128)S(1)}, f32[64]{0:T(128)}, u32[]{:S(2)}) copy-start(f32[64]{0:T(128)} %get-tuple-element.87) | copy-start | bytes 772
  57.5 35.4 %copy-start.24 = (f32[64]{0:T(128)S(1)}, f32[64]{0:T(128)}, u32[]{:S(2)}) copy-start(f32[64]{0:T(128)} %get-tuple-element.88) | copy-start | bytes 772
  57.5 35.4 %copy-start.25 = (f32[64]{0:T(128)S(1)}, f32[64]{0:T(128)}, u32[]{:S(2)}) copy-start(f32[64]{0:T(128)} %get-tuple-element.89) | copy-start | bytes 772
  57.6 35.4 %copy-start.26 = (f32[64]{0:T(128)S(1)}, f32[64]{0:T(128)}, u32[]{:S(2)}) copy-start(f32[64]{0:T(128)} %get-tuple-element.90) | copy-start | bytes 772
  57.6 35.4 %copy-start.27 = (f32[64]{0:T(128)S(1)}, f32[64]{0:T(128)}, u32[]{:S(2)}) copy-start(f32[64]{0:T(128)} %get-tuple-element.91) | copy-start | bytes 772
  57.6 35.4 %copy-start.28 = (f32[64]{0:T(128)S(1)}, f32[64]{0:T(128)}, u32[]{:S(2)}) copy-start(f32[64]{0:T(128)} %get-tuple-element.92) | copy-start | bytes 772
  57.6 35.4 %copy-start.29 = (f32[64]{0:T(128)S(1)}, f32[64]{0:T(128)}, u32[]{:S(2)}) copy-start(f32[64]{0:T(128)} %get-tuple-element.93) | copy-start | bytes 772
  57.6 35.4 %copy-start.30 = (f32[64]{0:T(128)S(1)}, f32[64]{0:T(128)}, u32[]{:S(2)}) copy-start(f32[64]{0:T(128)} %get-tuple-element.94) | copy-start | bytes 772
  84.5 7.5 %collective-permute-start.3 = (bf16[15,64]{1,0:T(8,128)(2,1)S(1)}, bf16[15,64]{1,0:T(8,128)(2,1)S(1)}, u32[]{:S(2)}, u32[]{:S(2)}) collective-permute-start(bf16[15,64]{1,0:T(8,128)(2,1)S(1)} %get-tuple-element.54), channel_id=1, source_target_pairs={{1,0},{2,1},{3,2},{4,3},{5,4},{6,5},{7,6},{8,7},{9,8},{10,9},{11,1... | collective-permute-start | bytes 5768 | tf_op jit(solution)/shard_map/ppermute | solution.py:21
  87.5 5.3 %collective-permute-start.2 = (bf16[15,64]{1,0:T(8,128)(2,1)S(1)}, bf16[15,64]{1,0:T(8,128)(2,1)S(1)}, u32[]{:S(2)}, u32[]{:S(2)}) collective-permute-start(bf16[15,64]{1,0:T(8,128)(2,1)S(1)} %get-tuple-element.53), channel_id=1, source_target_pairs={{0,1},{1,2},{2,3},{3,4},{4,5},{5,6},{6,7},{7,8},{8,9},{9,10},{10,1... | collective-permute-start | bytes 5768 | tf_op jit(solution)/shard_map/ppermute | solution.py:18
  93.0 18.1 %copy-start.31 = (f32[64]{0:T(128)S(1)}, f32[64]{0:T(128)}, u32[]{:S(2)}) copy-start(f32[64]{0:T(128)} %param.12) | copy-start | bytes 772
  111.9 8.0 %copy-start.2 = (f32[2048,1]{1,0:T(8,128)S(1)}, f32[2048,1]{1,0:T(8,128)}, u32[]{:S(2)}) copy-start(f32[2048,1]{1,0:T(8,128)} %get-tuple-element.12) | copy-start | bytes 24580
  112.0 9.1 %copy-start.1 = (bf16[2048,64]{1,0:T(8,128)(2,1)S(1)}, bf16[2048,64]{1,0:T(8,128)(2,1)}, u32[]{:S(2)}) copy-start(bf16[2048,64]{1,0:T(8,128)(2,1)} %get-tuple-element.10) | copy-start | bytes 786436
  112.9 8.2 %collective-permute-start.4 = (f32[15,64]{1,0:T(8,128)S(1)}, f32[15,64]{1,0:T(8,128)S(1)}, u32[]{:S(2)}, u32[]{:S(2)}) collective-permute-start(f32[15,64]{1,0:T(8,128)S(1)} %get-tuple-element.42), channel_id=1, source_target_pairs={{1,0},{2,1},{3,2},{4,3},{5,4},{6,5},{7,6},{8,7},{9,8},{10,9},{11,1... | collective-permute-start | bytes 11528 | tf_op jit(solution)/shard_map/ppermute | solution.py:21
  114.8 6.2 %collective-permute-start.5 = (f32[15,64]{1,0:T(8,128)S(1)}, f32[15,64]{1,0:T(8,128)S(1)}, u32[]{:S(2)}, u32[]{:S(2)}) collective-permute-start(f32[15,64]{1,0:T(8,128)S(1)} %get-tuple-element.43), channel_id=1, source_target_pairs={{0,1},{1,2},{2,3},{3,4},{4,5},{5,6},{6,7},{7,8},{8,9},{9,10},{10,1... | collective-permute-start | bytes 11528 | tf_op jit(solution)/shard_map/ppermute | solution.py:18
  169.1 9.7 %copy-start.3 = (bf16[2048,64]{1,0:T(8,128)(2,1)S(1)}, bf16[2048,64]{1,0:T(8,128)(2,1)}, u32[]{:S(2)}) copy-start(bf16[2048,64]{1,0:T(8,128)(2,1)} %get-tuple-element.13) | copy-start | bytes 786436
  171.8 13.0 %copy-start = (f32[4096,64]{1,0:T(8,128)S(1)}, f32[4096,64]{1,0:T(8,128)}, u32[]{:S(2)}) copy-start(f32[4096,64]{1,0:T(8,128)} %get-tuple-element.14) | copy-start | bytes 3145732
  172.7 7.0 %collective-permute-start.6 = (bf16[1024,128]{1,0:T(8,128)(2,1)}, bf16[1024,128]{1,0:T(8,128)(2,1)S(1)}, u32[]{:S(2)}, u32[]{:S(2)}) collective-permute-start(bf16[1024,128]{1,0:T(8,128)(2,1)} %get-tuple-element.40), channel_id=1, source_target_pairs={{0,1},{1,2},{2,3},{3,4},{4,5},{5,6},{6,7},{7,8},{8,9},{9,10},{10,1... | collective-permute-start | bytes 786440 | tf_op jit(solution)/shard_map/ppermute | solution.py:29
  176.0 8.9 %collective-permute-start.7 = (bf16[1024,128]{1,0:T(8,128)(2,1)}, bf16[1024,128]{1,0:T(8,128)(2,1)}, u32[]{:S(2)}, u32[]{:S(2)}) collective-permute-start(bf16[1024,128]{1,0:T(8,128)(2,1)} %get-tuple-element.41), channel_id=1, source_target_pairs={{1,0},{2,1},{3,2},{4,3},{5,4},{6,5},{7,6},{8,7},{9,8},{10,9},{11,1... | collective-permute-start | bytes 786440 | tf_op jit(solution)/shard_map/ppermute | solution.py:29

commit v3 on v2

--- a/solution.py
+++ b/solution.py
@@ -164,6 +164,76 @@
     return (lo, hi)
 
 
+CONV_PAD = 128
+CONV_CHUNK = 256
+
+
+def conv_chunk(x_ref, wt_ref, lo, hi, c0, sign):
+    window = x_ref[:, pl.ds(c0, CONV_CHUNK + 2 * CONV_PAD)]
+    width = window.shape[1]
+    total = jnp.zeros((window.shape[0], CONV_CHUNK), jnp.float32)
+    for tap in range(KERNEL):
+        d = sign * (tap - KERNEL // 2)
+        shifted = pltpu.roll(window, (width - d) % width, 1) if d else window
+        keep = (lo <= d) & (d < hi)
+        total = total + wt_ref[:, tap : tap + 1] * jnp.where(
+            keep, shifted[:, CONV_PAD : CONV_PAD + CONV_CHUNK], 0.0
+        )
+    return total
+
+
+def conv_forward_kernel(x_ref, wt_ref, gain_ref, cot_ref, lo_ref, hi_ref, out_ref, gc_ref):
+    gain = gain_ref[...]
+
+    def body(c, carry):
+        c0 = pl.multiple_of(c * CONV_CHUNK, CONV_CHUNK)
+        cols = pl.ds(c0, CONV_CHUNK)
+        conv_sum = conv_chunk(x_ref, wt_ref, lo_ref[:, cols], hi_ref[:, cols], c0, 1)
+        spread = jnp.sqrt(jnp.mean(conv_sum * conv_sum, axis=0, keepdims=True) + 1e-05)
+        normed = conv_sum / spread
+        pre_act = normed * gain
+        gate = 1.0 / (1.0 + jnp.exp(-pre_act))
+        out_ref[:, cols] = (pre_act * gate).astype(out_ref.dtype)
+        grad_pre = cot_ref[:, cols].astype(jnp.float32) * gate * (1.0 + pre_act * (1.0 - gate))
+        weighted = grad_pre * gain
+        gc_ref[:, cols] = (
+            weighted - normed * jnp.mean(weighted * normed, axis=0, keepdims=True)
+        ) / spread
+        return carry
+
+    lax.fori_loop(0, out_ref.shape[1] // CONV_CHUNK, body, 0)
+
+
+def conv_backward_kernel(y_ref, wt_ref, att_ref, lo_ref, hi_ref, ga_ref, delta_ref):
+    def body(c, carry):
+        c0 = pl.multiple_of(c * CONV_CHUNK, CONV_CHUNK)
+        cols = pl.ds(c0, CONV_CHUNK)
+        grad_sum = conv_chunk(y_ref, wt_ref, lo_ref[:, cols], hi_ref[:, cols], c0, -1)
+        grad_att = grad_sum.astype(ga_ref.dtype)
+        ga_ref[:, cols] = grad_att
+        delta_ref[:, cols] = jnp.sum(
+            grad_att.astype(jnp.float32) * att_ref[:, cols].astype(jnp.float32),
+            axis=0,
+            keepdims=True,
+        )
+        return carry
+
+    lax.fori_loop(0, ga_ref.shape[1] // CONV_CHUNK, body, 0)
+
+
+def padded_rims(block, half):
+    count = lax.axis_size("blk")
+    forward = [(i, i + 1) for i in range(count - 1)]
+    backward = [(target, source) for source, target in forward]
+    low = lax.ppermute(block[:, block.shape[1] - half :], "blk", forward)
+    high = lax.ppermute(block[:, :half], "blk", backward)
+    gap = jnp.zeros((block.shape[0], CONV_PAD - half), jnp.float32)
+    return jnp.concatenate(
+        [gap, low.astype(jnp.float32), block.astype(jnp.float32), high.astype(jnp.float32), gap],
+        axis=1,
+    )
+
+
 def on_device(queries, keys, values, lengths, conv_weight, norm_gain, cotangent):
     rows_in, width = queries.shape
     heads_total = width // HEAD_DIM
@@ -214,42 +284,33 @@
             jax.ShapeDtypeStruct((block_rows, 1), jnp.float32),
         ),
     )(lo_t, hi_t, local_q, k_flat, v_flat, qseg_col, kseg_row)
-    attended_ext = extended(attended, (("blk", 0),), conv_half)
-    conv_sum = jnp.zeros((block_rows, channels), jnp.float32)
-    for tap_index in range(KERNEL):
-        same_seg = (seg_conv[tap_index : tap_index + block_rows] == seg_own)[:, None]
-        conv_sum = conv_sum + conv_weight[tap_index][None, :] * jnp.where(
-            same_seg, attended_ext[tap_index : tap_index + block_rows].astype(jnp.float32), 0.0
-        )
-    grouped = conv_sum.reshape(block_rows, heads_here, HEAD_DIM)
-    spread = jnp.sqrt(jnp.mean(grouped * grouped, axis=2, keepdims=True) + 1e-05)
-    normed = grouped / spread
-    pre_act = normed.reshape(block_rows, channels) * norm_gain[None, :]
-    sigmoid_gate = jax.nn.sigmoid(pre_act)
-    conv_out = (pre_act * sigmoid_gate).astype(jnp.bfloat16)
-    grad_pre = (
-        cotangent.astype(jnp.float32).T * sigmoid_gate * (1.0 + pre_act * (1.0 - sigmoid_gate))
-    )
-    weighted = (grad_pre * norm_gain[None, :]).reshape(block_rows, heads_here, HEAD_DIM)
-    grad_conv = (
-        (weighted - normed * jnp.mean(weighted * normed, axis=2, keepdims=True)) / spread
-    ).reshape(block_rows, channels)
-    grad_ext = extended(grad_conv, (("blk", 0),), conv_half)
-    grad_sum = jnp.zeros((block_rows, channels), jnp.float32)
-    for tap_index in range(KERNEL):
-        offset = 2 * conv_half - tap_index
-        same_seg = (seg_conv[offset : offset + block_rows] == seg_own)[:, None]
-        grad_sum = grad_sum + conv_weight[tap_index][None, :] * jnp.where(
-            same_seg, grad_ext[offset : offset + block_rows], 0.0
-        )
-    grad_attended = grad_sum.astype(jnp.bfloat16)
-    row_delta = jnp.sum(
-        (grad_attended.astype(jnp.float32) * attended.astype(jnp.float32)).reshape(
-            block_rows, heads_here, HEAD_DIM
+    ends = jnp.cumsum(lengths)
+    seg_at = jnp.clip(seg_own, 0, lengths.shape[0] - 1)
+    frame_at = first_frame + jnp.arange(block_rows, dtype=jnp.int32)
+    lo_off = (ends[seg_at] - lengths[seg_at] - frame_at)[None, :].astype(jnp.int32)
+    hi_off = (ends[seg_at] - frame_at)[None, :].astype(jnp.int32)
+    weight_t = conv_weight.T
+    att_t = attended.T
+    conv_out_t, grad_conv_t = vmem_call(
+        conv_forward_kernel,
+        0,
+        6,
+        (
+            jax.ShapeDtypeStruct((HEAD_DIM, block_rows), jnp.bfloat16),
+            jax.ShapeDtypeStruct((HEAD_DIM, block_rows), jnp.float32),
         ),
-        axis=2,
-    )
-    grad_heads = grad_attended.reshape(block_rows, heads_here, HEAD_DIM)
+    )(padded_rims(att_t, conv_half), weight_t, norm_gain[:, None], cotangent, lo_off, hi_off)
+    grad_att_t, delta_row = vmem_call(
+        conv_backward_kernel,
+        0,
+        5,
+        (
+            jax.ShapeDtypeStruct((HEAD_DIM, block_rows), jnp.bfloat16),
+            jax.ShapeDtypeStruct((1, block_rows), jnp.float32),
+        ),
+    )(padded_rims(grad_conv_t, conv_half), weight_t, att_t, lo_off, hi_off)
+    grad_attended = grad_att_t.T
+    row_delta = delta_row.T
 
     grad_q, dk_ext, dv_ext = vmem_call(
         backward_kernel,
@@ -285,7 +346,7 @@
     grad_queries = grad_q.reshape(block_rows, channels)
     grad_keys = key_grads[:, :channels].astype(jnp.bfloat16)
     grad_values = key_grads[:, channels:].astype(jnp.bfloat16)
-    return (conv_out.T, grad_queries.T, grad_keys.T, grad_values.T)
+    return (conv_out_t, grad_queries.T, grad_keys.T, grad_values.T)
 
 
 def solution(mesh):

time: 190 us -> 248 us (1.31)
  the two profiles are of different devices: /device:TPU:9 before, /device:TPU:29 now
where the time goes in v3:
time: 248 us; the launch traced here: 246 us
  other arithmetic  88.7 us (36%)
  Pallas kernels  70.7 us (29%)
  starting transfers between devices  48.1 us (19%)
  local copies, waits for them, and re-layouts  30.2 us (12%)
  waiting for transfers between devices  7.5 us (3%)
    gather x1, other arithmetic, on_device(): lengths[seg_at]  40.2 us
    gather x1, other arithmetic, on_device(): ends[seg_at] - lengths[seg_at] - frame_at  39.9 us
    pallas_call x1, Pallas kernels, on_device(): vmem_call(backward_kernel, 2, 9, (jax.ShapeDtypeStruct((block_rows, HEAD_...  25.1 us
    pallas_call x1, Pallas kernels, on_device(): vmem_call(forward_kernel, 2, 5, (jax.ShapeDtypeStruct((block_rows, HEAD_D...  20.8 us
    ppermute x2, starting transfers between devices, passed_along(): return lax.ppermute(block, axis, route)  13.2 us
    ppermute x2, starting transfers between devices, padded_rims(): low = lax.ppermute(block[:, block.shape[1] - half:], 'blk', forward)  13 us
    pallas_call x1, Pallas kernels, on_device(): vmem_call(conv_forward_kernel, 0, 6, (jax.ShapeDtypeStruct((HEAD_DIM, blo...  12.8 us
    pallas_call x1, Pallas kernels, on_device(): vmem_call(conv_backward_kernel, 0, 5, (jax.ShapeDtypeStruct((HEAD_DIM, bl...  12 us
  transfers between devices with their start and end apart: 9, of which 4 were waited for; matrix products, arithmetic and copies ran while one was open for 39% of the time, Pallas kernels for 0%

profile of v3, /device:TPU:29, one launch (start us, length us, event | category | flops | bytes accessed | tf_op | source)
XLA Modules:
  0.0 246.2 jit_solution(11403010761460400878)
XLA Ops:
  0.6 1.1 copy.39
  1.8 1.1 copy.40
  2.9 1.1 copy.41
  4.1 1.0 copy.42
  5.1 10.9 %all-to-all-start = ((bf16[128,16,192]{0,2,1:T(8,128)(2,1)}), bf16[128,16,192]{0,2,1:T(8,128)(2,1)S(1)}, u32[]{:S(2)}, u32[]{:S(2)}) async-start(bf16[128,16,192]{0,2,1:T(8,128)(2,1)} %bitcast.4), calls=%async_computation | async-start | bytes 1572864 | tf_op jit(solution)/shard_map/all_to_all | solution.py:243
  16.0 0.7 fusion.20
  16.6 0.7 fusion.18
  17.4 0.7 fusion.17
  18.1 0.7 fusion.19
  19.8 0.7 fusion.15
  20.4 0.7 fusion.13
  21.1 0.7 fusion.14
  22.0 40.2 %select_select_fusion = (s32[2048]{0:T(1024)S(1)}, pred[2048]{0:T(1024)(128)(4,1)S(1)}, pred[2048]{0:T(1024)(128)(4,1)S(1)}, pred[2048]{0:T(1024)(128)(4,1)S(1)}...) fusion(s32[]{:T(128)} %bitcast.79, s32[]{:T(128)} %bitcast.80, ...), kind=kLoop, calls=%fused_computation.22 | loop fusion | flops 274432 | bytes 162048 | tf_op jit(solution)/shard_map/gather | solution.py:290
  62.4 39.9 %select_select_fusion.1 = s32[2048]{0:T(1024)S(1)} fusion(pred[2048]{0:T(1024)(128)(4,1)S(1)} %get-tuple-element.99, pred[2048]{0:T(1024)(128)(4,1)S(1)} %get-tuple-element.98, pred[2048]{0:T(1024)(128)(4,1)S(1)} %get-tuple-element.97, pred[2048]{0:T(1024)(128)(4,1)S(1)} %get-tuple-element.96, pred[2048]{0:T(1024)(128)(4,1)S(1)} %get-tuple-element.95, ...), kind=kLoop, calls=%fused_computation.23 | loop fusion | flops 129024 | bytes 137472 | tf_op jit(solution)/shard_map/gather | solution.py:290
  105.4 4.1 %collective-permute-start = (bf16[1024,128]{1,0:T(8,128)(2,1)S(1)}, bf16[1024,128]{1,0:T(8,128)(2,1)S(1)}, u32[]{:S(2)}, u32[]{:S(2)}) collective-permute-start(bf16[1024,128]{1,0:T(8,128)(2,1)S(1)} %get-tuple-element.107), channel_id=1, source_target_pairs={{0,1},{1,2},{2,3},{3,4},{4,5},{5,6},{6,7},{7,8},{8,9},{9,10},{10,1... | collective-permute-start | bytes 786440 | tf_op jit(solution)/shard_map/ppermute | solution.py:18
  109.5 1.9 collective-permute-start.1
  111.5 0.7 copy.49
  112.2 0.7 copy.50.gain_ref
  114.2 1.3 copy.47.qseg_ref
  116.1 1.0 copy.57
  117.2 1.0 collective-permute-done.1
  118.4 1.7 fusion.9
  120.2 20.8 %shard_map.102 = (bf16[2048,64]{1,0:T(8,128)(2,1)}, f32[2048,1]{1,0:T(8,128)}, f32[2048,1]{1,0:T(8,128)}) custom-call(s32[8]{0:T(128)} %get-tuple-element.102.lo_ref, s32[8]{0:T(128)} %get-tuple-element.101.hi_ref, bf16[2048,64]{1,0:T(8,128)(2,1)} %bitcast.158, bf16[4096,64]{1,0:T(8,128)(2,1)} %get-tuple-element.106.k_ref, ...), custom_call_target="tpu_custom_call" | custom-call | tf_op jit(solution)/shard_map/pallas_call | solution.py:277
  141.0 1.3 copy.48
  142.4 1.9 collective-permute-start.3
  144.3 9.1 %collective-permute-start.2 = (bf16[64,15]{1,0:T(8,128)(2,1)S(1)}, bf16[64,15]{1,0:T(8,128)(2,1)S(1)}, u32[]{:S(2)}, u32[]{:S(2)}) collective-permute-start(bf16[64,15]{1,0:T(8,128)(2,1)S(1)} %get-tuple-element.117), channel_id=1, source_target_pairs={{0,1},{1,2},{2,3},{3,4},{4,5},{5,6},{6,7},{7,8},{8,9},{9,10},{10,1... | collective-permute-start | bytes 5768 | tf_op jit(solution)/shard_map/ppermute | solution.py:228
  153.4 0.8 collective-permute-done.2
  154.2 0.9 concatenate.23.x_ref
  155.1 12.8 %shard_map.103 = (bf16[64,2048]{1,0:T(8,128)(2,1)}, f32[64,2048]{1,0:T(8,128)}) custom-call(f32[64,2304]{1,0:T(8,128)} %concatenate.23.x_ref, f32[64,31]{1,0:T(8,128)} %bitcast.169, f32[64,1]{1,0:T(8,128)} %copy.50.gain_ref, bf16[64,2048]{1,0:T(8,128)(2,1)} %cot_ref.1, s32[1,2048]{1,0:T(1,128)} %get-tuple-element.183.lo_ref, s32[1,2048]{1,0:T(1,128)} %get-tuple-element.182.hi_ref), custom_call_target="tpu_custom_call" | custom-call | tf_op jit(solution)/shard_map/pallas_call | solution.py:294
  167.9 0.9 fusion.11
  168.8 3.1 %collective-permute-start.5 = (f32[64,15]{1,0:T(8,128)S(1)}, f32[64,15]{1,0:T(8,128)S(1)}, u32[]{:S(2)}, u32[]{:S(2)}) collective-permute-start(f32[64,15]{1,0:T(8,128)S(1)} %get-tuple-element.114), channel_id=1, source_target_pairs={{1,0},{2,1},{3,2},{4,3},{5,4},{6,5},{7,6},{8,7},{9,8},{10,9},{11,1... | collective-permute-start | bytes 11528 | tf_op jit(solution)/shard_map/ppermute | solution.py:229
  171.9 3.9 %collective-permute-start.4 = (f32[64,15]{1,0:T(8,128)S(1)}, f32[64,15]{1,0:T(8,128)S(1)}, u32[]{:S(2)}, u32[]{:S(2)}) collective-permute-start(f32[64,15]{1,0:T(8,128)S(1)} %get-tuple-element.115), channel_id=1, source_target_pairs={{0,1},{1,2},{2,3},{3,4},{4,5},{5,6},{6,7},{7,8},{8,9},{9,10},{10,1... | collective-permute-start | bytes 11528 | tf_op jit(solution)/shard_map/ppermute | solution.py:228
  175.8 1.2 broadcast_divide_fusion.il_ref
  177.0 0.9 concatenate.24.y_ref
  177.9 12.0 %shard_map.104 = (bf16[64,2048]{1,0:T(8,128)(2,1)}, f32[1,2048]{1,0:T(1,128)}) custom-call(f32[64,2304]{1,0:T(8,128)} %concatenate.24.y_ref, f32[64,31]{1,0:T(8,128)} %bitcast.170, bf16[64,2048]{1,0:T(8,128)(2,1)} %bitcast.162, s32[1,2048]{1,0:T(1,128)} %get-tuple-element.183.lo_ref, s32[1,2048]{1,0:T(1,128)} %get-tuple-element.182.hi_ref), custom_call_target="tpu_custom_call" | custom-call | tf_op jit(solution)/shard_map/pallas_call | solution.py:303
  190.0 2.0 copy.51
  191.9 2.1 copy.53.d_ref
  194.0 25.1 %shard_map.105 = (bf16[2048,64]{1,0:T(8,128)(2,1)}, f32[4096,64]{1,0:T(8,128)}, f32[4096,64]{1,0:T(8,128)}) custom-call(s32[8]{0:T(128)} %get-tuple-element.102.lo_ref, s32[8]{0:T(128)} %get-tuple-element.101.hi_ref, bf16[2048,64]{1,0:T(8,128)(2,1)} %bitcast.159, bf16[4096,64]{1,0:T(8,128)(2,1)} %get-tuple-element.106.k_ref, ...), custom_call_target="tpu_custom_call" | custom-call | tf_op jit(solution)/shard_map/pallas_call | solution.py:315
  219.1 2.8 %maximum_convert_fusion = bf16[4096,128]{1,0:T(8,128)(2,1)S(1)} fusion(f32[4096,64]{1,0:T(8,128)} %get-tuple-element.23, f32[4096,64]{1,0:T(8,128)} %get-tuple-element.22), kind=kLoop, calls=%fused_computation.2 | loop fusion | flops 2097152 | bytes 3145728 | tf_op jit(solution)/shard_map/convert.4
  222.0 0.7 fusion.8
  222.7 11.2 %collective-permute-start.6 = (bf16[1024,128]{1,0:T(8,128)(2,1)}, bf16[1024,128]{1,0:T(8,128)(2,1)S(1)}, u32[]{:S(2)}, u32[]{:S(2)}) collective-permute-start(bf16[1024,128]{1,0:T(8,128)(2,1)} %get-tuple-element.103), channel_id=1, source_target_pairs={{0,1},{1,2},{2,3},{3,4},{4,5},{5,6},{6,7},{7,8},{8,9},{9,10},{10,1... | collective-permute-start | bytes 786440 | tf_op jit(solution)/shard_map/ppermute | solution.py:29
  234.0 1.9 collective-permute-start.7
  235.9 0.9 copy.54
  236.8 0.8 collective-permute-done.6
  237.6 4.9 %collective-permute-done.7 = bf16[1024,128]{1,0:T(8,128)(2,1)S(1)} collective-permute-done((bf16[1024,128]{1,0:T(8,128)(2,1)S(1)}, bf16[1024,128]{1,0:T(8,128)(2,1)S(1)}, u32[]{:S(2)}, u32[]{:S(2)}) %collective-permute-start.7) | collective-permute-done | bytes 262176 | tf_op jit(solution)/shard_map/ppermute | solution.py:29
  242.6 1.6 fusion.2
  244.4 0.9 copy.56
  245.3 0.9 copy.55
  (52 shorter events, 7.0 us)
Async XLA Ops:
  4.0 11.9 %copy-start.2 = (s32[64]{0:T(128)S(1)}, s32[64]{0:T(128)}, u32[]{:S(2)}) copy-start(s32[64]{0:T(128)} %param.10) | copy-start | bytes 772
  5.1 98.5 %all-to-all-start = ((bf16[128,16,192]{0,2,1:T(8,128)(2,1)}), bf16[128,16,192]{0,2,1:T(8,128)(2,1)S(1)}, u32[]{:S(2)}, u32[]{:S(2)}) async-start(bf16[128,16,192]{0,2,1:T(8,128)(2,1)} %bitcast.4), calls=%async_computation | async-start | bytes 1572864 | tf_op jit(solution)/shard_map/all_to_all | solution.py:243
  104.4 7.0 %copy-start.6 = (f32[31,64]{1,0:T(8,128)S(1)}, f32[31,64]{1,0:T(8,128)}, u32[]{:S(2)}) copy-start(f32[31,64]{1,0:T(8,128)} %param.11) | copy-start | bytes 23812
  104.5 7.7 %copy-start.7 = (f32[64]{0:T(128)S(1)}, f32[64]{0:T(128)}, u32[]{:S(2)}) copy-start(f32[64]{0:T(128)} %param.12) | copy-start | bytes 772
  105.4 11.8 %collective-permute-start = (bf16[1024,128]{1,0:T(8,128)(2,1)S(1)}, bf16[1024,128]{1,0:T(8,128)(2,1)S(1)}, u32[]{:S(2)}, u32[]{:S(2)}) collective-permute-start(bf16[1024,128]{1,0:T(8,128)(2,1)S(1)} %get-tuple-element.107), channel_id=1, source_target_pairs={{0,1},{1,2},{2,3},{3,4},{4,5},{5,6},{6,7},{7,8},{8,9},{9,10},{10,1... | collective-permute-start | bytes 786440 | tf_op jit(solution)/shard_map/ppermute | solution.py:18
  109.5 8.6 %collective-permute-start.1 = (bf16[1024,128]{1,0:T(8,128)(2,1)S(1)}, bf16[1024,128]{1,0:T(8,128)(2,1)S(1)}, u32[]{:S(2)}, u32[]{:S(2)}) collective-permute-start(bf16[1024,128]{1,0:T(8,128)(2,1)S(1)} %get-tuple-element.108), channel_id=1, source_target_pairs={{1,0},{2,1},{3,2},{4,3},{5,4},{6,5},{7,6},{8,7},{9,8},{10,9},{11,1... | collective-permute-start | bytes 786440 | tf_op jit(solution)/shard_map/ppermute | solution.py:21
  141.0 34.9 %copy-start.3 = (f32[2048,1]{1,0:T(8,128)S(1)}, f32[2048,1]{1,0:T(8,128)}, u32[]{:S(2)}) copy-start(f32[2048,1]{1,0:T(8,128)} %get-tuple-element.19) | copy-start | bytes 24580
  142.3 34.7 %copy-start.1 = (bf16[2048,64]{0,1:T(8,128)(2,1)}, bf16[2048,64]{0,1:T(8,128)(2,1)S(1)}, u32[]{:S(2)}) copy-start(bf16[2048,64]{0,1:T(8,128)(2,1)S(1)} %copy.48) | copy-start | bytes 786436
  142.4 11.0 %collective-permute-start.3 = (bf16[64,15]{1,0:T(8,128)(2,1)S(1)}, bf16[64,15]{1,0:T(8,128)(2,1)S(1)}, u32[]{:S(2)}, u32[]{:S(2)}) collective-permute-start(bf16[64,15]{1,0:T(8,128)(2,1)S(1)} %get-tuple-element.116), channel_id=1, source_target_pairs={{1,0},{2,1},{3,2},{4,3},{5,4},{6,5},{7,6},{8,7},{9,8},{10,9},{11,1... | collective-permute-start | bytes 5768 | tf_op jit(solution)/shard_map/ppermute | solution.py:229
  144.3 9.9 %collective-permute-start.2 = (bf16[64,15]{1,0:T(8,128)(2,1)S(1)}, bf16[64,15]{1,0:T(8,128)(2,1)S(1)}, u32[]{:S(2)}, u32[]{:S(2)}) collective-permute-start(bf16[64,15]{1,0:T(8,128)(2,1)S(1)} %get-tuple-element.117), channel_id=1, source_target_pairs={{0,1},{1,2},{2,3},{3,4},{4,5},{5,6},{6,7},{7,8},{8,9},{9,10},{10,1... | collective-permute-start | bytes 5768 | tf_op jit(solution)/shard_map/ppermute | solution.py:228
  167.9 9.1 %copy-start.4 = (f32[64,2048]{1,0:T(8,128)S(1)}, f32[64,2048]{1,0:T(8,128)}, u32[]{:S(2)}) copy-start(f32[64,2048]{1,0:T(8,128)} %get-tuple-element.16) | copy-start | bytes 1572868
  168.8 8.2 %collective-permute-start.5 = (f32[64,15]{1,0:T(8,128)S(1)}, f32[64,15]{1,0:T(8,128)S(1)}, u32[]{:S(2)}, u32[]{:S(2)}) collective-permute-start(f32[64,15]{1,0:T(8,128)S(1)} %get-tuple-element.114), channel_id=1, source_target_pairs={{1,0},{2,1},{3,2},{4,3},{5,4},{6,5},{7,6},{8,7},{9,8},{10,9},{11,1... | collective-permute-start | bytes 11528 | tf_op jit(solution)/shard_map/ppermute | solution.py:229
  171.9 5.1 %collective-permute-start.4 = (f32[64,15]{1,0:T(8,128)S(1)}, f32[64,15]{1,0:T(8,128)S(1)}, u32[]{:S(2)}, u32[]{:S(2)}) collective-permute-start(f32[64,15]{1,0:T(8,128)S(1)} %get-tuple-element.115), channel_id=1, source_target_pairs={{0,1},{1,2},{2,3},{3,4},{4,5},{5,6},{6,7},{7,8},{8,9},{9,10},{10,1... | collective-permute-start | bytes 11528 | tf_op jit(solution)/shard_map/ppermute | solution.py:228
  219.1 16.8 %copy-start.5 = (bf16[2048,64]{1,0:T(8,128)(2,1)S(1)}, bf16[2048,64]{1,0:T(8,128)(2,1)}, u32[]{:S(2)}) copy-start(bf16[2048,64]{1,0:T(8,128)(2,1)} %get-tuple-element.21) | copy-start | bytes 786436
  219.1 23.4 %copy-start = (f32[4096,64]{1,0:T(8,128)S(1)}, f32[4096,64]{1,0:T(8,128)}, u32[]{:S(2)}) copy-start(f32[4096,64]{1,0:T(8,128)} %get-tuple-element.22) | copy-start | bytes 3145732
  222.7 14.9 %collective-permute-start.6 = (bf16[1024,128]{1,0:T(8,128)(2,1)}, bf16[1024,128]{1,0:T(8,128)(2,1)S(1)}, u32[]{:S(2)}, u32[]{:S(2)}) collective-permute-start(bf16[1024,128]{1,0:T(8,128)(2,1)} %get-tuple-element.103), channel_id=1, source_target_pairs={{0,1},{1,2},{2,3},{3,4},{4,5},{5,6},{6,7},{7,8},{8,9},{9,10},{10,1... | collective-permute-start | bytes 786440 | tf_op jit(solution)/shard_map/ppermute | solution.py:29
  234.0 8.6 %collective-permute-start.7 = (bf16[1024,128]{1,0:T(8,128)(2,1)S(1)}, bf16[1024,128]{1,0:T(8,128)(2,1)S(1)}, u32[]{:S(2)}, u32[]{:S(2)}) collective-permute-start(bf16[1024,128]{1,0:T(8,128)(2,1)S(1)} %get-tuple-element.104), channel_id=1, source_target_pairs={{1,0},{2,1},{3,2},{4,3},{5,4},{6,5},{7,6},{8,7},{9,8},{10,9},{11,1... | collective-permute-start | bytes 786440 | tf_op jit(solution)/shard_map/ppermute | solution.py:29

commit v4 on v3

--- a/solution.py
+++ b/solution.py
@@ -152,13 +152,20 @@
     )
 
 
-def tile_ranges(lengths, seg_own, base, ext_rows):
+def segment_bounds(lengths, frames):
     ends = jnp.cumsum(lengths)
     starts = ends - lengths
-    first = seg_own[::TILE_Q]
-    last = seg_own[TILE_Q - 1 :: TILE_Q]
-    lo = (starts[first] - base) // TILE_K
-    hi = (ends[last] - base + TILE_K - 1) // TILE_K
+    seg_start = jnp.max(jnp.where(starts[None, :] <= frames[:, None], starts[None, :], 0), axis=1)
+    big = jnp.iinfo(jnp.int32).max
+    seg_end = jnp.min(jnp.where(ends[None, :] > frames[:, None], ends[None, :], big), axis=1)
+    return (seg_start, jnp.minimum(seg_end, ends[-1]))
+
+
+def tile_ranges(lengths, base, ext_rows, block_rows):
+    frames = base + (ext_rows - block_rows) // 2 + jnp.arange(block_rows, dtype=jnp.int32)
+    seg_start, seg_end = segment_bounds(lengths, frames)
+    lo = (seg_start[::TILE_Q] - base) // TILE_K
+    hi = (seg_end[TILE_Q - 1 :: TILE_Q] - base + TILE_K - 1) // TILE_K
     lo = jnp.clip(lo, 0, ext_rows // TILE_K).astype(jnp.int32)
     hi = jnp.clip(hi, lo, ext_rows // TILE_K).astype(jnp.int32)
     return (lo, hi)
@@ -269,7 +276,7 @@
     starts = jnp.arange(block_count, dtype=jnp.int32) * rows_q
 
     assert heads_here == 1
-    lo_t, hi_t = tile_ranges(lengths, seg_own, first_frame - maxlen, block_rows + 2 * maxlen)
+    lo_t, hi_t = tile_ranges(lengths, first_frame - maxlen, block_rows + 2 * maxlen, block_rows)
     qseg_col = seg_own[:, None].astype(jnp.int32)
     kseg_row = seg_ext[None, :].astype(jnp.int32)
     k_flat = k_ext.reshape(-1, HEAD_DIM)
@@ -284,11 +291,10 @@
             jax.ShapeDtypeStruct((block_rows, 1), jnp.float32),
         ),
     )(lo_t, hi_t, local_q, k_flat, v_flat, qseg_col, kseg_row)
-    ends = jnp.cumsum(lengths)
-    seg_at = jnp.clip(seg_own, 0, lengths.shape[0] - 1)
     frame_at = first_frame + jnp.arange(block_rows, dtype=jnp.int32)
-    lo_off = (ends[seg_at] - lengths[seg_at] - frame_at)[None, :].astype(jnp.int32)
-    hi_off = (ends[seg_at] - frame_at)[None, :].astype(jnp.int32)
+    seg_start, seg_end = segment_bounds(lengths, frame_at)
+    lo_off = (seg_start - frame_at)[None, :].astype(jnp.int32)
+    hi_off = (seg_end - frame_at)[None, :].astype(jnp.int32)
     weight_t = conv_weight.T
     att_t = attended.T
     conv_out_t, grad_conv_t = vmem_call(

time: 248 us -> 183 us (0.74)
  the two profiles are of different devices: /device:TPU:29 before, /device:TPU:9 now
where the time goes in v4:
time: 183 us
  Pallas kernels  84.6 us (46%)
  starting transfers between devices  36.6 us (20%)
  waiting for transfers between devices  27.2 us (15%)
  local copies, waits for them, and re-layouts  23.9 us (13%)
  other arithmetic  9.44 us (5%)
    pallas_call x1, Pallas kernels, on_device(): vmem_call(backward_kernel, 2, 9, (jax.ShapeDtypeStruct((block_rows, HEAD_...  32.5 us
    pallas_call x1, Pallas kernels, on_device(): vmem_call(forward_kernel, 2, 5, (jax.ShapeDtypeStruct((block_rows, HEAD_D...  27.2 us
    all_to_all x1, waiting for transfers between devices, on_device(): lax.all_to_all(stacked, 'uly', split_axis=1, concat_axis=0, tiled=True)  19.1 us
    pallas_call x1, Pallas kernels, on_device(): vmem_call(conv_forward_kernel, 0, 6, (jax.ShapeDtypeStruct((HEAD_DIM, blo...  12.8 us
    pallas_call x1, Pallas kernels, on_device(): vmem_call(conv_backward_kernel, 0, 5, (jax.ShapeDtypeStruct((HEAD_DIM, bl...  12 us
    all_to_all x1, starting transfers between devices, on_device(): lax.all_to_all(stacked, 'uly', split_axis=1, concat_axis=0, tiled=True)  10 us
    ppermute x2, starting transfers between devices, padded_rims(): low = lax.ppermute(block[:, block.shape[1] - half:], 'blk', forward)  9.64 us
    unnamed x26, local copies, waits for them, and re-layouts  8.38 us
  transfers between devices with their start and end apart: 9, of which 5 were waited for; matrix products, arithmetic and copies ran while one was open for 5% of the time, Pallas kernels for 0%

profile of v4, /device:TPU:9, one launch (start us, length us, event | category | flops | bytes accessed | tf_op | source)
XLA Modules:
  0.0 182.7 jit_solution(2722119783757564011)
XLA Ops:
  0.6 1.1 copy.39
  1.8 1.1 copy.40
  2.9 1.1 copy.41
  4.1 0.9 copy.42
  5.1 10.0 %all-to-all-start = ((bf16[128,16,192]{0,2,1:T(8,128)(2,1)}), bf16[128,16,192]{0,2,1:T(8,128)(2,1)S(1)}, u32[]{:S(2)}, u32[]{:S(2)}) async-start(bf16[128,16,192]{0,2,1:T(8,128)(2,1)} %bitcast.5), calls=%async_computation | async-start | bytes 1572864 | tf_op jit(solution)/shard_map/all_to_all | solution.py:250
  15.3 0.5 slice.86
  16.4 0.7 broadcast_minimum_fusion
  17.1 0.6 fusion.4
  17.7 0.6 and_select_fusion.kseg_ref
  18.3 19.1 %all-to-all-done = bf16[128,16,192]{0,2,1:T(8,128)(2,1)S(1)} async-done(((bf16[128,16,192]{0,2,1:T(8,128)(2,1)}), bf16[128,16,192]{0,2,1:T(8,128)(2,1)S(1)}, u32[]{:S(2)}, u32[]{:S(2)}) %all-to-all-start) | async-done | bytes 786464 | tf_op jit(solution)/shard_map/all_to_all | solution.py:250
  37.4 0.5 copy.43
  37.9 0.3 reshape.97
  38.9 0.3 fusion.3
  39.2 6.9 %collective-permute-start = (bf16[1024,128]{1,0:T(8,128)(2,1)S(1)}, bf16[1024,128]{1,0:T(8,128)(2,1)S(1)}, u32[]{:S(2)}, u32[]{:S(2)}) collective-permute-start(bf16[1024,128]{1,0:T(8,128)(2,1)S(1)} %get-tuple-element.44), channel_id=1, source_target_pairs={{0,1},{1,2},{2,3},{3,4},{4,5},{5,6},{6,7},{7,8},{8,9},{9,10},{10,1... | collective-permute-start | bytes 786440 | tf_op jit(solution)/shard_map/ppermute | solution.py:18
  46.1 1.9 %collective-permute-start.1 = (bf16[1024,128]{1,0:T(8,128)(2,1)S(1)}, bf16[1024,128]{1,0:T(8,128)(2,1)S(1)}, u32[]{:S(2)}, u32[]{:S(2)}) collective-permute-start(bf16[1024,128]{1,0:T(8,128)(2,1)S(1)} %get-tuple-element.45), channel_id=1, source_target_pairs={{1,0},{2,1},{3,2},{4,3},{5,4},{6,5},{7,6},{8,7},{9,8},{10,9},{11,1... | collective-permute-start | bytes 786440 | tf_op jit(solution)/shard_map/ppermute | solution.py:21
  48.2 0.7 copy.49
  48.9 0.7 copy.50.gain_ref
  49.7 1.4 copy.47.qseg_ref
  51.0 0.6 maximum_minimum_fusion
  51.6 1.0 copy.57
  52.6 2.1 %collective-permute-done.1 = bf16[1024,128]{1,0:T(8,128)(2,1)S(1)} collective-permute-done((bf16[1024,128]{1,0:T(8,128)(2,1)S(1)}, bf16[1024,128]{1,0:T(8,128)(2,1)S(1)}, u32[]{:S(2)}, u32[]{:S(2)}) %collective-permute-start.1) | collective-permute-done | bytes 262176 | tf_op jit(solution)/shard_map/ppermute | solution.py:21
  54.7 0.3 pad_maximum_fusion
  55.0 1.7 fusion.9
  56.7 27.2 %shard_map.102 = (bf16[2048,64]{1,0:T(8,128)(2,1)}, f32[2048,1]{1,0:T(8,128)}, f32[2048,1]{1,0:T(8,128)}) custom-call(s32[8]{0:T(128)} %get-tuple-element.39.lo_ref, s32[8]{0:T(128)} %get-tuple-element.38.hi_ref, bf16[2048,64]{1,0:T(8,128)(2,1)} %bitcast.31, bf16[4096,64]{1,0:T(8,128)(2,1)} %get-tuple-element.43.k_ref, ...), custom_call_target="tpu_custom_call" | custom-call | tf_op jit(solution)/shard_map/pallas_call | solution.py:284
  83.9 1.3 copy.48
  85.3 1.9 %collective-permute-start.3 = (bf16[64,15]{1,0:T(8,128)(2,1)S(1)}, bf16[64,15]{1,0:T(8,128)(2,1)S(1)}, u32[]{:S(2)}, u32[]{:S(2)}) collective-permute-start(bf16[64,15]{1,0:T(8,128)(2,1)S(1)} %get-tuple-element.53), channel_id=1, source_target_pairs={{1,0},{2,1},{3,2},{4,3},{5,4},{6,5},{7,6},{8,7},{9,8},{10,9},{11,1... | collective-permute-start | bytes 5768 | tf_op jit(solution)/shard_map/ppermute | solution.py:236
  87.2 4.5 %collective-permute-start.2 = (bf16[64,15]{1,0:T(8,128)(2,1)S(1)}, bf16[64,15]{1,0:T(8,128)(2,1)S(1)}, u32[]{:S(2)}, u32[]{:S(2)}) collective-permute-start(bf16[64,15]{1,0:T(8,128)(2,1)S(1)} %get-tuple-element.54), channel_id=1, source_target_pairs={{0,1},{1,2},{2,3},{3,4},{4,5},{5,6},{6,7},{7,8},{8,9},{9,10},{10,1... | collective-permute-start | bytes 5768 | tf_op jit(solution)/shard_map/ppermute | solution.py:235
  91.8 0.8 collective-permute-done.2
  92.6 0.9 concatenate.23.x_ref
  93.6 12.8 %shard_map.103 = (bf16[64,2048]{1,0:T(8,128)(2,1)}, f32[64,2048]{1,0:T(8,128)}) custom-call(f32[64,2304]{1,0:T(8,128)} %concatenate.23.x_ref, f32[64,31]{1,0:T(8,128)} %bitcast.41, f32[64,1]{1,0:T(8,128)} %copy.50.gain_ref, bf16[64,2048]{1,0:T(8,128)(2,1)} %cot_ref.1, s32[1,2048]{1,0:T(1,128)} %get-tuple-element.56.lo_ref, s32[1,2048]{1,0:T(1,128)} %get-tuple-element.55.hi_ref), custom_call_target="tpu_custom_call" | custom-call | tf_op jit(solution)/shard_map/pallas_call | solution.py:300
  106.3 0.9 fusion.11
  107.2 1.9 %collective-permute-start.5 = (f32[64,15]{1,0:T(8,128)S(1)}, f32[64,15]{1,0:T(8,128)S(1)}, u32[]{:S(2)}, u32[]{:S(2)}) collective-permute-start(f32[64,15]{1,0:T(8,128)S(1)} %get-tuple-element.51), channel_id=1, source_target_pairs={{1,0},{2,1},{3,2},{4,3},{5,4},{6,5},{7,6},{8,7},{9,8},{10,9},{11,1... | collective-permute-start | bytes 11528 | tf_op jit(solution)/shard_map/ppermute | solution.py:236
  109.2 5.1 %collective-permute-start.4 = (f32[64,15]{1,0:T(8,128)S(1)}, f32[64,15]{1,0:T(8,128)S(1)}, u32[]{:S(2)}, u32[]{:S(2)}) collective-permute-start(f32[64,15]{1,0:T(8,128)S(1)} %get-tuple-element.52), channel_id=1, source_target_pairs={{0,1},{1,2},{2,3},{3,4},{4,5},{5,6},{6,7},{7,8},{8,9},{9,10},{10,1... | collective-permute-start | bytes 11528 | tf_op jit(solution)/shard_map/ppermute | solution.py:235
  114.3 1.2 broadcast_divide_fusion.il_ref
  115.5 0.9 concatenate.24.y_ref
  116.4 12.0 %shard_map.104 = (bf16[64,2048]{1,0:T(8,128)(2,1)}, f32[1,2048]{1,0:T(1,128)}) custom-call(f32[64,2304]{1,0:T(8,128)} %concatenate.24.y_ref, f32[64,31]{1,0:T(8,128)} %bitcast.42, bf16[64,2048]{1,0:T(8,128)(2,1)} %bitcast.35, s32[1,2048]{1,0:T(1,128)} %get-tuple-element.56.lo_ref, s32[1,2048]{1,0:T(1,128)} %get-tuple-element.55.hi_ref), custom_call_target="tpu_custom_call" | custom-call | tf_op jit(solution)/shard_map/pallas_call | solution.py:309
  128.4 2.0 %copy.51 = bf16[64,2048]{0,1:T(8,128)(2,1)} copy(bf16[64,2048]{1,0:T(8,128)(2,1)} %get-tuple-element.17) | data formatting | bytes 524288 | tf_op jit(solution)/shard_map/pallas_call | solution.py:309
  130.4 2.0 %copy.53.d_ref = f32[2048,1]{1,0:T(8,128)} copy(f32[2048,1]{0,1:T(1,128)} %bitcast.47) | data formatting | bytes 16384 | tf_op jit(solution)/shard_map/transpose | solution.py:319
  132.4 32.5 %shard_map.105 = (bf16[2048,64]{1,0:T(8,128)(2,1)}, f32[4096,64]{1,0:T(8,128)}, f32[4096,64]{1,0:T(8,128)}) custom-call(s32[8]{0:T(128)} %get-tuple-element.39.lo_ref, s32[8]{0:T(128)} %get-tuple-element.38.hi_ref, bf16[2048,64]{1,0:T(8,128)(2,1)} %bitcast.32, bf16[4096,64]{1,0:T(8,128)(2,1)} %get-tuple-element.43.k_ref, ...), custom_call_target="tpu_custom_call" | custom-call | tf_op jit(solution)/shard_map/pallas_call | solution.py:321
  165.0 2.8 %maximum_convert_fusion = bf16[4096,128]{1,0:T(8,128)(2,1)S(1)} fusion(f32[4096,64]{1,0:T(8,128)} %get-tuple-element.23, f32[4096,64]{1,0:T(8,128)} %get-tuple-element.22), kind=kLoop, calls=%fused_computation | loop fusion | flops 2097152 | bytes 3145728 | tf_op jit(solution)/shard_map/convert.4
  167.8 0.7 fusion.8
  168.6 1.9 %collective-permute-start.6 = (bf16[1024,128]{1,0:T(8,128)(2,1)}, bf16[1024,128]{1,0:T(8,128)(2,1)S(1)}, u32[]{:S(2)}, u32[]{:S(2)}) collective-permute-start(bf16[1024,128]{1,0:T(8,128)(2,1)} %get-tuple-element.40), channel_id=1, source_target_pairs={{0,1},{1,2},{2,3},{3,4},{4,5},{5,6},{6,7},{7,8},{8,9},{9,10},{10,1... | collective-permute-start | bytes 786440 | tf_op jit(solution)/shard_map/ppermute | solution.py:29
  170.5 2.4 %collective-permute-start.7 = (bf16[1024,128]{1,0:T(8,128)(2,1)S(1)}, bf16[1024,128]{1,0:T(8,128)(2,1)S(1)}, u32[]{:S(2)}, u32[]{:S(2)}) collective-permute-start(bf16[1024,128]{1,0:T(8,128)(2,1)S(1)} %get-tuple-element.41), channel_id=1, source_target_pairs={{1,0},{2,1},{3,2},{4,3},{5,4},{6,5},{7,6},{8,7},{9,8},{10,9},{11,1... | collective-permute-start | bytes 786440 | tf_op jit(solution)/shard_map/ppermute | solution.py:29
  172.9 0.9 copy.54
  174.1 5.0 %collective-permute-done.7 = bf16[1024,128]{1,0:T(8,128)(2,1)S(1)} collective-permute-done((bf16[1024,128]{1,0:T(8,128)(2,1)S(1)}, bf16[1024,128]{1,0:T(8,128)(2,1)S(1)}, u32[]{:S(2)}, u32[]{:S(2)}) %collective-permute-start.7) | collective-permute-done | bytes 262176 | tf_op jit(solution)/shard_map/ppermute | solution.py:29
  179.1 1.6 fusion.2
  180.9 0.9 copy.56
  181.8 0.9 copy.55
  (41 shorter events, 2.3 us)
Async XLA Ops:
  4.0 11.1 %copy-start.6 = (s32[64]{0:T(128)S(1)}, s32[64]{0:T(128)}, u32[]{:S(2)}) copy-start(s32[64]{0:T(128)} %param.10) | copy-start | bytes 772
  5.1 32.3 %all-to-all-start = ((bf16[128,16,192]{0,2,1:T(8,128)(2,1)}), bf16[128,16,192]{0,2,1:T(8,128)(2,1)S(1)}, u32[]{:S(2)}, u32[]{:S(2)}) async-start(bf16[128,16,192]{0,2,1:T(8,128)(2,1)} %bitcast.5), calls=%async_computation | async-start | bytes 1572864 | tf_op jit(solution)/shard_map/all_to_all | solution.py:250
  38.3 10.0 %copy-start.5 = (f32[31,64]{1,0:T(8,128)S(1)}, f32[31,64]{1,0:T(8,128)}, u32[]{:S(2)}) copy-start(f32[31,64]{1,0:T(8,128)} %param.11) | copy-start | bytes 23812
  38.3 10.7 %copy-start.7 = (f32[64]{0:T(128)S(1)}, f32[64]{0:T(128)}, u32[]{:S(2)}) copy-start(f32[64]{0:T(128)} %param.12) | copy-start | bytes 772
  39.2 13.4 %collective-permute-start = (bf16[1024,128]{1,0:T(8,128)(2,1)S(1)}, bf16[1024,128]{1,0:T(8,128)(2,1)S(1)}, u32[]{:S(2)}, u32[]{:S(2)}) collective-permute-start(bf16[1024,128]{1,0:T(8,128)(2,1)S(1)} %get-tuple-element.44), channel_id=1, source_target_pairs={{0,1},{1,2},{2,3},{3,4},{4,5},{5,6},{6,7},{7,8},{8,9},{9,10},{10,1... | collective-permute-start | bytes 786440 | tf_op jit(solution)/shard_map/ppermute | solution.py:18
  46.1 8.6 %collective-permute-start.1 = (bf16[1024,128]{1,0:T(8,128)(2,1)S(1)}, bf16[1024,128]{1,0:T(8,128)(2,1)S(1)}, u32[]{:S(2)}, u32[]{:S(2)}) collective-permute-start(bf16[1024,128]{1,0:T(8,128)(2,1)S(1)} %get-tuple-element.45), channel_id=1, source_target_pairs={{1,0},{2,1},{3,2},{4,3},{5,4},{6,5},{7,6},{8,7},{9,8},{10,9},{11,1... | collective-permute-start | bytes 786440 | tf_op jit(solution)/shard_map/ppermute | solution.py:21
  83.9 30.4 %copy-start.2 = (f32[2048,1]{1,0:T(8,128)S(1)}, f32[2048,1]{1,0:T(8,128)}, u32[]{:S(2)}) copy-start(f32[2048,1]{1,0:T(8,128)} %get-tuple-element.19) | copy-start | bytes 24580
  85.2 30.2 %copy-start.1 = (bf16[2048,64]{0,1:T(8,128)(2,1)}, bf16[2048,64]{0,1:T(8,128)(2,1)S(1)}, u32[]{:S(2)}) copy-start(bf16[2048,64]{0,1:T(8,128)(2,1)S(1)} %copy.48) | copy-start | bytes 786436
  85.3 6.5 %collective-permute-start.3 = (bf16[64,15]{1,0:T(8,128)(2,1)S(1)}, bf16[64,15]{1,0:T(8,128)(2,1)S(1)}, u32[]{:S(2)}, u32[]{:S(2)}) collective-permute-start(bf16[64,15]{1,0:T(8,128)(2,1)S(1)} %get-tuple-element.53), channel_id=1, source_target_pairs={{1,0},{2,1},{3,2},{4,3},{5,4},{6,5},{7,6},{8,7},{9,8},{10,9},{11,1... | collective-permute-start | bytes 5768 | tf_op jit(solution)/shard_map/ppermute | solution.py:236
  87.2 5.4 %collective-permute-start.2 = (bf16[64,15]{1,0:T(8,128)(2,1)S(1)}, bf16[64,15]{1,0:T(8,128)(2,1)S(1)}, u32[]{:S(2)}, u32[]{:S(2)}) collective-permute-start(bf16[64,15]{1,0:T(8,128)(2,1)S(1)} %get-tuple-element.54), channel_id=1, source_target_pairs={{0,1},{1,2},{2,3},{3,4},{4,5},{5,6},{6,7},{7,8},{8,9},{9,10},{10,1... | collective-permute-start | bytes 5768 | tf_op jit(solution)/shard_map/ppermute | solution.py:235
  106.3 9.2 %copy-start.3 = (f32[64,2048]{1,0:T(8,128)S(1)}, f32[64,2048]{1,0:T(8,128)}, u32[]{:S(2)}) copy-start(f32[64,2048]{1,0:T(8,128)} %get-tuple-element.16) | copy-start | bytes 1572868
  107.2 8.2 %collective-permute-start.5 = (f32[64,15]{1,0:T(8,128)S(1)}, f32[64,15]{1,0:T(8,128)S(1)}, u32[]{:S(2)}, u32[]{:S(2)}) collective-permute-start(f32[64,15]{1,0:T(8,128)S(1)} %get-tuple-element.51), channel_id=1, source_target_pairs={{1,0},{2,1},{3,2},{4,3},{5,4},{6,5},{7,6},{8,7},{9,8},{10,9},{11,1... | collective-permute-start | bytes 11528 | tf_op jit(solution)/shard_map/ppermute | solution.py:236
  109.2 6.3 %collective-permute-start.4 = (f32[64,15]{1,0:T(8,128)S(1)}, f32[64,15]{1,0:T(8,128)S(1)}, u32[]{:S(2)}, u32[]{:S(2)}) collective-permute-start(f32[64,15]{1,0:T(8,128)S(1)} %get-tuple-element.52), channel_id=1, source_target_pairs={{0,1},{1,2},{2,3},{3,4},{4,5},{5,6},{6,7},{7,8},{8,9},{9,10},{10,1... | collective-permute-start | bytes 11528 | tf_op jit(solution)/shard_map/ppermute | solution.py:235
  165.0 7.9 %copy-start.4 = (bf16[2048,64]{1,0:T(8,128)(2,1)S(1)}, bf16[2048,64]{1,0:T(8,128)(2,1)}, u32[]{:S(2)}) copy-start(bf16[2048,64]{1,0:T(8,128)(2,1)} %get-tuple-element.21) | copy-start | bytes 786436
  165.0 14.1 %copy-start = (f32[4096,64]{1,0:T(8,128)S(1)}, f32[4096,64]{1,0:T(8,128)}, u32[]{:S(2)}) copy-start(f32[4096,64]{1,0:T(8,128)} %get-tuple-element.22) | copy-start | bytes 3145732
  168.6 5.5 %collective-permute-start.6 = (bf16[1024,128]{1,0:T(8,128)(2,1)}, bf16[1024,128]{1,0:T(8,128)(2,1)S(1)}, u32[]{:S(2)}, u32[]{:S(2)}) collective-permute-start(bf16[1024,128]{1,0:T(8,128)(2,1)} %get-tuple-element.40), channel_id=1, source_target_pairs={{0,1},{1,2},{2,3},{3,4},{4,5},{5,6},{6,7},{7,8},{8,9},{9,10},{10,1... | collective-permute-start | bytes 786440 | tf_op jit(solution)/shard_map/ppermute | solution.py:29
  170.5 8.6 %collective-permute-start.7 = (bf16[1024,128]{1,0:T(8,128)(2,1)S(1)}, bf16[1024,128]{1,0:T(8,128)(2,1)S(1)}, u32[]{:S(2)}, u32[]{:S(2)}) collective-permute-start(bf16[1024,128]{1,0:T(8,128)(2,1)S(1)} %get-tuple-element.41), channel_id=1, source_target_pairs={{1,0},{2,1},{3,2},{4,3},{5,4},{6,5},{7,6},{8,7},{9,8},{10,9},{11,1... | collective-permute-start | bytes 786440 | tf_op jit(solution)/shard_map/ppermute | solution.py:29

commit v5 on v4

--- a/solution.py
+++ b/solution.py
@@ -98,8 +98,8 @@
 
 
 def backward_kernel(
-    lo_ref, hi_ref, q_ref, k_ref, v_ref, do_ref, qseg_ref, kseg_ref, m_ref, il_ref, d_ref,
-    dq_ref, dk_ref, dv_ref,
+    lo_ref, hi_ref, q_ref, k_ref, v_ref, do_ref, qt_ref, dot_ref, qseg_ref, kseg_ref, m_ref,
+    il_ref, d_ref, dq_ref, dk_ref, dv_ref,
 ):
     scale = HEAD_DIM ** (-0.5)
     dk_ref[...] = jnp.zeros_like(dk_ref)
@@ -113,6 +113,8 @@
         m = m_ref[pl.ds(r0, TILE_Q), :]
         il = il_ref[pl.ds(r0, TILE_Q), :]
         dlt = d_ref[pl.ds(r0, TILE_Q), :]
+        q_t = qt_ref[:, pl.ds(r0, TILE_Q)]
+        do_t = dot_ref[:, pl.ds(r0, TILE_Q)]
 
         def k_body(j, dq):
             c0 = pl.multiple_of(j * TILE_K, TILE_K)
@@ -124,11 +126,9 @@
             p = jnp.where(mask, jnp.exp(s - m) * il, 0.0)
             dp = lax.dot_general(do, v, NT, preferred_element_type=jnp.float32)
             ds = (p * (dp - dlt)).astype(jnp.bfloat16)
-            dk_ref[pl.ds(c0, TILE_K), :] += lax.dot_general(
-                ds, q, TN, preferred_element_type=jnp.float32
-            )
-            dv_ref[pl.ds(c0, TILE_K), :] += lax.dot_general(
-                p.astype(jnp.bfloat16), do, TN, preferred_element_type=jnp.float32
+            dk_ref[:, pl.ds(c0, TILE_K)] += jnp.dot(q_t, ds, preferred_element_type=jnp.float32)
+            dv_ref[:, pl.ds(c0, TILE_K)] += jnp.dot(
+                do_t, p.astype(jnp.bfloat16), preferred_element_type=jnp.float32
             )
             return dq + jnp.dot(ds, k, preferred_element_type=jnp.float32)
 
@@ -318,14 +318,15 @@
     grad_attended = grad_att_t.T
     row_delta = delta_row.T
 
-    grad_q, dk_ext, dv_ext = vmem_call(
+    ext_rows = block_rows + 2 * maxlen
+    grad_q, dk_t, dv_t = vmem_call(
         backward_kernel,
         2,
-        9,
+        11,
         (
             jax.ShapeDtypeStruct((block_rows, HEAD_DIM), jnp.bfloat16),
-            jax.ShapeDtypeStruct((block_rows + 2 * maxlen, HEAD_DIM), jnp.float32),
-            jax.ShapeDtypeStruct((block_rows + 2 * maxlen, HEAD_DIM), jnp.float32),
+            jax.ShapeDtypeStruct((HEAD_DIM, ext_rows), jnp.float32),
+            jax.ShapeDtypeStruct((HEAD_DIM, ext_rows), jnp.float32),
         ),
     )(
         lo_t,
@@ -334,25 +335,27 @@
         k_flat,
         v_flat,
         grad_attended,
+        local_q.T,
+        grad_att_t,
         qseg_col,
         kseg_row,
         row_tops,
         1.0 / row_totals,
         row_delta,
     )
-    ext_terms = jnp.concatenate([dk_ext, dv_ext], axis=1)
+    ext_terms = jnp.concatenate([dk_t, dv_t], axis=0)
     received = []
-    for rim_part, direction in ((ext_terms[:maxlen], -1), (ext_terms[maxlen + block_rows :], 1)):
+    for rim_part, direction in ((ext_terms[:, :maxlen], -1), (ext_terms[:, maxlen + block_rows :], 1)):
         received.append(
             passed_along(rim_part.astype(jnp.bfloat16), "blk", direction).astype(rim_part.dtype)
         )
-    key_grads = ext_terms[maxlen : maxlen + block_rows] + jnp.concatenate(
-        [received[1], received[0]], axis=0
+    key_grads = ext_terms[:, maxlen : maxlen + block_rows] + jnp.concatenate(
+        [received[1], received[0]], axis=1
     )
     grad_queries = grad_q.reshape(block_rows, channels)
-    grad_keys = key_grads[:, :channels].astype(jnp.bfloat16)
-    grad_values = key_grads[:, channels:].astype(jnp.bfloat16)
-    return (conv_out_t, grad_queries.T, grad_keys.T, grad_values.T)
+    grad_keys = key_grads[:HEAD_DIM].astype(jnp.bfloat16)
+    grad_values = key_grads[HEAD_DIM:].astype(jnp.bfloat16)
+    return (conv_out_t, grad_queries.T, grad_keys, grad_values)
 
 
 def solution(mesh):

time: 183 us -> 176 us (0.962)
  the two profiles are of different devices: /device:TPU:9 before, /device:TPU:13 now
where the time goes in v5:
time: 176 us; the launch traced here: 175 us
  Pallas kernels  79.7 us (45%)
  starting transfers between devices  36.3 us (21%)
  waiting for transfers between devices  27.3 us (16%)
  local copies, waits for them, and re-layouts  25 us (14%)
  other arithmetic  5.71 us (3%)
    pallas_call x1, Pallas kernels, on_device(): vmem_call(backward_kernel, 2, 11, (jax.ShapeDtypeStruct((block_rows, HEAD...  27.7 us
    pallas_call x1, Pallas kernels, on_device(): vmem_call(forward_kernel, 2, 5, (jax.ShapeDtypeStruct((block_rows, HEAD_D...  27.2 us
    all_to_all x1, waiting for transfers between devices, on_device(): lax.all_to_all(stacked, 'uly', split_axis=1, concat_axis=0, tiled=True)  19 us
    pallas_call x1, Pallas kernels, on_device(): vmem_call(conv_forward_kernel, 0, 6, (jax.ShapeDtypeStruct((HEAD_DIM, blo...  12.8 us
    pallas_call x1, Pallas kernels, on_device(): vmem_call(conv_backward_kernel, 0, 5, (jax.ShapeDtypeStruct((HEAD_DIM, bl...  12 us
    all_to_all x1, starting transfers between devices, on_device(): lax.all_to_all(stacked, 'uly', split_axis=1, concat_axis=0, tiled=True)  10 us
    ppermute x2, starting transfers between devices, padded_rims(): low = lax.ppermute(block[:, block.shape[1] - half:], 'blk', forward)  9.64 us
    ppermute x1, starting transfers between devices, extended(): lax.ppermute(lax.slice_in_dim(block, block.shape[dim] - width, None, axis...  6.58 us
  transfers between devices with their start and end apart: 9, of which 4 were waited for; matrix products, arithmetic and copies ran while one was open for 6% of the time, Pallas kernels for 0%

profile of v5, /device:TPU:13, one launch (start us, length us, event | category | flops | bytes accessed | tf_op | source)
XLA Modules:
  0.0 174.9 jit_solution(9813405097083829811)
XLA Ops:
  0.6 1.1 copy.63
  1.8 1.1 copy.64
  2.9 1.1 copy.65
  4.1 0.9 copy.66
  5.1 10.0 %all-to-all-start = ((bf16[128,16,192]{0,2,1:T(8,128)(2,1)}), bf16[128,16,192]{0,2,1:T(8,128)(2,1)S(1)}, u32[]{:S(2)}, u32[]{:S(2)}) async-start(bf16[128,16,192]{0,2,1:T(8,128)(2,1)} %bitcast.5), calls=%async_computation | async-start | bytes 1572864 | tf_op jit(solution)/shard_map/all_to_all | solution.py:250
  15.3 0.5 slice.86
  16.0 0.2 select_reduce_fusion
  16.2 0.2 convert_reduce_fusion
  16.4 0.7 broadcast_minimum_fusion
  17.1 0.6 fusion.2
  17.7 0.6 and_select_fusion.kseg_ref
  18.4 19.0 %all-to-all-done = bf16[128,16,192]{0,2,1:T(8,128)(2,1)S(1)} async-done(((bf16[128,16,192]{0,2,1:T(8,128)(2,1)}), bf16[128,16,192]{0,2,1:T(8,128)(2,1)S(1)}, u32[]{:S(2)}, u32[]{:S(2)}) %all-to-all-start) | async-done | bytes 786464 | tf_op jit(solution)/shard_map/all_to_all | solution.py:250
  37.4 0.5 copy.67
  37.9 0.3 reshape.97
  38.3 0.8 slice_bitcast_fusion.2
  39.1 6.6 %collective-permute-start = (bf16[1024,128]{0,1:T(8,128)(2,1)S(1)}, bf16[1024,128]{0,1:T(8,128)(2,1)S(1)}, u32[]{:S(2)}, u32[]{:S(2)}) collective-permute-start(bf16[1024,128]{0,1:T(8,128)(2,1)S(1)} %get-tuple-element.56), channel_id=1, source_target_pairs={{0,1},{1,2},{2,3},{3,4},{4,5},{5,6},{6,7},{7,8},{8,9},{9,10},{10,1... | collective-permute-start | bytes 786440 | tf_op jit(solution)/shard_map/ppermute | solution.py:18
  45.7 1.9 %collective-permute-start.1 = (bf16[1024,128]{0,1:T(8,128)(2,1)S(1)}, bf16[1024,128]{0,1:T(8,128)(2,1)S(1)}, u32[]{:S(2)}, u32[]{:S(2)}) collective-permute-start(bf16[1024,128]{0,1:T(8,128)(2,1)S(1)} %get-tuple-element.57), channel_id=1, source_target_pairs={{1,0},{2,1},{3,2},{4,3},{5,4},{6,5},{7,6},{8,7},{9,8},{10,9},{11,1... | collective-permute-start | bytes 786440 | tf_op jit(solution)/shard_map/ppermute | solution.py:21
  47.9 0.7 copy.73
  48.6 0.7 copy.74.gain_ref
  49.3 1.3 copy.71.qseg_ref
  50.6 0.6 maximum_minimum_fusion
  51.2 1.1 copy.68.q_ref
  52.3 2.1 %collective-permute-done.1 = bf16[1024,128]{0,1:T(8,128)(2,1)S(1)} collective-permute-done((bf16[1024,128]{0,1:T(8,128)(2,1)S(1)}, bf16[1024,128]{0,1:T(8,128)(2,1)S(1)}, u32[]{:S(2)}, u32[]{:S(2)}) %collective-permute-start.1) | collective-permute-done | bytes 262176 | tf_op jit(solution)/shard_map/ppermute | solution.py:21
  54.5 1.3 copy.70.v_ref
  55.8 1.3 copy.69.k_ref
  57.2 27.2 %shard_map.102 = (bf16[2048,64]{1,0:T(8,128)(2,1)}, f32[2048,1]{1,0:T(8,128)}, f32[2048,1]{1,0:T(8,128)}) custom-call(s32[8]{0:T(128)} %get-tuple-element.43.lo_ref, s32[8]{0:T(128)} %get-tuple-element.42.hi_ref, bf16[2048,64]{1,0:T(8,128)(2,1)} %copy.68.q_ref, bf16[4096,64]{1,0:T(8,128)(2,1)} %copy.69.k_ref, bf16[4096,64]{1,0:T(8,128)(2,1)} %copy.70.v_ref, ...), custom_call_target="tpu_custom_call" | custom-call | tf_op jit(solution)/shard_map/pallas_call | solution.py:284
  84.4 1.3 copy.72
  85.8 1.9 %collective-permute-start.3 = (bf16[64,15]{1,0:T(8,128)(2,1)S(1)}, bf16[64,15]{1,0:T(8,128)(2,1)S(1)}, u32[]{:S(2)}, u32[]{:S(2)}) collective-permute-start(bf16[64,15]{1,0:T(8,128)(2,1)S(1)} %get-tuple-element.58), channel_id=1, source_target_pairs={{1,0},{2,1},{3,2},{4,3},{5,4},{6,5},{7,6},{8,7},{9,8},{10,9},{11,1... | collective-permute-start | bytes 5768 | tf_op jit(solution)/shard_map/ppermute | solution.py:236
  87.7 4.5 %collective-permute-start.2 = (bf16[64,15]{1,0:T(8,128)(2,1)S(1)}, bf16[64,15]{1,0:T(8,128)(2,1)S(1)}, u32[]{:S(2)}, u32[]{:S(2)}) collective-permute-start(bf16[64,15]{1,0:T(8,128)(2,1)S(1)} %get-tuple-element.59), channel_id=1, source_target_pairs={{0,1},{1,2},{2,3},{3,4},{4,5},{5,6},{6,7},{7,8},{8,9},{9,10},{10,1... | collective-permute-start | bytes 5768 | tf_op jit(solution)/shard_map/ppermute | solution.py:235
  92.3 0.8 collective-permute-done.2
  93.1 0.9 concatenate.23.x_ref
  94.0 12.8 %shard_map.103 = (bf16[64,2048]{1,0:T(8,128)(2,1)}, f32[64,2048]{1,0:T(8,128)}) custom-call(f32[64,2304]{1,0:T(8,128)} %concatenate.23.x_ref, f32[64,31]{1,0:T(8,128)} %bitcast.37, f32[64,1]{1,0:T(8,128)} %copy.74.gain_ref, bf16[64,2048]{1,0:T(8,128)(2,1)} %cot_ref.1, s32[1,2048]{1,0:T(1,128)} %get-tuple-element.61.lo_ref, s32[1,2048]{1,0:T(1,128)} %get-tuple-element.60.hi_ref), custom_call_target="tpu_custom_call" | custom-call | tf_op jit(solution)/shard_map/pallas_call | solution.py:300
  106.8 0.9 fusion.9
  107.7 1.9 %collective-permute-start.5 = (f32[64,15]{1,0:T(8,128)S(1)}, f32[64,15]{1,0:T(8,128)S(1)}, u32[]{:S(2)}, u32[]{:S(2)}) collective-permute-start(f32[64,15]{1,0:T(8,128)S(1)} %get-tuple-element.54), channel_id=1, source_target_pairs={{1,0},{2,1},{3,2},{4,3},{5,4},{6,5},{7,6},{8,7},{9,8},{10,9},{11,1... | collective-permute-start | bytes 11528 | tf_op jit(solution)/shard_map/ppermute | solution.py:236
  109.6 5.1 %collective-permute-start.4 = (f32[64,15]{1,0:T(8,128)S(1)}, f32[64,15]{1,0:T(8,128)S(1)}, u32[]{:S(2)}, u32[]{:S(2)}) collective-permute-start(f32[64,15]{1,0:T(8,128)S(1)} %get-tuple-element.55), channel_id=1, source_target_pairs={{0,1},{1,2},{2,3},{3,4},{4,5},{5,6},{6,7},{7,8},{8,9},{9,10},{10,1... | collective-permute-start | bytes 11528 | tf_op jit(solution)/shard_map/ppermute | solution.py:235
  114.8 1.1 broadcast_divide_fusion.il_ref
  115.9 0.9 concatenate.24.y_ref
  116.8 12.0 %shard_map.104 = (bf16[64,2048]{1,0:T(8,128)(2,1)}, f32[1,2048]{1,0:T(1,128)}) custom-call(f32[64,2304]{1,0:T(8,128)} %concatenate.24.y_ref, f32[64,31]{1,0:T(8,128)} %bitcast.38, bf16[64,2048]{1,0:T(8,128)(2,1)} %bitcast.31, s32[1,2048]{1,0:T(1,128)} %get-tuple-element.61.lo_ref, s32[1,2048]{1,0:T(1,128)} %get-tuple-element.60.hi_ref), custom_call_target="tpu_custom_call" | custom-call | tf_op jit(solution)/shard_map/pallas_call | solution.py:309
  128.9 2.0 %copy.75 = bf16[64,2048]{0,1:T(8,128)(2,1)} copy(bf16[64,2048]{1,0:T(8,128)(2,1)} %get-tuple-element.17.dot_ref) | data formatting | bytes 524288 | tf_op jit(solution)/shard_map/pallas_call | solution.py:309
  130.9 2.1 %copy.80.d_ref = f32[2048,1]{1,0:T(8,128)} copy(f32[2048,1]{0,1:T(1,128)} %bitcast.43) | data formatting | bytes 16384 | tf_op jit(solution)/shard_map/transpose | solution.py:319
  132.9 27.7 %shard_map.105 = (bf16[2048,64]{1,0:T(8,128)(2,1)}, f32[64,4096]{1,0:T(8,128)}, f32[64,4096]{1,0:T(8,128)}) custom-call(s32[8]{0:T(128)} %get-tuple-element.43.lo_ref, s32[8]{0:T(128)} %get-tuple-element.42.hi_ref, bf16[2048,64]{1,0:T(8,128)(2,1)} %copy.68.q_ref, bf16[4096,64]{1,0:T(8,128)(2,1)} %copy.69.k_ref, bf16[4096,64]{1,0:T(8,128)(2,1)} %copy.70.v_ref, ...), custom_call_target="tpu_custom_call" | custom-call | tf_op jit(solution)/shard_map/pallas_call | solution.py:322
  160.6 1.4 constant_dynamic-update-slice_fusion.1
  162.4 1.9 %collective-permute-start.6 = (bf16[128,1024]{1,0:T(8,128)(2,1)S(1)}, bf16[128,1024]{1,0:T(8,128)(2,1)S(1)}, u32[]{:S(2)}, u32[]{:S(2)}) collective-permute-start(bf16[128,1024]{1,0:T(8,128)(2,1)S(1)} %get-tuple-element.44), channel_id=1, source_target_pairs={{0,1},{1,2},{2,3},{3,4},{4,5},{5,6},{6,7},{7,8},{8,9},{9,10},{10,1... | collective-permute-start | bytes 786440 | tf_op jit(solution)/shard_map/ppermute | solution.py:29
  164.4 2.4 %collective-permute-start.7 = (bf16[128,1024]{1,0:T(8,128)(2,1)S(1)}, bf16[128,1024]{1,0:T(8,128)(2,1)}, u32[]{:S(2)}, u32[]{:S(2)}) collective-permute-start(bf16[128,1024]{1,0:T(8,128)(2,1)S(1)} %get-tuple-element.45), channel_id=1, source_target_pairs={{1,0},{2,1},{3,2},{4,3},{5,4},{6,5},{7,6},{8,7},{9,8},{10,9},{11,1... | collective-permute-start | bytes 786440 | tf_op jit(solution)/shard_map/ppermute | solution.py:29
  166.8 0.9 copy.81
  167.7 5.4 %collective-permute-done.7 = bf16[128,1024]{1,0:T(8,128)(2,1)} collective-permute-done((bf16[128,1024]{1,0:T(8,128)(2,1)S(1)}, bf16[128,1024]{1,0:T(8,128)(2,1)}, u32[]{:S(2)}, u32[]{:S(2)}) %collective-permute-start.7) | collective-permute-done | bytes 262176 | tf_op jit(solution)/shard_map/ppermute | solution.py:29
  173.1 1.1 fusion
  174.1 0.8 fusion.8
  (41 shorter events, 1.3 us)
Async XLA Ops:
  4.0 11.1 %copy-start.6 = (s32[64]{0:T(128)S(1)}, s32[64]{0:T(128)}, u32[]{:S(2)}) copy-start(s32[64]{0:T(128)} %param.10) | copy-start | bytes 772
  5.1 32.3 %all-to-all-start = ((bf16[128,16,192]{0,2,1:T(8,128)(2,1)}), bf16[128,16,192]{0,2,1:T(8,128)(2,1)S(1)}, u32[]{:S(2)}, u32[]{:S(2)}) async-start(bf16[128,16,192]{0,2,1:T(8,128)(2,1)} %bitcast.5), calls=%async_computation | async-start | bytes 1572864 | tf_op jit(solution)/shard_map/all_to_all | solution.py:250
  37.9 9.9 %copy-start.5 = (f32[31,64]{1,0:T(8,128)S(1)}, f32[31,64]{1,0:T(8,128)}, u32[]{:S(2)}) copy-start(f32[31,64]{1,0:T(8,128)} %param.11) | copy-start | bytes 23812
  37.9 10.6 %copy-start.7 = (f32[64]{0:T(128)S(1)}, f32[64]{0:T(128)}, u32[]{:S(2)}) copy-start(f32[64]{0:T(128)} %param.12) | copy-start | bytes 772
  39.1 13.1 %collective-permute-start = (bf16[1024,128]{0,1:T(8,128)(2,1)S(1)}, bf16[1024,128]{0,1:T(8,128)(2,1)S(1)}, u32[]{:S(2)}, u32[]{:S(2)}) collective-permute-start(bf16[1024,128]{0,1:T(8,128)(2,1)S(1)} %get-tuple-element.56), channel_id=1, source_target_pairs={{0,1},{1,2},{2,3},{3,4},{4,5},{5,6},{6,7},{7,8},{8,9},{9,10},{10,1... | collective-permute-start | bytes 786440 | tf_op jit(solution)/shard_map/ppermute | solution.py:18
  45.7 8.6 %collective-permute-start.1 = (bf16[1024,128]{0,1:T(8,128)(2,1)S(1)}, bf16[1024,128]{0,1:T(8,128)(2,1)S(1)}, u32[]{:S(2)}, u32[]{:S(2)}) collective-permute-start(bf16[1024,128]{0,1:T(8,128)(2,1)S(1)} %get-tuple-element.57), channel_id=1, source_target_pairs={{1,0},{2,1},{3,2},{4,3},{5,4},{6,5},{7,6},{8,7},{9,8},{10,9},{11,1... | collective-permute-start | bytes 786440 | tf_op jit(solution)/shard_map/ppermute | solution.py:21
  84.4 30.4 %copy-start.1 = (f32[2048,1]{1,0:T(8,128)S(1)}, f32[2048,1]{1,0:T(8,128)}, u32[]{:S(2)}) copy-start(f32[2048,1]{1,0:T(8,128)} %get-tuple-element.19) | copy-start | bytes 24580
  85.7 30.2 %copy-start = (bf16[2048,64]{0,1:T(8,128)(2,1)}, bf16[2048,64]{0,1:T(8,128)(2,1)S(1)}, u32[]{:S(2)}) copy-start(bf16[2048,64]{0,1:T(8,128)(2,1)S(1)} %copy.72) | copy-start | bytes 786436
  85.8 6.5 %collective-permute-start.3 = (bf16[64,15]{1,0:T(8,128)(2,1)S(1)}, bf16[64,15]{1,0:T(8,128)(2,1)S(1)}, u32[]{:S(2)}, u32[]{:S(2)}) collective-permute-start(bf16[64,15]{1,0:T(8,128)(2,1)S(1)} %get-tuple-element.58), channel_id=1, source_target_pairs={{1,0},{2,1},{3,2},{4,3},{5,4},{6,5},{7,6},{8,7},{9,8},{10,9},{11,1... | collective-permute-start | bytes 5768 | tf_op jit(solution)/shard_map/ppermute | solution.py:236
  87.7 5.4 %collective-permute-start.2 = (bf16[64,15]{1,0:T(8,128)(2,1)S(1)}, bf16[64,15]{1,0:T(8,128)(2,1)S(1)}, u32[]{:S(2)}, u32[]{:S(2)}) collective-permute-start(bf16[64,15]{1,0:T(8,128)(2,1)S(1)} %get-tuple-element.59), channel_id=1, source_target_pairs={{0,1},{1,2},{2,3},{3,4},{4,5},{5,6},{6,7},{7,8},{8,9},{9,10},{10,1... | collective-permute-start | bytes 5768 | tf_op jit(solution)/shard_map/ppermute | solution.py:235
  106.8 9.1 %copy-start.3 = (f32[64,2048]{1,0:T(8,128)S(1)}, f32[64,2048]{1,0:T(8,128)}, u32[]{:S(2)}) copy-start(f32[64,2048]{1,0:T(8,128)} %get-tuple-element.16) | copy-start | bytes 1572868
  107.7 8.2 %collective-permute-start.5 = (f32[64,15]{1,0:T(8,128)S(1)}, f32[64,15]{1,0:T(8,128)S(1)}, u32[]{:S(2)}, u32[]{:S(2)}) collective-permute-start(f32[64,15]{1,0:T(8,128)S(1)} %get-tuple-element.54), channel_id=1, source_target_pairs={{1,0},{2,1},{3,2},{4,3},{5,4},{6,5},{7,6},{8,7},{9,8},{10,9},{11,1... | collective-permute-start | bytes 11528 | tf_op jit(solution)/shard_map/ppermute | solution.py:236
  109.6 6.2 %collective-permute-start.4 = (f32[64,15]{1,0:T(8,128)S(1)}, f32[64,15]{1,0:T(8,128)S(1)}, u32[]{:S(2)}, u32[]{:S(2)}) collective-permute-start(f32[64,15]{1,0:T(8,128)S(1)} %get-tuple-element.55), channel_id=1, source_target_pairs={{0,1},{1,2},{2,3},{3,4},{4,5},{5,6},{6,7},{7,8},{8,9},{9,10},{10,1... | collective-permute-start | bytes 11528 | tf_op jit(solution)/shard_map/ppermute | solution.py:235
  160.6 1.5 copy-start.2
  162.2 4.5 %copy-start.4 = (bf16[2048,64]{1,0:T(8,128)(2,1)S(1)}, bf16[2048,64]{1,0:T(8,128)(2,1)}, u32[]{:S(2)}) copy-start(bf16[2048,64]{1,0:T(8,128)(2,1)} %get-tuple-element.21) | copy-start | bytes 786436
  162.4 5.3 %collective-permute-start.6 = (bf16[128,1024]{1,0:T(8,128)(2,1)S(1)}, bf16[128,1024]{1,0:T(8,128)(2,1)S(1)}, u32[]{:S(2)}, u32[]{:S(2)}) collective-permute-start(bf16[128,1024]{1,0:T(8,128)(2,1)S(1)} %get-tuple-element.44), channel_id=1, source_target_pairs={{0,1},{1,2},{2,3},{3,4},{4,5},{5,6},{6,7},{7,8},{8,9},{9,10},{10,1... | collective-permute-start | bytes 786440 | tf_op jit(solution)/shard_map/ppermute | solution.py:29
  164.4 8.7 %collective-permute-start.7 = (bf16[128,1024]{1,0:T(8,128)(2,1)S(1)}, bf16[128,1024]{1,0:T(8,128)(2,1)}, u32[]{:S(2)}, u32[]{:S(2)}) collective-permute-start(bf16[128,1024]{1,0:T(8,128)(2,1)S(1)} %get-tuple-element.45), channel_id=1, source_target_pairs={{1,0},{2,1},{3,2},{4,3},{5,4},{6,5},{7,6},{8,7},{9,8},{10,9},{11,1... | collective-permute-start | bytes 786440 | tf_op jit(solution)/shard_map/ppermute | solution.py:29

commit v6 on v5

--- a/solution.py
+++ b/solution.py
@@ -246,9 +246,10 @@
     heads_total = width // HEAD_DIM
     stacked = jnp.stack(
         [a.reshape(rows_in, heads_total, HEAD_DIM) for a in (queries, keys, values)], axis=2
-    ).reshape(rows_in, heads_total * 3 * HEAD_DIM)
-    local_qkv = lax.all_to_all(stacked, "uly", split_axis=1, concat_axis=0, tiled=True)
-    local_qkv = local_qkv.reshape(local_qkv.shape[0], -1, 3, HEAD_DIM)
+    )
+    stacked = jnp.transpose(stacked, (1, 0, 2, 3)).reshape(heads_total, rows_in * 3 * HEAD_DIM)
+    local_qkv = lax.all_to_all(stacked, "uly", split_axis=0, concat_axis=0, tiled=True)
+    local_qkv = local_qkv.reshape(-1, heads_total // lax.axis_size("uly"), 3, HEAD_DIM)
     local_q, local_k, local_v = (
         local_qkv[:, :, i].reshape(local_qkv.shape[0], -1) for i in range(3)
     )

time: 176 us -> 198 us (1.12)
  the two profiles are of different devices: /device:TPU:13 before, /device:TPU:9 now
where the time goes in v6:
time: 198 us; the launch traced here: 197 us
  Pallas kernels  78.7 us (40%)
  starting transfers between devices  37.3 us (19%)
  local copies, waits for them, and re-layouts  35.6 us (18%)
  waiting for transfers between devices  26.2 us (13%)
  other arithmetic  18.5 us (9%)
    pallas_call x1, Pallas kernels, on_device(): vmem_call(backward_kernel, 2, 11, (jax.ShapeDtypeStruct((block_rows, HEAD...  27.2 us
    pallas_call x1, Pallas kernels, on_device(): vmem_call(forward_kernel, 2, 5, (jax.ShapeDtypeStruct((block_rows, HEAD_D...  26.7 us
    all_to_all x1, waiting for transfers between devices, on_device(): lax.all_to_all(stacked, 'uly', split_axis=0, concat_axis=0, tiled=True)  19 us
    pallas_call x1, Pallas kernels, on_device(): vmem_call(conv_forward_kernel, 0, 6, (jax.ShapeDtypeStruct((HEAD_DIM, blo...  12.8 us
    all_to_all x2, other arithmetic, on_device(): lax.all_to_all(stacked, 'uly', split_axis=0, concat_axis=0, tiled=True)  12.3 us
    pallas_call x1, Pallas kernels, on_device(): vmem_call(conv_backward_kernel, 0, 5, (jax.ShapeDtypeStruct((HEAD_DIM, bl...  12 us
    unnamed x25, local copies, waits for them, and re-layouts  10.4 us
    all_to_all x1, starting transfers between devices, on_device(): lax.all_to_all(stacked, 'uly', split_axis=0, concat_axis=0, tiled=True)  10 us
  transfers between devices with their start and end apart: 9, of which 5 were waited for; matrix products, arithmetic and copies ran while one was open for 6% of the time, Pallas kernels for 0%

profile of v6, /device:TPU:9, one launch (start us, length us, event | category | flops | bytes accessed | tf_op | source)
XLA Modules:
  0.0 197.3 jit_solution(12704630067017382635)
XLA Ops:
  0.6 1.1 copy.61
  1.8 1.1 copy.62
  2.9 1.1 copy.63
  4.1 1.3 copy.64
  5.5 3.5 %all_to_all.8 = bf16[16,1,24576]{2,1,0:T(2,128)(2,1)} reshape(bf16[16,128,3,64]{3,2,1,0:T(4,128)(2,1)S(1)} %copy.64) | data formatting | bytes 1572864 | tf_op jit(solution)/shard_map/all_to_all | solution.py:251
  9.5 6.7 %reduce.2 = bf16[16,24576]{1,0:T(8,128)(2,1)S(1)} reduce(bf16[16,1,24576]{2,1,0:T(2,128)(2,1)} %all_to_all.8, bf16[]{:T(256)} %broadcast.113), dimensions={1}, to_apply=%all_to_all.8.reduce_sub_computation | reduce | bytes 1572866 | tf_op jit(solution)/shard_map/all_to_all | solution.py:251
  16.2 1.5 reshape.99
  17.6 10.0 %all-to-all-start = ((bf16[16,2,12288]{2,1,0:T(2,128)(2,1)}), bf16[16,2,12288]{2,1,0:T(2,128)(2,1)S(1)}, u32[]{:S(2)}, u32[]{:S(2)}) async-start(bf16[16,2,12288]{2,1,0:T(2,128)(2,1)} %reshape.99), calls=%async_computation | async-start | bytes 1572864 | tf_op jit(solution)/shard_map/all_to_all | solution.py:251
  29.0 0.7 broadcast_minimum_fusion
  29.7 0.6 fusion.2
  30.3 0.6 and_select_fusion.kseg_ref
  30.9 19.0 %all-to-all-done = bf16[16,2,12288]{2,1,0:T(2,128)(2,1)S(1)} async-done(((bf16[16,2,12288]{2,1,0:T(2,128)(2,1)}), bf16[16,2,12288]{2,1,0:T(2,128)(2,1)S(1)}, u32[]{:S(2)}, u32[]{:S(2)}) %all-to-all-start) | async-done | bytes 786464 | tf_op jit(solution)/shard_map/all_to_all | solution.py:251
  50.0 0.7 reshape.100
  50.7 5.7 %reduce.1 = bf16[16,24576]{1,0:T(8,128)(2,1)} reduce(bf16[16,1,24576]{2,1,0:T(2,128)(2,1)S(1)} %reshape.100, bf16[]{:T(256)} %constant.63), dimensions={1}, to_apply=%all_to_all.7.reduce_sub_computation | reduce | bytes 1572866 | tf_op jit(solution)/shard_map/all_to_all | solution.py:251
  56.4 2.8 %reshape.96 = bf16[2048,1,3,64]{3,2,0,1:T(4,128)(2,1)S(1)} reshape(bf16[16,24576]{1,0:T(8,128)(2,1)} %reduce.1) | data formatting | bytes 1572864 | tf_op jit(solution)/shard_map/reshape | solution.py:252
  59.2 2.3 %fusion.6 = (bf16[2048,1,1,64]{3,2,0,1:T(2,128)(2,1)S(1)}, bf16[2048,1,1,64]{3,2,0,1:T(2,128)(2,1)S(1)}, bf16[2048,1,1,64]{3,2,0,1:T(2,128)(2,1)S(1)}) fusion(bf16[2048,1,3,64]{3,2,0,1:T(4,128)(2,1)S(1)} %reshape.96), kind=kLoop, calls=%fused_computation.37 | loop fusion | bytes 1572864 | tf_op jit(solution)/shard_map/slice | solution.py:254
  62.0 6.9 %collective-permute-start = (bf16[1024,128]{1,0:T(8,128)(2,1)S(1)}, bf16[1024,128]{1,0:T(8,128)(2,1)S(1)}, u32[]{:S(2)}, u32[]{:S(2)}) collective-permute-start(bf16[1024,128]{1,0:T(8,128)(2,1)S(1)} %get-tuple-element.51), channel_id=1, source_target_pairs={{0,1},{1,2},{2,3},{3,4},{4,5},{5,6},{6,7},{7,8},{8,9},{9,10},{10,1... | collective-permute-start | bytes 786440 | tf_op jit(solution)/shard_map/ppermute | solution.py:18
  68.8 1.9 collective-permute-start.1
  71.0 0.7 copy.72
  71.7 0.7 copy.73.gain_ref
  72.4 1.3 copy.70.qseg_ref
  73.7 0.6 maximum_minimum_fusion
  74.3 1.7 copy.79
  76.0 0.9 copy.86
  77.7 1.7 fusion.8
  79.4 26.7 %shard_map.102 = (bf16[2048,64]{1,0:T(8,128)(2,1)}, f32[2048,1]{1,0:T(8,128)}, f32[2048,1]{1,0:T(8,128)}) custom-call(s32[8]{0:T(128)} %get-tuple-element.43.lo_ref, s32[8]{0:T(128)} %get-tuple-element.42.hi_ref, bf16[2048,64]{1,0:T(8,128)(2,1)} %bitcast.28, bf16[4096,64]{1,0:T(8,128)(2,1)} %get-tuple-element.50.k_ref, ...), custom_call_target="tpu_custom_call" | custom-call | tf_op jit(solution)/shard_map/pallas_call | solution.py:285
  106.1 1.3 copy.71
  107.5 1.9 collective-permute-start.3
  109.4 4.5 %collective-permute-start.2 = (bf16[64,15]{1,0:T(8,128)(2,1)S(1)}, bf16[64,15]{1,0:T(8,128)(2,1)S(1)}, u32[]{:S(2)}, u32[]{:S(2)}) collective-permute-start(bf16[64,15]{1,0:T(8,128)(2,1)S(1)} %get-tuple-element.58), channel_id=1, source_target_pairs={{0,1},{1,2},{2,3},{3,4},{4,5},{5,6},{6,7},{7,8},{8,9},{9,10},{10,1... | collective-permute-start | bytes 5768 | tf_op jit(solution)/shard_map/ppermute | solution.py:235
  114.0 0.8 collective-permute-done.2
  114.8 0.9 concatenate.23.x_ref
  115.8 12.8 %shard_map.103 = (bf16[64,2048]{1,0:T(8,128)(2,1)}, f32[64,2048]{1,0:T(8,128)}) custom-call(f32[64,2304]{1,0:T(8,128)} %concatenate.23.x_ref, f32[64,31]{1,0:T(8,128)} %bitcast.38, f32[64,1]{1,0:T(8,128)} %copy.73.gain_ref, bf16[64,2048]{1,0:T(8,128)(2,1)} %cot_ref.1, s32[1,2048]{1,0:T(1,128)} %get-tuple-element.60.lo_ref, s32[1,2048]{1,0:T(1,128)} %get-tuple-element.59.hi_ref), custom_call_target="tpu_custom_call" | custom-call | tf_op jit(solution)/shard_map/pallas_call | solution.py:301
  128.5 0.9 fusion.10
  129.4 1.9 collective-permute-start.5
  131.4 5.3 %collective-permute-start.4 = (f32[64,15]{1,0:T(8,128)S(1)}, f32[64,15]{1,0:T(8,128)S(1)}, u32[]{:S(2)}, u32[]{:S(2)}) collective-permute-start(f32[64,15]{1,0:T(8,128)S(1)} %get-tuple-element.56), channel_id=1, source_target_pairs={{0,1},{1,2},{2,3},{3,4},{4,5},{5,6},{6,7},{7,8},{8,9},{9,10},{10,1... | collective-permute-start | bytes 11528 | tf_op jit(solution)/shard_map/ppermute | solution.py:235
  136.7 1.1 broadcast_divide_fusion.il_ref
  137.8 0.9 concatenate.24.y_ref
  138.8 12.0 %shard_map.104 = (bf16[64,2048]{1,0:T(8,128)(2,1)}, f32[1,2048]{1,0:T(1,128)}) custom-call(f32[64,2304]{1,0:T(8,128)} %concatenate.24.y_ref, f32[64,31]{1,0:T(8,128)} %bitcast.39, bf16[64,2048]{1,0:T(8,128)(2,1)} %bitcast.31, s32[1,2048]{1,0:T(1,128)} %get-tuple-element.60.lo_ref, s32[1,2048]{1,0:T(1,128)} %get-tuple-element.59.hi_ref), custom_call_target="tpu_custom_call" | custom-call | tf_op jit(solution)/shard_map/pallas_call | solution.py:310
  150.8 2.0 %copy.74 = bf16[64,2048]{0,1:T(8,128)(2,1)} copy(bf16[64,2048]{1,0:T(8,128)(2,1)} %get-tuple-element.17.dot_ref) | data formatting | bytes 524288 | tf_op jit(solution)/shard_map/pallas_call | solution.py:310
  152.8 2.1 %copy.77.d_ref = f32[2048,1]{1,0:T(8,128)} copy(f32[2048,1]{0,1:T(1,128)} %bitcast.44) | data formatting | bytes 16384 | tf_op jit(solution)/shard_map/transpose | solution.py:320
  154.8 27.2 %shard_map.105 = (bf16[2048,64]{1,0:T(8,128)(2,1)}, f32[64,4096]{1,0:T(8,128)}, f32[64,4096]{1,0:T(8,128)}) custom-call(s32[8]{0:T(128)} %get-tuple-element.43.lo_ref, s32[8]{0:T(128)} %get-tuple-element.42.hi_ref, bf16[2048,64]{1,0:T(8,128)(2,1)} %bitcast.29, bf16[4096,64]{1,0:T(8,128)(2,1)} %get-tuple-element.50.k_ref, ...), custom_call_target="tpu_custom_call" | custom-call | tf_op jit(solution)/shard_map/pallas_call | solution.py:323
  182.0 1.4 constant_dynamic-update-slice_fusion.1
  183.9 2.8 %collective-permute-start.6 = (bf16[128,1024]{1,0:T(8,128)(2,1)S(1)}, bf16[128,1024]{1,0:T(8,128)(2,1)S(1)}, u32[]{:S(2)}, u32[]{:S(2)}) collective-permute-start(bf16[128,1024]{1,0:T(8,128)(2,1)S(1)} %get-tuple-element.47), channel_id=1, source_target_pairs={{0,1},{1,2},{2,3},{3,4},{4,5},{5,6},{6,7},{7,8},{8,9},{9,10},{10,1... | collective-permute-start | bytes 786440 | tf_op jit(solution)/shard_map/ppermute | solution.py:29
  186.7 1.9 collective-permute-start.7
  188.6 0.9 copy.78
  190.0 5.4 %collective-permute-done.7 = bf16[128,1024]{1,0:T(8,128)(2,1)} collective-permute-done((bf16[128,1024]{1,0:T(8,128)(2,1)S(1)}, bf16[128,1024]{1,0:T(8,128)(2,1)}, u32[]{:S(2)}, u32[]{:S(2)}) %collective-permute-start.7) | collective-permute-done | bytes 262176 | tf_op jit(solution)/shard_map/ppermute | solution.py:29
  195.4 1.1 fusion
  196.5 0.8 fusion.9
  (46 shorter events, 4.3 us)
Async XLA Ops:
  16.2 11.5 %copy-start.6 = (s32[64]{0:T(128)S(1)}, s32[64]{0:T(128)}, u32[]{:S(2)}) copy-start(s32[64]{0:T(128)} %param.10) | copy-start | bytes 772
  17.6 32.3 %all-to-all-start = ((bf16[16,2,12288]{2,1,0:T(2,128)(2,1)}), bf16[16,2,12288]{2,1,0:T(2,128)(2,1)S(1)}, u32[]{:S(2)}, u32[]{:S(2)}) async-start(bf16[16,2,12288]{2,1,0:T(2,128)(2,1)} %reshape.99), calls=%async_computation | async-start | bytes 1572864 | tf_op jit(solution)/shard_map/all_to_all | solution.py:251
  61.5 9.5 %copy-start.5 = (f32[31,64]{1,0:T(8,128)S(1)}, f32[31,64]{1,0:T(8,128)}, u32[]{:S(2)}) copy-start(f32[31,64]{1,0:T(8,128)} %param.11) | copy-start | bytes 23812
  61.5 10.2 %copy-start.7 = (f32[64]{0:T(128)S(1)}, f32[64]{0:T(128)}, u32[]{:S(2)}) copy-start(f32[64]{0:T(128)} %param.12) | copy-start | bytes 772
  62.0 15.0 %collective-permute-start = (bf16[1024,128]{1,0:T(8,128)(2,1)S(1)}, bf16[1024,128]{1,0:T(8,128)(2,1)S(1)}, u32[]{:S(2)}, u32[]{:S(2)}) collective-permute-start(bf16[1024,128]{1,0:T(8,128)(2,1)S(1)} %get-tuple-element.51), channel_id=1, source_target_pairs={{0,1},{1,2},{2,3},{3,4},{4,5},{5,6},{6,7},{7,8},{8,9},{9,10},{10,1... | collective-permute-start | bytes 786440 | tf_op jit(solution)/shard_map/ppermute | solution.py:18
  68.8 8.6 %collective-permute-start.1 = (bf16[1024,128]{1,0:T(8,128)(2,1)S(1)}, bf16[1024,128]{1,0:T(8,128)(2,1)S(1)}, u32[]{:S(2)}, u32[]{:S(2)}) collective-permute-start(bf16[1024,128]{1,0:T(8,128)(2,1)S(1)} %get-tuple-element.52), channel_id=1, source_target_pairs={{1,0},{2,1},{3,2},{4,3},{5,4},{6,5},{7,6},{8,7},{9,8},{10,9},{11,1... | collective-permute-start | bytes 786440 | tf_op jit(solution)/shard_map/ppermute | solution.py:21
  106.1 30.6 %copy-start.1 = (f32[2048,1]{1,0:T(8,128)S(1)}, f32[2048,1]{1,0:T(8,128)}, u32[]{:S(2)}) copy-start(f32[2048,1]{1,0:T(8,128)} %get-tuple-element.19) | copy-start | bytes 24580
  107.4 30.4 %copy-start = (bf16[2048,64]{0,1:T(8,128)(2,1)}, bf16[2048,64]{0,1:T(8,128)(2,1)S(1)}, u32[]{:S(2)}) copy-start(bf16[2048,64]{0,1:T(8,128)(2,1)S(1)} %copy.71) | copy-start | bytes 786436
  107.5 6.5 %collective-permute-start.3 = (bf16[64,15]{1,0:T(8,128)(2,1)S(1)}, bf16[64,15]{1,0:T(8,128)(2,1)S(1)}, u32[]{:S(2)}, u32[]{:S(2)}) collective-permute-start(bf16[64,15]{1,0:T(8,128)(2,1)S(1)} %get-tuple-element.57), channel_id=1, source_target_pairs={{1,0},{2,1},{3,2},{4,3},{5,4},{6,5},{7,6},{8,7},{9,8},{10,9},{11,1... | collective-permute-start | bytes 5768 | tf_op jit(solution)/shard_map/ppermute | solution.py:236
  109.4 5.4 %collective-permute-start.2 = (bf16[64,15]{1,0:T(8,128)(2,1)S(1)}, bf16[64,15]{1,0:T(8,128)(2,1)S(1)}, u32[]{:S(2)}, u32[]{:S(2)}) collective-permute-start(bf16[64,15]{1,0:T(8,128)(2,1)S(1)} %get-tuple-element.58), channel_id=1, source_target_pairs={{0,1},{1,2},{2,3},{3,4},{4,5},{5,6},{6,7},{7,8},{8,9},{9,10},{10,1... | collective-permute-start | bytes 5768 | tf_op jit(solution)/shard_map/ppermute | solution.py:235
  128.5 9.3 %copy-start.3 = (f32[64,2048]{1,0:T(8,128)S(1)}, f32[64,2048]{1,0:T(8,128)}, u32[]{:S(2)}) copy-start(f32[64,2048]{1,0:T(8,128)} %get-tuple-element.16) | copy-start | bytes 1572868
  129.4 8.4 %collective-permute-start.5 = (f32[64,15]{1,0:T(8,128)S(1)}, f32[64,15]{1,0:T(8,128)S(1)}, u32[]{:S(2)}, u32[]{:S(2)}) collective-permute-start(f32[64,15]{1,0:T(8,128)S(1)} %get-tuple-element.55), channel_id=1, source_target_pairs={{1,0},{2,1},{3,2},{4,3},{5,4},{6,5},{7,6},{8,7},{9,8},{10,9},{11,1... | collective-permute-start | bytes 11528 | tf_op jit(solution)/shard_map/ppermute | solution.py:236
  131.4 6.5 %collective-permute-start.4 = (f32[64,15]{1,0:T(8,128)S(1)}, f32[64,15]{1,0:T(8,128)S(1)}, u32[]{:S(2)}, u32[]{:S(2)}) collective-permute-start(f32[64,15]{1,0:T(8,128)S(1)} %get-tuple-element.56), channel_id=1, source_target_pairs={{0,1},{1,2},{2,3},{3,4},{4,5},{5,6},{6,7},{7,8},{8,9},{9,10},{10,1... | collective-permute-start | bytes 11528 | tf_op jit(solution)/shard_map/ppermute | solution.py:235
  182.0 1.5 copy-start.2
  183.7 5.0 %copy-start.4 = (bf16[2048,64]{1,0:T(8,128)(2,1)S(1)}, bf16[2048,64]{1,0:T(8,128)(2,1)}, u32[]{:S(2)}) copy-start(bf16[2048,64]{1,0:T(8,128)(2,1)} %get-tuple-element.21) | copy-start | bytes 786436
  183.9 6.2 %collective-permute-start.6 = (bf16[128,1024]{1,0:T(8,128)(2,1)S(1)}, bf16[128,1024]{1,0:T(8,128)(2,1)S(1)}, u32[]{:S(2)}, u32[]{:S(2)}) collective-permute-start(bf16[128,1024]{1,0:T(8,128)(2,1)S(1)} %get-tuple-element.47), channel_id=1, source_target_pairs={{0,1},{1,2},{2,3},{3,4},{4,5},{5,6},{6,7},{7,8},{8,9},{9,10},{10,1... | collective-permute-start | bytes 786440 | tf_op jit(solution)/shard_map/ppermute | solution.py:29
  186.7 8.7 %collective-permute-start.7 = (bf16[128,1024]{1,0:T(8,128)(2,1)S(1)}, bf16[128,1024]{1,0:T(8,128)(2,1)}, u32[]{:S(2)}, u32[]{:S(2)}) collective-permute-start(bf16[128,1024]{1,0:T(8,128)(2,1)S(1)} %get-tuple-element.48), channel_id=1, source_target_pairs={{1,0},{2,1},{3,2},{4,3},{5,4},{6,5},{7,6},{8,7},{9,8},{10,9},{11,1... | collective-permute-start | bytes 786440 | tf_op jit(solution)/shard_map/ppermute | solution.py:29

commit v7 on v5

--- a/solution.py
+++ b/solution.py
@@ -53,7 +53,7 @@
 
 
 TILE_Q = 256
-TILE_K = 256
+TILE_K = 512
 NT = (((1,), (1,)), ((), ()))
 TN = (((0,), (0,)), ((), ()))
 

time: 176 us -> 166 us (0.943)
  the two profiles are of different devices: /device:TPU:13 before, /device:TPU:9 now
where the time goes in v7:
time: 166 us; the launch traced here: 165 us
  Pallas kernels  66.3 us (40%)
  starting transfers between devices  39.2 us (24%)
  waiting for transfers between devices  27.8 us (17%)
  local copies, waits for them, and re-layouts  25 us (15%)
  other arithmetic  5.71 us (3%)
    pallas_call x1, Pallas kernels, on_device(): vmem_call(backward_kernel, 2, 11, (jax.ShapeDtypeStruct((block_rows, HEAD...  22 us
    pallas_call x1, Pallas kernels, on_device(): vmem_call(forward_kernel, 2, 5, (jax.ShapeDtypeStruct((block_rows, HEAD_D...  19.5 us
    all_to_all x1, waiting for transfers between devices, on_device(): lax.all_to_all(stacked, 'uly', split_axis=1, concat_axis=0, tiled=True)  19 us
    pallas_call x1, Pallas kernels, on_device(): vmem_call(conv_forward_kernel, 0, 6, (jax.ShapeDtypeStruct((HEAD_DIM, blo...  12.8 us
    pallas_call x1, Pallas kernels, on_device(): vmem_call(conv_backward_kernel, 0, 5, (jax.ShapeDtypeStruct((HEAD_DIM, bl...  12 us
    all_to_all x1, starting transfers between devices, on_device(): lax.all_to_all(stacked, 'uly', split_axis=1, concat_axis=0, tiled=True)  10 us
    ppermute x2, starting transfers between devices, padded_rims(): low = lax.ppermute(block[:, block.shape[1] - half:], 'blk', forward)  9.64 us
    ppermute x2, starting transfers between devices, passed_along(): return lax.ppermute(block, axis, route)  6.91 us
  transfers between devices with their start and end apart: 9, of which 5 were waited for; matrix products, arithmetic and copies ran while one was open for 6% of the time, Pallas kernels for 0%

profile of v7, /device:TPU:9, one launch (start us, length us, event | category | flops | bytes accessed | tf_op | source)
XLA Modules:
  0.0 164.9 jit_solution(2489410585742372951)
XLA Ops:
  0.6 1.1 copy.63
  1.8 1.1 copy.64
  2.9 1.1 copy.65
  4.1 0.9 copy.66
  5.1 10.0 %all-to-all-start = ((bf16[128,16,192]{0,2,1:T(8,128)(2,1)}), bf16[128,16,192]{0,2,1:T(8,128)(2,1)S(1)}, u32[]{:S(2)}, u32[]{:S(2)}) async-start(bf16[128,16,192]{0,2,1:T(8,128)(2,1)} %bitcast.5), calls=%async_computation | async-start | bytes 1572864 | tf_op jit(solution)/shard_map/all_to_all | solution.py:250
  15.3 0.5 slice.86
  16.0 0.2 select_reduce_fusion
  16.4 0.7 broadcast_minimum_fusion
  17.1 0.6 fusion.2
  17.7 0.6 and_select_fusion.kseg_ref
  18.4 19.0 %all-to-all-done = bf16[128,16,192]{0,2,1:T(8,128)(2,1)S(1)} async-done(((bf16[128,16,192]{0,2,1:T(8,128)(2,1)}), bf16[128,16,192]{0,2,1:T(8,128)(2,1)S(1)}, u32[]{:S(2)}, u32[]{:S(2)}) %all-to-all-start) | async-done | bytes 786464 | tf_op jit(solution)/shard_map/all_to_all | solution.py:250
  37.4 0.5 copy.67
  37.9 0.3 reshape.97
  38.3 0.8 slice_bitcast_fusion.2
  39.1 6.9 %collective-permute-start = (bf16[1024,128]{0,1:T(8,128)(2,1)S(1)}, bf16[1024,128]{0,1:T(8,128)(2,1)S(1)}, u32[]{:S(2)}, u32[]{:S(2)}) collective-permute-start(bf16[1024,128]{0,1:T(8,128)(2,1)S(1)} %get-tuple-element.56), channel_id=1, source_target_pairs={{0,1},{1,2},{2,3},{3,4},{4,5},{5,6},{6,7},{7,8},{8,9},{9,10},{10,1... | collective-permute-start | bytes 786440 | tf_op jit(solution)/shard_map/ppermute | solution.py:18
  46.0 1.9 %collective-permute-start.1 = (bf16[1024,128]{0,1:T(8,128)(2,1)S(1)}, bf16[1024,128]{0,1:T(8,128)(2,1)S(1)}, u32[]{:S(2)}, u32[]{:S(2)}) collective-permute-start(bf16[1024,128]{0,1:T(8,128)(2,1)S(1)} %get-tuple-element.57), channel_id=1, source_target_pairs={{1,0},{2,1},{3,2},{4,3},{5,4},{6,5},{7,6},{8,7},{9,8},{10,9},{11,1... | collective-permute-start | bytes 786440 | tf_op jit(solution)/shard_map/ppermute | solution.py:21
  48.1 0.7 copy.73
  48.9 0.7 copy.74.gain_ref
  49.6 1.3 copy.71.qseg_ref
  50.9 0.6 maximum_minimum_fusion
  51.5 1.1 copy.68.q_ref
  52.6 2.1 %collective-permute-done.1 = bf16[1024,128]{0,1:T(8,128)(2,1)S(1)} collective-permute-done((bf16[1024,128]{0,1:T(8,128)(2,1)S(1)}, bf16[1024,128]{0,1:T(8,128)(2,1)S(1)}, u32[]{:S(2)}, u32[]{:S(2)}) %collective-permute-start.1) | collective-permute-done | bytes 262176 | tf_op jit(solution)/shard_map/ppermute | solution.py:21
  54.8 1.3 copy.70.v_ref
  56.1 1.3 copy.69.k_ref
  57.5 19.5 %shard_map.102 = (bf16[2048,64]{1,0:T(8,128)(2,1)}, f32[2048,1]{1,0:T(8,128)}, f32[2048,1]{1,0:T(8,128)}) custom-call(s32[8]{0:T(128)} %get-tuple-element.43.lo_ref, s32[8]{0:T(128)} %get-tuple-element.42.hi_ref, bf16[2048,64]{1,0:T(8,128)(2,1)} %copy.68.q_ref, bf16[4096,64]{1,0:T(8,128)(2,1)} %copy.69.k_ref, bf16[4096,64]{1,0:T(8,128)(2,1)} %copy.70.v_ref, ...), custom_call_target="tpu_custom_call" | custom-call | tf_op jit(solution)/shard_map/pallas_call | solution.py:284
  77.0 1.3 copy.72
  78.4 1.9 %collective-permute-start.3 = (bf16[64,15]{1,0:T(8,128)(2,1)S(1)}, bf16[64,15]{1,0:T(8,128)(2,1)S(1)}, u32[]{:S(2)}, u32[]{:S(2)}) collective-permute-start(bf16[64,15]{1,0:T(8,128)(2,1)S(1)} %get-tuple-element.58), channel_id=1, source_target_pairs={{1,0},{2,1},{3,2},{4,3},{5,4},{6,5},{7,6},{8,7},{9,8},{10,9},{11,1... | collective-permute-start | bytes 5768 | tf_op jit(solution)/shard_map/ppermute | solution.py:236
  80.3 4.5 %collective-permute-start.2 = (bf16[64,15]{1,0:T(8,128)(2,1)S(1)}, bf16[64,15]{1,0:T(8,128)(2,1)S(1)}, u32[]{:S(2)}, u32[]{:S(2)}) collective-permute-start(bf16[64,15]{1,0:T(8,128)(2,1)S(1)} %get-tuple-element.59), channel_id=1, source_target_pairs={{0,1},{1,2},{2,3},{3,4},{4,5},{5,6},{6,7},{7,8},{8,9},{9,10},{10,1... | collective-permute-start | bytes 5768 | tf_op jit(solution)/shard_map/ppermute | solution.py:235
  84.9 0.8 collective-permute-done.2
  85.7 0.9 concatenate.23.x_ref
  86.6 12.8 %shard_map.103 = (bf16[64,2048]{1,0:T(8,128)(2,1)}, f32[64,2048]{1,0:T(8,128)}) custom-call(f32[64,2304]{1,0:T(8,128)} %concatenate.23.x_ref, f32[64,31]{1,0:T(8,128)} %bitcast.37, f32[64,1]{1,0:T(8,128)} %copy.74.gain_ref, bf16[64,2048]{1,0:T(8,128)(2,1)} %cot_ref.1, s32[1,2048]{1,0:T(1,128)} %get-tuple-element.61.lo_ref, s32[1,2048]{1,0:T(1,128)} %get-tuple-element.60.hi_ref), custom_call_target="tpu_custom_call" | custom-call | tf_op jit(solution)/shard_map/pallas_call | solution.py:300
  99.4 0.9 fusion.9
  100.3 1.9 %collective-permute-start.5 = (f32[64,15]{1,0:T(8,128)S(1)}, f32[64,15]{1,0:T(8,128)S(1)}, u32[]{:S(2)}, u32[]{:S(2)}) collective-permute-start(f32[64,15]{1,0:T(8,128)S(1)} %get-tuple-element.54), channel_id=1, source_target_pairs={{1,0},{2,1},{3,2},{4,3},{5,4},{6,5},{7,6},{8,7},{9,8},{10,9},{11,1... | collective-permute-start | bytes 11528 | tf_op jit(solution)/shard_map/ppermute | solution.py:236
  102.2 5.1 %collective-permute-start.4 = (f32[64,15]{1,0:T(8,128)S(1)}, f32[64,15]{1,0:T(8,128)S(1)}, u32[]{:S(2)}, u32[]{:S(2)}) collective-permute-start(f32[64,15]{1,0:T(8,128)S(1)} %get-tuple-element.55), channel_id=1, source_target_pairs={{0,1},{1,2},{2,3},{3,4},{4,5},{5,6},{6,7},{7,8},{8,9},{9,10},{10,1... | collective-permute-start | bytes 11528 | tf_op jit(solution)/shard_map/ppermute | solution.py:235
  107.3 1.1 broadcast_divide_fusion.il_ref
  108.5 0.9 concatenate.24.y_ref
  109.4 12.0 %shard_map.104 = (bf16[64,2048]{1,0:T(8,128)(2,1)}, f32[1,2048]{1,0:T(1,128)}) custom-call(f32[64,2304]{1,0:T(8,128)} %concatenate.24.y_ref, f32[64,31]{1,0:T(8,128)} %bitcast.38, bf16[64,2048]{1,0:T(8,128)(2,1)} %bitcast.31, s32[1,2048]{1,0:T(1,128)} %get-tuple-element.61.lo_ref, s32[1,2048]{1,0:T(1,128)} %get-tuple-element.60.hi_ref), custom_call_target="tpu_custom_call" | custom-call | tf_op jit(solution)/shard_map/pallas_call | solution.py:309
  121.5 2.0 %copy.75 = bf16[64,2048]{0,1:T(8,128)(2,1)} copy(bf16[64,2048]{1,0:T(8,128)(2,1)} %get-tuple-element.17.dot_ref) | data formatting | bytes 524288 | tf_op jit(solution)/shard_map/pallas_call | solution.py:309
  123.4 2.1 %copy.80.d_ref = f32[2048,1]{1,0:T(8,128)} copy(f32[2048,1]{0,1:T(1,128)} %bitcast.43) | data formatting | bytes 16384 | tf_op jit(solution)/shard_map/transpose | solution.py:319
  125.5 22.0 %shard_map.105 = (bf16[2048,64]{1,0:T(8,128)(2,1)}, f32[64,4096]{1,0:T(8,128)}, f32[64,4096]{1,0:T(8,128)}) custom-call(s32[8]{0:T(128)} %get-tuple-element.43.lo_ref, s32[8]{0:T(128)} %get-tuple-element.42.hi_ref, bf16[2048,64]{1,0:T(8,128)(2,1)} %copy.68.q_ref, bf16[4096,64]{1,0:T(8,128)(2,1)} %copy.69.k_ref, bf16[4096,64]{1,0:T(8,128)(2,1)} %copy.70.v_ref, ...), custom_call_target="tpu_custom_call" | custom-call | tf_op jit(solution)/shard_map/pallas_call | solution.py:322
  147.6 1.4 constant_dynamic-update-slice_fusion.1
  149.4 5.0 %collective-permute-start.6 = (bf16[128,1024]{1,0:T(8,128)(2,1)S(1)}, bf16[128,1024]{1,0:T(8,128)(2,1)S(1)}, u32[]{:S(2)}, u32[]{:S(2)}) collective-permute-start(bf16[128,1024]{1,0:T(8,128)(2,1)S(1)} %get-tuple-element.44), channel_id=1, source_target_pairs={{0,1},{1,2},{2,3},{3,4},{4,5},{5,6},{6,7},{7,8},{8,9},{9,10},{10,1... | collective-permute-start | bytes 786440 | tf_op jit(solution)/shard_map/ppermute | solution.py:29
  154.4 1.9 %collective-permute-start.7 = (bf16[128,1024]{1,0:T(8,128)(2,1)S(1)}, bf16[128,1024]{1,0:T(8,128)(2,1)}, u32[]{:S(2)}, u32[]{:S(2)}) collective-permute-start(bf16[128,1024]{1,0:T(8,128)(2,1)S(1)} %get-tuple-element.45), channel_id=1, source_target_pairs={{1,0},{2,1},{3,2},{4,3},{5,4},{6,5},{7,6},{8,7},{9,8},{10,9},{11,1... | collective-permute-start | bytes 786440 | tf_op jit(solution)/shard_map/ppermute | solution.py:29
  156.3 0.9 copy.81
  157.2 0.5 collective-permute-done.6
  157.7 5.4 %collective-permute-done.7 = bf16[128,1024]{1,0:T(8,128)(2,1)} collective-permute-done((bf16[128,1024]{1,0:T(8,128)(2,1)S(1)}, bf16[128,1024]{1,0:T(8,128)(2,1)}, u32[]{:S(2)}, u32[]{:S(2)}) %collective-permute-start.7) | collective-permute-done | bytes 262176 | tf_op jit(solution)/shard_map/ppermute | solution.py:29
  163.1 1.1 fusion
  164.1 0.8 fusion.8
  (41 shorter events, 1.5 us)
Async XLA Ops:
  4.0 11.1 %copy-start.6 = (s32[64]{0:T(128)S(1)}, s32[64]{0:T(128)}, u32[]{:S(2)}) copy-start(s32[64]{0:T(128)} %param.10) | copy-start | bytes 772
  5.1 32.3 %all-to-all-start = ((bf16[128,16,192]{0,2,1:T(8,128)(2,1)}), bf16[128,16,192]{0,2,1:T(8,128)(2,1)S(1)}, u32[]{:S(2)}, u32[]{:S(2)}) async-start(bf16[128,16,192]{0,2,1:T(8,128)(2,1)} %bitcast.5), calls=%async_computation | async-start | bytes 1572864 | tf_op jit(solution)/shard_map/all_to_all | solution.py:250
  37.9 10.2 %copy-start.5 = (f32[31,64]{1,0:T(8,128)S(1)}, f32[31,64]{1,0:T(8,128)}, u32[]{:S(2)}) copy-start(f32[31,64]{1,0:T(8,128)} %param.11) | copy-start | bytes 23812
  37.9 10.9 %copy-start.7 = (f32[64]{0:T(128)S(1)}, f32[64]{0:T(128)}, u32[]{:S(2)}) copy-start(f32[64]{0:T(128)} %param.12) | copy-start | bytes 772
  39.1 13.4 %collective-permute-start = (bf16[1024,128]{0,1:T(8,128)(2,1)S(1)}, bf16[1024,128]{0,1:T(8,128)(2,1)S(1)}, u32[]{:S(2)}, u32[]{:S(2)}) collective-permute-start(bf16[1024,128]{0,1:T(8,128)(2,1)S(1)} %get-tuple-element.56), channel_id=1, source_target_pairs={{0,1},{1,2},{2,3},{3,4},{4,5},{5,6},{6,7},{7,8},{8,9},{9,10},{10,1... | collective-permute-start | bytes 786440 | tf_op jit(solution)/shard_map/ppermute | solution.py:18
  46.0 8.6 %collective-permute-start.1 = (bf16[1024,128]{0,1:T(8,128)(2,1)S(1)}, bf16[1024,128]{0,1:T(8,128)(2,1)S(1)}, u32[]{:S(2)}, u32[]{:S(2)}) collective-permute-start(bf16[1024,128]{0,1:T(8,128)(2,1)S(1)} %get-tuple-element.57), channel_id=1, source_target_pairs={{1,0},{2,1},{3,2},{4,3},{5,4},{6,5},{7,6},{8,7},{9,8},{10,9},{11,1... | collective-permute-start | bytes 786440 | tf_op jit(solution)/shard_map/ppermute | solution.py:21
  77.0 30.4 %copy-start.1 = (f32[2048,1]{1,0:T(8,128)S(1)}, f32[2048,1]{1,0:T(8,128)}, u32[]{:S(2)}) copy-start(f32[2048,1]{1,0:T(8,128)} %get-tuple-element.19) | copy-start | bytes 24580
  78.3 30.2 %copy-start = (bf16[2048,64]{0,1:T(8,128)(2,1)}, bf16[2048,64]{0,1:T(8,128)(2,1)S(1)}, u32[]{:S(2)}) copy-start(bf16[2048,64]{0,1:T(8,128)(2,1)S(1)} %copy.72) | copy-start | bytes 786436
  78.4 6.5 %collective-permute-start.3 = (bf16[64,15]{1,0:T(8,128)(2,1)S(1)}, bf16[64,15]{1,0:T(8,128)(2,1)S(1)}, u32[]{:S(2)}, u32[]{:S(2)}) collective-permute-start(bf16[64,15]{1,0:T(8,128)(2,1)S(1)} %get-tuple-element.58), channel_id=1, source_target_pairs={{1,0},{2,1},{3,2},{4,3},{5,4},{6,5},{7,6},{8,7},{9,8},{10,9},{11,1... | collective-permute-start | bytes 5768 | tf_op jit(solution)/shard_map/ppermute | solution.py:236
  80.3 5.4 %collective-permute-start.2 = (bf16[64,15]{1,0:T(8,128)(2,1)S(1)}, bf16[64,15]{1,0:T(8,128)(2,1)S(1)}, u32[]{:S(2)}, u32[]{:S(2)}) collective-permute-start(bf16[64,15]{1,0:T(8,128)(2,1)S(1)} %get-tuple-element.59), channel_id=1, source_target_pairs={{0,1},{1,2},{2,3},{3,4},{4,5},{5,6},{6,7},{7,8},{8,9},{9,10},{10,1... | collective-permute-start | bytes 5768 | tf_op jit(solution)/shard_map/ppermute | solution.py:235
  99.4 9.1 %copy-start.3 = (f32[64,2048]{1,0:T(8,128)S(1)}, f32[64,2048]{1,0:T(8,128)}, u32[]{:S(2)}) copy-start(f32[64,2048]{1,0:T(8,128)} %get-tuple-element.16) | copy-start | bytes 1572868
  100.3 8.2 %collective-permute-start.5 = (f32[64,15]{1,0:T(8,128)S(1)}, f32[64,15]{1,0:T(8,128)S(1)}, u32[]{:S(2)}, u32[]{:S(2)}) collective-permute-start(f32[64,15]{1,0:T(8,128)S(1)} %get-tuple-element.54), channel_id=1, source_target_pairs={{1,0},{2,1},{3,2},{4,3},{5,4},{6,5},{7,6},{8,7},{9,8},{10,9},{11,1... | collective-permute-start | bytes 11528 | tf_op jit(solution)/shard_map/ppermute | solution.py:236
  102.2 6.2 %collective-permute-start.4 = (f32[64,15]{1,0:T(8,128)S(1)}, f32[64,15]{1,0:T(8,128)S(1)}, u32[]{:S(2)}, u32[]{:S(2)}) collective-permute-start(f32[64,15]{1,0:T(8,128)S(1)} %get-tuple-element.55), channel_id=1, source_target_pairs={{0,1},{1,2},{2,3},{3,4},{4,5},{5,6},{6,7},{7,8},{8,9},{9,10},{10,1... | collective-permute-start | bytes 11528 | tf_op jit(solution)/shard_map/ppermute | solution.py:235
  147.6 1.5 copy-start.2
  149.2 7.1 %copy-start.4 = (bf16[2048,64]{1,0:T(8,128)(2,1)S(1)}, bf16[2048,64]{1,0:T(8,128)(2,1)}, u32[]{:S(2)}) copy-start(bf16[2048,64]{1,0:T(8,128)(2,1)} %get-tuple-element.21) | copy-start | bytes 786436
  149.4 8.3 %collective-permute-start.6 = (bf16[128,1024]{1,0:T(8,128)(2,1)S(1)}, bf16[128,1024]{1,0:T(8,128)(2,1)S(1)}, u32[]{:S(2)}, u32[]{:S(2)}) collective-permute-start(bf16[128,1024]{1,0:T(8,128)(2,1)S(1)} %get-tuple-element.44), channel_id=1, source_target_pairs={{0,1},{1,2},{2,3},{3,4},{4,5},{5,6},{6,7},{7,8},{8,9},{9,10},{10,1... | collective-permute-start | bytes 786440 | tf_op jit(solution)/shard_map/ppermute | solution.py:29
  154.4 8.7 %collective-permute-start.7 = (bf16[128,1024]{1,0:T(8,128)(2,1)S(1)}, bf16[128,1024]{1,0:T(8,128)(2,1)}, u32[]{:S(2)}, u32[]{:S(2)}) collective-permute-start(bf16[128,1024]{1,0:T(8,128)(2,1)S(1)} %get-tuple-element.45), channel_id=1, source_target_pairs={{1,0},{2,1},{3,2},{4,3},{5,4},{6,5},{7,6},{8,7},{9,8},{10,9},{11,1... | collective-permute-start | bytes 786440 | tf_op jit(solution)/shard_map/ppermute | solution.py:29

commit v8 on v7

--- a/solution.py
+++ b/solution.py
@@ -52,7 +52,7 @@
     return jnp.where(same_seg, jnp.exp(scores - row_top), 0.0) / row_total
 
 
-TILE_Q = 256
+TILE_Q = 512
 TILE_K = 512
 NT = (((1,), (1,)), ((), ()))
 TN = (((0,), (0,)), ((), ()))

time: 166 us -> 164 us (0.988)
  Pallas kernels: 66.3 us -> 63.8 us
where the time goes in v8:
time: 164 us; the launch traced here: 163 us
  Pallas kernels  63.8 us (39%)
  starting transfers between devices  40.2 us (25%)
  waiting for transfers between devices  27.8 us (17%)
  local copies, waits for them, and re-layouts  24.9 us (15%)
  other arithmetic  5.71 us (3%)
    pallas_call x1, Pallas kernels, on_device(): vmem_call(backward_kernel, 2, 11, (jax.ShapeDtypeStruct((block_rows, HEAD...  21.1 us
    all_to_all x1, waiting for transfers between devices, on_device(): lax.all_to_all(stacked, 'uly', split_axis=1, concat_axis=0, tiled=True)  19 us
    pallas_call x1, Pallas kernels, on_device(): vmem_call(forward_kernel, 2, 5, (jax.ShapeDtypeStruct((block_rows, HEAD_D...  17.9 us
    pallas_call x1, Pallas kernels, on_device(): vmem_call(conv_forward_kernel, 0, 6, (jax.ShapeDtypeStruct((HEAD_DIM, blo...  12.8 us
    pallas_call x1, Pallas kernels, on_device(): vmem_call(conv_backward_kernel, 0, 5, (jax.ShapeDtypeStruct((HEAD_DIM, bl...  12 us
    all_to_all x1, starting transfers between devices, on_device(): lax.all_to_all(stacked, 'uly', split_axis=1, concat_axis=0, tiled=True)  10 us
    ppermute x2, starting transfers between devices, padded_rims(): low = lax.ppermute(block[:, block.shape[1] - half:], 'blk', forward)  9.64 us
    ppermute x2, starting transfers between devices, passed_along(): return lax.ppermute(block, axis, route)  7.94 us
  transfers between devices with their start and end apart: 9, of which 5 were waited for; matrix products, arithmetic and copies ran while one was open for 6% of the time, Pallas kernels for 0%

profile of v8, /device:TPU:9, one launch (start us, length us, event | category | flops | bytes accessed | tf_op | source)
XLA Modules:
  0.0 163.4 jit_solution(18428439580589090828)
XLA Ops:
  0.6 1.1 copy.63
  1.8 1.1 copy.64
  2.9 1.1 copy.65
  4.1 0.9 copy.66
  5.1 10.0 %all-to-all-start = ((bf16[128,16,192]{0,2,1:T(8,128)(2,1)}), bf16[128,16,192]{0,2,1:T(8,128)(2,1)S(1)}, u32[]{:S(2)}, u32[]{:S(2)}) async-start(bf16[128,16,192]{0,2,1:T(8,128)(2,1)} %bitcast.5), calls=%async_computation | async-start | bytes 1572864 | tf_op jit(solution)/shard_map/all_to_all | solution.py:250
  15.3 0.5 slice.86
  16.0 0.2 select_reduce_fusion
  16.4 0.7 broadcast_minimum_fusion
  17.1 0.6 fusion.2
  17.7 0.6 and_select_fusion.kseg_ref
  18.4 19.0 %all-to-all-done = bf16[128,16,192]{0,2,1:T(8,128)(2,1)S(1)} async-done(((bf16[128,16,192]{0,2,1:T(8,128)(2,1)}), bf16[128,16,192]{0,2,1:T(8,128)(2,1)S(1)}, u32[]{:S(2)}, u32[]{:S(2)}) %all-to-all-start) | async-done | bytes 786464 | tf_op jit(solution)/shard_map/all_to_all | solution.py:250
  37.4 0.5 copy.67
  37.9 0.3 reshape.97
  38.3 0.8 slice_bitcast_fusion.2
  39.1 6.9 %collective-permute-start = (bf16[1024,128]{0,1:T(8,128)(2,1)S(1)}, bf16[1024,128]{0,1:T(8,128)(2,1)S(1)}, u32[]{:S(2)}, u32[]{:S(2)}) collective-permute-start(bf16[1024,128]{0,1:T(8,128)(2,1)S(1)} %get-tuple-element.56), channel_id=1, source_target_pairs={{0,1},{1,2},{2,3},{3,4},{4,5},{5,6},{6,7},{7,8},{8,9},{9,10},{10,1... | collective-permute-start | bytes 786440 | tf_op jit(solution)/shard_map/ppermute | solution.py:18
  46.0 1.9 %collective-permute-start.1 = (bf16[1024,128]{0,1:T(8,128)(2,1)S(1)}, bf16[1024,128]{0,1:T(8,128)(2,1)S(1)}, u32[]{:S(2)}, u32[]{:S(2)}) collective-permute-start(bf16[1024,128]{0,1:T(8,128)(2,1)S(1)} %get-tuple-element.57), channel_id=1, source_target_pairs={{1,0},{2,1},{3,2},{4,3},{5,4},{6,5},{7,6},{8,7},{9,8},{10,9},{11,1... | collective-permute-start | bytes 786440 | tf_op jit(solution)/shard_map/ppermute | solution.py:21
  48.1 0.7 copy.73
  48.8 0.7 copy.74.gain_ref
  49.6 1.3 copy.71.qseg_ref
  50.9 0.6 maximum_minimum_fusion
  51.5 1.1 copy.68.q_ref
  52.5 2.1 %collective-permute-done.1 = bf16[1024,128]{0,1:T(8,128)(2,1)S(1)} collective-permute-done((bf16[1024,128]{0,1:T(8,128)(2,1)S(1)}, bf16[1024,128]{0,1:T(8,128)(2,1)S(1)}, u32[]{:S(2)}, u32[]{:S(2)}) %collective-permute-start.1) | collective-permute-done | bytes 262176 | tf_op jit(solution)/shard_map/ppermute | solution.py:21
  54.8 1.3 copy.70.v_ref
  56.1 1.3 copy.69.k_ref
  57.5 17.9 %shard_map.102 = (bf16[2048,64]{1,0:T(8,128)(2,1)}, f32[2048,1]{1,0:T(8,128)}, f32[2048,1]{1,0:T(8,128)}) custom-call(s32[4]{0:T(128)} %get-tuple-element.43.lo_ref, s32[4]{0:T(128)} %get-tuple-element.42.hi_ref, bf16[2048,64]{1,0:T(8,128)(2,1)} %copy.68.q_ref, bf16[4096,64]{1,0:T(8,128)(2,1)} %copy.69.k_ref, bf16[4096,64]{1,0:T(8,128)(2,1)} %copy.70.v_ref, ...), custom_call_target="tpu_custom_call" | custom-call | tf_op jit(solution)/shard_map/pallas_call | solution.py:284
  75.4 1.3 copy.72
  76.8 1.9 %collective-permute-start.3 = (bf16[64,15]{1,0:T(8,128)(2,1)S(1)}, bf16[64,15]{1,0:T(8,128)(2,1)S(1)}, u32[]{:S(2)}, u32[]{:S(2)}) collective-permute-start(bf16[64,15]{1,0:T(8,128)(2,1)S(1)} %get-tuple-element.58), channel_id=1, source_target_pairs={{1,0},{2,1},{3,2},{4,3},{5,4},{6,5},{7,6},{8,7},{9,8},{10,9},{11,1... | collective-permute-start | bytes 5768 | tf_op jit(solution)/shard_map/ppermute | solution.py:236
  78.7 4.5 %collective-permute-start.2 = (bf16[64,15]{1,0:T(8,128)(2,1)S(1)}, bf16[64,15]{1,0:T(8,128)(2,1)S(1)}, u32[]{:S(2)}, u32[]{:S(2)}) collective-permute-start(bf16[64,15]{1,0:T(8,128)(2,1)S(1)} %get-tuple-element.59), channel_id=1, source_target_pairs={{0,1},{1,2},{2,3},{3,4},{4,5},{5,6},{6,7},{7,8},{8,9},{9,10},{10,1... | collective-permute-start | bytes 5768 | tf_op jit(solution)/shard_map/ppermute | solution.py:235
  83.3 0.8 collective-permute-done.2
  84.1 0.9 concatenate.23.x_ref
  85.1 12.8 %shard_map.103 = (bf16[64,2048]{1,0:T(8,128)(2,1)}, f32[64,2048]{1,0:T(8,128)}) custom-call(f32[64,2304]{1,0:T(8,128)} %concatenate.23.x_ref, f32[64,31]{1,0:T(8,128)} %bitcast.37, f32[64,1]{1,0:T(8,128)} %copy.74.gain_ref, bf16[64,2048]{1,0:T(8,128)(2,1)} %cot_ref.1, s32[1,2048]{1,0:T(1,128)} %get-tuple-element.61.lo_ref, s32[1,2048]{1,0:T(1,128)} %get-tuple-element.60.hi_ref), custom_call_target="tpu_custom_call" | custom-call | tf_op jit(solution)/shard_map/pallas_call | solution.py:300
  97.8 0.9 fusion.9
  98.7 1.9 %collective-permute-start.5 = (f32[64,15]{1,0:T(8,128)S(1)}, f32[64,15]{1,0:T(8,128)S(1)}, u32[]{:S(2)}, u32[]{:S(2)}) collective-permute-start(f32[64,15]{1,0:T(8,128)S(1)} %get-tuple-element.54), channel_id=1, source_target_pairs={{1,0},{2,1},{3,2},{4,3},{5,4},{6,5},{7,6},{8,7},{9,8},{10,9},{11,1... | collective-permute-start | bytes 11528 | tf_op jit(solution)/shard_map/ppermute | solution.py:236
  100.7 5.1 %collective-permute-start.4 = (f32[64,15]{1,0:T(8,128)S(1)}, f32[64,15]{1,0:T(8,128)S(1)}, u32[]{:S(2)}, u32[]{:S(2)}) collective-permute-start(f32[64,15]{1,0:T(8,128)S(1)} %get-tuple-element.55), channel_id=1, source_target_pairs={{0,1},{1,2},{2,3},{3,4},{4,5},{5,6},{6,7},{7,8},{8,9},{9,10},{10,1... | collective-permute-start | bytes 11528 | tf_op jit(solution)/shard_map/ppermute | solution.py:235
  105.8 1.1 broadcast_divide_fusion.il_ref
  106.9 0.9 concatenate.24.y_ref
  107.8 12.0 %shard_map.104 = (bf16[64,2048]{1,0:T(8,128)(2,1)}, f32[1,2048]{1,0:T(1,128)}) custom-call(f32[64,2304]{1,0:T(8,128)} %concatenate.24.y_ref, f32[64,31]{1,0:T(8,128)} %bitcast.38, bf16[64,2048]{1,0:T(8,128)(2,1)} %bitcast.31, s32[1,2048]{1,0:T(1,128)} %get-tuple-element.61.lo_ref, s32[1,2048]{1,0:T(1,128)} %get-tuple-element.60.hi_ref), custom_call_target="tpu_custom_call" | custom-call | tf_op jit(solution)/shard_map/pallas_call | solution.py:309
  119.9 2.0 %copy.75 = bf16[64,2048]{0,1:T(8,128)(2,1)} copy(bf16[64,2048]{1,0:T(8,128)(2,1)} %get-tuple-element.17.dot_ref) | data formatting | bytes 524288 | tf_op jit(solution)/shard_map/pallas_call | solution.py:309
  121.9 2.1 %copy.80.d_ref = f32[2048,1]{1,0:T(8,128)} copy(f32[2048,1]{0,1:T(1,128)} %bitcast.43) | data formatting | bytes 16384 | tf_op jit(solution)/shard_map/transpose | solution.py:319
  123.9 21.1 %shard_map.105 = (bf16[2048,64]{1,0:T(8,128)(2,1)}, f32[64,4096]{1,0:T(8,128)}, f32[64,4096]{1,0:T(8,128)}) custom-call(s32[4]{0:T(128)} %get-tuple-element.43.lo_ref, s32[4]{0:T(128)} %get-tuple-element.42.hi_ref, bf16[2048,64]{1,0:T(8,128)(2,1)} %copy.68.q_ref, bf16[4096,64]{1,0:T(8,128)(2,1)} %copy.69.k_ref, bf16[4096,64]{1,0:T(8,128)(2,1)} %copy.70.v_ref, ...), custom_call_target="tpu_custom_call" | custom-call | tf_op jit(solution)/shard_map/pallas_call | solution.py:322
  145.0 1.4 constant_dynamic-update-slice_fusion.1
  146.8 6.0 %collective-permute-start.6 = (bf16[128,1024]{1,0:T(8,128)(2,1)S(1)}, bf16[128,1024]{1,0:T(8,128)(2,1)S(1)}, u32[]{:S(2)}, u32[]{:S(2)}) collective-permute-start(bf16[128,1024]{1,0:T(8,128)(2,1)S(1)} %get-tuple-element.44), channel_id=1, source_target_pairs={{0,1},{1,2},{2,3},{3,4},{4,5},{5,6},{6,7},{7,8},{8,9},{9,10},{10,1... | collective-permute-start | bytes 786440 | tf_op jit(solution)/shard_map/ppermute | solution.py:29
  152.9 1.9 %collective-permute-start.7 = (bf16[128,1024]{1,0:T(8,128)(2,1)S(1)}, bf16[128,1024]{1,0:T(8,128)(2,1)}, u32[]{:S(2)}, u32[]{:S(2)}) collective-permute-start(bf16[128,1024]{1,0:T(8,128)(2,1)S(1)} %get-tuple-element.45), channel_id=1, source_target_pairs={{1,0},{2,1},{3,2},{4,3},{5,4},{6,5},{7,6},{8,7},{9,8},{10,9},{11,1... | collective-permute-start | bytes 786440 | tf_op jit(solution)/shard_map/ppermute | solution.py:29
  154.8 0.9 copy.81
  155.7 0.5 collective-permute-done.6
  156.2 5.4 %collective-permute-done.7 = bf16[128,1024]{1,0:T(8,128)(2,1)} collective-permute-done((bf16[128,1024]{1,0:T(8,128)(2,1)S(1)}, bf16[128,1024]{1,0:T(8,128)(2,1)}, u32[]{:S(2)}, u32[]{:S(2)}) %collective-permute-start.7) | collective-permute-done | bytes 262176 | tf_op jit(solution)/shard_map/ppermute | solution.py:29
  161.6 1.1 fusion
  162.6 0.8 fusion.8
  (41 shorter events, 1.5 us)
Async XLA Ops:
  4.0 11.1 %copy-start.6 = (s32[64]{0:T(128)S(1)}, s32[64]{0:T(128)}, u32[]{:S(2)}) copy-start(s32[64]{0:T(128)} %param.10) | copy-start | bytes 772
  5.1 32.3 %all-to-all-start = ((bf16[128,16,192]{0,2,1:T(8,128)(2,1)}), bf16[128,16,192]{0,2,1:T(8,128)(2,1)S(1)}, u32[]{:S(2)}, u32[]{:S(2)}) async-start(bf16[128,16,192]{0,2,1:T(8,128)(2,1)} %bitcast.5), calls=%async_computation | async-start | bytes 1572864 | tf_op jit(solution)/shard_map/all_to_all | solution.py:250
  37.9 10.2 %copy-start.5 = (f32[31,64]{1,0:T(8,128)S(1)}, f32[31,64]{1,0:T(8,128)}, u32[]{:S(2)}) copy-start(f32[31,64]{1,0:T(8,128)} %param.11) | copy-start | bytes 23812
  37.9 10.9 %copy-start.7 = (f32[64]{0:T(128)S(1)}, f32[64]{0:T(128)}, u32[]{:S(2)}) copy-start(f32[64]{0:T(128)} %param.12) | copy-start | bytes 772
  39.1 13.4 %collective-permute-start = (bf16[1024,128]{0,1:T(8,128)(2,1)S(1)}, bf16[1024,128]{0,1:T(8,128)(2,1)S(1)}, u32[]{:S(2)}, u32[]{:S(2)}) collective-permute-start(bf16[1024,128]{0,1:T(8,128)(2,1)S(1)} %get-tuple-element.56), channel_id=1, source_target_pairs={{0,1},{1,2},{2,3},{3,4},{4,5},{5,6},{6,7},{7,8},{8,9},{9,10},{10,1... | collective-permute-start | bytes 786440 | tf_op jit(solution)/shard_map/ppermute | solution.py:18
  46.0 8.6 %collective-permute-start.1 = (bf16[1024,128]{0,1:T(8,128)(2,1)S(1)}, bf16[1024,128]{0,1:T(8,128)(2,1)S(1)}, u32[]{:S(2)}, u32[]{:S(2)}) collective-permute-start(bf16[1024,128]{0,1:T(8,128)(2,1)S(1)} %get-tuple-element.57), channel_id=1, source_target_pairs={{1,0},{2,1},{3,2},{4,3},{5,4},{6,5},{7,6},{8,7},{9,8},{10,9},{11,1... | collective-permute-start | bytes 786440 | tf_op jit(solution)/shard_map/ppermute | solution.py:21
  75.4 30.4 %copy-start.1 = (f32[2048,1]{1,0:T(8,128)S(1)}, f32[2048,1]{1,0:T(8,128)}, u32[]{:S(2)}) copy-start(f32[2048,1]{1,0:T(8,128)} %get-tuple-element.19) | copy-start | bytes 24580
  76.7 30.2 %copy-start = (bf16[2048,64]{0,1:T(8,128)(2,1)}, bf16[2048,64]{0,1:T(8,128)(2,1)S(1)}, u32[]{:S(2)}) copy-start(bf16[2048,64]{0,1:T(8,128)(2,1)S(1)} %copy.72) | copy-start | bytes 786436
  76.8 6.5 %collective-permute-start.3 = (bf16[64,15]{1,0:T(8,128)(2,1)S(1)}, bf16[64,15]{1,0:T(8,128)(2,1)S(1)}, u32[]{:S(2)}, u32[]{:S(2)}) collective-permute-start(bf16[64,15]{1,0:T(8,128)(2,1)S(1)} %get-tuple-element.58), channel_id=1, source_target_pairs={{1,0},{2,1},{3,2},{4,3},{5,4},{6,5},{7,6},{8,7},{9,8},{10,9},{11,1... | collective-permute-start | bytes 5768 | tf_op jit(solution)/shard_map/ppermute | solution.py:236
  78.7 5.4 %collective-permute-start.2 = (bf16[64,15]{1,0:T(8,128)(2,1)S(1)}, bf16[64,15]{1,0:T(8,128)(2,1)S(1)}, u32[]{:S(2)}, u32[]{:S(2)}) collective-permute-start(bf16[64,15]{1,0:T(8,128)(2,1)S(1)} %get-tuple-element.59), channel_id=1, source_target_pairs={{0,1},{1,2},{2,3},{3,4},{4,5},{5,6},{6,7},{7,8},{8,9},{9,10},{10,1... | collective-permute-start | bytes 5768 | tf_op jit(solution)/shard_map/ppermute | solution.py:235
  97.8 9.1 %copy-start.3 = (f32[64,2048]{1,0:T(8,128)S(1)}, f32[64,2048]{1,0:T(8,128)}, u32[]{:S(2)}) copy-start(f32[64,2048]{1,0:T(8,128)} %get-tuple-element.16) | copy-start | bytes 1572868
  98.7 8.2 %collective-permute-start.5 = (f32[64,15]{1,0:T(8,128)S(1)}, f32[64,15]{1,0:T(8,128)S(1)}, u32[]{:S(2)}, u32[]{:S(2)}) collective-permute-start(f32[64,15]{1,0:T(8,128)S(1)} %get-tuple-element.54), channel_id=1, source_target_pairs={{1,0},{2,1},{3,2},{4,3},{5,4},{6,5},{7,6},{8,7},{9,8},{10,9},{11,1... | collective-permute-start | bytes 11528 | tf_op jit(solution)/shard_map/ppermute | solution.py:236
  100.7 6.2 %collective-permute-start.4 = (f32[64,15]{1,0:T(8,128)S(1)}, f32[64,15]{1,0:T(8,128)S(1)}, u32[]{:S(2)}, u32[]{:S(2)}) collective-permute-start(f32[64,15]{1,0:T(8,128)S(1)} %get-tuple-element.55), channel_id=1, source_target_pairs={{0,1},{1,2},{2,3},{3,4},{4,5},{5,6},{6,7},{7,8},{8,9},{9,10},{10,1... | collective-permute-start | bytes 11528 | tf_op jit(solution)/shard_map/ppermute | solution.py:235
  145.0 1.5 copy-start.2
  146.7 8.1 %copy-start.4 = (bf16[2048,64]{1,0:T(8,128)(2,1)S(1)}, bf16[2048,64]{1,0:T(8,128)(2,1)}, u32[]{:S(2)}) copy-start(bf16[2048,64]{1,0:T(8,128)(2,1)} %get-tuple-element.21) | copy-start | bytes 786436
  146.8 9.4 %collective-permute-start.6 = (bf16[128,1024]{1,0:T(8,128)(2,1)S(1)}, bf16[128,1024]{1,0:T(8,128)(2,1)S(1)}, u32[]{:S(2)}, u32[]{:S(2)}) collective-permute-start(bf16[128,1024]{1,0:T(8,128)(2,1)S(1)} %get-tuple-element.44), channel_id=1, source_target_pairs={{0,1},{1,2},{2,3},{3,4},{4,5},{5,6},{6,7},{7,8},{8,9},{9,10},{10,1... | collective-permute-start | bytes 786440 | tf_op jit(solution)/shard_map/ppermute | solution.py:29
  152.9 8.7 %collective-permute-start.7 = (bf16[128,1024]{1,0:T(8,128)(2,1)S(1)}, bf16[128,1024]{1,0:T(8,128)(2,1)}, u32[]{:S(2)}, u32[]{:S(2)}) collective-permute-start(bf16[128,1024]{1,0:T(8,128)(2,1)S(1)} %get-tuple-element.45), channel_id=1, source_target_pairs={{1,0},{2,1},{3,2},{4,3},{5,4},{6,5},{7,6},{8,7},{9,8},{10,9},{11,1... | collective-permute-start | bytes 786440 | tf_op jit(solution)/shard_map/ppermute | solution.py:29

commit v9 on v8

--- a/solution.py
+++ b/solution.py
@@ -63,7 +63,7 @@
 
     def q_body(i, carry):
         r0 = pl.multiple_of(i * TILE_Q, TILE_Q)
-        q = q_ref[pl.ds(r0, TILE_Q), :]
+        q = q_ref[pl.ds(r0, TILE_Q), :] * jnp.asarray(scale, q_ref.dtype)
         qs = qseg_ref[pl.ds(r0, TILE_Q), :]
 
         def k_body(j, c):
@@ -72,11 +72,11 @@
             k = k_ref[pl.ds(c0, TILE_K), :]
             v = v_ref[pl.ds(c0, TILE_K), :]
             ks = kseg_ref[:, pl.ds(c0, TILE_K)]
-            s = scale * lax.dot_general(q, k, NT, preferred_element_type=jnp.float32)
-            mask = qs == ks
-            m_new = jnp.maximum(m, jnp.max(jnp.where(mask, s, -1e30), axis=1, keepdims=True))
+            s = lax.dot_general(q, k, NT, preferred_element_type=jnp.float32)
+            s = jnp.where(qs == ks, s, -1e30)
+            m_new = jnp.maximum(m, jnp.max(s, axis=1, keepdims=True))
             alpha = jnp.exp(m - m_new)
-            p = jnp.where(mask, jnp.exp(s - m_new), 0.0)
+            p = jnp.exp(s - m_new)
             l = alpha * l + jnp.sum(p, axis=1, keepdims=True)
             acc = alpha * acc + jnp.dot(
                 p.astype(jnp.bfloat16), v, preferred_element_type=jnp.float32
@@ -98,8 +98,8 @@
 
 
 def backward_kernel(
-    lo_ref, hi_ref, q_ref, k_ref, v_ref, do_ref, qt_ref, dot_ref, qseg_ref, kseg_ref, m_ref,
-    il_ref, d_ref, dq_ref, dk_ref, dv_ref,
+    lo_ref, hi_ref, q_ref, k_ref, v_ref, do_ref, qt_ref, dot_ref, qseg_ref, kseg_ref, lse_ref,
+    d_ref, dq_ref, dk_ref, dv_ref,
 ):
     scale = HEAD_DIM ** (-0.5)
     dk_ref[...] = jnp.zeros_like(dk_ref)
@@ -107,11 +107,10 @@
 
     def q_body(i, carry):
         r0 = pl.multiple_of(i * TILE_Q, TILE_Q)
-        q = q_ref[pl.ds(r0, TILE_Q), :]
+        q = q_ref[pl.ds(r0, TILE_Q), :] * jnp.asarray(scale, q_ref.dtype)
         do = do_ref[pl.ds(r0, TILE_Q), :]
         qs = qseg_ref[pl.ds(r0, TILE_Q), :]
-        m = m_ref[pl.ds(r0, TILE_Q), :]
-        il = il_ref[pl.ds(r0, TILE_Q), :]
+        lse = lse_ref[pl.ds(r0, TILE_Q), :]
         dlt = d_ref[pl.ds(r0, TILE_Q), :]
         q_t = qt_ref[:, pl.ds(r0, TILE_Q)]
         do_t = dot_ref[:, pl.ds(r0, TILE_Q)]
@@ -121,9 +120,8 @@
             k = k_ref[pl.ds(c0, TILE_K), :]
             v = v_ref[pl.ds(c0, TILE_K), :]
             ks = kseg_ref[:, pl.ds(c0, TILE_K)]
-            s = scale * lax.dot_general(q, k, NT, preferred_element_type=jnp.float32)
-            mask = qs == ks
-            p = jnp.where(mask, jnp.exp(s - m) * il, 0.0)
+            s = lax.dot_general(q, k, NT, preferred_element_type=jnp.float32)
+            p = jnp.exp(jnp.where(qs == ks, s, -1e30) - lse)
             dp = lax.dot_general(do, v, NT, preferred_element_type=jnp.float32)
             ds = (p * (dp - dlt)).astype(jnp.bfloat16)
             dk_ref[:, pl.ds(c0, TILE_K)] += jnp.dot(q_t, ds, preferred_element_type=jnp.float32)
@@ -322,7 +320,7 @@
     grad_q, dk_t, dv_t = vmem_call(
         backward_kernel,
         2,
-        11,
+        10,
         (
             jax.ShapeDtypeStruct((block_rows, HEAD_DIM), jnp.bfloat16),
             jax.ShapeDtypeStruct((HEAD_DIM, ext_rows), jnp.float32),
@@ -339,8 +337,7 @@
         grad_att_t,
         qseg_col,
         kseg_row,
-        row_tops,
-        1.0 / row_totals,
+        row_tops + jnp.log(row_totals),
         row_delta,
     )
     ext_terms = jnp.concatenate([dk_t, dv_t], axis=0)

time: 164 us -> 160 us (0.976)
  Pallas kernels: 63.8 us -> 60.8 us
    pallas_call x1, Pallas kernels: 21.1 us -> 19.1 us  [on_device(): vmem_call(backward_kernel, 2, 10, (jax.ShapeDtypeStruct((block_rows, HEAD...]
    unnamed x22 -> x24, local copies, waits for them, and re-layouts: 6.52 us -> 6.54 us
where the time goes in v9:
time: 160 us; the launch traced here: 159 us
  Pallas kernels  60.8 us (38%)
  starting transfers between devices  39.1 us (24%)
  waiting for transfers between devices  27.9 us (17%)
  local copies, waits for them, and re-layouts  25 us (16%)
  other arithmetic  5.65 us (4%)
    pallas_call x1, Pallas kernels, on_device(): vmem_call(backward_kernel, 2, 10, (jax.ShapeDtypeStruct((block_rows, HEAD...  19.1 us
    all_to_all x1, waiting for transfers between devices, on_device(): lax.all_to_all(stacked, 'uly', split_axis=1, concat_axis=0, tiled=True)  19 us
    pallas_call x1, Pallas kernels, on_device(): vmem_call(forward_kernel, 2, 5, (jax.ShapeDtypeStruct((block_rows, HEAD_D...  16.9 us
    pallas_call x1, Pallas kernels, on_device(): vmem_call(conv_forward_kernel, 0, 6, (jax.ShapeDtypeStruct((HEAD_DIM, blo...  12.8 us
    pallas_call x1, Pallas kernels, on_device(): vmem_call(conv_backward_kernel, 0, 5, (jax.ShapeDtypeStruct((HEAD_DIM, bl...  12 us
    all_to_all x1, starting transfers between devices, on_device(): lax.all_to_all(stacked, 'uly', split_axis=1, concat_axis=0, tiled=True)  10 us
    ppermute x2, starting transfers between devices, padded_rims(): low = lax.ppermute(block[:, block.shape[1] - half:], 'blk', forward)  9.64 us
    ppermute x1, starting transfers between devices, extended(): lax.ppermute(lax.slice_in_dim(block, block.shape[dim] - width, None, axis...  6.87 us
  transfers between devices with their start and end apart: 9, of which 5 were waited for; matrix products, arithmetic and copies ran while one was open for 6% of the time, Pallas kernels for 0%

profile of v9, /device:TPU:9, one launch (start us, length us, event | category | flops | bytes accessed | tf_op | source)
XLA Modules:
  0.0 159.4 jit_solution(14731163018946032762)
XLA Ops:
  0.6 1.1 copy.63
  1.8 1.1 copy.64
  2.9 1.1 copy.65
  4.1 0.9 copy.66
  5.1 10.0 %all-to-all-start = ((bf16[128,16,192]{0,2,1:T(8,128)(2,1)}), bf16[128,16,192]{0,2,1:T(8,128)(2,1)S(1)}, u32[]{:S(2)}, u32[]{:S(2)}) async-start(bf16[128,16,192]{0,2,1:T(8,128)(2,1)} %bitcast.5), calls=%async_computation | async-start | bytes 1572864 | tf_op jit(solution)/shard_map/all_to_all | solution.py:248
  15.3 0.5 slice.86
  16.0 0.2 select_reduce_fusion
  16.4 0.7 broadcast_minimum_fusion
  17.1 0.6 fusion.2
  17.7 0.6 and_select_fusion.kseg_ref
  18.3 19.0 %all-to-all-done = bf16[128,16,192]{0,2,1:T(8,128)(2,1)S(1)} async-done(((bf16[128,16,192]{0,2,1:T(8,128)(2,1)}), bf16[128,16,192]{0,2,1:T(8,128)(2,1)S(1)}, u32[]{:S(2)}, u32[]{:S(2)}) %all-to-all-start) | async-done | bytes 786464 | tf_op jit(solution)/shard_map/all_to_all | solution.py:248
  37.4 0.5 copy.67
  37.9 0.3 reshape.97
  38.3 0.8 slice_bitcast_fusion.2
  39.1 6.9 %collective-permute-start = (bf16[1024,128]{0,1:T(8,128)(2,1)S(1)}, bf16[1024,128]{0,1:T(8,128)(2,1)S(1)}, u32[]{:S(2)}, u32[]{:S(2)}) collective-permute-start(bf16[1024,128]{0,1:T(8,128)(2,1)S(1)} %get-tuple-element.56), channel_id=1, source_target_pairs={{0,1},{1,2},{2,3},{3,4},{4,5},{5,6},{6,7},{7,8},{8,9},{9,10},{10,1... | collective-permute-start | bytes 786440 | tf_op jit(solution)/shard_map/ppermute | solution.py:18
  46.0 1.9 %collective-permute-start.1 = (bf16[1024,128]{0,1:T(8,128)(2,1)S(1)}, bf16[1024,128]{0,1:T(8,128)(2,1)S(1)}, u32[]{:S(2)}, u32[]{:S(2)}) collective-permute-start(bf16[1024,128]{0,1:T(8,128)(2,1)S(1)} %get-tuple-element.57), channel_id=1, source_target_pairs={{1,0},{2,1},{3,2},{4,3},{5,4},{6,5},{7,6},{8,7},{9,8},{10,9},{11,1... | collective-permute-start | bytes 786440 | tf_op jit(solution)/shard_map/ppermute | solution.py:21
  48.1 0.7 copy.73
  48.8 0.7 copy.74.gain_ref
  49.6 1.3 copy.71.qseg_ref
  50.9 0.5 maximum_minimum_fusion
  51.4 1.0 copy.68.q_ref
  52.5 2.1 %collective-permute-done.1 = bf16[1024,128]{0,1:T(8,128)(2,1)S(1)} collective-permute-done((bf16[1024,128]{0,1:T(8,128)(2,1)S(1)}, bf16[1024,128]{0,1:T(8,128)(2,1)S(1)}, u32[]{:S(2)}, u32[]{:S(2)}) %collective-permute-start.1) | collective-permute-done | bytes 262176 | tf_op jit(solution)/shard_map/ppermute | solution.py:21
  54.8 1.3 copy.70.v_ref
  56.1 1.3 copy.69.k_ref
  57.5 16.9 %shard_map.102 = (bf16[2048,64]{1,0:T(8,128)(2,1)}, f32[2048,1]{1,0:T(8,128)}, f32[2048,1]{1,0:T(8,128)}) custom-call(s32[4]{0:T(128)} %get-tuple-element.43.lo_ref, s32[4]{0:T(128)} %get-tuple-element.42.hi_ref, bf16[2048,64]{1,0:T(8,128)(2,1)} %copy.68.q_ref, bf16[4096,64]{1,0:T(8,128)(2,1)} %copy.69.k_ref, bf16[4096,64]{1,0:T(8,128)(2,1)} %copy.70.v_ref, ...), custom_call_target="tpu_custom_call" | custom-call | tf_op jit(solution)/shard_map/pallas_call | solution.py:282
  74.4 1.4 copy.72
  75.8 1.9 %collective-permute-start.3 = (bf16[64,15]{1,0:T(8,128)(2,1)S(1)}, bf16[64,15]{1,0:T(8,128)(2,1)S(1)}, u32[]{:S(2)}, u32[]{:S(2)}) collective-permute-start(bf16[64,15]{1,0:T(8,128)(2,1)S(1)} %get-tuple-element.58), channel_id=1, source_target_pairs={{1,0},{2,1},{3,2},{4,3},{5,4},{6,5},{7,6},{8,7},{9,8},{10,9},{11,1... | collective-permute-start | bytes 5768 | tf_op jit(solution)/shard_map/ppermute | solution.py:234
  77.8 4.5 %collective-permute-start.2 = (bf16[64,15]{1,0:T(8,128)(2,1)S(1)}, bf16[64,15]{1,0:T(8,128)(2,1)S(1)}, u32[]{:S(2)}, u32[]{:S(2)}) collective-permute-start(bf16[64,15]{1,0:T(8,128)(2,1)S(1)} %get-tuple-element.59), channel_id=1, source_target_pairs={{0,1},{1,2},{2,3},{3,4},{4,5},{5,6},{6,7},{7,8},{8,9},{9,10},{10,1... | collective-permute-start | bytes 5768 | tf_op jit(solution)/shard_map/ppermute | solution.py:233
  82.4 0.8 collective-permute-done.2
  83.2 0.9 concatenate.23.x_ref
  84.1 12.8 %shard_map.103 = (bf16[64,2048]{1,0:T(8,128)(2,1)}, f32[64,2048]{1,0:T(8,128)}) custom-call(f32[64,2304]{1,0:T(8,128)} %concatenate.23.x_ref, f32[64,31]{1,0:T(8,128)} %bitcast.37, f32[64,1]{1,0:T(8,128)} %copy.74.gain_ref, bf16[64,2048]{1,0:T(8,128)(2,1)} %cot_ref.1, s32[1,2048]{1,0:T(1,128)} %get-tuple-element.61.lo_ref, s32[1,2048]{1,0:T(1,128)} %get-tuple-element.60.hi_ref), custom_call_target="tpu_custom_call" | custom-call | tf_op jit(solution)/shard_map/pallas_call | solution.py:298
  96.9 0.9 fusion.9
  97.8 1.9 %collective-permute-start.5 = (f32[64,15]{1,0:T(8,128)S(1)}, f32[64,15]{1,0:T(8,128)S(1)}, u32[]{:S(2)}, u32[]{:S(2)}) collective-permute-start(f32[64,15]{1,0:T(8,128)S(1)} %get-tuple-element.54), channel_id=1, source_target_pairs={{1,0},{2,1},{3,2},{4,3},{5,4},{6,5},{7,6},{8,7},{9,8},{10,9},{11,1... | collective-permute-start | bytes 11528 | tf_op jit(solution)/shard_map/ppermute | solution.py:234
  99.7 5.1 %collective-permute-start.4 = (f32[64,15]{1,0:T(8,128)S(1)}, f32[64,15]{1,0:T(8,128)S(1)}, u32[]{:S(2)}, u32[]{:S(2)}) collective-permute-start(f32[64,15]{1,0:T(8,128)S(1)} %get-tuple-element.55), channel_id=1, source_target_pairs={{0,1},{1,2},{2,3},{3,4},{4,5},{5,6},{6,7},{7,8},{8,9},{9,10},{10,1... | collective-permute-start | bytes 11528 | tf_op jit(solution)/shard_map/ppermute | solution.py:233
  104.8 1.1 log_add_fusion.lse_ref
  106.0 0.9 concatenate.24.y_ref
  106.9 12.0 %shard_map.104 = (bf16[64,2048]{1,0:T(8,128)(2,1)}, f32[1,2048]{1,0:T(1,128)}) custom-call(f32[64,2304]{1,0:T(8,128)} %concatenate.24.y_ref, f32[64,31]{1,0:T(8,128)} %bitcast.38, bf16[64,2048]{1,0:T(8,128)(2,1)} %bitcast.31, s32[1,2048]{1,0:T(1,128)} %get-tuple-element.61.lo_ref, s32[1,2048]{1,0:T(1,128)} %get-tuple-element.60.hi_ref), custom_call_target="tpu_custom_call" | custom-call | tf_op jit(solution)/shard_map/pallas_call | solution.py:307
  118.9 2.0 %copy.75 = bf16[64,2048]{0,1:T(8,128)(2,1)} copy(bf16[64,2048]{1,0:T(8,128)(2,1)} %get-tuple-element.17.dot_ref) | data formatting | bytes 524288 | tf_op jit(solution)/shard_map/pallas_call | solution.py:307
  120.9 2.0 %copy.80.d_ref = f32[2048,1]{1,0:T(8,128)} copy(f32[2048,1]{0,1:T(1,128)} %bitcast.43) | data formatting | bytes 16384 | tf_op jit(solution)/shard_map/transpose | solution.py:317
  123.0 19.1 %shard_map.105 = (bf16[2048,64]{1,0:T(8,128)(2,1)}, f32[64,4096]{1,0:T(8,128)}, f32[64,4096]{1,0:T(8,128)}) custom-call(s32[4]{0:T(128)} %get-tuple-element.43.lo_ref, s32[4]{0:T(128)} %get-tuple-element.42.hi_ref, bf16[2048,64]{1,0:T(8,128)(2,1)} %copy.68.q_ref, bf16[4096,64]{1,0:T(8,128)(2,1)} %copy.69.k_ref, bf16[4096,64]{1,0:T(8,128)(2,1)} %copy.70.v_ref, ...), custom_call_target="tpu_custom_call" | custom-call | tf_op jit(solution)/shard_map/pallas_call | solution.py:320
  142.1 1.4 constant_dynamic-update-slice_fusion.1
  143.9 4.9 %collective-permute-start.6 = (bf16[128,1024]{1,0:T(8,128)(2,1)S(1)}, bf16[128,1024]{1,0:T(8,128)(2,1)S(1)}, u32[]{:S(2)}, u32[]{:S(2)}) collective-permute-start(bf16[128,1024]{1,0:T(8,128)(2,1)S(1)} %get-tuple-element.44), channel_id=1, source_target_pairs={{0,1},{1,2},{2,3},{3,4},{4,5},{5,6},{6,7},{7,8},{8,9},{9,10},{10,1... | collective-permute-start | bytes 786440 | tf_op jit(solution)/shard_map/ppermute | solution.py:29
  148.8 1.9 %collective-permute-start.7 = (bf16[128,1024]{1,0:T(8,128)(2,1)S(1)}, bf16[128,1024]{1,0:T(8,128)(2,1)}, u32[]{:S(2)}, u32[]{:S(2)}) collective-permute-start(bf16[128,1024]{1,0:T(8,128)(2,1)S(1)} %get-tuple-element.45), channel_id=1, source_target_pairs={{1,0},{2,1},{3,2},{4,3},{5,4},{6,5},{7,6},{8,7},{9,8},{10,9},{11,1... | collective-permute-start | bytes 786440 | tf_op jit(solution)/shard_map/ppermute | solution.py:29
  150.8 0.9 copy.81
  151.7 0.5 collective-permute-done.6
  152.1 5.4 %collective-permute-done.7 = bf16[128,1024]{1,0:T(8,128)(2,1)} collective-permute-done((bf16[128,1024]{1,0:T(8,128)(2,1)S(1)}, bf16[128,1024]{1,0:T(8,128)(2,1)}, u32[]{:S(2)}, u32[]{:S(2)}) %collective-permute-start.7) | collective-permute-done | bytes 262176 | tf_op jit(solution)/shard_map/ppermute | solution.py:29
  157.5 1.1 fusion
  158.6 0.8 fusion.8
  (43 shorter events, 1.5 us)
Async XLA Ops:
  4.0 11.1 %copy-start.7 = (s32[64]{0:T(128)S(1)}, s32[64]{0:T(128)}, u32[]{:S(2)}) copy-start(s32[64]{0:T(128)} %param.10) | copy-start | bytes 772
  5.1 32.3 %all-to-all-start = ((bf16[128,16,192]{0,2,1:T(8,128)(2,1)}), bf16[128,16,192]{0,2,1:T(8,128)(2,1)S(1)}, u32[]{:S(2)}, u32[]{:S(2)}) async-start(bf16[128,16,192]{0,2,1:T(8,128)(2,1)} %bitcast.5), calls=%async_computation | async-start | bytes 1572864 | tf_op jit(solution)/shard_map/all_to_all | solution.py:248
  37.9 10.2 %copy-start.6 = (f32[31,64]{1,0:T(8,128)S(1)}, f32[31,64]{1,0:T(8,128)}, u32[]{:S(2)}) copy-start(f32[31,64]{1,0:T(8,128)} %param.11) | copy-start | bytes 23812
  37.9 10.9 %copy-start.8 = (f32[64]{0:T(128)S(1)}, f32[64]{0:T(128)}, u32[]{:S(2)}) copy-start(f32[64]{0:T(128)} %param.12) | copy-start | bytes 772
  39.1 13.3 %collective-permute-start = (bf16[1024,128]{0,1:T(8,128)(2,1)S(1)}, bf16[1024,128]{0,1:T(8,128)(2,1)S(1)}, u32[]{:S(2)}, u32[]{:S(2)}) collective-permute-start(bf16[1024,128]{0,1:T(8,128)(2,1)S(1)} %get-tuple-element.56), channel_id=1, source_target_pairs={{0,1},{1,2},{2,3},{3,4},{4,5},{5,6},{6,7},{7,8},{8,9},{9,10},{10,1... | collective-permute-start | bytes 786440 | tf_op jit(solution)/shard_map/ppermute | solution.py:18
  46.0 8.6 %collective-permute-start.1 = (bf16[1024,128]{0,1:T(8,128)(2,1)S(1)}, bf16[1024,128]{0,1:T(8,128)(2,1)S(1)}, u32[]{:S(2)}, u32[]{:S(2)}) collective-permute-start(bf16[1024,128]{0,1:T(8,128)(2,1)S(1)} %get-tuple-element.57), channel_id=1, source_target_pairs={{1,0},{2,1},{3,2},{4,3},{5,4},{6,5},{7,6},{8,7},{9,8},{10,9},{11,1... | collective-permute-start | bytes 786440 | tf_op jit(solution)/shard_map/ppermute | solution.py:21
  74.4 30.4 %copy-start.1 = (f32[2048,1]{1,0:T(8,128)S(1)}, f32[2048,1]{1,0:T(8,128)}, u32[]{:S(2)}) copy-start(f32[2048,1]{1,0:T(8,128)} %get-tuple-element.18) | copy-start | bytes 24580
  74.4 30.4 %copy-start.2 = (f32[2048,1]{1,0:T(8,128)S(1)}, f32[2048,1]{1,0:T(8,128)}, u32[]{:S(2)}) copy-start(f32[2048,1]{1,0:T(8,128)} %get-tuple-element.19) | copy-start | bytes 24580
  75.7 30.2 %copy-start = (bf16[2048,64]{0,1:T(8,128)(2,1)}, bf16[2048,64]{0,1:T(8,128)(2,1)S(1)}, u32[]{:S(2)}) copy-start(bf16[2048,64]{0,1:T(8,128)(2,1)S(1)} %copy.72) | copy-start | bytes 786436
  75.8 6.5 %collective-permute-start.3 = (bf16[64,15]{1,0:T(8,128)(2,1)S(1)}, bf16[64,15]{1,0:T(8,128)(2,1)S(1)}, u32[]{:S(2)}, u32[]{:S(2)}) collective-permute-start(bf16[64,15]{1,0:T(8,128)(2,1)S(1)} %get-tuple-element.58), channel_id=1, source_target_pairs={{1,0},{2,1},{3,2},{4,3},{5,4},{6,5},{7,6},{8,7},{9,8},{10,9},{11,1... | collective-permute-start | bytes 5768 | tf_op jit(solution)/shard_map/ppermute | solution.py:234
  77.8 5.4 %collective-permute-start.2 = (bf16[64,15]{1,0:T(8,128)(2,1)S(1)}, bf16[64,15]{1,0:T(8,128)(2,1)S(1)}, u32[]{:S(2)}, u32[]{:S(2)}) collective-permute-start(bf16[64,15]{1,0:T(8,128)(2,1)S(1)} %get-tuple-element.59), channel_id=1, source_target_pairs={{0,1},{1,2},{2,3},{3,4},{4,5},{5,6},{6,7},{7,8},{8,9},{9,10},{10,1... | collective-permute-start | bytes 5768 | tf_op jit(solution)/shard_map/ppermute | solution.py:233
  96.9 9.1 %copy-start.4 = (f32[64,2048]{1,0:T(8,128)S(1)}, f32[64,2048]{1,0:T(8,128)}, u32[]{:S(2)}) copy-start(f32[64,2048]{1,0:T(8,128)} %get-tuple-element.16) | copy-start | bytes 1572868
  97.8 8.2 %collective-permute-start.5 = (f32[64,15]{1,0:T(8,128)S(1)}, f32[64,15]{1,0:T(8,128)S(1)}, u32[]{:S(2)}, u32[]{:S(2)}) collective-permute-start(f32[64,15]{1,0:T(8,128)S(1)} %get-tuple-element.54), channel_id=1, source_target_pairs={{1,0},{2,1},{3,2},{4,3},{5,4},{6,5},{7,6},{8,7},{9,8},{10,9},{11,1... | collective-permute-start | bytes 11528 | tf_op jit(solution)/shard_map/ppermute | solution.py:234
  99.7 6.3 %collective-permute-start.4 = (f32[64,15]{1,0:T(8,128)S(1)}, f32[64,15]{1,0:T(8,128)S(1)}, u32[]{:S(2)}, u32[]{:S(2)}) collective-permute-start(f32[64,15]{1,0:T(8,128)S(1)} %get-tuple-element.55), channel_id=1, source_target_pairs={{0,1},{1,2},{2,3},{3,4},{4,5},{5,6},{6,7},{7,8},{8,9},{9,10},{10,1... | collective-permute-start | bytes 11528 | tf_op jit(solution)/shard_map/ppermute | solution.py:233
  142.1 1.5 copy-start.3
  143.7 7.1 %copy-start.5 = (bf16[2048,64]{1,0:T(8,128)(2,1)S(1)}, bf16[2048,64]{1,0:T(8,128)(2,1)}, u32[]{:S(2)}) copy-start(bf16[2048,64]{1,0:T(8,128)(2,1)} %get-tuple-element.21) | copy-start | bytes 786436
  143.9 8.2 %collective-permute-start.6 = (bf16[128,1024]{1,0:T(8,128)(2,1)S(1)}, bf16[128,1024]{1,0:T(8,128)(2,1)S(1)}, u32[]{:S(2)}, u32[]{:S(2)}) collective-permute-start(bf16[128,1024]{1,0:T(8,128)(2,1)S(1)} %get-tuple-element.44), channel_id=1, source_target_pairs={{0,1},{1,2},{2,3},{3,4},{4,5},{5,6},{6,7},{7,8},{8,9},{9,10},{10,1... | collective-permute-start | bytes 786440 | tf_op jit(solution)/shard_map/ppermute | solution.py:29
  148.8 8.7 %collective-permute-start.7 = (bf16[128,1024]{1,0:T(8,128)(2,1)S(1)}, bf16[128,1024]{1,0:T(8,128)(2,1)}, u32[]{:S(2)}, u32[]{:S(2)}) collective-permute-start(bf16[128,1024]{1,0:T(8,128)(2,1)S(1)} %get-tuple-element.45), channel_id=1, source_target_pairs={{1,0},{2,1},{3,2},{4,3},{5,4},{6,5},{7,6},{8,7},{9,8},{10,9},{11,1... | collective-permute-start | bytes 786440 | tf_op jit(solution)/shard_map/ppermute | solution.py:29

commit v10 on v9

--- a/solution.py
+++ b/solution.py
@@ -140,10 +140,11 @@
     dk_ref[...] = scale * dk_ref[...]
 
 
-def vmem_call(kernel, n_smem, n_vmem, out_shape):
+def vmem_call(kernel, n_smem, n_vmem, out_shape, scratch=()):
     return pl.pallas_call(
         kernel,
         out_shape=out_shape,
+        scratch_shapes=list(scratch),
         in_specs=[pl.BlockSpec(memory_space=pltpu.SMEM)] * n_smem
         + [pl.BlockSpec(memory_space=pltpu.VMEM)] * n_vmem,
         out_specs=[pl.BlockSpec(memory_space=pltpu.VMEM)] * len(out_shape),
@@ -173,27 +174,52 @@
 CONV_CHUNK = 256
 
 
-def conv_chunk(x_ref, wt_ref, lo, hi, c0, sign):
-    window = x_ref[:, pl.ds(c0, CONV_CHUNK + 2 * CONV_PAD)]
-    width = window.shape[1]
-    total = jnp.zeros((window.shape[0], CONV_CHUNK), jnp.float32)
+def conv_group(x_ref, wb_ref, mask_ref, c0, g8, sign):
+    win = [x_ref[pl.ds(g8, 8), pl.ds(c0 + 128 * i, 128)] for i in range(4)]
+    lane = lax.broadcasted_iota(jnp.int32, (8, 128), 1)
+    total = [jnp.zeros((8, 128), jnp.float32) for _ in range(2)]
     for tap in range(KERNEL):
         d = sign * (tap - KERNEL // 2)
-        shifted = pltpu.roll(window, (width - d) % width, 1) if d else window
-        keep = (lo <= d) & (d < hi)
-        total = total + wt_ref[:, tap : tap + 1] * jnp.where(
-            keep, shifted[:, CONV_PAD : CONV_PAD + CONV_CHUNK], 0.0
-        )
-    return total
-
-
-def conv_forward_kernel(x_ref, wt_ref, gain_ref, cot_ref, lo_ref, hi_ref, out_ref, gc_ref):
+        if d == 0:
+            outs = [win[1], win[2]]
+        elif d > 0:
+            r = [pltpu.roll(win[i], 128 - d, 1) for i in (1, 2, 3)]
+            outs = [jnp.where(lane < 128 - d, r[k], r[k + 1]) for k in range(2)]
+        else:
+            r = [pltpu.roll(win[i], -d, 1) for i in (0, 1, 2)]
+            outs = [jnp.where(lane >= -d, r[k + 1], r[k]) for k in range(2)]
+        w = wb_ref[tap, pl.ds(g8, 8), :]
+        for k in range(2):
+            total[k] = total[k] + w * (mask_ref[tap, :, pl.ds(128 * k, 128)] * outs[k])
+    return jnp.concatenate(total, axis=1)
+
+
+def conv_chunk(x_ref, wb_ref, lo, hi, c0, sign, mask_ref, cs_ref):
+    for tap in range(KERNEL):
+        d = sign * (tap - KERNEL // 2)
+        keep = ((lo <= d) & (d < hi)).astype(jnp.float32)
+        mask_ref[tap] = jnp.broadcast_to(keep, (8, CONV_CHUNK))
+
+    def group(g, carry):
+        g8 = pl.multiple_of(g * 8, 8)
+        cs_ref[pl.ds(g8, 8), :] = conv_group(x_ref, wb_ref, mask_ref, c0, g8, sign)
+        return carry
+
+    lax.fori_loop(0, cs_ref.shape[0] // 8, group, 0)
+    return cs_ref[...]
+
+
+def conv_forward_kernel(
+    x_ref, wt_ref, gain_ref, cot_ref, lo_ref, hi_ref, out_ref, gc_ref, mask_ref, cs_ref
+):
     gain = gain_ref[...]
 
     def body(c, carry):
         c0 = pl.multiple_of(c * CONV_CHUNK, CONV_CHUNK)
         cols = pl.ds(c0, CONV_CHUNK)
-        conv_sum = conv_chunk(x_ref, wt_ref, lo_ref[:, cols], hi_ref[:, cols], c0, 1)
+        conv_sum = conv_chunk(
+            x_ref, wt_ref, lo_ref[:, cols], hi_ref[:, cols], c0, 1, mask_ref, cs_ref
+        )
         spread = jnp.sqrt(jnp.mean(conv_sum * conv_sum, axis=0, keepdims=True) + 1e-05)
         normed = conv_sum / spread
         pre_act = normed * gain
@@ -209,11 +235,15 @@
     lax.fori_loop(0, out_ref.shape[1] // CONV_CHUNK, body, 0)
 
 
-def conv_backward_kernel(y_ref, wt_ref, att_ref, lo_ref, hi_ref, ga_ref, delta_ref):
+def conv_backward_kernel(
+    y_ref, wt_ref, att_ref, lo_ref, hi_ref, ga_ref, delta_ref, mask_ref, cs_ref
+):
     def body(c, carry):
         c0 = pl.multiple_of(c * CONV_CHUNK, CONV_CHUNK)
         cols = pl.ds(c0, CONV_CHUNK)
-        grad_sum = conv_chunk(y_ref, wt_ref, lo_ref[:, cols], hi_ref[:, cols], c0, -1)
+        grad_sum = conv_chunk(
+            y_ref, wt_ref, lo_ref[:, cols], hi_ref[:, cols], c0, -1, mask_ref, cs_ref
+        )
         grad_att = grad_sum.astype(ga_ref.dtype)
         ga_ref[:, cols] = grad_att
         delta_ref[:, cols] = jnp.sum(
@@ -293,7 +323,11 @@
     seg_start, seg_end = segment_bounds(lengths, frame_at)
     lo_off = (seg_start - frame_at)[None, :].astype(jnp.int32)
     hi_off = (seg_end - frame_at)[None, :].astype(jnp.int32)
-    weight_t = conv_weight.T
+    weight_t = jnp.broadcast_to(conv_weight[:, :, None], conv_weight.shape + (128,))
+    conv_scratch = (
+        pltpu.VMEM((KERNEL, 8, CONV_CHUNK), jnp.float32),
+        pltpu.VMEM((HEAD_DIM, CONV_CHUNK), jnp.float32),
+    )
     att_t = attended.T
     conv_out_t, grad_conv_t = vmem_call(
         conv_forward_kernel,
@@ -303,6 +337,7 @@
             jax.ShapeDtypeStruct((HEAD_DIM, block_rows), jnp.bfloat16),
             jax.ShapeDtypeStruct((HEAD_DIM, block_rows), jnp.float32),
         ),
+        conv_scratch,
     )(padded_rims(att_t, conv_half), weight_t, norm_gain[:, None], cotangent, lo_off, hi_off)
     grad_att_t, delta_row = vmem_call(
         conv_backward_kernel,
@@ -312,6 +347,7 @@
             jax.ShapeDtypeStruct((HEAD_DIM, block_rows), jnp.bfloat16),
             jax.ShapeDtypeStruct((1, block_rows), jnp.float32),
         ),
+        conv_scratch,
     )(padded_rims(grad_conv_t, conv_half), weight_t, att_t, lo_off, hi_off)
     grad_attended = grad_att_t.T
     row_delta = delta_row.T

time: 160 us -> 164 us (1.025)
  starting transfers between devices: 39.1 us -> 41 us
    ppermute x2, starting transfers between devices: 6.86 us -> 8.72 us  [passed_along(): return lax.ppermute(block, axis, route)]
    pallas_call x1, Pallas kernels: 19.1 us -> 17.2 us  [on_device(): vmem_call(backward_kernel, 2, 10, (jax.ShapeDtypeStruct((block_rows, HEAD...]
    pallas_call x1, Pallas kernels: 16.9 us -> 15.2 us  [on_device(): vmem_call(forward_kernel, 2, 5, (jax.ShapeDtypeStruct((block_rows, HEAD_D...]
    unnamed x24 -> x23, local copies, waits for them, and re-layouts: 6.54 us -> 5.83 us
where the time goes in v10:
time: 164 us; the launch traced here: 162 us
  Pallas kernels  60.3 us (37%)
  starting transfers between devices  41 us (25%)
  waiting for transfers between devices  28.6 us (17%)
  local copies, waits for them, and re-layouts  25.4 us (15%)
  other arithmetic  5.65 us (3%)
    all_to_all x1, waiting for transfers between devices, on_device(): lax.all_to_all(stacked, 'uly', split_axis=1, concat_axis=0, tiled=True)  19.1 us
    pallas_call x1, Pallas kernels, on_device(): vmem_call(backward_kernel, 2, 10, (jax.ShapeDtypeStruct((block_rows, HEAD...  17.2 us
    pallas_call x1, Pallas kernels, on_device(): vmem_call(forward_kernel, 2, 5, (jax.ShapeDtypeStruct((block_rows, HEAD_D...  15.2 us
    pallas_call x1, Pallas kernels, on_device(): vmem_call(conv_forward_kernel, 0, 6, (jax.ShapeDtypeStruct((HEAD_DIM, blo...  14.3 us
    pallas_call x1, Pallas kernels, on_device(): vmem_call(conv_backward_kernel, 0, 5, (jax.ShapeDtypeStruct((HEAD_DIM, bl...  13.5 us
    all_to_all x1, starting transfers between devices, on_device(): lax.all_to_all(stacked, 'uly', split_axis=1, concat_axis=0, tiled=True)  10 us
    ppermute x2, starting transfers between devices, padded_rims(): low = lax.ppermute(block[:, block.shape[1] - half:], 'blk', forward)  9.65 us
    ppermute x2, starting transfers between devices, passed_along(): return lax.ppermute(block, axis, route)  8.72 us
  transfers between devices with their start and end apart: 9, of which 5 were waited for; matrix products, arithmetic and copies ran while one was open for 6% of the time, Pallas kernels for 0%

profile of v10, /device:TPU:9, one launch (start us, length us, event | category | flops | bytes accessed | tf_op | source)
XLA Modules:
  0.0 161.9 jit_solution(577920641218139597)
XLA Ops:
  0.6 1.1 copy.60
  1.8 1.1 copy.61
  2.9 1.1 copy.62
  4.1 0.9 copy.63
  5.1 10.0 %all-to-all-start = ((bf16[128,16,192]{0,2,1:T(8,128)(2,1)}), bf16[128,16,192]{0,2,1:T(8,128)(2,1)S(1)}, u32[]{:S(2)}, u32[]{:S(2)}) async-start(bf16[128,16,192]{0,2,1:T(8,128)(2,1)} %bitcast.5), calls=%async_computation | async-start | bytes 1572864 | tf_op jit(solution)/shard_map/all_to_all | solution.py:278
  15.3 0.5 slice.86
  16.0 0.2 select_reduce_fusion
  16.4 0.7 broadcast_minimum_fusion
  17.1 0.6 fusion.2
  17.7 0.6 and_select_fusion.kseg_ref
  18.3 19.1 %all-to-all-done = bf16[128,16,192]{0,2,1:T(8,128)(2,1)S(1)} async-done(((bf16[128,16,192]{0,2,1:T(8,128)(2,1)}), bf16[128,16,192]{0,2,1:T(8,128)(2,1)S(1)}, u32[]{:S(2)}, u32[]{:S(2)}) %all-to-all-start) | async-done | bytes 786464 | tf_op jit(solution)/shard_map/all_to_all | solution.py:278
  37.4 0.5 copy.64
  37.9 0.3 reshape.98
  38.3 0.8 slice_bitcast_fusion.2
  39.1 6.9 %collective-permute-start = (bf16[1024,128]{0,1:T(8,128)(2,1)S(1)}, bf16[1024,128]{0,1:T(8,128)(2,1)S(1)}, u32[]{:S(2)}, u32[]{:S(2)}) collective-permute-start(bf16[1024,128]{0,1:T(8,128)(2,1)S(1)} %get-tuple-element.56), channel_id=1, source_target_pairs={{0,1},{1,2},{2,3},{3,4},{4,5},{5,6},{6,7},{7,8},{8,9},{9,10},{10,1... | collective-permute-start | bytes 786440 | tf_op jit(solution)/shard_map/ppermute | solution.py:18
  46.0 1.9 %collective-permute-start.1 = (bf16[1024,128]{0,1:T(8,128)(2,1)S(1)}, bf16[1024,128]{0,1:T(8,128)(2,1)S(1)}, u32[]{:S(2)}, u32[]{:S(2)}) collective-permute-start(bf16[1024,128]{0,1:T(8,128)(2,1)S(1)} %get-tuple-element.57), channel_id=1, source_target_pairs={{1,0},{2,1},{3,2},{4,3},{5,4},{6,5},{7,6},{8,7},{9,8},{10,9},{11,1... | collective-permute-start | bytes 786440 | tf_op jit(solution)/shard_map/ppermute | solution.py:21
  48.1 0.7 copy.70.gain_ref
  48.8 1.3 copy.68.qseg_ref
  50.2 0.5 maximum_minimum_fusion
  50.7 1.0 copy.65.q_ref
  51.7 2.8 %collective-permute-done.1 = bf16[1024,128]{0,1:T(8,128)(2,1)S(1)} collective-permute-done((bf16[1024,128]{0,1:T(8,128)(2,1)S(1)}, bf16[1024,128]{0,1:T(8,128)(2,1)S(1)}, u32[]{:S(2)}, u32[]{:S(2)}) %collective-permute-start.1) | collective-permute-done | bytes 262176 | tf_op jit(solution)/shard_map/ppermute | solution.py:21
  54.8 1.3 copy.67.v_ref
  56.1 1.3 copy.66.k_ref
  57.4 15.2 %shard_map.102 = (bf16[2048,64]{1,0:T(8,128)(2,1)}, f32[2048,1]{1,0:T(8,128)}, f32[2048,1]{1,0:T(8,128)}) custom-call(s32[4]{0:T(128)} %get-tuple-element.43.lo_ref, s32[4]{0:T(128)} %get-tuple-element.42.hi_ref, bf16[2048,64]{1,0:T(8,128)(2,1)} %copy.65.q_ref, bf16[4096,64]{1,0:T(8,128)(2,1)} %copy.66.k_ref, bf16[4096,64]{1,0:T(8,128)(2,1)} %copy.67.v_ref, ...), custom_call_target="tpu_custom_call" | custom-call | tf_op jit(solution)/shard_map/pallas_call | solution.py:312
  72.7 1.2 copy.69
  74.0 1.9 %collective-permute-start.3 = (bf16[64,15]{1,0:T(8,128)(2,1)S(1)}, bf16[64,15]{1,0:T(8,128)(2,1)S(1)}, u32[]{:S(2)}, u32[]{:S(2)}) collective-permute-start(bf16[64,15]{1,0:T(8,128)(2,1)S(1)} %get-tuple-element.58), channel_id=1, source_target_pairs={{1,0},{2,1},{3,2},{4,3},{5,4},{6,5},{7,6},{8,7},{9,8},{10,9},{11,1... | collective-permute-start | bytes 5768 | tf_op jit(solution)/shard_map/ppermute | solution.py:264
  75.9 4.5 %collective-permute-start.2 = (bf16[64,15]{1,0:T(8,128)(2,1)S(1)}, bf16[64,15]{1,0:T(8,128)(2,1)S(1)}, u32[]{:S(2)}, u32[]{:S(2)}) collective-permute-start(bf16[64,15]{1,0:T(8,128)(2,1)S(1)} %get-tuple-element.59), channel_id=1, source_target_pairs={{0,1},{1,2},{2,3},{3,4},{4,5},{5,6},{6,7},{7,8},{8,9},{9,10},{10,1... | collective-permute-start | bytes 5768 | tf_op jit(solution)/shard_map/ppermute | solution.py:263
  80.6 0.8 collective-permute-done.2
  81.4 0.9 concatenate.23.x_ref
  82.3 1.3 broadcast_in_dim.58.wt_ref
  83.6 14.3 %shard_map.103 = (bf16[64,2048]{1,0:T(8,128)(2,1)}, f32[64,2048]{1,0:T(8,128)}) custom-call(f32[64,2304]{1,0:T(8,128)} %concatenate.23.x_ref, f32[31,64,128]{2,1,0:T(8,128)} %broadcast_in_dim.58.wt_ref, f32[64,1]{1,0:T(8,128)} %copy.70.gain_ref, bf16[64,2048]{1,0:T(8,128)(2,1)} %cot_ref.1, s32[1,2048]{1,0:T(1,128)} %get-tuple-element.61.lo_ref, ...), custom_call_target="tpu_custom_call" | custom-call | tf_op jit(solution)/shard_map/pallas_call | solution.py:332
  97.9 0.9 fusion.9
  98.8 1.9 %collective-permute-start.5 = (f32[64,15]{1,0:T(8,128)S(1)}, f32[64,15]{1,0:T(8,128)S(1)}, u32[]{:S(2)}, u32[]{:S(2)}) collective-permute-start(f32[64,15]{1,0:T(8,128)S(1)} %get-tuple-element.54), channel_id=1, source_target_pairs={{1,0},{2,1},{3,2},{4,3},{5,4},{6,5},{7,6},{8,7},{9,8},{10,9},{11,1... | collective-permute-start | bytes 11528 | tf_op jit(solution)/shard_map/ppermute | solution.py:264
  100.7 5.1 %collective-permute-start.4 = (f32[64,15]{1,0:T(8,128)S(1)}, f32[64,15]{1,0:T(8,128)S(1)}, u32[]{:S(2)}, u32[]{:S(2)}) collective-permute-start(f32[64,15]{1,0:T(8,128)S(1)} %get-tuple-element.55), channel_id=1, source_target_pairs={{0,1},{1,2},{2,3},{3,4},{4,5},{5,6},{6,7},{7,8},{8,9},{9,10},{10,1... | collective-permute-start | bytes 11528 | tf_op jit(solution)/shard_map/ppermute | solution.py:263
  105.9 1.1 log_add_fusion.lse_ref
  107.0 0.9 concatenate.24.y_ref
  107.9 13.5 %shard_map.104 = (bf16[64,2048]{1,0:T(8,128)(2,1)}, f32[1,2048]{1,0:T(1,128)}) custom-call(f32[64,2304]{1,0:T(8,128)} %concatenate.24.y_ref, f32[31,64,128]{2,1,0:T(8,128)} %broadcast_in_dim.58.wt_ref, bf16[64,2048]{1,0:T(8,128)(2,1)} %bitcast.30, s32[1,2048]{1,0:T(1,128)} %get-tuple-element.61.lo_ref, s32[1,2048]{1,0:T(1,128)} %get-tuple-element.60.hi_ref), custom_call_target="tpu_custom_call" | custom-call | tf_op jit(solution)/shard_map/pallas_call | solution.py:342
  121.4 2.0 %copy.71 = bf16[64,2048]{0,1:T(8,128)(2,1)} copy(bf16[64,2048]{1,0:T(8,128)(2,1)} %get-tuple-element.17.dot_ref) | data formatting | bytes 524288 | tf_op jit(solution)/shard_map/pallas_call | solution.py:342
  123.4 2.0 %copy.76.d_ref = f32[2048,1]{1,0:T(8,128)} copy(f32[2048,1]{0,1:T(1,128)} %bitcast.40) | data formatting | bytes 16384 | tf_op jit(solution)/shard_map/transpose | solution.py:353
  125.5 17.2 %shard_map.105 = (bf16[2048,64]{1,0:T(8,128)(2,1)}, f32[64,4096]{1,0:T(8,128)}, f32[64,4096]{1,0:T(8,128)}) custom-call(s32[4]{0:T(128)} %get-tuple-element.43.lo_ref, s32[4]{0:T(128)} %get-tuple-element.42.hi_ref, bf16[2048,64]{1,0:T(8,128)(2,1)} %copy.65.q_ref, bf16[4096,64]{1,0:T(8,128)(2,1)} %copy.66.k_ref, bf16[4096,64]{1,0:T(8,128)(2,1)} %copy.67.v_ref, ...), custom_call_target="tpu_custom_call" | custom-call | tf_op jit(solution)/shard_map/pallas_call | solution.py:356
  142.7 1.4 constant_dynamic-update-slice_fusion.1
  144.5 6.8 %collective-permute-start.6 = (bf16[128,1024]{1,0:T(8,128)(2,1)S(1)}, bf16[128,1024]{1,0:T(8,128)(2,1)S(1)}, u32[]{:S(2)}, u32[]{:S(2)}) collective-permute-start(bf16[128,1024]{1,0:T(8,128)(2,1)S(1)} %get-tuple-element.44), channel_id=1, source_target_pairs={{0,1},{1,2},{2,3},{3,4},{4,5},{5,6},{6,7},{7,8},{8,9},{9,10},{10,1... | collective-permute-start | bytes 786440 | tf_op jit(solution)/shard_map/ppermute | solution.py:29
  151.3 1.9 %collective-permute-start.7 = (bf16[128,1024]{1,0:T(8,128)(2,1)S(1)}, bf16[128,1024]{1,0:T(8,128)(2,1)}, u32[]{:S(2)}, u32[]{:S(2)}) collective-permute-start(bf16[128,1024]{1,0:T(8,128)(2,1)S(1)} %get-tuple-element.45), channel_id=1, source_target_pairs={{1,0},{2,1},{3,2},{4,3},{5,4},{6,5},{7,6},{8,7},{9,8},{10,9},{11,1... | collective-permute-start | bytes 786440 | tf_op jit(solution)/shard_map/ppermute | solution.py:29
  153.3 0.9 copy.77
  154.2 0.5 collective-permute-done.6
  154.6 5.4 %collective-permute-done.7 = bf16[128,1024]{1,0:T(8,128)(2,1)} collective-permute-done((bf16[128,1024]{1,0:T(8,128)(2,1)S(1)}, bf16[128,1024]{1,0:T(8,128)(2,1)}, u32[]{:S(2)}, u32[]{:S(2)}) %collective-permute-start.7) | collective-permute-done | bytes 262176 | tf_op jit(solution)/shard_map/ppermute | solution.py:29
  160.0 1.1 fusion
  161.1 0.8 fusion.8
  (43 shorter events, 1.5 us)
Async XLA Ops:
  4.0 11.1 %copy-start.7 = (s32[64]{0:T(128)S(1)}, s32[64]{0:T(128)}, u32[]{:S(2)}) copy-start(s32[64]{0:T(128)} %param.10) | copy-start | bytes 772
  5.1 32.3 %all-to-all-start = ((bf16[128,16,192]{0,2,1:T(8,128)(2,1)}), bf16[128,16,192]{0,2,1:T(8,128)(2,1)S(1)}, u32[]{:S(2)}, u32[]{:S(2)}) async-start(bf16[128,16,192]{0,2,1:T(8,128)(2,1)} %bitcast.5), calls=%async_computation | async-start | bytes 1572864 | tf_op jit(solution)/shard_map/all_to_all | solution.py:278
  37.9 10.2 %copy-start.8 = (f32[64]{0:T(128)S(1)}, f32[64]{0:T(128)}, u32[]{:S(2)}) copy-start(f32[64]{0:T(128)} %param.12) | copy-start | bytes 772
  39.1 12.6 %collective-permute-start = (bf16[1024,128]{0,1:T(8,128)(2,1)S(1)}, bf16[1024,128]{0,1:T(8,128)(2,1)S(1)}, u32[]{:S(2)}, u32[]{:S(2)}) collective-permute-start(bf16[1024,128]{0,1:T(8,128)(2,1)S(1)} %get-tuple-element.56), channel_id=1, source_target_pairs={{0,1},{1,2},{2,3},{3,4},{4,5},{5,6},{6,7},{7,8},{8,9},{9,10},{10,1... | collective-permute-start | bytes 786440 | tf_op jit(solution)/shard_map/ppermute | solution.py:18
  46.0 8.6 %collective-permute-start.1 = (bf16[1024,128]{0,1:T(8,128)(2,1)S(1)}, bf16[1024,128]{0,1:T(8,128)(2,1)S(1)}, u32[]{:S(2)}, u32[]{:S(2)}) collective-permute-start(bf16[1024,128]{0,1:T(8,128)(2,1)S(1)} %get-tuple-element.57), channel_id=1, source_target_pairs={{1,0},{2,1},{3,2},{4,3},{5,4},{6,5},{7,6},{8,7},{9,8},{10,9},{11,1... | collective-permute-start | bytes 786440 | tf_op jit(solution)/shard_map/ppermute | solution.py:21
  72.7 9.6 %copy-start.6 = (f32[31,64]{1,0:T(8,128)S(1)}, f32[31,64]{1,0:T(8,128)}, u32[]{:S(2)}) copy-start(f32[31,64]{1,0:T(8,128)} %param.11) | copy-start | bytes 23812
  73.9 24.0 %copy-start = (bf16[2048,64]{0,1:T(8,128)(2,1)}, bf16[2048,64]{0,1:T(8,128)(2,1)S(1)}, u32[]{:S(2)}) copy-start(bf16[2048,64]{0,1:T(8,128)(2,1)S(1)} %copy.69) | copy-start | bytes 786436
  74.0 6.5 %collective-permute-start.3 = (bf16[64,15]{1,0:T(8,128)(2,1)S(1)}, bf16[64,15]{1,0:T(8,128)(2,1)S(1)}, u32[]{:S(2)}, u32[]{:S(2)}) collective-permute-start(bf16[64,15]{1,0:T(8,128)(2,1)S(1)} %get-tuple-element.58), channel_id=1, source_target_pairs={{1,0},{2,1},{3,2},{4,3},{5,4},{6,5},{7,6},{8,7},{9,8},{10,9},{11,1... | collective-permute-start | bytes 5768 | tf_op jit(solution)/shard_map/ppermute | solution.py:264
  75.9 5.4 %collective-permute-start.2 = (bf16[64,15]{1,0:T(8,128)(2,1)S(1)}, bf16[64,15]{1,0:T(8,128)(2,1)S(1)}, u32[]{:S(2)}, u32[]{:S(2)}) collective-permute-start(bf16[64,15]{1,0:T(8,128)(2,1)S(1)} %get-tuple-element.59), channel_id=1, source_target_pairs={{0,1},{1,2},{2,3},{3,4},{4,5},{5,6},{6,7},{7,8},{8,9},{9,10},{10,1... | collective-permute-start | bytes 5768 | tf_op jit(solution)/shard_map/ppermute | solution.py:263
  81.3 24.5 %copy-start.1 = (f32[2048,1]{1,0:T(8,128)S(1)}, f32[2048,1]{1,0:T(8,128)}, u32[]{:S(2)}) copy-start(f32[2048,1]{1,0:T(8,128)} %get-tuple-element.18) | copy-start | bytes 24580
  81.4 24.5 %copy-start.2 = (f32[2048,1]{1,0:T(8,128)S(1)}, f32[2048,1]{1,0:T(8,128)}, u32[]{:S(2)}) copy-start(f32[2048,1]{1,0:T(8,128)} %get-tuple-element.19) | copy-start | bytes 24580
  97.9 9.1 %copy-start.4 = (f32[64,2048]{1,0:T(8,128)S(1)}, f32[64,2048]{1,0:T(8,128)}, u32[]{:S(2)}) copy-start(f32[64,2048]{1,0:T(8,128)} %get-tuple-element.16) | copy-start | bytes 1572868
  98.8 8.2 %collective-permute-start.5 = (f32[64,15]{1,0:T(8,128)S(1)}, f32[64,15]{1,0:T(8,128)S(1)}, u32[]{:S(2)}, u32[]{:S(2)}) collective-permute-start(f32[64,15]{1,0:T(8,128)S(1)} %get-tuple-element.54), channel_id=1, source_target_pairs={{1,0},{2,1},{3,2},{4,3},{5,4},{6,5},{7,6},{8,7},{9,8},{10,9},{11,1... | collective-permute-start | bytes 11528 | tf_op jit(solution)/shard_map/ppermute | solution.py:264
  100.7 6.3 %collective-permute-start.4 = (f32[64,15]{1,0:T(8,128)S(1)}, f32[64,15]{1,0:T(8,128)S(1)}, u32[]{:S(2)}, u32[]{:S(2)}) collective-permute-start(f32[64,15]{1,0:T(8,128)S(1)} %get-tuple-element.55), channel_id=1, source_target_pairs={{0,1},{1,2},{2,3},{3,4},{4,5},{5,6},{6,7},{7,8},{8,9},{9,10},{10,1... | collective-permute-start | bytes 11528 | tf_op jit(solution)/shard_map/ppermute | solution.py:263
  142.7 1.5 copy-start.3
  144.3 8.9 %copy-start.5 = (bf16[2048,64]{1,0:T(8,128)(2,1)S(1)}, bf16[2048,64]{1,0:T(8,128)(2,1)}, u32[]{:S(2)}) copy-start(bf16[2048,64]{1,0:T(8,128)(2,1)} %get-tuple-element.21) | copy-start | bytes 786436
  144.5 10.1 %collective-permute-start.6 = (bf16[128,1024]{1,0:T(8,128)(2,1)S(1)}, bf16[128,1024]{1,0:T(8,128)(2,1)S(1)}, u32[]{:S(2)}, u32[]{:S(2)}) collective-permute-start(bf16[128,1024]{1,0:T(8,128)(2,1)S(1)} %get-tuple-element.44), channel_id=1, source_target_pairs={{0,1},{1,2},{2,3},{3,4},{4,5},{5,6},{6,7},{7,8},{8,9},{9,10},{10,1... | collective-permute-start | bytes 786440 | tf_op jit(solution)/shard_map/ppermute | solution.py:29
  151.3 8.7 %collective-permute-start.7 = (bf16[128,1024]{1,0:T(8,128)(2,1)S(1)}, bf16[128,1024]{1,0:T(8,128)(2,1)}, u32[]{:S(2)}, u32[]{:S(2)}) collective-permute-start(bf16[128,1024]{1,0:T(8,128)(2,1)S(1)} %get-tuple-element.45), channel_id=1, source_target_pairs={{1,0},{2,1},{3,2},{4,3},{5,4},{6,5},{7,6},{8,7},{9,8},{10,9},{11,1... | collective-permute-start | bytes 786440 | tf_op jit(solution)/shard_map/ppermute | solution.py:29

commit v11 on v9

--- a/solution.py
+++ b/solution.py
@@ -67,7 +67,7 @@
         qs = qseg_ref[pl.ds(r0, TILE_Q), :]
 
         def k_body(j, c):
-            m, l, acc = c
+            m, acc = c
             c0 = pl.multiple_of(j * TILE_K, TILE_K)
             k = k_ref[pl.ds(c0, TILE_K), :]
             v = v_ref[pl.ds(c0, TILE_K), :]
@@ -77,19 +77,18 @@
             m_new = jnp.maximum(m, jnp.max(s, axis=1, keepdims=True))
             alpha = jnp.exp(m - m_new)
             p = jnp.exp(s - m_new)
-            l = alpha * l + jnp.sum(p, axis=1, keepdims=True)
             acc = alpha * acc + jnp.dot(
                 p.astype(jnp.bfloat16), v, preferred_element_type=jnp.float32
             )
-            return (m_new, l, acc)
+            return (m_new, acc)
 
         init = (
             jnp.full((TILE_Q, 1), -1e30, jnp.float32),
-            jnp.zeros((TILE_Q, 1), jnp.float32),
-            jnp.zeros((TILE_Q, HEAD_DIM), jnp.float32),
-        )
-        m, l, acc = lax.fori_loop(lo_ref[i], hi_ref[i], k_body, init)
-        o_ref[pl.ds(r0, TILE_Q), :] = (acc / l).astype(o_ref.dtype)
+            jnp.zeros((TILE_Q, v_ref.shape[1]), jnp.float32),
+        )
+        m, acc = lax.fori_loop(lo_ref[i], hi_ref[i], k_body, init)
+        l = acc[:, HEAD_DIM : HEAD_DIM + 1]
+        o_ref[pl.ds(r0, TILE_Q), :] = (acc[:, :HEAD_DIM] / l).astype(o_ref.dtype)
         m_ref[pl.ds(r0, TILE_Q), :] = m
         l_ref[pl.ds(r0, TILE_Q), :] = l
         return carry
@@ -157,6 +156,12 @@
     big = jnp.iinfo(jnp.int32).max
     seg_end = jnp.min(jnp.where(ends[None, :] > frames[:, None], ends[None, :], big), axis=1)
     return (seg_start, jnp.minimum(seg_end, ends[-1]))
+
+
+def with_ones(v):
+    rows = v.shape[0]
+    ones = jnp.ones((rows, 1), v.dtype)
+    return jnp.concatenate([v, ones, jnp.zeros((rows, 127 - v.shape[1]), v.dtype)], axis=1)
 
 
 def tile_ranges(lengths, base, ext_rows, block_rows):
@@ -288,7 +293,7 @@
             jax.ShapeDtypeStruct((block_rows, 1), jnp.float32),
             jax.ShapeDtypeStruct((block_rows, 1), jnp.float32),
         ),
-    )(lo_t, hi_t, local_q, k_flat, v_flat, qseg_col, kseg_row)
+    )(lo_t, hi_t, local_q, k_flat, with_ones(v_flat), qseg_col, kseg_row)
     frame_at = first_frame + jnp.arange(block_rows, dtype=jnp.int32)
     seg_start, seg_end = segment_bounds(lengths, frame_at)
     lo_off = (seg_start - frame_at)[None, :].astype(jnp.int32)

time: 160 us -> 161 us (level)
  the two profiles are of different devices: /device:TPU:9 before, /device:TPU:11 now
where the time goes in v11:
time: 161 us
  Pallas kernels  60.4 us (38%)
  starting transfers between devices  38.7 us (24%)
  waiting for transfers between devices  27.7 us (17%)
  local copies, waits for them, and re-layouts  26.9 us (17%)
  other arithmetic  5.85 us (4%)
    pallas_call x1, Pallas kernels, on_device(): vmem_call(backward_kernel, 2, 10, (jax.ShapeDtypeStruct((block_rows, HEAD...  19.1 us
    all_to_all x1, waiting for transfers between devices, on_device(): lax.all_to_all(stacked, 'uly', split_axis=1, concat_axis=0, tiled=True)  19.1 us
    pallas_call x1, Pallas kernels, on_device(): vmem_call(forward_kernel, 2, 5, (jax.ShapeDtypeStruct((block_rows, HEAD_D...  16.5 us
    pallas_call x1, Pallas kernels, on_device(): vmem_call(conv_forward_kernel, 0, 6, (jax.ShapeDtypeStruct((HEAD_DIM, blo...  12.8 us
    pallas_call x1, Pallas kernels, on_device(): vmem_call(conv_backward_kernel, 0, 5, (jax.ShapeDtypeStruct((HEAD_DIM, bl...  12 us
    all_to_all x1, starting transfers between devices, on_device(): lax.all_to_all(stacked, 'uly', split_axis=1, concat_axis=0, tiled=True)  10 us
    ppermute x2, starting transfers between devices, padded_rims(): low = lax.ppermute(block[:, block.shape[1] - half:], 'blk', forward)  9.64 us
    ppermute x1, starting transfers between devices, extended(): lax.ppermute(lax.slice_in_dim(block, block.shape[dim] - width, None, axis...  6.87 us
  transfers between devices with their start and end apart: 9, of which 5 were waited for; matrix products, arithmetic and copies ran while one was open for 7% of the time, Pallas kernels for 0%

profile of v11, /device:TPU:11, one launch (start us, length us, event | category | flops | bytes accessed | tf_op | source)
XLA Modules:
  0.0 160.6 jit_solution(13423607138658754022)
XLA Ops:
  0.6 1.1 copy.63
  1.8 1.1 copy.64
  2.9 1.1 copy.65
  4.1 0.9 copy.66
  5.1 10.0 %all-to-all-start = ((bf16[128,16,192]{0,2,1:T(8,128)(2,1)}), bf16[128,16,192]{0,2,1:T(8,128)(2,1)S(1)}, u32[]{:S(2)}, u32[]{:S(2)}) async-start(bf16[128,16,192]{0,2,1:T(8,128)(2,1)} %bitcast.5), calls=%async_computation | async-start | bytes 1572864 | tf_op jit(solution)/shard_map/all_to_all | solution.py:253
  15.3 0.5 slice.86
  16.4 0.7 broadcast_minimum_fusion
  17.1 0.6 fusion.2
  17.7 0.6 and_select_fusion.kseg_ref
  18.3 19.1 %all-to-all-done = bf16[128,16,192]{0,2,1:T(8,128)(2,1)S(1)} async-done(((bf16[128,16,192]{0,2,1:T(8,128)(2,1)}), bf16[128,16,192]{0,2,1:T(8,128)(2,1)S(1)}, u32[]{:S(2)}, u32[]{:S(2)}) %all-to-all-start) | async-done | bytes 786464 | tf_op jit(solution)/shard_map/all_to_all | solution.py:253
  37.4 0.5 copy.67
  37.9 0.3 reshape.97
  38.3 0.8 slice_bitcast_fusion.2
  39.1 6.9 %collective-permute-start = (bf16[1024,128]{0,1:T(8,128)(2,1)S(1)}, bf16[1024,128]{0,1:T(8,128)(2,1)S(1)}, u32[]{:S(2)}, u32[]{:S(2)}) collective-permute-start(bf16[1024,128]{0,1:T(8,128)(2,1)S(1)} %get-tuple-element.56), channel_id=1, source_target_pairs={{0,1},{1,2},{2,3},{3,4},{4,5},{5,6},{6,7},{7,8},{8,9},{9,10},{10,1... | collective-permute-start | bytes 786440 | tf_op jit(solution)/shard_map/ppermute | solution.py:18
  46.0 1.9 %collective-permute-start.1 = (bf16[1024,128]{0,1:T(8,128)(2,1)S(1)}, bf16[1024,128]{0,1:T(8,128)(2,1)S(1)}, u32[]{:S(2)}, u32[]{:S(2)}) collective-permute-start(bf16[1024,128]{0,1:T(8,128)(2,1)S(1)} %get-tuple-element.57), channel_id=1, source_target_pairs={{1,0},{2,1},{3,2},{4,3},{5,4},{6,5},{7,6},{8,7},{9,8},{10,9},{11,1... | collective-permute-start | bytes 786440 | tf_op jit(solution)/shard_map/ppermute | solution.py:21
  48.3 0.7 copy.73
  49.0 0.7 copy.74.gain_ref
  49.7 1.4 copy.71.qseg_ref
  51.1 0.5 maximum_minimum_fusion
  51.6 1.0 copy.68.q_ref
  52.7 2.0 %collective-permute-done.1 = bf16[1024,128]{0,1:T(8,128)(2,1)S(1)} collective-permute-done((bf16[1024,128]{0,1:T(8,128)(2,1)S(1)}, bf16[1024,128]{0,1:T(8,128)(2,1)S(1)}, u32[]{:S(2)}, u32[]{:S(2)}) %collective-permute-start.1) | collective-permute-done | bytes 262176 | tf_op jit(solution)/shard_map/ppermute | solution.py:21
  54.8 1.3 copy.69.k_ref
  56.3 1.3 copy.70.v_ref
  57.6 16.5 %shard_map.102 = (bf16[2048,64]{1,0:T(8,128)(2,1)}, f32[2048,1]{1,0:T(8,128)}, f32[2048,1]{1,0:T(8,128)}) custom-call(s32[4]{0:T(128)} %get-tuple-element.43.lo_ref, s32[4]{0:T(128)} %get-tuple-element.42.hi_ref, bf16[2048,64]{1,0:T(8,128)(2,1)} %copy.68.q_ref, bf16[4096,64]{1,0:T(8,128)(2,1)} %copy.69.k_ref, bf16[4096,128]{1,0:T(8,128)(2,1)} %copy.70.v_ref, ...), custom_call_target="tpu_custom_call" | custom-call | tf_op jit(solution)/shard_map/pallas_call | solution.py:287
  74.2 1.4 copy.72
  75.7 1.9 %collective-permute-start.3 = (bf16[64,15]{1,0:T(8,128)(2,1)S(1)}, bf16[64,15]{1,0:T(8,128)(2,1)S(1)}, u32[]{:S(2)}, u32[]{:S(2)}) collective-permute-start(bf16[64,15]{1,0:T(8,128)(2,1)S(1)} %get-tuple-element.58), channel_id=1, source_target_pairs={{1,0},{2,1},{3,2},{4,3},{5,4},{6,5},{7,6},{8,7},{9,8},{10,9},{11,1... | collective-permute-start | bytes 5768 | tf_op jit(solution)/shard_map/ppermute | solution.py:239
  77.6 4.5 %collective-permute-start.2 = (bf16[64,15]{1,0:T(8,128)(2,1)S(1)}, bf16[64,15]{1,0:T(8,128)(2,1)S(1)}, u32[]{:S(2)}, u32[]{:S(2)}) collective-permute-start(bf16[64,15]{1,0:T(8,128)(2,1)S(1)} %get-tuple-element.59), channel_id=1, source_target_pairs={{0,1},{1,2},{2,3},{3,4},{4,5},{5,6},{6,7},{7,8},{8,9},{9,10},{10,1... | collective-permute-start | bytes 5768 | tf_op jit(solution)/shard_map/ppermute | solution.py:238
  82.2 0.8 collective-permute-done.2
  83.0 0.9 concatenate.27.x_ref
  83.9 12.8 %shard_map.103 = (bf16[64,2048]{1,0:T(8,128)(2,1)}, f32[64,2048]{1,0:T(8,128)}) custom-call(f32[64,2304]{1,0:T(8,128)} %concatenate.27.x_ref, f32[64,31]{1,0:T(8,128)} %bitcast.38, f32[64,1]{1,0:T(8,128)} %copy.74.gain_ref, bf16[64,2048]{1,0:T(8,128)(2,1)} %cot_ref.1, s32[1,2048]{1,0:T(1,128)} %get-tuple-element.61.lo_ref, s32[1,2048]{1,0:T(1,128)} %get-tuple-element.60.hi_ref), custom_call_target="tpu_custom_call" | custom-call | tf_op jit(solution)/shard_map/pallas_call | solution.py:303
  96.6 1.4 fusion.9
  98.0 1.9 %collective-permute-start.5 = (f32[64,15]{1,0:T(8,128)}, f32[64,15]{1,0:T(8,128)S(1)}, u32[]{:S(2)}, u32[]{:S(2)}) collective-permute-start(f32[64,15]{1,0:T(8,128)} %get-tuple-element.54), channel_id=1, source_target_pairs={{1,0},{2,1},{3,2},{4,3},{5,4},{6,5},{7,6},{8,7},{9,8},{10,9},{11,1... | collective-permute-start | bytes 11528 | tf_op jit(solution)/shard_map/ppermute | solution.py:239
  99.9 5.1 %collective-permute-start.4 = (f32[64,15]{1,0:T(8,128)S(1)}, f32[64,15]{1,0:T(8,128)S(1)}, u32[]{:S(2)}, u32[]{:S(2)}) collective-permute-start(f32[64,15]{1,0:T(8,128)S(1)} %get-tuple-element.55), channel_id=1, source_target_pairs={{0,1},{1,2},{2,3},{3,4},{4,5},{5,6},{6,7},{7,8},{8,9},{9,10},{10,1... | collective-permute-start | bytes 11528 | tf_op jit(solution)/shard_map/ppermute | solution.py:238
  105.1 1.1 log_add_fusion.lse_ref
  106.2 1.3 copy.78.v_ref
  107.6 0.9 concatenate.28.y_ref
  108.5 12.0 %shard_map.104 = (bf16[64,2048]{1,0:T(8,128)(2,1)}, f32[1,2048]{1,0:T(1,128)}) custom-call(f32[64,2304]{1,0:T(8,128)} %concatenate.28.y_ref, f32[64,31]{1,0:T(8,128)} %bitcast.39, bf16[64,2048]{1,0:T(8,128)(2,1)} %bitcast.32, s32[1,2048]{1,0:T(1,128)} %get-tuple-element.61.lo_ref, s32[1,2048]{1,0:T(1,128)} %get-tuple-element.60.hi_ref), custom_call_target="tpu_custom_call" | custom-call | tf_op jit(solution)/shard_map/pallas_call | solution.py:312
  120.5 2.0 %copy.75 = bf16[64,2048]{0,1:T(8,128)(2,1)} copy(bf16[64,2048]{1,0:T(8,128)(2,1)} %get-tuple-element.17.dot_ref) | data formatting | bytes 524288 | tf_op jit(solution)/shard_map/pallas_call | solution.py:312
  122.5 2.0 %copy.80.d_ref = f32[2048,1]{1,0:T(8,128)} copy(f32[2048,1]{0,1:T(1,128)} %bitcast.44) | data formatting | bytes 16384 | tf_op jit(solution)/shard_map/transpose | solution.py:322
  124.6 19.1 %shard_map.105 = (bf16[2048,64]{1,0:T(8,128)(2,1)}, f32[64,4096]{1,0:T(8,128)}, f32[64,4096]{1,0:T(8,128)}) custom-call(s32[4]{0:T(128)} %get-tuple-element.43.lo_ref, s32[4]{0:T(128)} %get-tuple-element.42.hi_ref, bf16[2048,64]{1,0:T(8,128)(2,1)} %copy.68.q_ref, bf16[4096,64]{1,0:T(8,128)(2,1)} %copy.69.k_ref, bf16[4096,64]{1,0:T(8,128)(2,1)} %copy.78.v_ref, ...), custom_call_target="tpu_custom_call" | custom-call | tf_op jit(solution)/shard_map/pallas_call | solution.py:325
  143.6 1.4 constant_dynamic-update-slice_fusion.1
  145.4 4.5 %collective-permute-start.6 = (bf16[128,1024]{1,0:T(8,128)(2,1)S(1)}, bf16[128,1024]{1,0:T(8,128)(2,1)S(1)}, u32[]{:S(2)}, u32[]{:S(2)}) collective-permute-start(bf16[128,1024]{1,0:T(8,128)(2,1)S(1)} %get-tuple-element.44), channel_id=1, source_target_pairs={{0,1},{1,2},{2,3},{3,4},{4,5},{5,6},{6,7},{7,8},{8,9},{9,10},{10,1... | collective-permute-start | bytes 786440 | tf_op jit(solution)/shard_map/ppermute | solution.py:29
  150.0 1.9 %collective-permute-start.7 = (bf16[128,1024]{1,0:T(8,128)(2,1)S(1)}, bf16[128,1024]{1,0:T(8,128)(2,1)}, u32[]{:S(2)}, u32[]{:S(2)}) collective-permute-start(bf16[128,1024]{1,0:T(8,128)(2,1)S(1)} %get-tuple-element.45), channel_id=1, source_target_pairs={{1,0},{2,1},{3,2},{4,3},{5,4},{6,5},{7,6},{8,7},{9,8},{10,9},{11,1... | collective-permute-start | bytes 786440 | tf_op jit(solution)/shard_map/ppermute | solution.py:29
  151.9 0.9 copy.81
  152.8 0.5 collective-permute-done.6
  153.3 5.4 %collective-permute-done.7 = bf16[128,1024]{1,0:T(8,128)(2,1)} collective-permute-done((bf16[128,1024]{1,0:T(8,128)(2,1)S(1)}, bf16[128,1024]{1,0:T(8,128)(2,1)}, u32[]{:S(2)}, u32[]{:S(2)}) %collective-permute-start.7) | collective-permute-done | bytes 262176 | tf_op jit(solution)/shard_map/ppermute | solution.py:29
  158.7 1.1 fusion
  159.7 0.8 fusion.8
  (48 shorter events, 2.1 us)
Async XLA Ops:
  4.0 11.1 %copy-start.7 = (s32[64]{0:T(128)S(1)}, s32[64]{0:T(128)}, u32[]{:S(2)}) copy-start(s32[64]{0:T(128)} %param.10) | copy-start | bytes 772
  5.1 32.3 %all-to-all-start = ((bf16[128,16,192]{0,2,1:T(8,128)(2,1)}), bf16[128,16,192]{0,2,1:T(8,128)(2,1)S(1)}, u32[]{:S(2)}, u32[]{:S(2)}) async-start(bf16[128,16,192]{0,2,1:T(8,128)(2,1)} %bitcast.5), calls=%async_computation | async-start | bytes 1572864 | tf_op jit(solution)/shard_map/all_to_all | solution.py:253
  37.9 10.4 %copy-start.6 = (f32[31,64]{1,0:T(8,128)S(1)}, f32[31,64]{1,0:T(8,128)}, u32[]{:S(2)}) copy-start(f32[31,64]{1,0:T(8,128)} %param.11) | copy-start | bytes 23812
  37.9 11.1 %copy-start.8 = (f32[64]{0:T(128)S(1)}, f32[64]{0:T(128)}, u32[]{:S(2)}) copy-start(f32[64]{0:T(128)} %param.12) | copy-start | bytes 772
  39.1 13.5 %collective-permute-start = (bf16[1024,128]{0,1:T(8,128)(2,1)S(1)}, bf16[1024,128]{0,1:T(8,128)(2,1)S(1)}, u32[]{:S(2)}, u32[]{:S(2)}) collective-permute-start(bf16[1024,128]{0,1:T(8,128)(2,1)S(1)} %get-tuple-element.56), channel_id=1, source_target_pairs={{0,1},{1,2},{2,3},{3,4},{4,5},{5,6},{6,7},{7,8},{8,9},{9,10},{10,1... | collective-permute-start | bytes 786440 | tf_op jit(solution)/shard_map/ppermute | solution.py:18
  46.0 8.6 %collective-permute-start.1 = (bf16[1024,128]{0,1:T(8,128)(2,1)S(1)}, bf16[1024,128]{0,1:T(8,128)(2,1)S(1)}, u32[]{:S(2)}, u32[]{:S(2)}) collective-permute-start(bf16[1024,128]{0,1:T(8,128)(2,1)S(1)} %get-tuple-element.57), channel_id=1, source_target_pairs={{1,0},{2,1},{3,2},{4,3},{5,4},{6,5},{7,6},{8,7},{9,8},{10,9},{11,1... | collective-permute-start | bytes 786440 | tf_op jit(solution)/shard_map/ppermute | solution.py:21
  74.2 30.9 %copy-start.1 = (f32[2048,1]{1,0:T(8,128)S(1)}, f32[2048,1]{1,0:T(8,128)}, u32[]{:S(2)}) copy-start(f32[2048,1]{1,0:T(8,128)} %get-tuple-element.18) | copy-start | bytes 24580
  74.2 30.9 %copy-start.2 = (f32[2048,1]{1,0:T(8,128)S(1)}, f32[2048,1]{1,0:T(8,128)}, u32[]{:S(2)}) copy-start(f32[2048,1]{1,0:T(8,128)} %get-tuple-element.19) | copy-start | bytes 24580
  75.6 30.7 %copy-start = (bf16[2048,64]{0,1:T(8,128)(2,1)}, bf16[2048,64]{0,1:T(8,128)(2,1)S(1)}, u32[]{:S(2)}) copy-start(bf16[2048,64]{0,1:T(8,128)(2,1)S(1)} %copy.72) | copy-start | bytes 786436
  75.7 6.5 %collective-permute-start.3 = (bf16[64,15]{1,0:T(8,128)(2,1)S(1)}, bf16[64,15]{1,0:T(8,128)(2,1)S(1)}, u32[]{:S(2)}, u32[]{:S(2)}) collective-permute-start(bf16[64,15]{1,0:T(8,128)(2,1)S(1)} %get-tuple-element.58), channel_id=1, source_target_pairs={{1,0},{2,1},{3,2},{4,3},{5,4},{6,5},{7,6},{8,7},{9,8},{10,9},{11,1... | collective-permute-start | bytes 5768 | tf_op jit(solution)/shard_map/ppermute | solution.py:239
  77.6 5.4 %collective-permute-start.2 = (bf16[64,15]{1,0:T(8,128)(2,1)S(1)}, bf16[64,15]{1,0:T(8,128)(2,1)S(1)}, u32[]{:S(2)}, u32[]{:S(2)}) collective-permute-start(bf16[64,15]{1,0:T(8,128)(2,1)S(1)} %get-tuple-element.59), channel_id=1, source_target_pairs={{0,1},{1,2},{2,3},{3,4},{4,5},{5,6},{6,7},{7,8},{8,9},{9,10},{10,1... | collective-permute-start | bytes 5768 | tf_op jit(solution)/shard_map/ppermute | solution.py:238
  98.0 9.5 %collective-permute-start.5 = (f32[64,15]{1,0:T(8,128)}, f32[64,15]{1,0:T(8,128)S(1)}, u32[]{:S(2)}, u32[]{:S(2)}) collective-permute-start(f32[64,15]{1,0:T(8,128)} %get-tuple-element.54), channel_id=1, source_target_pairs={{1,0},{2,1},{3,2},{4,3},{5,4},{6,5},{7,6},{8,7},{9,8},{10,9},{11,1... | collective-permute-start | bytes 11528 | tf_op jit(solution)/shard_map/ppermute | solution.py:239
  99.9 7.6 %collective-permute-start.4 = (f32[64,15]{1,0:T(8,128)S(1)}, f32[64,15]{1,0:T(8,128)S(1)}, u32[]{:S(2)}, u32[]{:S(2)}) collective-permute-start(f32[64,15]{1,0:T(8,128)S(1)} %get-tuple-element.55), channel_id=1, source_target_pairs={{0,1},{1,2},{2,3},{3,4},{4,5},{5,6},{6,7},{7,8},{8,9},{9,10},{10,1... | collective-permute-start | bytes 11528 | tf_op jit(solution)/shard_map/ppermute | solution.py:238
  105.1 2.5 %copy-start.4 = (f32[64,2048]{1,0:T(8,128)S(1)}, f32[64,2048]{1,0:T(8,128)}, u32[]{:S(2)}) copy-start(f32[64,2048]{1,0:T(8,128)} %get-tuple-element.16) | copy-start | bytes 1572868
  143.6 1.5 copy-start.3
  145.3 6.7 %copy-start.5 = (bf16[2048,64]{1,0:T(8,128)(2,1)S(1)}, bf16[2048,64]{1,0:T(8,128)(2,1)}, u32[]{:S(2)}) copy-start(bf16[2048,64]{1,0:T(8,128)(2,1)} %get-tuple-element.21) | copy-start | bytes 786436
  145.4 7.8 %collective-permute-start.6 = (bf16[128,1024]{1,0:T(8,128)(2,1)S(1)}, bf16[128,1024]{1,0:T(8,128)(2,1)S(1)}, u32[]{:S(2)}, u32[]{:S(2)}) collective-permute-start(bf16[128,1024]{1,0:T(8,128)(2,1)S(1)} %get-tuple-element.44), channel_id=1, source_target_pairs={{0,1},{1,2},{2,3},{3,4},{4,5},{5,6},{6,7},{7,8},{8,9},{9,10},{10,1... | collective-permute-start | bytes 786440 | tf_op jit(solution)/shard_map/ppermute | solution.py:29
  150.0 8.7 %collective-permute-start.7 = (bf16[128,1024]{1,0:T(8,128)(2,1)S(1)}, bf16[128,1024]{1,0:T(8,128)(2,1)}, u32[]{:S(2)}, u32[]{:S(2)}) collective-permute-start(bf16[128,1024]{1,0:T(8,128)(2,1)S(1)} %get-tuple-element.45), channel_id=1, source_target_pairs={{1,0},{2,1},{3,2},{4,3},{5,4},{6,5},{7,6},{8,7},{9,8},{10,9},{11,1... | collective-permute-start | bytes 786440 | tf_op jit(solution)/shard_map/ppermute | solution.py:29

commit v12 on v9

--- a/solution.py
+++ b/solution.py
@@ -58,7 +58,7 @@
 TN = (((0,), (0,)), ((), ()))
 
 
-def forward_kernel(lo_ref, hi_ref, q_ref, k_ref, v_ref, qseg_ref, kseg_ref, o_ref, m_ref, l_ref):
+def forward_kernel(lo_ref, hi_ref, q_ref, kv_ref, qseg_ref, kseg_ref, o_ref, m_ref, l_ref):
     scale = HEAD_DIM ** (-0.5)
 
     def q_body(i, carry):
@@ -69,27 +69,26 @@
         def k_body(j, c):
             m, l, acc = c
             c0 = pl.multiple_of(j * TILE_K, TILE_K)
-            k = k_ref[pl.ds(c0, TILE_K), :]
-            v = v_ref[pl.ds(c0, TILE_K), :]
+            kv = kv_ref[pl.ds(c0, TILE_K), :]
             ks = kseg_ref[:, pl.ds(c0, TILE_K)]
-            s = lax.dot_general(q, k, NT, preferred_element_type=jnp.float32)
+            s = lax.dot_general(q, kv, NT, preferred_element_type=jnp.float32)
             s = jnp.where(qs == ks, s, -1e30)
             m_new = jnp.maximum(m, jnp.max(s, axis=1, keepdims=True))
             alpha = jnp.exp(m - m_new)
             p = jnp.exp(s - m_new)
             l = alpha * l + jnp.sum(p, axis=1, keepdims=True)
             acc = alpha * acc + jnp.dot(
-                p.astype(jnp.bfloat16), v, preferred_element_type=jnp.float32
+                p.astype(jnp.bfloat16), kv, preferred_element_type=jnp.float32
             )
             return (m_new, l, acc)
 
         init = (
             jnp.full((TILE_Q, 1), -1e30, jnp.float32),
             jnp.zeros((TILE_Q, 1), jnp.float32),
-            jnp.zeros((TILE_Q, HEAD_DIM), jnp.float32),
+            jnp.zeros((TILE_Q, kv_ref.shape[1]), jnp.float32),
         )
         m, l, acc = lax.fori_loop(lo_ref[i], hi_ref[i], k_body, init)
-        o_ref[pl.ds(r0, TILE_Q), :] = (acc / l).astype(o_ref.dtype)
+        o_ref[pl.ds(r0, TILE_Q), :] = (acc[:, HEAD_DIM:] / l).astype(o_ref.dtype)
         m_ref[pl.ds(r0, TILE_Q), :] = m
         l_ref[pl.ds(r0, TILE_Q), :] = l
         return carry
@@ -98,7 +97,7 @@
 
 
 def backward_kernel(
-    lo_ref, hi_ref, q_ref, k_ref, v_ref, do_ref, qt_ref, dot_ref, qseg_ref, kseg_ref, lse_ref,
+    lo_ref, hi_ref, q_ref, kv_ref, do_ref, qt_ref, dot_ref, qseg_ref, kseg_ref, lse_ref,
     d_ref, dq_ref, dk_ref, dv_ref,
 ):
     scale = HEAD_DIM ** (-0.5)
@@ -117,23 +116,22 @@
 
         def k_body(j, dq):
             c0 = pl.multiple_of(j * TILE_K, TILE_K)
-            k = k_ref[pl.ds(c0, TILE_K), :]
-            v = v_ref[pl.ds(c0, TILE_K), :]
+            kv = kv_ref[pl.ds(c0, TILE_K), :]
             ks = kseg_ref[:, pl.ds(c0, TILE_K)]
-            s = lax.dot_general(q, k, NT, preferred_element_type=jnp.float32)
+            s = lax.dot_general(q, kv, NT, preferred_element_type=jnp.float32)
             p = jnp.exp(jnp.where(qs == ks, s, -1e30) - lse)
-            dp = lax.dot_general(do, v, NT, preferred_element_type=jnp.float32)
+            dp = lax.dot_general(do, kv, NT, preferred_element_type=jnp.float32)
             ds = (p * (dp - dlt)).astype(jnp.bfloat16)
             dk_ref[:, pl.ds(c0, TILE_K)] += jnp.dot(q_t, ds, preferred_element_type=jnp.float32)
             dv_ref[:, pl.ds(c0, TILE_K)] += jnp.dot(
                 do_t, p.astype(jnp.bfloat16), preferred_element_type=jnp.float32
             )
-            return dq + jnp.dot(ds, k, preferred_element_type=jnp.float32)
+            return dq + jnp.dot(ds, kv, preferred_element_type=jnp.float32)
 
         dq = lax.fori_loop(
-            lo_ref[i], hi_ref[i], k_body, jnp.zeros((TILE_Q, HEAD_DIM), jnp.float32)
-        )
-        dq_ref[pl.ds(r0, TILE_Q), :] = (scale * dq).astype(dq_ref.dtype)
+            lo_ref[i], hi_ref[i], k_body, jnp.zeros((TILE_Q, kv_ref.shape[1]), jnp.float32)
+        )
+        dq_ref[pl.ds(r0, TILE_Q), :] = (scale * dq[:, :HEAD_DIM]).astype(dq_ref.dtype)
         return carry
 
     lax.fori_loop(0, q_ref.shape[0] // TILE_Q, q_body, 0)
@@ -277,18 +275,18 @@
     lo_t, hi_t = tile_ranges(lengths, first_frame - maxlen, block_rows + 2 * maxlen, block_rows)
     qseg_col = seg_own[:, None].astype(jnp.int32)
     kseg_row = seg_ext[None, :].astype(jnp.int32)
-    k_flat = k_ext.reshape(-1, HEAD_DIM)
-    v_flat = v_ext.reshape(-1, HEAD_DIM)
+    lane_gap = jnp.zeros((block_rows, HEAD_DIM), jnp.bfloat16)
+    q_wide = jnp.concatenate([local_q, lane_gap], axis=1)
     attended, row_tops, row_totals = vmem_call(
         forward_kernel,
         2,
-        5,
+        4,
         (
             jax.ShapeDtypeStruct((block_rows, HEAD_DIM), jnp.bfloat16),
             jax.ShapeDtypeStruct((block_rows, 1), jnp.float32),
             jax.ShapeDtypeStruct((block_rows, 1), jnp.float32),
         ),
-    )(lo_t, hi_t, local_q, k_flat, v_flat, qseg_col, kseg_row)
+    )(lo_t, hi_t, q_wide, near_pairs, qseg_col, kseg_row)
     frame_at = first_frame + jnp.arange(block_rows, dtype=jnp.int32)
     seg_start, seg_end = segment_bounds(lengths, frame_at)
     lo_off = (seg_start - frame_at)[None, :].astype(jnp.int32)
@@ -320,7 +318,7 @@
     grad_q, dk_t, dv_t = vmem_call(
         backward_kernel,
         2,
-        10,
+        9,
         (
             jax.ShapeDtypeStruct((block_rows, HEAD_DIM), jnp.bfloat16),
             jax.ShapeDtypeStruct((HEAD_DIM, ext_rows), jnp.float32),
@@ -329,10 +327,9 @@
     )(
         lo_t,
         hi_t,
-        local_q,
-        k_flat,
-        v_flat,
-        grad_attended,
+        q_wide,
+        near_pairs,
+        jnp.concatenate([lane_gap, grad_attended], axis=1),
         local_q.T,
         grad_att_t,
         qseg_col,

time: 160 us -> 159 us (level); the launches traced: 159 us -> 157 us
  starting transfers between devices: 39.1 us -> 36.6 us
    concatenate x0 -> x3, local copies, waits for them, and re-layouts: none -> 3.24 us  [the longest x1 1.32 us: extended(): block = jnp.concatenate([low, block, high], axis=dim)]
    slice x3 -> x0, local copies, waits for them, and re-layouts: 2.76 us -> none  [the longest x2 1.43 us: on_device(): v_ext = near_pairs[:, channels:].reshape(-1, heads_here, HEAD_DIM)]
    ppermute x2, starting transfers between devices: 6.86 us -> 4.33 us  [passed_along(): return lax.ppermute(block, axis, route)]
    unnamed x24 -> x25, local copies, waits for them, and re-layouts: 6.54 us -> 6.8 us
where the time goes in v12:
time: 159 us; the launch traced here: 157 us
  Pallas kernels  62 us (39%)
  starting transfers between devices  36.6 us (23%)
  waiting for transfers between devices  27.5 us (17%)
  local copies, waits for them, and re-layouts  23.9 us (15%)
  other arithmetic  5.62 us (4%)
    pallas_call x1, Pallas kernels, on_device(): vmem_call(backward_kernel, 2, 9, (jax.ShapeDtypeStruct((block_rows, HEAD_...  19.7 us
    all_to_all x1, waiting for transfers between devices, on_device(): lax.all_to_all(stacked, 'uly', split_axis=1, concat_axis=0, tiled=True)  19 us
    pallas_call x1, Pallas kernels, on_device(): vmem_call(forward_kernel, 2, 4, (jax.ShapeDtypeStruct((block_rows, HEAD_D...  17.5 us
    pallas_call x1, Pallas kernels, on_device(): vmem_call(conv_forward_kernel, 0, 6, (jax.ShapeDtypeStruct((HEAD_DIM, blo...  12.7 us
    pallas_call x1, Pallas kernels, on_device(): vmem_call(conv_backward_kernel, 0, 5, (jax.ShapeDtypeStruct((HEAD_DIM, bl...  12 us
    all_to_all x1, starting transfers between devices, on_device(): lax.all_to_all(stacked, 'uly', split_axis=1, concat_axis=0, tiled=True)  10 us
    ppermute x2, starting transfers between devices, padded_rims(): low = lax.ppermute(block[:, block.shape[1] - half:], 'blk', forward)  9.64 us
    ppermute x1, starting transfers between devices, extended(): lax.ppermute(lax.slice_in_dim(block, block.shape[dim] - width, None, axis...  6.87 us
  transfers between devices with their start and end apart: 9, of which 5 were waited for; matrix products, arithmetic and copies ran while one was open for 6% of the time, Pallas kernels for 0%

profile of v12, /device:TPU:9, one launch (start us, length us, event | category | flops | bytes accessed | tf_op | source)
XLA Modules:
  0.0 156.6 jit_solution(7389524945383598659)
XLA Ops:
  0.6 1.1 copy.57
  1.8 1.1 copy.58
  2.9 1.1 copy.59
  4.1 0.9 copy.60
  5.1 10.0 %all-to-all-start = ((bf16[128,16,192]{0,2,1:T(8,128)(2,1)}), bf16[128,16,192]{0,2,1:T(8,128)(2,1)S(1)}, u32[]{:S(2)}, u32[]{:S(2)}) async-start(bf16[128,16,192]{0,2,1:T(8,128)(2,1)} %bitcast.5), calls=%async_computation | async-start | bytes 1572864 | tf_op jit(solution)/shard_map/all_to_all | solution.py:246
  15.3 0.5 slice.78
  16.4 0.7 broadcast_minimum_fusion
  17.1 0.6 fusion.2
  17.7 0.6 and_select_fusion.kseg_ref
  18.4 19.0 %all-to-all-done = bf16[128,16,192]{0,2,1:T(8,128)(2,1)S(1)} async-done(((bf16[128,16,192]{0,2,1:T(8,128)(2,1)}), bf16[128,16,192]{0,2,1:T(8,128)(2,1)S(1)}, u32[]{:S(2)}, u32[]{:S(2)}) %all-to-all-start) | async-done | bytes 786464 | tf_op jit(solution)/shard_map/all_to_all | solution.py:246
  37.4 0.5 copy.61
  37.9 0.3 reshape.97
  38.3 0.8 slice_bitcast_fusion.2
  39.1 6.9 %collective-permute-start = (bf16[1024,128]{0,1:T(8,128)(2,1)S(1)}, bf16[1024,128]{0,1:T(8,128)(2,1)S(1)}, u32[]{:S(2)}, u32[]{:S(2)}) collective-permute-start(bf16[1024,128]{0,1:T(8,128)(2,1)S(1)} %get-tuple-element.54), channel_id=1, source_target_pairs={{0,1},{1,2},{2,3},{3,4},{4,5},{5,6},{6,7},{7,8},{8,9},{9,10},{10,1... | collective-permute-start | bytes 786440 | tf_op jit(solution)/shard_map/ppermute | solution.py:18
  46.0 1.9 %collective-permute-start.1 = (bf16[1024,128]{0,1:T(8,128)(2,1)S(1)}, bf16[1024,128]{0,1:T(8,128)(2,1)S(1)}, u32[]{:S(2)}, u32[]{:S(2)}) collective-permute-start(bf16[1024,128]{0,1:T(8,128)(2,1)S(1)} %get-tuple-element.55), channel_id=1, source_target_pairs={{1,0},{2,1},{3,2},{4,3},{5,4},{6,5},{7,6},{8,7},{9,8},{10,9},{11,1... | collective-permute-start | bytes 786440 | tf_op jit(solution)/shard_map/ppermute | solution.py:21
  48.1 0.7 copy.66
  48.8 0.7 copy.67.gain_ref
  49.6 1.4 copy.64.qseg_ref
  50.9 0.5 maximum_minimum_fusion
  51.5 0.3 copy.74
  51.7 0.9 concatenate.27.clone.q_ref
  52.7 2.0 %collective-permute-done.1 = bf16[1024,128]{0,1:T(8,128)(2,1)S(1)} collective-permute-done((bf16[1024,128]{0,1:T(8,128)(2,1)S(1)}, bf16[1024,128]{0,1:T(8,128)(2,1)S(1)}, u32[]{:S(2)}, u32[]{:S(2)}) %collective-permute-start.1) | collective-permute-done | bytes 262176 | tf_op jit(solution)/shard_map/ppermute | solution.py:21
  54.7 1.3 copy.63.kv_ref
  56.0 17.5 %shard_map.102 = (bf16[2048,64]{1,0:T(8,128)(2,1)}, f32[2048,1]{1,0:T(8,128)}, f32[2048,1]{1,0:T(8,128)}) custom-call(s32[4]{0:T(128)} %get-tuple-element.43.lo_ref, s32[4]{0:T(128)} %get-tuple-element.42.hi_ref, bf16[2048,128]{1,0:T(8,128)(2,1)} %concatenate.27.clone.q_ref, bf16[4096,128]{1,0:T(8,128)(2,1)} %copy.63.kv_ref, s32[2048,1]{1,0:T(8,128)} %copy.64.qseg_ref, ...), custom_call_target="tpu_custom_call" | custom-call | tf_op jit(solution)/shard_map/pallas_call | solution.py:280
  73.5 1.4 copy.65
  75.0 1.9 %collective-permute-start.3 = (bf16[64,15]{1,0:T(8,128)(2,1)S(1)}, bf16[64,15]{1,0:T(8,128)(2,1)S(1)}, u32[]{:S(2)}, u32[]{:S(2)}) collective-permute-start(bf16[64,15]{1,0:T(8,128)(2,1)S(1)} %get-tuple-element.56), channel_id=1, source_target_pairs={{1,0},{2,1},{3,2},{4,3},{5,4},{6,5},{7,6},{8,7},{9,8},{10,9},{11,1... | collective-permute-start | bytes 5768 | tf_op jit(solution)/shard_map/ppermute | solution.py:232
  76.9 4.5 %collective-permute-start.2 = (bf16[64,15]{1,0:T(8,128)(2,1)S(1)}, bf16[64,15]{1,0:T(8,128)(2,1)S(1)}, u32[]{:S(2)}, u32[]{:S(2)}) collective-permute-start(bf16[64,15]{1,0:T(8,128)(2,1)S(1)} %get-tuple-element.57), channel_id=1, source_target_pairs={{0,1},{1,2},{2,3},{3,4},{4,5},{5,6},{6,7},{7,8},{8,9},{9,10},{10,1... | collective-permute-start | bytes 5768 | tf_op jit(solution)/shard_map/ppermute | solution.py:231
  81.5 0.8 collective-permute-done.2
  82.3 0.9 concatenate.30.x_ref
  83.2 12.7 %shard_map.103 = (bf16[64,2048]{1,0:T(8,128)(2,1)}, f32[64,2048]{1,0:T(8,128)}) custom-call(f32[64,2304]{1,0:T(8,128)} %concatenate.30.x_ref, f32[64,31]{1,0:T(8,128)} %bitcast.37, f32[64,1]{1,0:T(8,128)} %copy.67.gain_ref, bf16[64,2048]{1,0:T(8,128)(2,1)} %cot_ref.1, s32[1,2048]{1,0:T(1,128)} %get-tuple-element.59.lo_ref, s32[1,2048]{1,0:T(1,128)} %get-tuple-element.58.hi_ref), custom_call_target="tpu_custom_call" | custom-call | tf_op jit(solution)/shard_map/pallas_call | solution.py:296
  96.0 0.9 fusion.8
  96.9 1.9 %collective-permute-start.5 = (f32[64,15]{1,0:T(8,128)S(1)}, f32[64,15]{1,0:T(8,128)S(1)}, u32[]{:S(2)}, u32[]{:S(2)}) collective-permute-start(f32[64,15]{1,0:T(8,128)S(1)} %get-tuple-element.52), channel_id=1, source_target_pairs={{1,0},{2,1},{3,2},{4,3},{5,4},{6,5},{7,6},{8,7},{9,8},{10,9},{11,1... | collective-permute-start | bytes 11528 | tf_op jit(solution)/shard_map/ppermute | solution.py:232
  98.8 5.1 %collective-permute-start.4 = (f32[64,15]{1,0:T(8,128)S(1)}, f32[64,15]{1,0:T(8,128)S(1)}, u32[]{:S(2)}, u32[]{:S(2)}) collective-permute-start(f32[64,15]{1,0:T(8,128)S(1)} %get-tuple-element.53), channel_id=1, source_target_pairs={{0,1},{1,2},{2,3},{3,4},{4,5},{5,6},{6,7},{7,8},{8,9},{9,10},{10,1... | collective-permute-start | bytes 11528 | tf_op jit(solution)/shard_map/ppermute | solution.py:231
  103.9 1.1 log_add_fusion.lse_ref
  105.0 0.9 concatenate.31.y_ref
  105.9 12.0 %shard_map.104 = (bf16[64,2048]{1,0:T(8,128)(2,1)}, f32[1,2048]{1,0:T(1,128)}) custom-call(f32[64,2304]{1,0:T(8,128)} %concatenate.31.y_ref, f32[64,31]{1,0:T(8,128)} %bitcast.38, bf16[64,2048]{1,0:T(8,128)(2,1)} %bitcast.31, s32[1,2048]{1,0:T(1,128)} %get-tuple-element.59.lo_ref, s32[1,2048]{1,0:T(1,128)} %get-tuple-element.58.hi_ref), custom_call_target="tpu_custom_call" | custom-call | tf_op jit(solution)/shard_map/pallas_call | solution.py:305
  118.0 1.2 copy.68
  119.2 1.0 concatenate.32.do_ref
  120.2 2.1 %copy.72.d_ref = f32[2048,1]{1,0:T(8,128)} copy(f32[2048,1]{0,1:T(1,128)} %bitcast.43) | data formatting | bytes 16384 | tf_op jit(solution)/shard_map/transpose | solution.py:315
  122.3 19.7 %shard_map.105 = (bf16[2048,64]{1,0:T(8,128)(2,1)}, f32[64,4096]{1,0:T(8,128)}, f32[64,4096]{1,0:T(8,128)}) custom-call(s32[4]{0:T(128)} %get-tuple-element.43.lo_ref, s32[4]{0:T(128)} %get-tuple-element.42.hi_ref, bf16[2048,128]{1,0:T(8,128)(2,1)} %concatenate.27.clone.q_ref, bf16[4096,128]{1,0:T(8,128)(2,1)} %copy.63.kv_ref, ...), custom_call_target="tpu_custom_call" | custom-call | tf_op jit(solution)/shard_map/pallas_call | solution.py:318
  142.0 1.4 constant_dynamic-update-slice_fusion.1
  143.8 2.2 %collective-permute-start.6 = (bf16[128,1024]{1,0:T(8,128)(2,1)S(1)}, bf16[128,1024]{1,0:T(8,128)(2,1)S(1)}, u32[]{:S(2)}, u32[]{:S(2)}) collective-permute-start(bf16[128,1024]{1,0:T(8,128)(2,1)S(1)} %get-tuple-element.44), channel_id=1, source_target_pairs={{0,1},{1,2},{2,3},{3,4},{4,5},{5,6},{6,7},{7,8},{8,9},{9,10},{10,1... | collective-permute-start | bytes 786440 | tf_op jit(solution)/shard_map/ppermute | solution.py:29
  146.0 2.1 %collective-permute-start.7 = (bf16[128,1024]{1,0:T(8,128)(2,1)S(1)}, bf16[128,1024]{1,0:T(8,128)(2,1)}, u32[]{:S(2)}, u32[]{:S(2)}) collective-permute-start(bf16[128,1024]{1,0:T(8,128)(2,1)S(1)} %get-tuple-element.45), channel_id=1, source_target_pairs={{1,0},{2,1},{3,2},{4,3},{5,4},{6,5},{7,6},{8,7},{9,8},{10,9},{11,1... | collective-permute-start | bytes 786440 | tf_op jit(solution)/shard_map/ppermute | solution.py:29
  148.2 0.9 copy.73
  149.1 0.3 collective-permute-done.6
  149.3 5.4 %collective-permute-done.7 = bf16[128,1024]{1,0:T(8,128)(2,1)} collective-permute-done((bf16[128,1024]{1,0:T(8,128)(2,1)S(1)}, bf16[128,1024]{1,0:T(8,128)(2,1)}, u32[]{:S(2)}, u32[]{:S(2)}) %collective-permute-start.7) | collective-permute-done | bytes 262176 | tf_op jit(solution)/shard_map/ppermute | solution.py:29
  154.7 1.1 fusion
  155.8 0.8 fusion.7
  (43 shorter events, 1.7 us)
Async XLA Ops:
  4.0 11.1 %copy-start.7 = (s32[64]{0:T(128)S(1)}, s32[64]{0:T(128)}, u32[]{:S(2)}) copy-start(s32[64]{0:T(128)} %param.10) | copy-start | bytes 772
  5.1 32.3 %all-to-all-start = ((bf16[128,16,192]{0,2,1:T(8,128)(2,1)}), bf16[128,16,192]{0,2,1:T(8,128)(2,1)S(1)}, u32[]{:S(2)}, u32[]{:S(2)}) async-start(bf16[128,16,192]{0,2,1:T(8,128)(2,1)} %bitcast.5), calls=%async_computation | async-start | bytes 1572864 | tf_op jit(solution)/shard_map/all_to_all | solution.py:246
  37.9 10.2 %copy-start.6 = (f32[31,64]{1,0:T(8,128)S(1)}, f32[31,64]{1,0:T(8,128)}, u32[]{:S(2)}) copy-start(f32[31,64]{1,0:T(8,128)} %param.11) | copy-start | bytes 23812
  37.9 10.9 %copy-start.8 = (f32[64]{0:T(128)S(1)}, f32[64]{0:T(128)}, u32[]{:S(2)}) copy-start(f32[64]{0:T(128)} %param.12) | copy-start | bytes 772
  39.1 13.5 %collective-permute-start = (bf16[1024,128]{0,1:T(8,128)(2,1)S(1)}, bf16[1024,128]{0,1:T(8,128)(2,1)S(1)}, u32[]{:S(2)}, u32[]{:S(2)}) collective-permute-start(bf16[1024,128]{0,1:T(8,128)(2,1)S(1)} %get-tuple-element.54), channel_id=1, source_target_pairs={{0,1},{1,2},{2,3},{3,4},{4,5},{5,6},{6,7},{7,8},{8,9},{9,10},{10,1... | collective-permute-start | bytes 786440 | tf_op jit(solution)/shard_map/ppermute | solution.py:18
  46.0 8.6 %collective-permute-start.1 = (bf16[1024,128]{0,1:T(8,128)(2,1)S(1)}, bf16[1024,128]{0,1:T(8,128)(2,1)S(1)}, u32[]{:S(2)}, u32[]{:S(2)}) collective-permute-start(bf16[1024,128]{0,1:T(8,128)(2,1)S(1)} %get-tuple-element.55), channel_id=1, source_target_pairs={{1,0},{2,1},{3,2},{4,3},{5,4},{6,5},{7,6},{8,7},{9,8},{10,9},{11,1... | collective-permute-start | bytes 786440 | tf_op jit(solution)/shard_map/ppermute | solution.py:21
  73.5 30.4 %copy-start.1 = (f32[2048,1]{1,0:T(8,128)S(1)}, f32[2048,1]{1,0:T(8,128)}, u32[]{:S(2)}) copy-start(f32[2048,1]{1,0:T(8,128)} %get-tuple-element.18) | copy-start | bytes 24580
  73.5 30.4 %copy-start.2 = (f32[2048,1]{1,0:T(8,128)S(1)}, f32[2048,1]{1,0:T(8,128)}, u32[]{:S(2)}) copy-start(f32[2048,1]{1,0:T(8,128)} %get-tuple-element.19) | copy-start | bytes 24580
  74.9 30.1 %copy-start = (bf16[2048,64]{0,1:T(8,128)(2,1)}, bf16[2048,64]{0,1:T(8,128)(2,1)S(1)}, u32[]{:S(2)}) copy-start(bf16[2048,64]{0,1:T(8,128)(2,1)S(1)} %copy.65) | copy-start | bytes 786436
  75.0 6.5 %collective-permute-start.3 = (bf16[64,15]{1,0:T(8,128)(2,1)S(1)}, bf16[64,15]{1,0:T(8,128)(2,1)S(1)}, u32[]{:S(2)}, u32[]{:S(2)}) collective-permute-start(bf16[64,15]{1,0:T(8,128)(2,1)S(1)} %get-tuple-element.56), channel_id=1, source_target_pairs={{1,0},{2,1},{3,2},{4,3},{5,4},{6,5},{7,6},{8,7},{9,8},{10,9},{11,1... | collective-permute-start | bytes 5768 | tf_op jit(solution)/shard_map/ppermute | solution.py:232
  76.9 5.4 %collective-permute-start.2 = (bf16[64,15]{1,0:T(8,128)(2,1)S(1)}, bf16[64,15]{1,0:T(8,128)(2,1)S(1)}, u32[]{:S(2)}, u32[]{:S(2)}) collective-permute-start(bf16[64,15]{1,0:T(8,128)(2,1)S(1)} %get-tuple-element.57), channel_id=1, source_target_pairs={{0,1},{1,2},{2,3},{3,4},{4,5},{5,6},{6,7},{7,8},{8,9},{9,10},{10,1... | collective-permute-start | bytes 5768 | tf_op jit(solution)/shard_map/ppermute | solution.py:231
  95.9 9.1 %copy-start.4 = (f32[64,2048]{1,0:T(8,128)S(1)}, f32[64,2048]{1,0:T(8,128)}, u32[]{:S(2)}) copy-start(f32[64,2048]{1,0:T(8,128)} %get-tuple-element.16) | copy-start | bytes 1572868
  96.9 8.2 %collective-permute-start.5 = (f32[64,15]{1,0:T(8,128)S(1)}, f32[64,15]{1,0:T(8,128)S(1)}, u32[]{:S(2)}, u32[]{:S(2)}) collective-permute-start(f32[64,15]{1,0:T(8,128)S(1)} %get-tuple-element.52), channel_id=1, source_target_pairs={{1,0},{2,1},{3,2},{4,3},{5,4},{6,5},{7,6},{8,7},{9,8},{10,9},{11,1... | collective-permute-start | bytes 11528 | tf_op jit(solution)/shard_map/ppermute | solution.py:232
  98.8 6.2 %collective-permute-start.4 = (f32[64,15]{1,0:T(8,128)S(1)}, f32[64,15]{1,0:T(8,128)S(1)}, u32[]{:S(2)}, u32[]{:S(2)}) collective-permute-start(f32[64,15]{1,0:T(8,128)S(1)} %get-tuple-element.53), channel_id=1, source_target_pairs={{0,1},{1,2},{2,3},{3,4},{4,5},{5,6},{6,7},{7,8},{8,9},{9,10},{10,1... | collective-permute-start | bytes 11528 | tf_op jit(solution)/shard_map/ppermute | solution.py:231
  142.0 1.5 copy-start.3
  143.6 4.5 %copy-start.5 = (bf16[2048,64]{1,0:T(8,128)(2,1)S(1)}, bf16[2048,64]{1,0:T(8,128)(2,1)}, u32[]{:S(2)}) copy-start(bf16[2048,64]{1,0:T(8,128)(2,1)} %get-tuple-element.21) | copy-start | bytes 786436
  143.8 5.5 %collective-permute-start.6 = (bf16[128,1024]{1,0:T(8,128)(2,1)S(1)}, bf16[128,1024]{1,0:T(8,128)(2,1)S(1)}, u32[]{:S(2)}, u32[]{:S(2)}) collective-permute-start(bf16[128,1024]{1,0:T(8,128)(2,1)S(1)} %get-tuple-element.44), channel_id=1, source_target_pairs={{0,1},{1,2},{2,3},{3,4},{4,5},{5,6},{6,7},{7,8},{8,9},{9,10},{10,1... | collective-permute-start | bytes 786440 | tf_op jit(solution)/shard_map/ppermute | solution.py:29
  146.0 8.7 %collective-permute-start.7 = (bf16[128,1024]{1,0:T(8,128)(2,1)S(1)}, bf16[128,1024]{1,0:T(8,128)(2,1)}, u32[]{:S(2)}, u32[]{:S(2)}) collective-permute-start(bf16[128,1024]{1,0:T(8,128)(2,1)S(1)} %get-tuple-element.45), channel_id=1, source_target_pairs={{1,0},{2,1},{3,2},{4,3},{5,4},{6,5},{7,6},{8,7},{9,8},{10,9},{11,1... | collective-permute-start | bytes 786440 | tf_op jit(solution)/shard_map/ppermute | solution.py:29

commit v13 on v12

--- a/solution.py
+++ b/solution.py
@@ -58,7 +58,7 @@
 TN = (((0,), (0,)), ((), ()))
 
 
-def forward_kernel(lo_ref, hi_ref, q_ref, kv_ref, qseg_ref, kseg_ref, o_ref, m_ref, l_ref):
+def forward_kernel(lo_ref, hi_ref, q_ref, kv_ref, qseg_ref, kseg_ref, o_ref, lse_ref):
     scale = HEAD_DIM ** (-0.5)
 
     def q_body(i, carry):
@@ -88,9 +88,8 @@
             jnp.zeros((TILE_Q, kv_ref.shape[1]), jnp.float32),
         )
         m, l, acc = lax.fori_loop(lo_ref[i], hi_ref[i], k_body, init)
-        o_ref[pl.ds(r0, TILE_Q), :] = (acc[:, HEAD_DIM:] / l).astype(o_ref.dtype)
-        m_ref[pl.ds(r0, TILE_Q), :] = m
-        l_ref[pl.ds(r0, TILE_Q), :] = l
+        o_ref[:, pl.ds(r0, TILE_Q)] = (acc / l).T[HEAD_DIM:].astype(o_ref.dtype)
+        lse_ref[pl.ds(r0, TILE_Q), :] = m + jnp.log(l)
         return carry
 
     lax.fori_loop(0, q_ref.shape[0] // TILE_Q, q_body, 0)
@@ -207,18 +206,19 @@
     lax.fori_loop(0, out_ref.shape[1] // CONV_CHUNK, body, 0)
 
 
-def conv_backward_kernel(y_ref, wt_ref, att_ref, lo_ref, hi_ref, ga_ref, delta_ref):
+def conv_backward_kernel(y_ref, wt_ref, att_ref, lo_ref, hi_ref, ga_ref, dop_ref, delta_ref):
     def body(c, carry):
         c0 = pl.multiple_of(c * CONV_CHUNK, CONV_CHUNK)
         cols = pl.ds(c0, CONV_CHUNK)
         grad_sum = conv_chunk(y_ref, wt_ref, lo_ref[:, cols], hi_ref[:, cols], c0, -1)
         grad_att = grad_sum.astype(ga_ref.dtype)
         ga_ref[:, cols] = grad_att
-        delta_ref[:, cols] = jnp.sum(
-            grad_att.astype(jnp.float32) * att_ref[:, cols].astype(jnp.float32),
-            axis=0,
-            keepdims=True,
-        )
+        grad_f32 = grad_att.astype(jnp.float32)
+        delta = jnp.sum(grad_f32 * att_ref[:, cols].astype(jnp.float32), axis=0, keepdims=True)
+        rows = pl.ds(c0, CONV_CHUNK)
+        delta_ref[rows, :] = jnp.broadcast_to(delta, (8, CONV_CHUNK)).T[:, :1]
+        wide = jnp.concatenate([jnp.zeros_like(grad_f32), grad_f32], axis=0)
+        dop_ref[rows, :] = wide.T.astype(dop_ref.dtype)
         return carry
 
     lax.fori_loop(0, ga_ref.shape[1] // CONV_CHUNK, body, 0)
@@ -277,13 +277,12 @@
     kseg_row = seg_ext[None, :].astype(jnp.int32)
     lane_gap = jnp.zeros((block_rows, HEAD_DIM), jnp.bfloat16)
     q_wide = jnp.concatenate([local_q, lane_gap], axis=1)
-    attended, row_tops, row_totals = vmem_call(
+    att_t, lse_col = vmem_call(
         forward_kernel,
         2,
         4,
         (
-            jax.ShapeDtypeStruct((block_rows, HEAD_DIM), jnp.bfloat16),
-            jax.ShapeDtypeStruct((block_rows, 1), jnp.float32),
+            jax.ShapeDtypeStruct((HEAD_DIM, block_rows), jnp.bfloat16),
             jax.ShapeDtypeStruct((block_rows, 1), jnp.float32),
         ),
     )(lo_t, hi_t, q_wide, near_pairs, qseg_col, kseg_row)
@@ -292,7 +291,6 @@
     lo_off = (seg_start - frame_at)[None, :].astype(jnp.int32)
     hi_off = (seg_end - frame_at)[None, :].astype(jnp.int32)
     weight_t = conv_weight.T
-    att_t = attended.T
     conv_out_t, grad_conv_t = vmem_call(
         conv_forward_kernel,
         0,
@@ -302,17 +300,16 @@
             jax.ShapeDtypeStruct((HEAD_DIM, block_rows), jnp.float32),
         ),
     )(padded_rims(att_t, conv_half), weight_t, norm_gain[:, None], cotangent, lo_off, hi_off)
-    grad_att_t, delta_row = vmem_call(
+    grad_att_t, grad_wide, row_delta = vmem_call(
         conv_backward_kernel,
         0,
         5,
         (
             jax.ShapeDtypeStruct((HEAD_DIM, block_rows), jnp.bfloat16),
-            jax.ShapeDtypeStruct((1, block_rows), jnp.float32),
+            jax.ShapeDtypeStruct((block_rows, 2 * HEAD_DIM), jnp.bfloat16),
+            jax.ShapeDtypeStruct((block_rows, 1), jnp.float32),
         ),
     )(padded_rims(grad_conv_t, conv_half), weight_t, att_t, lo_off, hi_off)
-    grad_attended = grad_att_t.T
-    row_delta = delta_row.T
 
     ext_rows = block_rows + 2 * maxlen
     grad_q, dk_t, dv_t = vmem_call(
@@ -329,12 +326,12 @@
         hi_t,
         q_wide,
         near_pairs,
-        jnp.concatenate([lane_gap, grad_attended], axis=1),
+        grad_wide,
         local_q.T,
         grad_att_t,
         qseg_col,
         kseg_row,
-        row_tops + jnp.log(row_totals),
+        lse_col,
         row_delta,
     )
     ext_terms = jnp.concatenate([dk_t, dv_t], axis=0)

time: 159 us -> 157 us (0.987)
  starting transfers between devices: 36.6 us -> 39.7 us
  local copies, waits for them, and re-layouts: 23.9 us -> 20.9 us
  Pallas kernels: 62 us -> 59.3 us
  waiting for transfers between devices: 27.5 us -> 29.8 us
    ppermute x2, starting transfers between devices: 4.33 us -> 8 us  [passed_along(): return lax.ppermute(block, axis, route)]
    pallas_call x2 -> x0, local copies, waits for them, and re-layouts: 2.6 us -> none  [the longest x1 1.38 us: on_device(): vmem_call(forward_kernel, 2, 4, (jax.ShapeDtypeStruct((block_rows, HEAD_D...]
    pallas_call x1, Pallas kernels: 17.5 us -> 15.3 us  [on_device(): vmem_call(forward_kernel, 2, 4, (jax.ShapeDtypeStruct((HEAD_DIM, block_ro...]
    transpose x1 -> x0, local copies, waits for them, and re-layouts: 2.08 us -> none  [on_device(): row_delta = delta_row.T]
    concatenate x2, local copies, waits for them, and re-layouts: 1.8 us -> 3.8 us  [padded_rims(): jnp.concatenate([gap, low.astype(jnp.float32), block.astype(jnp.float32),...]
    pallas_call x1, Pallas kernels: 19.7 us -> 17.9 us  [on_device(): vmem_call(backward_kernel, 2, 9, (jax.ShapeDtypeStruct((block_rows, HEAD_...]
    unnamed x25 -> x17, local copies, waits for them, and re-layouts: 6.8 us -> 6.79 us
where the time goes in v13:
time: 157 us; the launch traced here: 155 us
  Pallas kernels  59.3 us (38%)
  starting transfers between devices  39.7 us (25%)
  waiting for transfers between devices  29.8 us (19%)
  local copies, waits for them, and re-layouts  20.9 us (13%)
  other arithmetic  4.53 us (3%)
    all_to_all x1, waiting for transfers between devices, on_device(): lax.all_to_all(stacked, 'uly', split_axis=1, concat_axis=0, tiled=True)  20.3 us
    pallas_call x1, Pallas kernels, on_device(): vmem_call(backward_kernel, 2, 9, (jax.ShapeDtypeStruct((block_rows, HEAD_...  17.9 us
    pallas_call x1, Pallas kernels, on_device(): vmem_call(forward_kernel, 2, 4, (jax.ShapeDtypeStruct((HEAD_DIM, block_ro...  15.3 us
    pallas_call x1, Pallas kernels, on_device(): vmem_call(conv_backward_kernel, 0, 5, (jax.ShapeDtypeStruct((HEAD_DIM, bl...  13.4 us
    pallas_call x1, Pallas kernels, on_device(): vmem_call(conv_forward_kernel, 0, 6, (jax.ShapeDtypeStruct((HEAD_DIM, blo...  12.8 us
    all_to_all x1, starting transfers between devices, on_device(): lax.all_to_all(stacked, 'uly', split_axis=1, concat_axis=0, tiled=True)  10 us
    ppermute x2, starting transfers between devices, padded_rims(): low = lax.ppermute(block[:, block.shape[1] - half:], 'blk', forward)  9.08 us
    ppermute x2, starting transfers between devices, passed_along(): return lax.ppermute(block, axis, route)  8 us
  transfers between devices with their start and end apart: 9, of which 5 were waited for; matrix products, arithmetic and copies ran while one was open for 6% of the time, Pallas kernels for 0%

profile of v13, /device:TPU:9, one launch (start us, length us, event | category | flops | bytes accessed | tf_op | source)
XLA Modules:
  0.0 155.2 jit_solution(7705977707694263680)
XLA Ops:
  0.6 1.1 copy.49
  1.8 1.1 copy.50
  2.9 1.1 copy.51
  4.1 0.9 copy.52
  5.1 10.0 %all-to-all-start = ((bf16[128,16,192]{0,2,1:T(8,128)(2,1)}), bf16[128,16,192]{0,2,1:T(8,128)(2,1)S(1)}, u32[]{:S(2)}, u32[]{:S(2)}) async-start(bf16[128,16,192]{0,2,1:T(8,128)(2,1)} %bitcast.5), calls=%async_computation | async-start | bytes 1572864 | tf_op jit(solution)/shard_map/all_to_all | solution.py:246
  15.4 0.2 select_reduce_fusion
  15.7 0.5 slice.78
  16.2 0.2 convert_reduce_fusion
  16.5 0.6 and_select_fusion.kseg_ref
  17.1 20.3 %all-to-all-done = bf16[128,16,192]{0,2,1:T(8,128)(2,1)S(1)} async-done(((bf16[128,16,192]{0,2,1:T(8,128)(2,1)}), bf16[128,16,192]{0,2,1:T(8,128)(2,1)S(1)}, u32[]{:S(2)}, u32[]{:S(2)}) %all-to-all-start) | async-done | bytes 786464 | tf_op jit(solution)/shard_map/all_to_all | solution.py:246
  37.4 0.5 copy.53
  37.9 0.3 reshape.97
  38.3 0.8 slice_bitcast_fusion.2
  39.1 6.9 %collective-permute-start = (bf16[1024,128]{0,1:T(8,128)(2,1)S(1)}, bf16[1024,128]{0,1:T(8,128)(2,1)S(1)}, u32[]{:S(2)}, u32[]{:S(2)}) collective-permute-start(bf16[1024,128]{0,1:T(8,128)(2,1)S(1)} %get-tuple-element.54), channel_id=1, source_target_pairs={{0,1},{1,2},{2,3},{3,4},{4,5},{5,6},{6,7},{7,8},{8,9},{9,10},{10,1... | collective-permute-start | bytes 786440 | tf_op jit(solution)/shard_map/ppermute | solution.py:18
  46.0 1.9 %collective-permute-start.1 = (bf16[1024,128]{0,1:T(8,128)(2,1)S(1)}, bf16[1024,128]{0,1:T(8,128)(2,1)S(1)}, u32[]{:S(2)}, u32[]{:S(2)}) collective-permute-start(bf16[1024,128]{0,1:T(8,128)(2,1)S(1)} %get-tuple-element.55), channel_id=1, source_target_pairs={{1,0},{2,1},{3,2},{4,3},{5,4},{6,5},{7,6},{8,7},{9,8},{10,9},{11,1... | collective-permute-start | bytes 786440 | tf_op jit(solution)/shard_map/ppermute | solution.py:21
  47.9 0.7 broadcast_minimum_fusion
  48.8 1.4 copy.56.qseg_ref
  50.1 0.6 maximum_minimum_fusion
  50.7 0.3 copy.63
  51.0 0.9 concatenate.24.clone.q_ref
  51.9 2.7 %collective-permute-done.1 = bf16[1024,128]{0,1:T(8,128)(2,1)S(1)} collective-permute-done((bf16[1024,128]{0,1:T(8,128)(2,1)S(1)}, bf16[1024,128]{0,1:T(8,128)(2,1)S(1)}, u32[]{:S(2)}, u32[]{:S(2)}) %collective-permute-start.1) | collective-permute-done | bytes 262176 | tf_op jit(solution)/shard_map/ppermute | solution.py:21
  54.7 1.3 copy.55.kv_ref
  56.0 15.3 %shard_map.102 = (bf16[64,2048]{1,0:T(8,128)(2,1)}, f32[2048,1]{1,0:T(8,128)}) custom-call(s32[4]{0:T(128)} %get-tuple-element.43.lo_ref, s32[4]{0:T(128)} %get-tuple-element.42.hi_ref, bf16[2048,128]{1,0:T(8,128)(2,1)} %concatenate.24.clone.q_ref, bf16[4096,128]{1,0:T(8,128)(2,1)} %copy.55.kv_ref, s32[2048,1]{1,0:T(8,128)} %copy.56.qseg_ref, ...), custom_call_target="tpu_custom_call" | custom-call | tf_op jit(solution)/shard_map/pallas_call | solution.py:280
  71.3 0.8 fusion.9
  72.1 1.9 %collective-permute-start.3 = (bf16[64,15]{1,0:T(8,128)(2,1)S(1)}, bf16[64,15]{1,0:T(8,128)(2,1)S(1)}, u32[]{:S(2)}, u32[]{:S(2)}) collective-permute-start(bf16[64,15]{1,0:T(8,128)(2,1)S(1)} %get-tuple-element.56), channel_id=1, source_target_pairs={{1,0},{2,1},{3,2},{4,3},{5,4},{6,5},{7,6},{8,7},{9,8},{10,9},{11,1... | collective-permute-start | bytes 5768 | tf_op jit(solution)/shard_map/ppermute | solution.py:232
  74.1 4.5 %collective-permute-start.2 = (bf16[64,15]{1,0:T(8,128)(2,1)S(1)}, bf16[64,15]{1,0:T(8,128)(2,1)S(1)}, u32[]{:S(2)}, u32[]{:S(2)}) collective-permute-start(bf16[64,15]{1,0:T(8,128)(2,1)S(1)} %get-tuple-element.57), channel_id=1, source_target_pairs={{0,1},{1,2},{2,3},{3,4},{4,5},{5,6},{6,7},{7,8},{8,9},{9,10},{10,1... | collective-permute-start | bytes 5768 | tf_op jit(solution)/shard_map/ppermute | solution.py:231
  78.6 0.6 fusion.2
  79.2 0.7 copy.57
  79.9 0.7 copy.58.gain_ref
  80.7 1.8 %concatenate.27.x_ref = f32[64,2304]{1,0:T(8,128)} concatenate(f32[64,113]{1,0:T(8,128)S(1)} %broadcast.102, bf16[64,15]{1,0:T(8,128)(2,1)S(1)} %collective-permute-done.2, bf16[64,2048]{1,0:T(8,128)(2,1)} %get-tuple-element.14.att_ref, bf16[64,15]{1,0:T(8,128)(2,1)S(1)} %collective-permute-done.3, f32[64,113]{1,0:T(8,128)S(1)} %broadcast.102), dimensions={1} | concatenate | bytes 913664 | tf_op jit(solution)/shard_map/concatenate | solution.py:234
  82.5 12.8 %shard_map.103 = (bf16[64,2048]{1,0:T(8,128)(2,1)}, f32[64,2048]{1,0:T(8,128)}) custom-call(f32[64,2304]{1,0:T(8,128)} %concatenate.27.x_ref, f32[64,31]{1,0:T(8,128)} %bitcast.30, f32[64,1]{1,0:T(8,128)} %copy.58.gain_ref, bf16[64,2048]{1,0:T(8,128)(2,1)} %cot_ref.1, s32[1,2048]{1,0:T(1,128)} %get-tuple-element.59.lo_ref, s32[1,2048]{1,0:T(1,128)} %get-tuple-element.58.hi_ref), custom_call_target="tpu_custom_call" | custom-call | tf_op jit(solution)/shard_map/pallas_call | solution.py:294
  95.3 0.8 fusion.8
  96.1 1.9 %collective-permute-start.5 = (f32[64,15]{1,0:T(8,128)S(1)}, f32[64,15]{1,0:T(8,128)S(1)}, u32[]{:S(2)}, u32[]{:S(2)}) collective-permute-start(f32[64,15]{1,0:T(8,128)S(1)} %get-tuple-element.52), channel_id=1, source_target_pairs={{1,0},{2,1},{3,2},{4,3},{5,4},{6,5},{7,6},{8,7},{9,8},{10,9},{11,1... | collective-permute-start | bytes 11528 | tf_op jit(solution)/shard_map/ppermute | solution.py:232
  98.0 4.5 %collective-permute-start.4 = (f32[64,15]{1,0:T(8,128)S(1)}, f32[64,15]{1,0:T(8,128)S(1)}, u32[]{:S(2)}, u32[]{:S(2)}) collective-permute-start(f32[64,15]{1,0:T(8,128)S(1)} %get-tuple-element.53), channel_id=1, source_target_pairs={{0,1},{1,2},{2,3},{3,4},{4,5},{5,6},{6,7},{7,8},{8,9},{9,10},{10,1... | collective-permute-start | bytes 11528 | tf_op jit(solution)/shard_map/ppermute | solution.py:231
  102.6 1.0 collective-permute-done.4
  103.6 1.9 %concatenate.28.y_ref = f32[64,2304]{1,0:T(8,128)} concatenate(f32[64,113]{1,0:T(8,128)S(1)} %broadcast.102, f32[64,15]{1,0:T(8,128)S(1)} %collective-permute-done.4, f32[64,2048]{1,0:T(8,128)} %get-tuple-element.16, f32[64,15]{1,0:T(8,128)S(1)} %collective-permute-done.5, f32[64,113]{1,0:T(8,128)S(1)} %broadcast.102), dimensions={1} | concatenate | bytes 1179648 | tf_op jit(solution)/shard_map/concatenate | solution.py:234
  105.5 13.4 %shard_map.104 = (bf16[64,2048]{1,0:T(8,128)(2,1)}, bf16[2048,128]{1,0:T(8,128)(2,1)}, f32[2048,1]{1,0:T(8,128)}) custom-call(f32[64,2304]{1,0:T(8,128)} %concatenate.28.y_ref, f32[64,31]{1,0:T(8,128)} %bitcast.31, bf16[64,2048]{1,0:T(8,128)(2,1)} %get-tuple-element.14.att_ref, s32[1,2048]{1,0:T(1,128)} %get-tuple-element.59.lo_ref, ...), custom_call_target="tpu_custom_call" | custom-call | tf_op jit(solution)/shard_map/pallas_call | solution.py:303
  118.9 17.9 %shard_map.105 = (bf16[2048,64]{1,0:T(8,128)(2,1)}, f32[64,4096]{1,0:T(8,128)}, f32[64,4096]{1,0:T(8,128)}) custom-call(s32[4]{0:T(128)} %get-tuple-element.43.lo_ref, s32[4]{0:T(128)} %get-tuple-element.42.hi_ref, bf16[2048,128]{1,0:T(8,128)(2,1)} %concatenate.24.clone.q_ref, bf16[4096,128]{1,0:T(8,128)(2,1)} %copy.55.kv_ref, ...), custom_call_target="tpu_custom_call" | custom-call | tf_op jit(solution)/shard_map/pallas_call | solution.py:315
  136.8 1.4 constant_dynamic-update-slice_fusion.1
  138.2 0.1 copy-done
  138.4 0.1 convert.9
  138.6 6.1 %collective-permute-start.6 = (bf16[128,1024]{1,0:T(8,128)(2,1)S(1)}, bf16[128,1024]{1,0:T(8,128)(2,1)S(1)}, u32[]{:S(2)}, u32[]{:S(2)}) collective-permute-start(bf16[128,1024]{1,0:T(8,128)(2,1)S(1)} %get-tuple-element.44), channel_id=1, source_target_pairs={{0,1},{1,2},{2,3},{3,4},{4,5},{5,6},{6,7},{7,8},{8,9},{9,10},{10,1... | collective-permute-start | bytes 786440 | tf_op jit(solution)/shard_map/ppermute | solution.py:29
  144.7 1.9 %collective-permute-start.7 = (bf16[128,1024]{1,0:T(8,128)(2,1)S(1)}, bf16[128,1024]{1,0:T(8,128)(2,1)}, u32[]{:S(2)}, u32[]{:S(2)}) collective-permute-start(bf16[128,1024]{1,0:T(8,128)(2,1)S(1)} %get-tuple-element.45), channel_id=1, source_target_pairs={{1,0},{2,1},{3,2},{4,3},{5,4},{6,5},{7,6},{8,7},{9,8},{10,9},{11,1... | collective-permute-start | bytes 786440 | tf_op jit(solution)/shard_map/ppermute | solution.py:29
  146.6 0.9 copy.62
  147.5 0.5 collective-permute-done.6
  148.0 5.4 %collective-permute-done.7 = bf16[128,1024]{1,0:T(8,128)(2,1)} collective-permute-done((bf16[128,1024]{1,0:T(8,128)(2,1)S(1)}, bf16[128,1024]{1,0:T(8,128)(2,1)}, u32[]{:S(2)}, u32[]{:S(2)}) %collective-permute-start.7) | collective-permute-done | bytes 262176 | tf_op jit(solution)/shard_map/ppermute | solution.py:29
  153.4 1.1 fusion
  154.4 0.8 fusion.7
  (29 shorter events, 0.8 us)
Async XLA Ops:
  4.0 11.1 %copy-start.3 = (s32[64]{0:T(128)S(1)}, s32[64]{0:T(128)}, u32[]{:S(2)}) copy-start(s32[64]{0:T(128)} %param.10) | copy-start | bytes 772
  5.1 32.3 %all-to-all-start = ((bf16[128,16,192]{0,2,1:T(8,128)(2,1)}), bf16[128,16,192]{0,2,1:T(8,128)(2,1)S(1)}, u32[]{:S(2)}, u32[]{:S(2)}) async-start(bf16[128,16,192]{0,2,1:T(8,128)(2,1)} %bitcast.5), calls=%async_computation | async-start | bytes 1572864 | tf_op jit(solution)/shard_map/all_to_all | solution.py:246
  39.1 12.8 %collective-permute-start = (bf16[1024,128]{0,1:T(8,128)(2,1)S(1)}, bf16[1024,128]{0,1:T(8,128)(2,1)S(1)}, u32[]{:S(2)}, u32[]{:S(2)}) collective-permute-start(bf16[1024,128]{0,1:T(8,128)(2,1)S(1)} %get-tuple-element.54), channel_id=1, source_target_pairs={{0,1},{1,2},{2,3},{3,4},{4,5},{5,6},{6,7},{7,8},{8,9},{9,10},{10,1... | collective-permute-start | bytes 786440 | tf_op jit(solution)/shard_map/ppermute | solution.py:18
  46.0 8.6 %collective-permute-start.1 = (bf16[1024,128]{0,1:T(8,128)(2,1)S(1)}, bf16[1024,128]{0,1:T(8,128)(2,1)S(1)}, u32[]{:S(2)}, u32[]{:S(2)}) collective-permute-start(bf16[1024,128]{0,1:T(8,128)(2,1)S(1)} %get-tuple-element.55), channel_id=1, source_target_pairs={{1,0},{2,1},{3,2},{4,3},{5,4},{6,5},{7,6},{8,7},{9,8},{10,9},{11,1... | collective-permute-start | bytes 786440 | tf_op jit(solution)/shard_map/ppermute | solution.py:21
  54.7 24.6 %copy-start.2 = (f32[31,64]{1,0:T(8,128)S(1)}, f32[31,64]{1,0:T(8,128)}, u32[]{:S(2)}) copy-start(f32[31,64]{1,0:T(8,128)} %param.11) | copy-start | bytes 23812
  54.7 25.3 %copy-start.4 = (f32[64]{0:T(128)S(1)}, f32[64]{0:T(128)}, u32[]{:S(2)}) copy-start(f32[64]{0:T(128)} %param.12) | copy-start | bytes 772
  72.1 8.5 %collective-permute-start.3 = (bf16[64,15]{1,0:T(8,128)(2,1)S(1)}, bf16[64,15]{1,0:T(8,128)(2,1)S(1)}, u32[]{:S(2)}, u32[]{:S(2)}) collective-permute-start(bf16[64,15]{1,0:T(8,128)(2,1)S(1)} %get-tuple-element.56), channel_id=1, source_target_pairs={{1,0},{2,1},{3,2},{4,3},{5,4},{6,5},{7,6},{8,7},{9,8},{10,9},{11,1... | collective-permute-start | bytes 5768 | tf_op jit(solution)/shard_map/ppermute | solution.py:232
  74.1 6.6 %collective-permute-start.2 = (bf16[64,15]{1,0:T(8,128)(2,1)S(1)}, bf16[64,15]{1,0:T(8,128)(2,1)S(1)}, u32[]{:S(2)}, u32[]{:S(2)}) collective-permute-start(bf16[64,15]{1,0:T(8,128)(2,1)S(1)} %get-tuple-element.57), channel_id=1, source_target_pairs={{0,1},{1,2},{2,3},{3,4},{4,5},{5,6},{6,7},{7,8},{8,9},{9,10},{10,1... | collective-permute-start | bytes 5768 | tf_op jit(solution)/shard_map/ppermute | solution.py:231
  96.1 6.5 %collective-permute-start.5 = (f32[64,15]{1,0:T(8,128)S(1)}, f32[64,15]{1,0:T(8,128)S(1)}, u32[]{:S(2)}, u32[]{:S(2)}) collective-permute-start(f32[64,15]{1,0:T(8,128)S(1)} %get-tuple-element.52), channel_id=1, source_target_pairs={{1,0},{2,1},{3,2},{4,3},{5,4},{6,5},{7,6},{8,7},{9,8},{10,9},{11,1... | collective-permute-start | bytes 11528 | tf_op jit(solution)/shard_map/ppermute | solution.py:232
  98.0 5.6 %collective-permute-start.4 = (f32[64,15]{1,0:T(8,128)S(1)}, f32[64,15]{1,0:T(8,128)S(1)}, u32[]{:S(2)}, u32[]{:S(2)}) collective-permute-start(f32[64,15]{1,0:T(8,128)S(1)} %get-tuple-element.53), channel_id=1, source_target_pairs={{0,1},{1,2},{2,3},{3,4},{4,5},{5,6},{6,7},{7,8},{8,9},{9,10},{10,1... | collective-permute-start | bytes 11528 | tf_op jit(solution)/shard_map/ppermute | solution.py:231
  136.8 1.5 copy-start
  138.4 8.2 %copy-start.1 = (bf16[2048,64]{1,0:T(8,128)(2,1)S(1)}, bf16[2048,64]{1,0:T(8,128)(2,1)}, u32[]{:S(2)}) copy-start(bf16[2048,64]{1,0:T(8,128)(2,1)} %get-tuple-element.21) | copy-start | bytes 786436
  138.6 9.4 %collective-permute-start.6 = (bf16[128,1024]{1,0:T(8,128)(2,1)S(1)}, bf16[128,1024]{1,0:T(8,128)(2,1)S(1)}, u32[]{:S(2)}, u32[]{:S(2)}) collective-permute-start(bf16[128,1024]{1,0:T(8,128)(2,1)S(1)} %get-tuple-element.44), channel_id=1, source_target_pairs={{0,1},{1,2},{2,3},{3,4},{4,5},{5,6},{6,7},{7,8},{8,9},{9,10},{10,1... | collective-permute-start | bytes 786440 | tf_op jit(solution)/shard_map/ppermute | solution.py:29
  144.7 8.7 %collective-permute-start.7 = (bf16[128,1024]{1,0:T(8,128)(2,1)S(1)}, bf16[128,1024]{1,0:T(8,128)(2,1)}, u32[]{:S(2)}, u32[]{:S(2)}) collective-permute-start(bf16[128,1024]{1,0:T(8,128)(2,1)S(1)} %get-tuple-element.45), channel_id=1, source_target_pairs={{1,0},{2,1},{3,2},{4,3},{5,4},{6,5},{7,6},{8,7},{9,8},{10,9},{11,1... | collective-permute-start | bytes 786440 | tf_op jit(solution)/shard_map/ppermute | solution.py:29

commit v14 on v13

--- a/solution.py
+++ b/solution.py
@@ -240,14 +240,9 @@
 def on_device(queries, keys, values, lengths, conv_weight, norm_gain, cotangent):
     rows_in, width = queries.shape
     heads_total = width // HEAD_DIM
-    stacked = jnp.stack(
-        [a.reshape(rows_in, heads_total, HEAD_DIM) for a in (queries, keys, values)], axis=2
-    ).reshape(rows_in, heads_total * 3 * HEAD_DIM)
-    local_qkv = lax.all_to_all(stacked, "uly", split_axis=1, concat_axis=0, tiled=True)
-    local_qkv = local_qkv.reshape(local_qkv.shape[0], -1, 3, HEAD_DIM)
-    local_q, local_k, local_v = (
-        local_qkv[:, :, i].reshape(local_qkv.shape[0], -1) for i in range(3)
-    )
+    stacked = jnp.stack([queries, keys, values], axis=0)
+    local_qkv = lax.all_to_all(stacked, "uly", split_axis=2, concat_axis=1, tiled=True)
+    local_q, local_k, local_v = (local_qkv[i] for i in range(3))
     block_rows, channels = local_q.shape
     heads_here = channels // HEAD_DIM
     maxlen = block_rows // 2

time: 157 us -> 161 us (1.025)
  local copies, waits for them, and re-layouts: 20.9 us -> 16.1 us
  waiting for transfers between devices: 29.8 us -> 34.1 us
  other arithmetic: 4.53 us -> 7.1 us
  Pallas kernels: 59.3 us -> 61.1 us
    all_to_all x1, waiting for transfers between devices: 20.3 us -> 24.8 us  [on_device(): lax.all_to_all(stacked, 'uly', split_axis=2, concat_axis=1, tiled=True)]
    unnamed x17, local copies, waits for them, and re-layouts: 6.79 us -> 3.5 us
where the time goes in v14:
time: 161 us; the launch traced here: 159 us
  Pallas kernels  61.1 us (38%)
  starting transfers between devices  40 us (25%)
  waiting for transfers between devices  34.1 us (21%)
  local copies, waits for them, and re-layouts  16.1 us (10%)
  other arithmetic  7.1 us (4%)
    all_to_all x1, waiting for transfers between devices, on_device(): lax.all_to_all(stacked, 'uly', split_axis=2, concat_axis=1, tiled=True)  24.8 us
    pallas_call x1, Pallas kernels, on_device(): vmem_call(backward_kernel, 2, 9, (jax.ShapeDtypeStruct((block_rows, HEAD_...  18.8 us
    pallas_call x1, Pallas kernels, on_device(): vmem_call(forward_kernel, 2, 4, (jax.ShapeDtypeStruct((HEAD_DIM, block_ro...  16.2 us
    pallas_call x1, Pallas kernels, on_device(): vmem_call(conv_backward_kernel, 0, 5, (jax.ShapeDtypeStruct((HEAD_DIM, bl...  13.4 us
    pallas_call x1, Pallas kernels, on_device(): vmem_call(conv_forward_kernel, 0, 6, (jax.ShapeDtypeStruct((HEAD_DIM, blo...  12.8 us
    all_to_all x1, starting transfers between devices, on_device(): lax.all_to_all(stacked, 'uly', split_axis=2, concat_axis=1, tiled=True)  10 us
    ppermute x2, starting transfers between devices, padded_rims(): low = lax.ppermute(block[:, block.shape[1] - half:], 'blk', forward)  9.08 us
    ppermute x1, starting transfers between devices, extended(): lax.ppermute(lax.slice_in_dim(block, block.shape[dim] - width, None, axis...  8.12 us
  transfers between devices with their start and end apart: 9, of which 5 were waited for; matrix products, arithmetic and copies ran while one was open for 6% of the time, Pallas kernels for 0%

profile of v14, /device:TPU:9, one launch (start us, length us, event | category | flops | bytes accessed | tf_op | source)
XLA Modules:
  0.0 159.3 jit_solution(351655060257324202)
XLA Ops:
  0.6 1.2 pad_maximum_fusion.1
  1.8 1.4 copy.63
  3.3 10.0 %all-to-all-start = ((bf16[3,128,1024]{1,0,2:T(4,128)(2,1)}), bf16[3,128,1024]{1,0,2:T(4,128)(2,1)S(1)}, u32[]{:S(2)}, u32[]{:S(2)}) async-start(bf16[3,128,1024]{1,0,2:T(4,128)(2,1)} %copy.63), calls=%async_computation | async-start | bytes 2097152 | tf_op jit(solution)/shard_map/all_to_all | solution.py:244
  13.7 0.2 select_reduce_fusion
  13.9 0.5 slice.81
  14.4 0.2 convert_reduce_fusion
  14.7 0.6 and_select_fusion.kseg_ref
  15.3 24.8 %all-to-all-done = bf16[3,128,1024]{1,0,2:T(4,128)(2,1)S(1)} async-done(((bf16[3,128,1024]{1,0,2:T(4,128)(2,1)}), bf16[3,128,1024]{1,0,2:T(4,128)(2,1)S(1)}, u32[]{:S(2)}, u32[]{:S(2)}) %all-to-all-start) | async-done | bytes 786464 | tf_op jit(solution)/shard_map/all_to_all | solution.py:244
  40.1 0.1 copy.64
  40.3 0.3 copy.66
  40.6 0.3 copy.67
  40.9 0.3 fusion.1
  41.2 8.1 %collective-permute-start = (bf16[1024,128]{1,0:T(8,128)(2,1)S(1)}, bf16[1024,128]{1,0:T(8,128)(2,1)S(1)}, u32[]{:S(2)}, u32[]{:S(2)}) collective-permute-start(bf16[1024,128]{1,0:T(8,128)(2,1)S(1)} %get-tuple-element.50), channel_id=1, source_target_pairs={{0,1},{1,2},{2,3},{3,4},{4,5},{5,6},{6,7},{7,8},{8,9},{9,10},{10,1... | collective-permute-start | bytes 786440 | tf_op jit(solution)/shard_map/ppermute | solution.py:18
  49.3 1.9 %collective-permute-start.1 = (bf16[1024,128]{1,0:T(8,128)(2,1)S(1)}, bf16[1024,128]{1,0:T(8,128)(2,1)S(1)}, u32[]{:S(2)}, u32[]{:S(2)}) collective-permute-start(bf16[1024,128]{1,0:T(8,128)(2,1)S(1)} %get-tuple-element.51), channel_id=1, source_target_pairs={{1,0},{2,1},{3,2},{4,3},{5,4},{6,5},{7,6},{8,7},{9,8},{10,9},{11,1... | collective-permute-start | bytes 786440 | tf_op jit(solution)/shard_map/ppermute | solution.py:21
  51.2 0.7 broadcast_minimum_fusion
  52.1 1.4 copy.69.qseg_ref
  53.4 0.6 maximum_minimum_fusion
  54.0 0.2 copy.65
  54.3 0.3 copy.75
  54.6 0.9 concatenate.24.clone.q_ref
  55.5 2.4 %collective-permute-done.1 = bf16[1024,128]{1,0:T(8,128)(2,1)S(1)} collective-permute-done((bf16[1024,128]{1,0:T(8,128)(2,1)S(1)}, bf16[1024,128]{1,0:T(8,128)(2,1)S(1)}, u32[]{:S(2)}, u32[]{:S(2)}) %collective-permute-start.1) | collective-permute-done | bytes 262176 | tf_op jit(solution)/shard_map/ppermute | solution.py:21
  57.9 1.3 pad_maximum_fusion.kv_ref
  59.2 16.2 %shard_map.102 = (bf16[64,2048]{1,0:T(8,128)(2,1)}, f32[2048,1]{1,0:T(8,128)}) custom-call(s32[4]{0:T(128)} %get-tuple-element.47.lo_ref, s32[4]{0:T(128)} %get-tuple-element.46.hi_ref, bf16[2048,128]{1,0:T(8,128)(2,1)} %concatenate.24.clone.q_ref, bf16[4096,128]{1,0:T(8,128)(2,1)} %pad_maximum_fusion.kv_ref, s32[2048,1]{1,0:T(8,128)} %copy.69.qseg_ref, ...), custom_call_target="tpu_custom_call" | custom-call | tf_op jit(solution)/shard_map/pallas_call | solution.py:275
  75.3 0.9 fusion.11
  76.2 1.9 %collective-permute-start.3 = (bf16[64,15]{1,0:T(8,128)(2,1)S(1)}, bf16[64,15]{1,0:T(8,128)(2,1)S(1)}, u32[]{:S(2)}, u32[]{:S(2)}) collective-permute-start(bf16[64,15]{1,0:T(8,128)(2,1)S(1)} %get-tuple-element.61), channel_id=1, source_target_pairs={{1,0},{2,1},{3,2},{4,3},{5,4},{6,5},{7,6},{8,7},{9,8},{10,9},{11,1... | collective-permute-start | bytes 5768 | tf_op jit(solution)/shard_map/ppermute | solution.py:232
  78.1 4.5 %collective-permute-start.2 = (bf16[64,15]{1,0:T(8,128)(2,1)S(1)}, bf16[64,15]{1,0:T(8,128)(2,1)S(1)}, u32[]{:S(2)}, u32[]{:S(2)}) collective-permute-start(bf16[64,15]{1,0:T(8,128)(2,1)S(1)} %get-tuple-element.62), channel_id=1, source_target_pairs={{0,1},{1,2},{2,3},{3,4},{4,5},{5,6},{6,7},{7,8},{8,9},{9,10},{10,1... | collective-permute-start | bytes 5768 | tf_op jit(solution)/shard_map/ppermute | solution.py:231
  82.7 0.6 fusion.2
  83.3 0.7 copy.70
  84.0 0.7 copy.71.gain_ref
  84.7 1.8 %concatenate.27.x_ref = f32[64,2304]{1,0:T(8,128)} concatenate(f32[64,113]{1,0:T(8,128)S(1)} %broadcast.102, bf16[64,15]{1,0:T(8,128)(2,1)S(1)} %collective-permute-done.2, bf16[64,2048]{1,0:T(8,128)(2,1)} %get-tuple-element.14.att_ref, bf16[64,15]{1,0:T(8,128)(2,1)S(1)} %collective-permute-done.3, f32[64,113]{1,0:T(8,128)S(1)} %broadcast.102), dimensions={1} | concatenate | bytes 913664 | tf_op jit(solution)/shard_map/concatenate | solution.py:234
  86.6 12.8 %shard_map.103 = (bf16[64,2048]{1,0:T(8,128)(2,1)}, f32[64,2048]{1,0:T(8,128)}) custom-call(f32[64,2304]{1,0:T(8,128)} %concatenate.27.x_ref, f32[64,31]{1,0:T(8,128)} %bitcast.38, f32[64,1]{1,0:T(8,128)} %copy.71.gain_ref, bf16[64,2048]{1,0:T(8,128)(2,1)} %cot_ref.1, s32[1,2048]{1,0:T(1,128)} %get-tuple-element.64.lo_ref, s32[1,2048]{1,0:T(1,128)} %get-tuple-element.63.hi_ref), custom_call_target="tpu_custom_call" | custom-call | tf_op jit(solution)/shard_map/pallas_call | solution.py:289
  99.3 0.8 fusion.10
  100.2 1.9 %collective-permute-start.5 = (f32[64,15]{1,0:T(8,128)S(1)}, f32[64,15]{1,0:T(8,128)S(1)}, u32[]{:S(2)}, u32[]{:S(2)}) collective-permute-start(f32[64,15]{1,0:T(8,128)S(1)} %get-tuple-element.57), channel_id=1, source_target_pairs={{1,0},{2,1},{3,2},{4,3},{5,4},{6,5},{7,6},{8,7},{9,8},{10,9},{11,1... | collective-permute-start | bytes 11528 | tf_op jit(solution)/shard_map/ppermute | solution.py:232
  102.1 4.5 %collective-permute-start.4 = (f32[64,15]{1,0:T(8,128)S(1)}, f32[64,15]{1,0:T(8,128)S(1)}, u32[]{:S(2)}, u32[]{:S(2)}) collective-permute-start(f32[64,15]{1,0:T(8,128)S(1)} %get-tuple-element.58), channel_id=1, source_target_pairs={{0,1},{1,2},{2,3},{3,4},{4,5},{5,6},{6,7},{7,8},{8,9},{9,10},{10,1... | collective-permute-start | bytes 11528 | tf_op jit(solution)/shard_map/ppermute | solution.py:231
  106.7 1.0 collective-permute-done.4
  107.6 1.9 %concatenate.28.y_ref = f32[64,2304]{1,0:T(8,128)} concatenate(f32[64,113]{1,0:T(8,128)S(1)} %broadcast.102, f32[64,15]{1,0:T(8,128)S(1)} %collective-permute-done.4, f32[64,2048]{1,0:T(8,128)} %get-tuple-element.16, f32[64,15]{1,0:T(8,128)S(1)} %collective-permute-done.5, f32[64,113]{1,0:T(8,128)S(1)} %broadcast.102), dimensions={1} | concatenate | bytes 1179648 | tf_op jit(solution)/shard_map/concatenate | solution.py:234
  109.6 13.4 %shard_map.104 = (bf16[64,2048]{1,0:T(8,128)(2,1)}, bf16[2048,128]{1,0:T(8,128)(2,1)}, f32[2048,1]{1,0:T(8,128)}) custom-call(f32[64,2304]{1,0:T(8,128)} %concatenate.28.y_ref, f32[64,31]{1,0:T(8,128)} %bitcast.39, bf16[64,2048]{1,0:T(8,128)(2,1)} %get-tuple-element.14.att_ref, s32[1,2048]{1,0:T(1,128)} %get-tuple-element.64.lo_ref, ...), custom_call_target="tpu_custom_call" | custom-call | tf_op jit(solution)/shard_map/pallas_call | solution.py:298
  122.9 18.8 %shard_map.105 = (bf16[2048,64]{1,0:T(8,128)(2,1)}, f32[64,4096]{1,0:T(8,128)}, f32[64,4096]{1,0:T(8,128)}) custom-call(s32[4]{0:T(128)} %get-tuple-element.47.lo_ref, s32[4]{0:T(128)} %get-tuple-element.46.hi_ref, bf16[2048,128]{1,0:T(8,128)(2,1)} %concatenate.24.clone.q_ref, bf16[4096,128]{1,0:T(8,128)(2,1)} %pad_maximum_fusion.kv_ref, ...), custom_call_target="tpu_custom_call" | custom-call | tf_op jit(solution)/shard_map/pallas_call | solution.py:310
  141.7 1.4 constant_dynamic-update-slice_fusion.1
  143.1 0.1 copy-done.1
  143.4 0.1 convert.9
  143.5 5.1 %collective-permute-start.6 = (bf16[128,1024]{1,0:T(8,128)(2,1)S(1)}, bf16[128,1024]{1,0:T(8,128)(2,1)S(1)}, u32[]{:S(2)}, u32[]{:S(2)}) collective-permute-start(bf16[128,1024]{1,0:T(8,128)(2,1)S(1)} %get-tuple-element.48), channel_id=1, source_target_pairs={{0,1},{1,2},{2,3},{3,4},{4,5},{5,6},{6,7},{7,8},{8,9},{9,10},{10,1... | collective-permute-start | bytes 786440 | tf_op jit(solution)/shard_map/ppermute | solution.py:29
  148.7 1.9 %collective-permute-start.7 = (bf16[128,1024]{1,0:T(8,128)(2,1)S(1)}, bf16[128,1024]{1,0:T(8,128)(2,1)}, u32[]{:S(2)}, u32[]{:S(2)}) collective-permute-start(bf16[128,1024]{1,0:T(8,128)(2,1)S(1)} %get-tuple-element.49), channel_id=1, source_target_pairs={{1,0},{2,1},{3,2},{4,3},{5,4},{6,5},{7,6},{8,7},{9,8},{10,9},{11,1... | collective-permute-start | bytes 786440 | tf_op jit(solution)/shard_map/ppermute | solution.py:29
  150.6 0.9 copy.74
  151.5 0.5 collective-permute-done.6
  152.0 5.4 %collective-permute-done.7 = bf16[128,1024]{1,0:T(8,128)(2,1)} collective-permute-done((bf16[128,1024]{1,0:T(8,128)(2,1)S(1)}, bf16[128,1024]{1,0:T(8,128)(2,1)}, u32[]{:S(2)}, u32[]{:S(2)}) %collective-permute-start.7) | collective-permute-done | bytes 262176 | tf_op jit(solution)/shard_map/ppermute | solution.py:29
  157.4 1.1 fusion
  158.5 0.8 fusion.9
  (30 shorter events, 0.8 us)
Async XLA Ops:
  1.8 11.5 %copy-start.4 = (s32[64]{0:T(128)S(1)}, s32[64]{0:T(128)}, u32[]{:S(2)}) copy-start(s32[64]{0:T(128)} %param.10) | copy-start | bytes 772
  3.3 36.8 %all-to-all-start = ((bf16[3,128,1024]{1,0,2:T(4,128)(2,1)}), bf16[3,128,1024]{1,0,2:T(4,128)(2,1)S(1)}, u32[]{:S(2)}, u32[]{:S(2)}) async-start(bf16[3,128,1024]{1,0,2:T(4,128)(2,1)} %copy.63), calls=%async_computation | async-start | bytes 2097152 | tf_op jit(solution)/shard_map/all_to_all | solution.py:244
  41.2 14.3 %collective-permute-start = (bf16[1024,128]{1,0:T(8,128)(2,1)S(1)}, bf16[1024,128]{1,0:T(8,128)(2,1)S(1)}, u32[]{:S(2)}, u32[]{:S(2)}) collective-permute-start(bf16[1024,128]{1,0:T(8,128)(2,1)S(1)} %get-tuple-element.50), channel_id=1, source_target_pairs={{0,1},{1,2},{2,3},{3,4},{4,5},{5,6},{6,7},{7,8},{8,9},{9,10},{10,1... | collective-permute-start | bytes 786440 | tf_op jit(solution)/shard_map/ppermute | solution.py:18
  49.3 8.6 %collective-permute-start.1 = (bf16[1024,128]{1,0:T(8,128)(2,1)S(1)}, bf16[1024,128]{1,0:T(8,128)(2,1)S(1)}, u32[]{:S(2)}, u32[]{:S(2)}) collective-permute-start(bf16[1024,128]{1,0:T(8,128)(2,1)S(1)} %get-tuple-element.51), channel_id=1, source_target_pairs={{1,0},{2,1},{3,2},{4,3},{5,4},{6,5},{7,6},{8,7},{9,8},{10,9},{11,1... | collective-permute-start | bytes 786440 | tf_op jit(solution)/shard_map/ppermute | solution.py:21
  54.3 4.9 %copy-start = (bf16[8,8,16,128]{3,1,2,0:T(8,128)(2,1)}, bf16[8,8,16,128]{3,1,2,0:T(8,128)(2,1)S(1)}, u32[]{:S(2)}) copy-start(bf16[8,8,16,128]{3,1,2,0:T(8,128)(2,1)S(1)} %copy.80) | copy-start | bytes 786436
  55.5 27.8 %copy-start.3 = (f32[31,64]{1,0:T(8,128)S(1)}, f32[31,64]{1,0:T(8,128)}, u32[]{:S(2)}) copy-start(f32[31,64]{1,0:T(8,128)} %param.11) | copy-start | bytes 23812
  55.5 28.5 %copy-start.5 = (f32[64]{0:T(128)S(1)}, f32[64]{0:T(128)}, u32[]{:S(2)}) copy-start(f32[64]{0:T(128)} %param.12) | copy-start | bytes 772
  76.2 8.5 %collective-permute-start.3 = (bf16[64,15]{1,0:T(8,128)(2,1)S(1)}, bf16[64,15]{1,0:T(8,128)(2,1)S(1)}, u32[]{:S(2)}, u32[]{:S(2)}) collective-permute-start(bf16[64,15]{1,0:T(8,128)(2,1)S(1)} %get-tuple-element.61), channel_id=1, source_target_pairs={{1,0},{2,1},{3,2},{4,3},{5,4},{6,5},{7,6},{8,7},{9,8},{10,9},{11,1... | collective-permute-start | bytes 5768 | tf_op jit(solution)/shard_map/ppermute | solution.py:232
  78.1 6.6 %collective-permute-start.2 = (bf16[64,15]{1,0:T(8,128)(2,1)S(1)}, bf16[64,15]{1,0:T(8,128)(2,1)S(1)}, u32[]{:S(2)}, u32[]{:S(2)}) collective-permute-start(bf16[64,15]{1,0:T(8,128)(2,1)S(1)} %get-tuple-element.62), channel_id=1, source_target_pairs={{0,1},{1,2},{2,3},{3,4},{4,5},{5,6},{6,7},{7,8},{8,9},{9,10},{10,1... | collective-permute-start | bytes 5768 | tf_op jit(solution)/shard_map/ppermute | solution.py:231
  100.2 6.5 %collective-permute-start.5 = (f32[64,15]{1,0:T(8,128)S(1)}, f32[64,15]{1,0:T(8,128)S(1)}, u32[]{:S(2)}, u32[]{:S(2)}) collective-permute-start(f32[64,15]{1,0:T(8,128)S(1)} %get-tuple-element.57), channel_id=1, source_target_pairs={{1,0},{2,1},{3,2},{4,3},{5,4},{6,5},{7,6},{8,7},{9,8},{10,9},{11,1... | collective-permute-start | bytes 11528 | tf_op jit(solution)/shard_map/ppermute | solution.py:232
  102.1 5.6 %collective-permute-start.4 = (f32[64,15]{1,0:T(8,128)S(1)}, f32[64,15]{1,0:T(8,128)S(1)}, u32[]{:S(2)}, u32[]{:S(2)}) collective-permute-start(f32[64,15]{1,0:T(8,128)S(1)} %get-tuple-element.58), channel_id=1, source_target_pairs={{0,1},{1,2},{2,3},{3,4},{4,5},{5,6},{6,7},{7,8},{8,9},{9,10},{10,1... | collective-permute-start | bytes 11528 | tf_op jit(solution)/shard_map/ppermute | solution.py:231
  141.7 1.5 copy-start.1
  143.4 7.3 %copy-start.2 = (bf16[2048,64]{1,0:T(8,128)(2,1)S(1)}, bf16[2048,64]{1,0:T(8,128)(2,1)}, u32[]{:S(2)}) copy-start(bf16[2048,64]{1,0:T(8,128)(2,1)} %get-tuple-element.21) | copy-start | bytes 786436
  143.5 8.5 %collective-permute-start.6 = (bf16[128,1024]{1,0:T(8,128)(2,1)S(1)}, bf16[128,1024]{1,0:T(8,128)(2,1)S(1)}, u32[]{:S(2)}, u32[]{:S(2)}) collective-permute-start(bf16[128,1024]{1,0:T(8,128)(2,1)S(1)} %get-tuple-element.48), channel_id=1, source_target_pairs={{0,1},{1,2},{2,3},{3,4},{4,5},{5,6},{6,7},{7,8},{8,9},{9,10},{10,1... | collective-permute-start | bytes 786440 | tf_op jit(solution)/shard_map/ppermute | solution.py:29
  148.7 8.7 %collective-permute-start.7 = (bf16[128,1024]{1,0:T(8,128)(2,1)S(1)}, bf16[128,1024]{1,0:T(8,128)(2,1)}, u32[]{:S(2)}, u32[]{:S(2)}) collective-permute-start(bf16[128,1024]{1,0:T(8,128)(2,1)S(1)} %get-tuple-element.49), channel_id=1, source_target_pairs={{1,0},{2,1},{3,2},{4,3},{5,4},{6,5},{7,6},{8,7},{9,8},{10,9},{11,1... | collective-permute-start | bytes 786440 | tf_op jit(solution)/shard_map/ppermute | solution.py:29

commit v15 on v13

--- a/solution.py
+++ b/solution.py
@@ -167,7 +167,7 @@
 
 
 CONV_PAD = 128
-CONV_CHUNK = 256
+CONV_CHUNK = 512
 
 
 def conv_chunk(x_ref, wt_ref, lo, hi, c0, sign):

time: 157 us -> 149 us (0.949)
  Pallas kernels: 59.3 us -> 51.4 us
    pallas_call x1, Pallas kernels: 13.4 us -> 10.2 us  [on_device(): vmem_call(conv_backward_kernel, 0, 5, (jax.ShapeDtypeStruct((HEAD_DIM, bl...]
    pallas_call x1, Pallas kernels: 12.8 us -> 9.73 us  [on_device(): vmem_call(conv_forward_kernel, 0, 6, (jax.ShapeDtypeStruct((HEAD_DIM, blo...]
where the time goes in v15:
time: 149 us; the launch traced here: 148 us
  Pallas kernels  51.4 us (34%)
  starting transfers between devices  40.6 us (27%)
  waiting for transfers between devices  29.8 us (20%)
  local copies, waits for them, and re-layouts  20.9 us (14%)
  other arithmetic  4.53 us (3%)
    all_to_all x1, waiting for transfers between devices, on_device(): lax.all_to_all(stacked, 'uly', split_axis=1, concat_axis=0, tiled=True)  20.3 us
    pallas_call x1, Pallas kernels, on_device(): vmem_call(backward_kernel, 2, 9, (jax.ShapeDtypeStruct((block_rows, HEAD_...  16.9 us
    pallas_call x1, Pallas kernels, on_device(): vmem_call(forward_kernel, 2, 4, (jax.ShapeDtypeStruct((HEAD_DIM, block_ro...  14.5 us
    pallas_call x1, Pallas kernels, on_device(): vmem_call(conv_backward_kernel, 0, 5, (jax.ShapeDtypeStruct((HEAD_DIM, bl...  10.2 us
    all_to_all x1, starting transfers between devices, on_device(): lax.all_to_all(stacked, 'uly', split_axis=1, concat_axis=0, tiled=True)  10 us
    pallas_call x1, Pallas kernels, on_device(): vmem_call(conv_forward_kernel, 0, 6, (jax.ShapeDtypeStruct((HEAD_DIM, blo...  9.73 us
    ppermute x2, starting transfers between devices, padded_rims(): low = lax.ppermute(block[:, block.shape[1] - half:], 'blk', forward)  9.08 us
    ppermute x2, starting transfers between devices, passed_along(): return lax.ppermute(block, axis, route)  8.88 us
  transfers between devices with their start and end apart: 9, of which 5 were waited for; matrix products, arithmetic and copies ran while one was open for 6% of the time, Pallas kernels for 0%

profile of v15, /device:TPU:9, one launch (start us, length us, event | category | flops | bytes accessed | tf_op | source)
XLA Modules:
  0.0 148.2 jit_solution(9382248686505416742)
XLA Ops:
  0.6 1.1 copy.49
  1.8 1.1 copy.50
  2.9 1.1 copy.51
  4.1 0.9 copy.52
  5.1 10.0 %all-to-all-start = ((bf16[128,16,192]{0,2,1:T(8,128)(2,1)}), bf16[128,16,192]{0,2,1:T(8,128)(2,1)S(1)}, u32[]{:S(2)}, u32[]{:S(2)}) async-start(bf16[128,16,192]{0,2,1:T(8,128)(2,1)} %bitcast.5), calls=%async_computation | async-start | bytes 1572864 | tf_op jit(solution)/shard_map/all_to_all | solution.py:246
  15.4 0.2 select_reduce_fusion
  15.7 0.5 slice.78
  16.2 0.2 convert_reduce_fusion
  16.5 0.6 and_select_fusion.kseg_ref
  17.1 20.3 %all-to-all-done = bf16[128,16,192]{0,2,1:T(8,128)(2,1)S(1)} async-done(((bf16[128,16,192]{0,2,1:T(8,128)(2,1)}), bf16[128,16,192]{0,2,1:T(8,128)(2,1)S(1)}, u32[]{:S(2)}, u32[]{:S(2)}) %all-to-all-start) | async-done | bytes 786464 | tf_op jit(solution)/shard_map/all_to_all | solution.py:246
  37.4 0.5 copy.53
  37.9 0.3 reshape.97
  38.3 0.8 slice_bitcast_fusion.2
  39.1 6.9 %collective-permute-start = (bf16[1024,128]{0,1:T(8,128)(2,1)S(1)}, bf16[1024,128]{0,1:T(8,128)(2,1)S(1)}, u32[]{:S(2)}, u32[]{:S(2)}) collective-permute-start(bf16[1024,128]{0,1:T(8,128)(2,1)S(1)} %get-tuple-element.54), channel_id=1, source_target_pairs={{0,1},{1,2},{2,3},{3,4},{4,5},{5,6},{6,7},{7,8},{8,9},{9,10},{10,1... | collective-permute-start | bytes 786440 | tf_op jit(solution)/shard_map/ppermute | solution.py:18
  46.0 1.9 %collective-permute-start.1 = (bf16[1024,128]{0,1:T(8,128)(2,1)S(1)}, bf16[1024,128]{0,1:T(8,128)(2,1)S(1)}, u32[]{:S(2)}, u32[]{:S(2)}) collective-permute-start(bf16[1024,128]{0,1:T(8,128)(2,1)S(1)} %get-tuple-element.55), channel_id=1, source_target_pairs={{1,0},{2,1},{3,2},{4,3},{5,4},{6,5},{7,6},{8,7},{9,8},{10,9},{11,1... | collective-permute-start | bytes 786440 | tf_op jit(solution)/shard_map/ppermute | solution.py:21
  47.9 0.7 broadcast_minimum_fusion
  48.8 1.4 copy.56.qseg_ref
  50.1 0.6 maximum_minimum_fusion
  50.7 0.3 copy.63
  51.0 0.9 concatenate.24.clone.q_ref
  51.9 2.7 %collective-permute-done.1 = bf16[1024,128]{0,1:T(8,128)(2,1)S(1)} collective-permute-done((bf16[1024,128]{0,1:T(8,128)(2,1)S(1)}, bf16[1024,128]{0,1:T(8,128)(2,1)S(1)}, u32[]{:S(2)}, u32[]{:S(2)}) %collective-permute-start.1) | collective-permute-done | bytes 262176 | tf_op jit(solution)/shard_map/ppermute | solution.py:21
  54.7 1.3 copy.55.kv_ref
  56.0 14.5 %shard_map.102 = (bf16[64,2048]{1,0:T(8,128)(2,1)}, f32[2048,1]{1,0:T(8,128)}) custom-call(s32[4]{0:T(128)} %get-tuple-element.43.lo_ref, s32[4]{0:T(128)} %get-tuple-element.42.hi_ref, bf16[2048,128]{1,0:T(8,128)(2,1)} %concatenate.24.clone.q_ref, bf16[4096,128]{1,0:T(8,128)(2,1)} %copy.55.kv_ref, s32[2048,1]{1,0:T(8,128)} %copy.56.qseg_ref, ...), custom_call_target="tpu_custom_call" | custom-call | tf_op jit(solution)/shard_map/pallas_call | solution.py:280
  70.5 0.8 fusion.9
  71.3 1.9 %collective-permute-start.3 = (bf16[64,15]{1,0:T(8,128)(2,1)S(1)}, bf16[64,15]{1,0:T(8,128)(2,1)S(1)}, u32[]{:S(2)}, u32[]{:S(2)}) collective-permute-start(bf16[64,15]{1,0:T(8,128)(2,1)S(1)} %get-tuple-element.56), channel_id=1, source_target_pairs={{1,0},{2,1},{3,2},{4,3},{5,4},{6,5},{7,6},{8,7},{9,8},{10,9},{11,1... | collective-permute-start | bytes 5768 | tf_op jit(solution)/shard_map/ppermute | solution.py:232
  73.2 4.5 %collective-permute-start.2 = (bf16[64,15]{1,0:T(8,128)(2,1)S(1)}, bf16[64,15]{1,0:T(8,128)(2,1)S(1)}, u32[]{:S(2)}, u32[]{:S(2)}) collective-permute-start(bf16[64,15]{1,0:T(8,128)(2,1)S(1)} %get-tuple-element.57), channel_id=1, source_target_pairs={{0,1},{1,2},{2,3},{3,4},{4,5},{5,6},{6,7},{7,8},{8,9},{9,10},{10,1... | collective-permute-start | bytes 5768 | tf_op jit(solution)/shard_map/ppermute | solution.py:231
  77.8 0.6 fusion.2
  78.4 0.7 copy.57
  79.1 0.7 copy.58.gain_ref
  79.8 1.8 %concatenate.27.x_ref = f32[64,2304]{1,0:T(8,128)} concatenate(f32[64,113]{1,0:T(8,128)S(1)} %broadcast.102, bf16[64,15]{1,0:T(8,128)(2,1)S(1)} %collective-permute-done.2, bf16[64,2048]{1,0:T(8,128)(2,1)} %get-tuple-element.14.att_ref, bf16[64,15]{1,0:T(8,128)(2,1)S(1)} %collective-permute-done.3, f32[64,113]{1,0:T(8,128)S(1)} %broadcast.102), dimensions={1} | concatenate | bytes 913664 | tf_op jit(solution)/shard_map/concatenate | solution.py:234
  81.7 9.7 %shard_map.103 = (bf16[64,2048]{1,0:T(8,128)(2,1)}, f32[64,2048]{1,0:T(8,128)}) custom-call(f32[64,2304]{1,0:T(8,128)} %concatenate.27.x_ref, f32[64,31]{1,0:T(8,128)} %bitcast.30, f32[64,1]{1,0:T(8,128)} %copy.58.gain_ref, bf16[64,2048]{1,0:T(8,128)(2,1)} %cot_ref.1, s32[1,2048]{1,0:T(1,128)} %get-tuple-element.59.lo_ref, s32[1,2048]{1,0:T(1,128)} %get-tuple-element.58.hi_ref), custom_call_target="tpu_custom_call" | custom-call | tf_op jit(solution)/shard_map/pallas_call | solution.py:294
  91.4 0.8 fusion.8
  92.3 1.9 %collective-permute-start.5 = (f32[64,15]{1,0:T(8,128)S(1)}, f32[64,15]{1,0:T(8,128)S(1)}, u32[]{:S(2)}, u32[]{:S(2)}) collective-permute-start(f32[64,15]{1,0:T(8,128)S(1)} %get-tuple-element.52), channel_id=1, source_target_pairs={{1,0},{2,1},{3,2},{4,3},{5,4},{6,5},{7,6},{8,7},{9,8},{10,9},{11,1... | collective-permute-start | bytes 11528 | tf_op jit(solution)/shard_map/ppermute | solution.py:232
  94.2 4.5 %collective-permute-start.4 = (f32[64,15]{1,0:T(8,128)S(1)}, f32[64,15]{1,0:T(8,128)S(1)}, u32[]{:S(2)}, u32[]{:S(2)}) collective-permute-start(f32[64,15]{1,0:T(8,128)S(1)} %get-tuple-element.53), channel_id=1, source_target_pairs={{0,1},{1,2},{2,3},{3,4},{4,5},{5,6},{6,7},{7,8},{8,9},{9,10},{10,1... | collective-permute-start | bytes 11528 | tf_op jit(solution)/shard_map/ppermute | solution.py:231
  98.8 1.0 collective-permute-done.4
  99.7 1.9 %concatenate.28.y_ref = f32[64,2304]{1,0:T(8,128)} concatenate(f32[64,113]{1,0:T(8,128)S(1)} %broadcast.102, f32[64,15]{1,0:T(8,128)S(1)} %collective-permute-done.4, f32[64,2048]{1,0:T(8,128)} %get-tuple-element.16, f32[64,15]{1,0:T(8,128)S(1)} %collective-permute-done.5, f32[64,113]{1,0:T(8,128)S(1)} %broadcast.102), dimensions={1} | concatenate | bytes 1179648 | tf_op jit(solution)/shard_map/concatenate | solution.py:234
  101.7 10.2 %shard_map.104 = (bf16[64,2048]{1,0:T(8,128)(2,1)}, bf16[2048,128]{1,0:T(8,128)(2,1)}, f32[2048,1]{1,0:T(8,128)}) custom-call(f32[64,2304]{1,0:T(8,128)} %concatenate.28.y_ref, f32[64,31]{1,0:T(8,128)} %bitcast.31, bf16[64,2048]{1,0:T(8,128)(2,1)} %get-tuple-element.14.att_ref, s32[1,2048]{1,0:T(1,128)} %get-tuple-element.59.lo_ref, ...), custom_call_target="tpu_custom_call" | custom-call | tf_op jit(solution)/shard_map/pallas_call | solution.py:303
  111.9 16.9 %shard_map.105 = (bf16[2048,64]{1,0:T(8,128)(2,1)}, f32[64,4096]{1,0:T(8,128)}, f32[64,4096]{1,0:T(8,128)}) custom-call(s32[4]{0:T(128)} %get-tuple-element.43.lo_ref, s32[4]{0:T(128)} %get-tuple-element.42.hi_ref, bf16[2048,128]{1,0:T(8,128)(2,1)} %concatenate.24.clone.q_ref, bf16[4096,128]{1,0:T(8,128)(2,1)} %copy.55.kv_ref, ...), custom_call_target="tpu_custom_call" | custom-call | tf_op jit(solution)/shard_map/pallas_call | solution.py:315
  128.8 1.4 constant_dynamic-update-slice_fusion.1
  130.2 0.1 copy-done
  130.5 0.1 convert.9
  130.6 7.0 %collective-permute-start.6 = (bf16[128,1024]{1,0:T(8,128)(2,1)S(1)}, bf16[128,1024]{1,0:T(8,128)(2,1)S(1)}, u32[]{:S(2)}, u32[]{:S(2)}) collective-permute-start(bf16[128,1024]{1,0:T(8,128)(2,1)S(1)} %get-tuple-element.44), channel_id=1, source_target_pairs={{0,1},{1,2},{2,3},{3,4},{4,5},{5,6},{6,7},{7,8},{8,9},{9,10},{10,1... | collective-permute-start | bytes 786440 | tf_op jit(solution)/shard_map/ppermute | solution.py:29
  137.6 1.9 %collective-permute-start.7 = (bf16[128,1024]{1,0:T(8,128)(2,1)S(1)}, bf16[128,1024]{1,0:T(8,128)(2,1)}, u32[]{:S(2)}, u32[]{:S(2)}) collective-permute-start(bf16[128,1024]{1,0:T(8,128)(2,1)S(1)} %get-tuple-element.45), channel_id=1, source_target_pairs={{1,0},{2,1},{3,2},{4,3},{5,4},{6,5},{7,6},{8,7},{9,8},{10,9},{11,1... | collective-permute-start | bytes 786440 | tf_op jit(solution)/shard_map/ppermute | solution.py:29
  139.6 0.9 copy.62
  140.5 0.5 collective-permute-done.6
  141.0 5.4 %collective-permute-done.7 = bf16[128,1024]{1,0:T(8,128)(2,1)} collective-permute-done((bf16[128,1024]{1,0:T(8,128)(2,1)S(1)}, bf16[128,1024]{1,0:T(8,128)(2,1)}, u32[]{:S(2)}, u32[]{:S(2)}) %collective-permute-start.7) | collective-permute-done | bytes 262176 | tf_op jit(solution)/shard_map/ppermute | solution.py:29
  146.3 1.1 fusion
  147.4 0.8 fusion.7
  (29 shorter events, 0.8 us)
Async XLA Ops:
  4.0 11.1 %copy-start.3 = (s32[64]{0:T(128)S(1)}, s32[64]{0:T(128)}, u32[]{:S(2)}) copy-start(s32[64]{0:T(128)} %param.10) | copy-start | bytes 772
  5.1 32.3 %all-to-all-start = ((bf16[128,16,192]{0,2,1:T(8,128)(2,1)}), bf16[128,16,192]{0,2,1:T(8,128)(2,1)S(1)}, u32[]{:S(2)}, u32[]{:S(2)}) async-start(bf16[128,16,192]{0,2,1:T(8,128)(2,1)} %bitcast.5), calls=%async_computation | async-start | bytes 1572864 | tf_op jit(solution)/shard_map/all_to_all | solution.py:246
  39.1 12.8 %collective-permute-start = (bf16[1024,128]{0,1:T(8,128)(2,1)S(1)}, bf16[1024,128]{0,1:T(8,128)(2,1)S(1)}, u32[]{:S(2)}, u32[]{:S(2)}) collective-permute-start(bf16[1024,128]{0,1:T(8,128)(2,1)S(1)} %get-tuple-element.54), channel_id=1, source_target_pairs={{0,1},{1,2},{2,3},{3,4},{4,5},{5,6},{6,7},{7,8},{8,9},{9,10},{10,1... | collective-permute-start | bytes 786440 | tf_op jit(solution)/shard_map/ppermute | solution.py:18
  46.0 8.6 %collective-permute-start.1 = (bf16[1024,128]{0,1:T(8,128)(2,1)S(1)}, bf16[1024,128]{0,1:T(8,128)(2,1)S(1)}, u32[]{:S(2)}, u32[]{:S(2)}) collective-permute-start(bf16[1024,128]{0,1:T(8,128)(2,1)S(1)} %get-tuple-element.55), channel_id=1, source_target_pairs={{1,0},{2,1},{3,2},{4,3},{5,4},{6,5},{7,6},{8,7},{9,8},{10,9},{11,1... | collective-permute-start | bytes 786440 | tf_op jit(solution)/shard_map/ppermute | solution.py:21
  54.7 23.7 %copy-start.2 = (f32[31,64]{1,0:T(8,128)S(1)}, f32[31,64]{1,0:T(8,128)}, u32[]{:S(2)}) copy-start(f32[31,64]{1,0:T(8,128)} %param.11) | copy-start | bytes 23812
  54.7 24.4 %copy-start.4 = (f32[64]{0:T(128)S(1)}, f32[64]{0:T(128)}, u32[]{:S(2)}) copy-start(f32[64]{0:T(128)} %param.12) | copy-start | bytes 772
  71.3 8.5 %collective-permute-start.3 = (bf16[64,15]{1,0:T(8,128)(2,1)S(1)}, bf16[64,15]{1,0:T(8,128)(2,1)S(1)}, u32[]{:S(2)}, u32[]{:S(2)}) collective-permute-start(bf16[64,15]{1,0:T(8,128)(2,1)S(1)} %get-tuple-element.56), channel_id=1, source_target_pairs={{1,0},{2,1},{3,2},{4,3},{5,4},{6,5},{7,6},{8,7},{9,8},{10,9},{11,1... | collective-permute-start | bytes 5768 | tf_op jit(solution)/shard_map/ppermute | solution.py:232
  73.2 6.6 %collective-permute-start.2 = (bf16[64,15]{1,0:T(8,128)(2,1)S(1)}, bf16[64,15]{1,0:T(8,128)(2,1)S(1)}, u32[]{:S(2)}, u32[]{:S(2)}) collective-permute-start(bf16[64,15]{1,0:T(8,128)(2,1)S(1)} %get-tuple-element.57), channel_id=1, source_target_pairs={{0,1},{1,2},{2,3},{3,4},{4,5},{5,6},{6,7},{7,8},{8,9},{9,10},{10,1... | collective-permute-start | bytes 5768 | tf_op jit(solution)/shard_map/ppermute | solution.py:231
  92.3 6.5 %collective-permute-start.5 = (f32[64,15]{1,0:T(8,128)S(1)}, f32[64,15]{1,0:T(8,128)S(1)}, u32[]{:S(2)}, u32[]{:S(2)}) collective-permute-start(f32[64,15]{1,0:T(8,128)S(1)} %get-tuple-element.52), channel_id=1, source_target_pairs={{1,0},{2,1},{3,2},{4,3},{5,4},{6,5},{7,6},{8,7},{9,8},{10,9},{11,1... | collective-permute-start | bytes 11528 | tf_op jit(solution)/shard_map/ppermute | solution.py:232
  94.2 5.6 %collective-permute-start.4 = (f32[64,15]{1,0:T(8,128)S(1)}, f32[64,15]{1,0:T(8,128)S(1)}, u32[]{:S(2)}, u32[]{:S(2)}) collective-permute-start(f32[64,15]{1,0:T(8,128)S(1)} %get-tuple-element.53), channel_id=1, source_target_pairs={{0,1},{1,2},{2,3},{3,4},{4,5},{5,6},{6,7},{7,8},{8,9},{9,10},{10,1... | collective-permute-start | bytes 11528 | tf_op jit(solution)/shard_map/ppermute | solution.py:231
  128.8 1.5 %copy-start = (f32[64,4096]{1,0:T(8,128)S(1)}, f32[64,4096]{1,0:T(8,128)}, u32[]{:S(2)}) copy-start(f32[64,4096]{1,0:T(8,128)} %get-tuple-element.23) | copy-start | bytes 3145732
  130.5 9.1 %copy-start.1 = (bf16[2048,64]{1,0:T(8,128)(2,1)S(1)}, bf16[2048,64]{1,0:T(8,128)(2,1)}, u32[]{:S(2)}) copy-start(bf16[2048,64]{1,0:T(8,128)(2,1)} %get-tuple-element.21) | copy-start | bytes 786436
  130.6 10.3 %collective-permute-start.6 = (bf16[128,1024]{1,0:T(8,128)(2,1)S(1)}, bf16[128,1024]{1,0:T(8,128)(2,1)S(1)}, u32[]{:S(2)}, u32[]{:S(2)}) collective-permute-start(bf16[128,1024]{1,0:T(8,128)(2,1)S(1)} %get-tuple-element.44), channel_id=1, source_target_pairs={{0,1},{1,2},{2,3},{3,4},{4,5},{5,6},{6,7},{7,8},{8,9},{9,10},{10,1... | collective-permute-start | bytes 786440 | tf_op jit(solution)/shard_map/ppermute | solution.py:29
  137.6 8.7 %collective-permute-start.7 = (bf16[128,1024]{1,0:T(8,128)(2,1)S(1)}, bf16[128,1024]{1,0:T(8,128)(2,1)}, u32[]{:S(2)}, u32[]{:S(2)}) collective-permute-start(bf16[128,1024]{1,0:T(8,128)(2,1)S(1)} %get-tuple-element.45), channel_id=1, source_target_pairs={{1,0},{2,1},{3,2},{4,3},{5,4},{6,5},{7,6},{8,7},{9,8},{10,9},{11,1... | collective-permute-start | bytes 786440 | tf_op jit(solution)/shard_map/ppermute | solution.py:29

commit v16 on v15

--- a/solution.py
+++ b/solution.py
@@ -167,7 +167,7 @@
 
 
 CONV_PAD = 128
-CONV_CHUNK = 512
+CONV_CHUNK = 1024
 
 
 def conv_chunk(x_ref, wt_ref, lo, hi, c0, sign):

time: 149 us -> 148 us (level)
  no operation moved by 1% of the time
where the time goes in v16:
time: 148 us
  Pallas kernels  50.8 us (34%)
  starting transfers between devices  40.8 us (28%)
  waiting for transfers between devices  29.7 us (20%)
  local copies, waits for them, and re-layouts  20.9 us (14%)
  other arithmetic  4.53 us (3%)
    all_to_all x1, waiting for transfers between devices, on_device(): lax.all_to_all(stacked, 'uly', split_axis=1, concat_axis=0, tiled=True)  20.3 us
    pallas_call x1, Pallas kernels, on_device(): vmem_call(backward_kernel, 2, 9, (jax.ShapeDtypeStruct((block_rows, HEAD_...  17.9 us
    pallas_call x1, Pallas kernels, on_device(): vmem_call(forward_kernel, 2, 4, (jax.ShapeDtypeStruct((HEAD_DIM, block_ro...  15.3 us
    all_to_all x1, starting transfers between devices, on_device(): lax.all_to_all(stacked, 'uly', split_axis=1, concat_axis=0, tiled=True)  10 us
    ppermute x2, starting transfers between devices, padded_rims(): low = lax.ppermute(block[:, block.shape[1] - half:], 'blk', forward)  9.26 us
    pallas_call x1, Pallas kernels, on_device(): vmem_call(conv_backward_kernel, 0, 5, (jax.ShapeDtypeStruct((HEAD_DIM, bl...  8.91 us
    ppermute x2, starting transfers between devices, passed_along(): return lax.ppermute(block, axis, route)  8.89 us
    pallas_call x1, Pallas kernels, on_device(): vmem_call(conv_forward_kernel, 0, 6, (jax.ShapeDtypeStruct((HEAD_DIM, blo...  8.65 us
  transfers between devices with their start and end apart: 9, of which 5 were waited for; matrix products, arithmetic and copies ran while one was open for 6% of the time, Pallas kernels for 0%

profile of v16, /device:TPU:9, one launch (start us, length us, event | category | flops | bytes accessed | tf_op | source)
XLA Modules:
  0.0 147.6 jit_solution(10413612853789250192)
XLA Ops:
  0.6 1.1 copy.49
  1.8 1.1 copy.50
  2.9 1.1 copy.51
  4.1 0.9 copy.52
  5.1 10.0 %all-to-all-start = ((bf16[128,16,192]{0,2,1:T(8,128)(2,1)}), bf16[128,16,192]{0,2,1:T(8,128)(2,1)S(1)}, u32[]{:S(2)}, u32[]{:S(2)}) async-start(bf16[128,16,192]{0,2,1:T(8,128)(2,1)} %bitcast.5), calls=%async_computation | async-start | bytes 1572864 | tf_op jit(solution)/shard_map/all_to_all | solution.py:246
  15.4 0.2 select_reduce_fusion
  15.7 0.5 slice.78
  16.2 0.2 convert_reduce_fusion
  16.5 0.6 and_select_fusion.kseg_ref
  17.1 20.3 %all-to-all-done = bf16[128,16,192]{0,2,1:T(8,128)(2,1)S(1)} async-done(((bf16[128,16,192]{0,2,1:T(8,128)(2,1)}), bf16[128,16,192]{0,2,1:T(8,128)(2,1)S(1)}, u32[]{:S(2)}, u32[]{:S(2)}) %all-to-all-start) | async-done | bytes 786464 | tf_op jit(solution)/shard_map/all_to_all | solution.py:246
  37.4 0.5 copy.53
  37.9 0.3 reshape.97
  38.3 0.8 slice_bitcast_fusion.2
  39.1 6.9 %collective-permute-start = (bf16[1024,128]{0,1:T(8,128)(2,1)S(1)}, bf16[1024,128]{0,1:T(8,128)(2,1)S(1)}, u32[]{:S(2)}, u32[]{:S(2)}) collective-permute-start(bf16[1024,128]{0,1:T(8,128)(2,1)S(1)} %get-tuple-element.54), channel_id=1, source_target_pairs={{0,1},{1,2},{2,3},{3,4},{4,5},{5,6},{6,7},{7,8},{8,9},{9,10},{10,1... | collective-permute-start | bytes 786440 | tf_op jit(solution)/shard_map/ppermute | solution.py:18
  46.0 1.9 %collective-permute-start.1 = (bf16[1024,128]{0,1:T(8,128)(2,1)S(1)}, bf16[1024,128]{0,1:T(8,128)(2,1)S(1)}, u32[]{:S(2)}, u32[]{:S(2)}) collective-permute-start(bf16[1024,128]{0,1:T(8,128)(2,1)S(1)} %get-tuple-element.55), channel_id=1, source_target_pairs={{1,0},{2,1},{3,2},{4,3},{5,4},{6,5},{7,6},{8,7},{9,8},{10,9},{11,1... | collective-permute-start | bytes 786440 | tf_op jit(solution)/shard_map/ppermute | solution.py:21
  47.9 0.7 broadcast_minimum_fusion
  48.8 1.4 copy.56.qseg_ref
  50.1 0.6 maximum_minimum_fusion
  50.7 0.3 copy.63
  51.0 0.9 concatenate.24.clone.q_ref
  51.9 2.7 %collective-permute-done.1 = bf16[1024,128]{0,1:T(8,128)(2,1)S(1)} collective-permute-done((bf16[1024,128]{0,1:T(8,128)(2,1)S(1)}, bf16[1024,128]{0,1:T(8,128)(2,1)S(1)}, u32[]{:S(2)}, u32[]{:S(2)}) %collective-permute-start.1) | collective-permute-done | bytes 262176 | tf_op jit(solution)/shard_map/ppermute | solution.py:21
  54.7 1.3 copy.55.kv_ref
  56.0 15.3 %shard_map.102 = (bf16[64,2048]{1,0:T(8,128)(2,1)}, f32[2048,1]{1,0:T(8,128)}) custom-call(s32[4]{0:T(128)} %get-tuple-element.43.lo_ref, s32[4]{0:T(128)} %get-tuple-element.42.hi_ref, bf16[2048,128]{1,0:T(8,128)(2,1)} %concatenate.24.clone.q_ref, bf16[4096,128]{1,0:T(8,128)(2,1)} %copy.55.kv_ref, s32[2048,1]{1,0:T(8,128)} %copy.56.qseg_ref, ...), custom_call_target="tpu_custom_call" | custom-call | tf_op jit(solution)/shard_map/pallas_call | solution.py:280
  71.3 0.8 fusion.9
  72.1 1.9 %collective-permute-start.3 = (bf16[64,15]{1,0:T(8,128)(2,1)S(1)}, bf16[64,15]{1,0:T(8,128)(2,1)S(1)}, u32[]{:S(2)}, u32[]{:S(2)}) collective-permute-start(bf16[64,15]{1,0:T(8,128)(2,1)S(1)} %get-tuple-element.56), channel_id=1, source_target_pairs={{1,0},{2,1},{3,2},{4,3},{5,4},{6,5},{7,6},{8,7},{9,8},{10,9},{11,1... | collective-permute-start | bytes 5768 | tf_op jit(solution)/shard_map/ppermute | solution.py:232
  74.1 4.5 %collective-permute-start.2 = (bf16[64,15]{1,0:T(8,128)(2,1)S(1)}, bf16[64,15]{1,0:T(8,128)(2,1)S(1)}, u32[]{:S(2)}, u32[]{:S(2)}) collective-permute-start(bf16[64,15]{1,0:T(8,128)(2,1)S(1)} %get-tuple-element.57), channel_id=1, source_target_pairs={{0,1},{1,2},{2,3},{3,4},{4,5},{5,6},{6,7},{7,8},{8,9},{9,10},{10,1... | collective-permute-start | bytes 5768 | tf_op jit(solution)/shard_map/ppermute | solution.py:231
  78.6 0.6 fusion.2
  79.2 0.7 copy.57
  79.9 0.7 copy.58.gain_ref
  80.7 1.8 %concatenate.27.x_ref = f32[64,2304]{1,0:T(8,128)} concatenate(f32[64,113]{1,0:T(8,128)S(1)} %broadcast.102, bf16[64,15]{1,0:T(8,128)(2,1)S(1)} %collective-permute-done.2, bf16[64,2048]{1,0:T(8,128)(2,1)} %get-tuple-element.14.att_ref, bf16[64,15]{1,0:T(8,128)(2,1)S(1)} %collective-permute-done.3, f32[64,113]{1,0:T(8,128)S(1)} %broadcast.102), dimensions={1} | concatenate | bytes 913664 | tf_op jit(solution)/shard_map/concatenate | solution.py:234
  82.5 8.6 %shard_map.103 = (bf16[64,2048]{1,0:T(8,128)(2,1)}, f32[64,2048]{1,0:T(8,128)}) custom-call(f32[64,2304]{1,0:T(8,128)} %concatenate.27.x_ref, f32[64,31]{1,0:T(8,128)} %bitcast.30, f32[64,1]{1,0:T(8,128)} %copy.58.gain_ref, bf16[64,2048]{1,0:T(8,128)(2,1)} %cot_ref.1, s32[1,2048]{1,0:T(1,128)} %get-tuple-element.59.lo_ref, s32[1,2048]{1,0:T(1,128)} %get-tuple-element.58.hi_ref), custom_call_target="tpu_custom_call" | custom-call | tf_op jit(solution)/shard_map/pallas_call | solution.py:294
  91.2 0.8 fusion.8
  92.0 1.9 %collective-permute-start.5 = (f32[64,15]{1,0:T(8,128)S(1)}, f32[64,15]{1,0:T(8,128)S(1)}, u32[]{:S(2)}, u32[]{:S(2)}) collective-permute-start(f32[64,15]{1,0:T(8,128)S(1)} %get-tuple-element.52), channel_id=1, source_target_pairs={{1,0},{2,1},{3,2},{4,3},{5,4},{6,5},{7,6},{8,7},{9,8},{10,9},{11,1... | collective-permute-start | bytes 11528 | tf_op jit(solution)/shard_map/ppermute | solution.py:232
  93.9 4.7 %collective-permute-start.4 = (f32[64,15]{1,0:T(8,128)S(1)}, f32[64,15]{1,0:T(8,128)S(1)}, u32[]{:S(2)}, u32[]{:S(2)}) collective-permute-start(f32[64,15]{1,0:T(8,128)S(1)} %get-tuple-element.53), channel_id=1, source_target_pairs={{0,1},{1,2},{2,3},{3,4},{4,5},{5,6},{6,7},{7,8},{8,9},{9,10},{10,1... | collective-permute-start | bytes 11528 | tf_op jit(solution)/shard_map/ppermute | solution.py:231
  98.7 0.8 collective-permute-done.4
  99.5 1.9 %concatenate.28.y_ref = f32[64,2304]{1,0:T(8,128)} concatenate(f32[64,113]{1,0:T(8,128)S(1)} %broadcast.102, f32[64,15]{1,0:T(8,128)S(1)} %collective-permute-done.4, f32[64,2048]{1,0:T(8,128)} %get-tuple-element.16, f32[64,15]{1,0:T(8,128)S(1)} %collective-permute-done.5, f32[64,113]{1,0:T(8,128)S(1)} %broadcast.102), dimensions={1} | concatenate | bytes 1179648 | tf_op jit(solution)/shard_map/concatenate | solution.py:234
  101.4 8.9 %shard_map.104 = (bf16[64,2048]{1,0:T(8,128)(2,1)}, bf16[2048,128]{1,0:T(8,128)(2,1)}, f32[2048,1]{1,0:T(8,128)}) custom-call(f32[64,2304]{1,0:T(8,128)} %concatenate.28.y_ref, f32[64,31]{1,0:T(8,128)} %bitcast.31, bf16[64,2048]{1,0:T(8,128)(2,1)} %get-tuple-element.14.att_ref, s32[1,2048]{1,0:T(1,128)} %get-tuple-element.59.lo_ref, ...), custom_call_target="tpu_custom_call" | custom-call | tf_op jit(solution)/shard_map/pallas_call | solution.py:303
  110.3 17.9 %shard_map.105 = (bf16[2048,64]{1,0:T(8,128)(2,1)}, f32[64,4096]{1,0:T(8,128)}, f32[64,4096]{1,0:T(8,128)}) custom-call(s32[4]{0:T(128)} %get-tuple-element.43.lo_ref, s32[4]{0:T(128)} %get-tuple-element.42.hi_ref, bf16[2048,128]{1,0:T(8,128)(2,1)} %concatenate.24.clone.q_ref, bf16[4096,128]{1,0:T(8,128)(2,1)} %copy.55.kv_ref, ...), custom_call_target="tpu_custom_call" | custom-call | tf_op jit(solution)/shard_map/pallas_call | solution.py:315
  128.2 1.4 constant_dynamic-update-slice_fusion.1
  129.6 0.1 copy-done
  129.8 0.1 convert.9
  130.0 7.0 %collective-permute-start.6 = (bf16[128,1024]{1,0:T(8,128)(2,1)S(1)}, bf16[128,1024]{1,0:T(8,128)(2,1)S(1)}, u32[]{:S(2)}, u32[]{:S(2)}) collective-permute-start(bf16[128,1024]{1,0:T(8,128)(2,1)S(1)} %get-tuple-element.44), channel_id=1, source_target_pairs={{0,1},{1,2},{2,3},{3,4},{4,5},{5,6},{6,7},{7,8},{8,9},{9,10},{10,1... | collective-permute-start | bytes 786440 | tf_op jit(solution)/shard_map/ppermute | solution.py:29
  137.0 1.9 %collective-permute-start.7 = (bf16[128,1024]{1,0:T(8,128)(2,1)S(1)}, bf16[128,1024]{1,0:T(8,128)(2,1)}, u32[]{:S(2)}, u32[]{:S(2)}) collective-permute-start(bf16[128,1024]{1,0:T(8,128)(2,1)S(1)} %get-tuple-element.45), channel_id=1, source_target_pairs={{1,0},{2,1},{3,2},{4,3},{5,4},{6,5},{7,6},{8,7},{9,8},{10,9},{11,1... | collective-permute-start | bytes 786440 | tf_op jit(solution)/shard_map/ppermute | solution.py:29
  138.9 0.9 copy.62
  139.8 0.5 collective-permute-done.6
  140.3 5.4 %collective-permute-done.7 = bf16[128,1024]{1,0:T(8,128)(2,1)} collective-permute-done((bf16[128,1024]{1,0:T(8,128)(2,1)S(1)}, bf16[128,1024]{1,0:T(8,128)(2,1)}, u32[]{:S(2)}, u32[]{:S(2)}) %collective-permute-start.7) | collective-permute-done | bytes 262176 | tf_op jit(solution)/shard_map/ppermute | solution.py:29
  145.7 1.1 fusion
  146.7 0.8 fusion.7
  (29 shorter events, 0.8 us)
Async XLA Ops:
  4.0 11.1 %copy-start.3 = (s32[64]{0:T(128)S(1)}, s32[64]{0:T(128)}, u32[]{:S(2)}) copy-start(s32[64]{0:T(128)} %param.10) | copy-start | bytes 772
  5.1 32.3 %all-to-all-start = ((bf16[128,16,192]{0,2,1:T(8,128)(2,1)}), bf16[128,16,192]{0,2,1:T(8,128)(2,1)S(1)}, u32[]{:S(2)}, u32[]{:S(2)}) async-start(bf16[128,16,192]{0,2,1:T(8,128)(2,1)} %bitcast.5), calls=%async_computation | async-start | bytes 1572864 | tf_op jit(solution)/shard_map/all_to_all | solution.py:246
  39.1 12.8 %collective-permute-start = (bf16[1024,128]{0,1:T(8,128)(2,1)S(1)}, bf16[1024,128]{0,1:T(8,128)(2,1)S(1)}, u32[]{:S(2)}, u32[]{:S(2)}) collective-permute-start(bf16[1024,128]{0,1:T(8,128)(2,1)S(1)} %get-tuple-element.54), channel_id=1, source_target_pairs={{0,1},{1,2},{2,3},{3,4},{4,5},{5,6},{6,7},{7,8},{8,9},{9,10},{10,1... | collective-permute-start | bytes 786440 | tf_op jit(solution)/shard_map/ppermute | solution.py:18
  46.0 8.6 %collective-permute-start.1 = (bf16[1024,128]{0,1:T(8,128)(2,1)S(1)}, bf16[1024,128]{0,1:T(8,128)(2,1)S(1)}, u32[]{:S(2)}, u32[]{:S(2)}) collective-permute-start(bf16[1024,128]{0,1:T(8,128)(2,1)S(1)} %get-tuple-element.55), channel_id=1, source_target_pairs={{1,0},{2,1},{3,2},{4,3},{5,4},{6,5},{7,6},{8,7},{9,8},{10,9},{11,1... | collective-permute-start | bytes 786440 | tf_op jit(solution)/shard_map/ppermute | solution.py:21
  54.7 24.6 %copy-start.2 = (f32[31,64]{1,0:T(8,128)S(1)}, f32[31,64]{1,0:T(8,128)}, u32[]{:S(2)}) copy-start(f32[31,64]{1,0:T(8,128)} %param.11) | copy-start | bytes 23812
  54.7 25.3 %copy-start.4 = (f32[64]{0:T(128)S(1)}, f32[64]{0:T(128)}, u32[]{:S(2)}) copy-start(f32[64]{0:T(128)} %param.12) | copy-start | bytes 772
  72.1 8.5 %collective-permute-start.3 = (bf16[64,15]{1,0:T(8,128)(2,1)S(1)}, bf16[64,15]{1,0:T(8,128)(2,1)S(1)}, u32[]{:S(2)}, u32[]{:S(2)}) collective-permute-start(bf16[64,15]{1,0:T(8,128)(2,1)S(1)} %get-tuple-element.56), channel_id=1, source_target_pairs={{1,0},{2,1},{3,2},{4,3},{5,4},{6,5},{7,6},{8,7},{9,8},{10,9},{11,1... | collective-permute-start | bytes 5768 | tf_op jit(solution)/shard_map/ppermute | solution.py:232
  74.1 6.6 %collective-permute-start.2 = (bf16[64,15]{1,0:T(8,128)(2,1)S(1)}, bf16[64,15]{1,0:T(8,128)(2,1)S(1)}, u32[]{:S(2)}, u32[]{:S(2)}) collective-permute-start(bf16[64,15]{1,0:T(8,128)(2,1)S(1)} %get-tuple-element.57), channel_id=1, source_target_pairs={{0,1},{1,2},{2,3},{3,4},{4,5},{5,6},{6,7},{7,8},{8,9},{9,10},{10,1... | collective-permute-start | bytes 5768 | tf_op jit(solution)/shard_map/ppermute | solution.py:231
  92.0 6.7 %collective-permute-start.5 = (f32[64,15]{1,0:T(8,128)S(1)}, f32[64,15]{1,0:T(8,128)S(1)}, u32[]{:S(2)}, u32[]{:S(2)}) collective-permute-start(f32[64,15]{1,0:T(8,128)S(1)} %get-tuple-element.52), channel_id=1, source_target_pairs={{1,0},{2,1},{3,2},{4,3},{5,4},{6,5},{7,6},{8,7},{9,8},{10,9},{11,1... | collective-permute-start | bytes 11528 | tf_op jit(solution)/shard_map/ppermute | solution.py:232
  93.9 5.6 %collective-permute-start.4 = (f32[64,15]{1,0:T(8,128)S(1)}, f32[64,15]{1,0:T(8,128)S(1)}, u32[]{:S(2)}, u32[]{:S(2)}) collective-permute-start(f32[64,15]{1,0:T(8,128)S(1)} %get-tuple-element.53), channel_id=1, source_target_pairs={{0,1},{1,2},{2,3},{3,4},{4,5},{5,6},{6,7},{7,8},{8,9},{9,10},{10,1... | collective-permute-start | bytes 11528 | tf_op jit(solution)/shard_map/ppermute | solution.py:231
  128.2 1.5 %copy-start = (f32[64,4096]{1,0:T(8,128)S(1)}, f32[64,4096]{1,0:T(8,128)}, u32[]{:S(2)}) copy-start(f32[64,4096]{1,0:T(8,128)} %get-tuple-element.23) | copy-start | bytes 3145732
  129.8 9.1 %copy-start.1 = (bf16[2048,64]{1,0:T(8,128)(2,1)S(1)}, bf16[2048,64]{1,0:T(8,128)(2,1)}, u32[]{:S(2)}) copy-start(bf16[2048,64]{1,0:T(8,128)(2,1)} %get-tuple-element.21) | copy-start | bytes 786436
  130.0 10.3 %collective-permute-start.6 = (bf16[128,1024]{1,0:T(8,128)(2,1)S(1)}, bf16[128,1024]{1,0:T(8,128)(2,1)S(1)}, u32[]{:S(2)}, u32[]{:S(2)}) collective-permute-start(bf16[128,1024]{1,0:T(8,128)(2,1)S(1)} %get-tuple-element.44), channel_id=1, source_target_pairs={{0,1},{1,2},{2,3},{3,4},{4,5},{5,6},{6,7},{7,8},{8,9},{9,10},{10,1... | collective-permute-start | bytes 786440 | tf_op jit(solution)/shard_map/ppermute | solution.py:29
  137.0 8.7 %collective-permute-start.7 = (bf16[128,1024]{1,0:T(8,128)(2,1)S(1)}, bf16[128,1024]{1,0:T(8,128)(2,1)}, u32[]{:S(2)}, u32[]{:S(2)}) collective-permute-start(bf16[128,1024]{1,0:T(8,128)(2,1)S(1)} %get-tuple-element.45), channel_id=1, source_target_pairs={{1,0},{2,1},{3,2},{4,3},{5,4},{6,5},{7,6},{8,7},{9,8},{10,9},{11,1... | collective-permute-start | bytes 786440 | tf_op jit(solution)/shard_map/ppermute | solution.py:29

commit v17 on v16

--- a/solution.py
+++ b/solution.py
@@ -167,7 +167,7 @@
 
 
 CONV_PAD = 128
-CONV_CHUNK = 1024
+CONV_CHUNK = 2048
 
 
 def conv_chunk(x_ref, wt_ref, lo, hi, c0, sign):

time: 148 us -> 147 us (level); the launches traced: 148 us -> 145 us
  starting transfers between devices: 40.8 us -> 38 us
    ppermute x2, starting transfers between devices: 8.89 us -> 6.11 us  [passed_along(): return lax.ppermute(block, axis, route)]
where the time goes in v17:
time: 147 us; the launch traced here: 145 us
  Pallas kernels  50.7 us (34%)
  starting transfers between devices  38 us (26%)
  waiting for transfers between devices  29.7 us (20%)
  local copies, waits for them, and re-layouts  20.9 us (14%)
  other arithmetic  4.53 us (3%)
    all_to_all x1, waiting for transfers between devices, on_device(): lax.all_to_all(stacked, 'uly', split_axis=1, concat_axis=0, tiled=True)  20.3 us
    pallas_call x1, Pallas kernels, on_device(): vmem_call(backward_kernel, 2, 9, (jax.ShapeDtypeStruct((block_rows, HEAD_...  17.9 us
    pallas_call x1, Pallas kernels, on_device(): vmem_call(forward_kernel, 2, 4, (jax.ShapeDtypeStruct((HEAD_DIM, block_ro...  15.3 us
    all_to_all x1, starting transfers between devices, on_device(): lax.all_to_all(stacked, 'uly', split_axis=1, concat_axis=0, tiled=True)  10 us
    ppermute x2, starting transfers between devices, padded_rims(): low = lax.ppermute(block[:, block.shape[1] - half:], 'blk', forward)  9.26 us
    pallas_call x1, Pallas kernels, on_device(): vmem_call(conv_forward_kernel, 0, 6, (jax.ShapeDtypeStruct((HEAD_DIM, blo...  8.86 us
    pallas_call x1, Pallas kernels, on_device(): vmem_call(conv_backward_kernel, 0, 5, (jax.ShapeDtypeStruct((HEAD_DIM, bl...  8.68 us
    ppermute x1, starting transfers between devices, extended(): lax.ppermute(lax.slice_in_dim(block, block.shape[dim] - width, None, axis...  6.87 us
  transfers between devices with their start and end apart: 9, of which 5 were waited for; matrix products, arithmetic and copies ran while one was open for 6% of the time, Pallas kernels for 0%

profile of v17, /device:TPU:9, one launch (start us, length us, event | category | flops | bytes accessed | tf_op | source)
XLA Modules:
  0.0 144.8 jit_solution(1185848846592304185)
XLA Ops:
  0.6 1.1 copy.49
  1.8 1.1 copy.50
  2.9 1.1 copy.51
  4.1 0.9 copy.52
  5.1 10.0 %all-to-all-start = ((bf16[128,16,192]{0,2,1:T(8,128)(2,1)}), bf16[128,16,192]{0,2,1:T(8,128)(2,1)S(1)}, u32[]{:S(2)}, u32[]{:S(2)}) async-start(bf16[128,16,192]{0,2,1:T(8,128)(2,1)} %bitcast.5), calls=%async_computation | async-start | bytes 1572864 | tf_op jit(solution)/shard_map/all_to_all | solution.py:246
  15.4 0.2 select_reduce_fusion
  15.7 0.5 slice.78
  16.2 0.2 convert_reduce_fusion
  16.5 0.6 and_select_fusion.kseg_ref
  17.1 20.3 %all-to-all-done = bf16[128,16,192]{0,2,1:T(8,128)(2,1)S(1)} async-done(((bf16[128,16,192]{0,2,1:T(8,128)(2,1)}), bf16[128,16,192]{0,2,1:T(8,128)(2,1)S(1)}, u32[]{:S(2)}, u32[]{:S(2)}) %all-to-all-start) | async-done | bytes 786464 | tf_op jit(solution)/shard_map/all_to_all | solution.py:246
  37.4 0.5 copy.53
  37.9 0.3 reshape.97
  38.3 0.8 slice_bitcast_fusion.2
  39.1 6.9 %collective-permute-start = (bf16[1024,128]{0,1:T(8,128)(2,1)S(1)}, bf16[1024,128]{0,1:T(8,128)(2,1)S(1)}, u32[]{:S(2)}, u32[]{:S(2)}) collective-permute-start(bf16[1024,128]{0,1:T(8,128)(2,1)S(1)} %get-tuple-element.54), channel_id=1, source_target_pairs={{0,1},{1,2},{2,3},{3,4},{4,5},{5,6},{6,7},{7,8},{8,9},{9,10},{10,1... | collective-permute-start | bytes 786440 | tf_op jit(solution)/shard_map/ppermute | solution.py:18
  46.0 1.9 %collective-permute-start.1 = (bf16[1024,128]{0,1:T(8,128)(2,1)S(1)}, bf16[1024,128]{0,1:T(8,128)(2,1)S(1)}, u32[]{:S(2)}, u32[]{:S(2)}) collective-permute-start(bf16[1024,128]{0,1:T(8,128)(2,1)S(1)} %get-tuple-element.55), channel_id=1, source_target_pairs={{1,0},{2,1},{3,2},{4,3},{5,4},{6,5},{7,6},{8,7},{9,8},{10,9},{11,1... | collective-permute-start | bytes 786440 | tf_op jit(solution)/shard_map/ppermute | solution.py:21
  47.9 0.7 broadcast_minimum_fusion
  48.8 1.4 copy.56.qseg_ref
  50.1 0.6 maximum_minimum_fusion
  50.7 0.3 copy.63
  51.0 0.9 concatenate.24.clone.q_ref
  51.9 2.7 %collective-permute-done.1 = bf16[1024,128]{0,1:T(8,128)(2,1)S(1)} collective-permute-done((bf16[1024,128]{0,1:T(8,128)(2,1)S(1)}, bf16[1024,128]{0,1:T(8,128)(2,1)S(1)}, u32[]{:S(2)}, u32[]{:S(2)}) %collective-permute-start.1) | collective-permute-done | bytes 262176 | tf_op jit(solution)/shard_map/ppermute | solution.py:21
  54.7 1.3 copy.55.kv_ref
  56.0 15.3 %shard_map.102 = (bf16[64,2048]{1,0:T(8,128)(2,1)}, f32[2048,1]{1,0:T(8,128)}) custom-call(s32[4]{0:T(128)} %get-tuple-element.43.lo_ref, s32[4]{0:T(128)} %get-tuple-element.42.hi_ref, bf16[2048,128]{1,0:T(8,128)(2,1)} %concatenate.24.clone.q_ref, bf16[4096,128]{1,0:T(8,128)(2,1)} %copy.55.kv_ref, s32[2048,1]{1,0:T(8,128)} %copy.56.qseg_ref, ...), custom_call_target="tpu_custom_call" | custom-call | tf_op jit(solution)/shard_map/pallas_call | solution.py:280
  71.3 0.8 fusion.9
  72.1 1.9 %collective-permute-start.3 = (bf16[64,15]{1,0:T(8,128)(2,1)S(1)}, bf16[64,15]{1,0:T(8,128)(2,1)S(1)}, u32[]{:S(2)}, u32[]{:S(2)}) collective-permute-start(bf16[64,15]{1,0:T(8,128)(2,1)S(1)} %get-tuple-element.56), channel_id=1, source_target_pairs={{1,0},{2,1},{3,2},{4,3},{5,4},{6,5},{7,6},{8,7},{9,8},{10,9},{11,1... | collective-permute-start | bytes 5768 | tf_op jit(solution)/shard_map/ppermute | solution.py:232
  74.1 4.5 %collective-permute-start.2 = (bf16[64,15]{1,0:T(8,128)(2,1)S(1)}, bf16[64,15]{1,0:T(8,128)(2,1)S(1)}, u32[]{:S(2)}, u32[]{:S(2)}) collective-permute-start(bf16[64,15]{1,0:T(8,128)(2,1)S(1)} %get-tuple-element.57), channel_id=1, source_target_pairs={{0,1},{1,2},{2,3},{3,4},{4,5},{5,6},{6,7},{7,8},{8,9},{9,10},{10,1... | collective-permute-start | bytes 5768 | tf_op jit(solution)/shard_map/ppermute | solution.py:231
  78.6 0.6 fusion.2
  79.2 0.7 copy.57
  79.9 0.7 copy.58.gain_ref
  80.7 1.8 %concatenate.27.x_ref = f32[64,2304]{1,0:T(8,128)} concatenate(f32[64,113]{1,0:T(8,128)S(1)} %broadcast.102, bf16[64,15]{1,0:T(8,128)(2,1)S(1)} %collective-permute-done.2, bf16[64,2048]{1,0:T(8,128)(2,1)} %get-tuple-element.14.att_ref, bf16[64,15]{1,0:T(8,128)(2,1)S(1)} %collective-permute-done.3, f32[64,113]{1,0:T(8,128)S(1)} %broadcast.102), dimensions={1} | concatenate | bytes 913664 | tf_op jit(solution)/shard_map/concatenate | solution.py:234
  82.5 8.9 %shard_map.103 = (bf16[64,2048]{1,0:T(8,128)(2,1)}, f32[64,2048]{1,0:T(8,128)}) custom-call(f32[64,2304]{1,0:T(8,128)} %concatenate.27.x_ref, f32[64,31]{1,0:T(8,128)} %bitcast.30, f32[64,1]{1,0:T(8,128)} %copy.58.gain_ref, bf16[64,2048]{1,0:T(8,128)(2,1)} %cot_ref.1, s32[1,2048]{1,0:T(1,128)} %get-tuple-element.59.lo_ref, s32[1,2048]{1,0:T(1,128)} %get-tuple-element.58.hi_ref), custom_call_target="tpu_custom_call" | custom-call | tf_op jit(solution)/shard_map/pallas_call | solution.py:294
  91.4 0.8 fusion.8
  92.2 1.9 %collective-permute-start.5 = (f32[64,15]{1,0:T(8,128)S(1)}, f32[64,15]{1,0:T(8,128)S(1)}, u32[]{:S(2)}, u32[]{:S(2)}) collective-permute-start(f32[64,15]{1,0:T(8,128)S(1)} %get-tuple-element.52), channel_id=1, source_target_pairs={{1,0},{2,1},{3,2},{4,3},{5,4},{6,5},{7,6},{8,7},{9,8},{10,9},{11,1... | collective-permute-start | bytes 11528 | tf_op jit(solution)/shard_map/ppermute | solution.py:232
  94.1 4.7 %collective-permute-start.4 = (f32[64,15]{1,0:T(8,128)S(1)}, f32[64,15]{1,0:T(8,128)S(1)}, u32[]{:S(2)}, u32[]{:S(2)}) collective-permute-start(f32[64,15]{1,0:T(8,128)S(1)} %get-tuple-element.53), channel_id=1, source_target_pairs={{0,1},{1,2},{2,3},{3,4},{4,5},{5,6},{6,7},{7,8},{8,9},{9,10},{10,1... | collective-permute-start | bytes 11528 | tf_op jit(solution)/shard_map/ppermute | solution.py:231
  98.9 0.8 collective-permute-done.4
  99.7 1.9 %concatenate.28.y_ref = f32[64,2304]{1,0:T(8,128)} concatenate(f32[64,113]{1,0:T(8,128)S(1)} %broadcast.102, f32[64,15]{1,0:T(8,128)S(1)} %collective-permute-done.4, f32[64,2048]{1,0:T(8,128)} %get-tuple-element.16, f32[64,15]{1,0:T(8,128)S(1)} %collective-permute-done.5, f32[64,113]{1,0:T(8,128)S(1)} %broadcast.102), dimensions={1} | concatenate | bytes 1179648 | tf_op jit(solution)/shard_map/concatenate | solution.py:234
  101.6 8.7 %shard_map.104 = (bf16[64,2048]{1,0:T(8,128)(2,1)}, bf16[2048,128]{1,0:T(8,128)(2,1)}, f32[2048,1]{1,0:T(8,128)}) custom-call(f32[64,2304]{1,0:T(8,128)} %concatenate.28.y_ref, f32[64,31]{1,0:T(8,128)} %bitcast.31, bf16[64,2048]{1,0:T(8,128)(2,1)} %get-tuple-element.14.att_ref, s32[1,2048]{1,0:T(1,128)} %get-tuple-element.59.lo_ref, ...), custom_call_target="tpu_custom_call" | custom-call | tf_op jit(solution)/shard_map/pallas_call | solution.py:303
  110.3 17.9 %shard_map.105 = (bf16[2048,64]{1,0:T(8,128)(2,1)}, f32[64,4096]{1,0:T(8,128)}, f32[64,4096]{1,0:T(8,128)}) custom-call(s32[4]{0:T(128)} %get-tuple-element.43.lo_ref, s32[4]{0:T(128)} %get-tuple-element.42.hi_ref, bf16[2048,128]{1,0:T(8,128)(2,1)} %concatenate.24.clone.q_ref, bf16[4096,128]{1,0:T(8,128)(2,1)} %copy.55.kv_ref, ...), custom_call_target="tpu_custom_call" | custom-call | tf_op jit(solution)/shard_map/pallas_call | solution.py:315
  128.2 1.4 constant_dynamic-update-slice_fusion.1
  129.6 0.1 copy-done
  129.8 0.1 convert.9
  130.0 4.2 %collective-permute-start.6 = (bf16[128,1024]{1,0:T(8,128)(2,1)S(1)}, bf16[128,1024]{1,0:T(8,128)(2,1)S(1)}, u32[]{:S(2)}, u32[]{:S(2)}) collective-permute-start(bf16[128,1024]{1,0:T(8,128)(2,1)S(1)} %get-tuple-element.44), channel_id=1, source_target_pairs={{0,1},{1,2},{2,3},{3,4},{4,5},{5,6},{6,7},{7,8},{8,9},{9,10},{10,1... | collective-permute-start | bytes 786440 | tf_op jit(solution)/shard_map/ppermute | solution.py:29
  134.2 1.9 %collective-permute-start.7 = (bf16[128,1024]{1,0:T(8,128)(2,1)S(1)}, bf16[128,1024]{1,0:T(8,128)(2,1)}, u32[]{:S(2)}, u32[]{:S(2)}) collective-permute-start(bf16[128,1024]{1,0:T(8,128)(2,1)S(1)} %get-tuple-element.45), channel_id=1, source_target_pairs={{1,0},{2,1},{3,2},{4,3},{5,4},{6,5},{7,6},{8,7},{9,8},{10,9},{11,1... | collective-permute-start | bytes 786440 | tf_op jit(solution)/shard_map/ppermute | solution.py:29
  136.1 0.9 copy.62
  137.0 0.5 collective-permute-done.6
  137.5 5.4 %collective-permute-done.7 = bf16[128,1024]{1,0:T(8,128)(2,1)} collective-permute-done((bf16[128,1024]{1,0:T(8,128)(2,1)S(1)}, bf16[128,1024]{1,0:T(8,128)(2,1)}, u32[]{:S(2)}, u32[]{:S(2)}) %collective-permute-start.7) | collective-permute-done | bytes 262176 | tf_op jit(solution)/shard_map/ppermute | solution.py:29
  142.9 1.1 fusion
  144.0 0.8 fusion.7
  (29 shorter events, 0.8 us)
Async XLA Ops:
  4.0 11.1 %copy-start.3 = (s32[64]{0:T(128)S(1)}, s32[64]{0:T(128)}, u32[]{:S(2)}) copy-start(s32[64]{0:T(128)} %param.10) | copy-start | bytes 772
  5.1 32.3 %all-to-all-start = ((bf16[128,16,192]{0,2,1:T(8,128)(2,1)}), bf16[128,16,192]{0,2,1:T(8,128)(2,1)S(1)}, u32[]{:S(2)}, u32[]{:S(2)}) async-start(bf16[128,16,192]{0,2,1:T(8,128)(2,1)} %bitcast.5), calls=%async_computation | async-start | bytes 1572864 | tf_op jit(solution)/shard_map/all_to_all | solution.py:246
  39.1 12.8 %collective-permute-start = (bf16[1024,128]{0,1:T(8,128)(2,1)S(1)}, bf16[1024,128]{0,1:T(8,128)(2,1)S(1)}, u32[]{:S(2)}, u32[]{:S(2)}) collective-permute-start(bf16[1024,128]{0,1:T(8,128)(2,1)S(1)} %get-tuple-element.54), channel_id=1, source_target_pairs={{0,1},{1,2},{2,3},{3,4},{4,5},{5,6},{6,7},{7,8},{8,9},{9,10},{10,1... | collective-permute-start | bytes 786440 | tf_op jit(solution)/shard_map/ppermute | solution.py:18
  46.0 8.6 %collective-permute-start.1 = (bf16[1024,128]{0,1:T(8,128)(2,1)S(1)}, bf16[1024,128]{0,1:T(8,128)(2,1)S(1)}, u32[]{:S(2)}, u32[]{:S(2)}) collective-permute-start(bf16[1024,128]{0,1:T(8,128)(2,1)S(1)} %get-tuple-element.55), channel_id=1, source_target_pairs={{1,0},{2,1},{3,2},{4,3},{5,4},{6,5},{7,6},{8,7},{9,8},{10,9},{11,1... | collective-permute-start | bytes 786440 | tf_op jit(solution)/shard_map/ppermute | solution.py:21
  54.7 24.6 %copy-start.2 = (f32[31,64]{1,0:T(8,128)S(1)}, f32[31,64]{1,0:T(8,128)}, u32[]{:S(2)}) copy-start(f32[31,64]{1,0:T(8,128)} %param.11) | copy-start | bytes 23812
  54.7 25.3 %copy-start.4 = (f32[64]{0:T(128)S(1)}, f32[64]{0:T(128)}, u32[]{:S(2)}) copy-start(f32[64]{0:T(128)} %param.12) | copy-start | bytes 772
  72.1 8.5 %collective-permute-start.3 = (bf16[64,15]{1,0:T(8,128)(2,1)S(1)}, bf16[64,15]{1,0:T(8,128)(2,1)S(1)}, u32[]{:S(2)}, u32[]{:S(2)}) collective-permute-start(bf16[64,15]{1,0:T(8,128)(2,1)S(1)} %get-tuple-element.56), channel_id=1, source_target_pairs={{1,0},{2,1},{3,2},{4,3},{5,4},{6,5},{7,6},{8,7},{9,8},{10,9},{11,1... | collective-permute-start | bytes 5768 | tf_op jit(solution)/shard_map/ppermute | solution.py:232
  74.1 6.6 %collective-permute-start.2 = (bf16[64,15]{1,0:T(8,128)(2,1)S(1)}, bf16[64,15]{1,0:T(8,128)(2,1)S(1)}, u32[]{:S(2)}, u32[]{:S(2)}) collective-permute-start(bf16[64,15]{1,0:T(8,128)(2,1)S(1)} %get-tuple-element.57), channel_id=1, source_target_pairs={{0,1},{1,2},{2,3},{3,4},{4,5},{5,6},{6,7},{7,8},{8,9},{9,10},{10,1... | collective-permute-start | bytes 5768 | tf_op jit(solution)/shard_map/ppermute | solution.py:231
  92.2 6.7 %collective-permute-start.5 = (f32[64,15]{1,0:T(8,128)S(1)}, f32[64,15]{1,0:T(8,128)S(1)}, u32[]{:S(2)}, u32[]{:S(2)}) collective-permute-start(f32[64,15]{1,0:T(8,128)S(1)} %get-tuple-element.52), channel_id=1, source_target_pairs={{1,0},{2,1},{3,2},{4,3},{5,4},{6,5},{7,6},{8,7},{9,8},{10,9},{11,1... | collective-permute-start | bytes 11528 | tf_op jit(solution)/shard_map/ppermute | solution.py:232
  94.1 5.6 %collective-permute-start.4 = (f32[64,15]{1,0:T(8,128)S(1)}, f32[64,15]{1,0:T(8,128)S(1)}, u32[]{:S(2)}, u32[]{:S(2)}) collective-permute-start(f32[64,15]{1,0:T(8,128)S(1)} %get-tuple-element.53), channel_id=1, source_target_pairs={{0,1},{1,2},{2,3},{3,4},{4,5},{5,6},{6,7},{7,8},{8,9},{9,10},{10,1... | collective-permute-start | bytes 11528 | tf_op jit(solution)/shard_map/ppermute | solution.py:231
  128.2 1.5 %copy-start = (f32[64,4096]{1,0:T(8,128)S(1)}, f32[64,4096]{1,0:T(8,128)}, u32[]{:S(2)}) copy-start(f32[64,4096]{1,0:T(8,128)} %get-tuple-element.23) | copy-start | bytes 3145732
  129.8 6.3 %copy-start.1 = (bf16[2048,64]{1,0:T(8,128)(2,1)S(1)}, bf16[2048,64]{1,0:T(8,128)(2,1)}, u32[]{:S(2)}) copy-start(bf16[2048,64]{1,0:T(8,128)(2,1)} %get-tuple-element.21) | copy-start | bytes 786436
  130.0 7.5 %collective-permute-start.6 = (bf16[128,1024]{1,0:T(8,128)(2,1)S(1)}, bf16[128,1024]{1,0:T(8,128)(2,1)S(1)}, u32[]{:S(2)}, u32[]{:S(2)}) collective-permute-start(bf16[128,1024]{1,0:T(8,128)(2,1)S(1)} %get-tuple-element.44), channel_id=1, source_target_pairs={{0,1},{1,2},{2,3},{3,4},{4,5},{5,6},{6,7},{7,8},{8,9},{9,10},{10,1... | collective-permute-start | bytes 786440 | tf_op jit(solution)/shard_map/ppermute | solution.py:29
  134.2 8.7 %collective-permute-start.7 = (bf16[128,1024]{1,0:T(8,128)(2,1)S(1)}, bf16[128,1024]{1,0:T(8,128)(2,1)}, u32[]{:S(2)}, u32[]{:S(2)}) collective-permute-start(bf16[128,1024]{1,0:T(8,128)(2,1)S(1)} %get-tuple-element.45), channel_id=1, source_target_pairs={{1,0},{2,1},{3,2},{4,3},{5,4},{6,5},{7,6},{8,7},{9,8},{10,9},{11,1... | collective-permute-start | bytes 786440 | tf_op jit(solution)/shard_map/ppermute | solution.py:29

commit v18 on v17

--- a/solution.py
+++ b/solution.py
@@ -192,7 +192,8 @@
         cols = pl.ds(c0, CONV_CHUNK)
         conv_sum = conv_chunk(x_ref, wt_ref, lo_ref[:, cols], hi_ref[:, cols], c0, 1)
         spread = jnp.sqrt(jnp.mean(conv_sum * conv_sum, axis=0, keepdims=True) + 1e-05)
-        normed = conv_sum / spread
+        inv_spread = 1.0 / spread
+        normed = conv_sum * inv_spread
         pre_act = normed * gain
         gate = 1.0 / (1.0 + jnp.exp(-pre_act))
         out_ref[:, cols] = (pre_act * gate).astype(out_ref.dtype)
@@ -200,7 +201,7 @@
         weighted = grad_pre * gain
         gc_ref[:, cols] = (
             weighted - normed * jnp.mean(weighted * normed, axis=0, keepdims=True)
-        ) / spread
+        ) * inv_spread
         return carry
 
     lax.fori_loop(0, out_ref.shape[1] // CONV_CHUNK, body, 0)

time: 147 us -> 148 us (level); the launches traced: 145 us -> 148 us
  starting transfers between devices: 38 us -> 40.8 us
    ppermute x2, starting transfers between devices: 6.11 us -> 8.89 us  [passed_along(): return lax.ppermute(block, axis, route)]
where the time goes in v18:
time: 148 us
  Pallas kernels  50.7 us (34%)
  starting transfers between devices  40.8 us (28%)
  waiting for transfers between devices  29.7 us (20%)
  local copies, waits for them, and re-layouts  20.9 us (14%)
  other arithmetic  4.53 us (3%)
    all_to_all x1, waiting for transfers between devices, on_device(): lax.all_to_all(stacked, 'uly', split_axis=1, concat_axis=0, tiled=True)  20.3 us
    pallas_call x1, Pallas kernels, on_device(): vmem_call(backward_kernel, 2, 9, (jax.ShapeDtypeStruct((block_rows, HEAD_...  17.9 us
    pallas_call x1, Pallas kernels, on_device(): vmem_call(forward_kernel, 2, 4, (jax.ShapeDtypeStruct((HEAD_DIM, block_ro...  15.3 us
    all_to_all x1, starting transfers between devices, on_device(): lax.all_to_all(stacked, 'uly', split_axis=1, concat_axis=0, tiled=True)  10 us
    ppermute x2, starting transfers between devices, padded_rims(): low = lax.ppermute(block[:, block.shape[1] - half:], 'blk', forward)  9.26 us
    ppermute x2, starting transfers between devices, passed_along(): return lax.ppermute(block, axis, route)  8.89 us
    pallas_call x1, Pallas kernels, on_device(): vmem_call(conv_forward_kernel, 0, 6, (jax.ShapeDtypeStruct((HEAD_DIM, blo...  8.86 us
    pallas_call x1, Pallas kernels, on_device(): vmem_call(conv_backward_kernel, 0, 5, (jax.ShapeDtypeStruct((HEAD_DIM, bl...  8.68 us
  transfers between devices with their start and end apart: 9, of which 5 were waited for; matrix products, arithmetic and copies ran while one was open for 6% of the time, Pallas kernels for 0%

profile of v18, /device:TPU:9, one launch (start us, length us, event | category | flops | bytes accessed | tf_op | source)
XLA Modules:
  0.0 147.5 jit_solution(1185848846592304185)
XLA Ops:
  0.6 1.1 copy.49
  1.8 1.1 copy.50
  2.9 1.1 copy.51
  4.1 0.9 copy.52
  5.1 10.0 %all-to-all-start = ((bf16[128,16,192]{0,2,1:T(8,128)(2,1)}), bf16[128,16,192]{0,2,1:T(8,128)(2,1)S(1)}, u32[]{:S(2)}, u32[]{:S(2)}) async-start(bf16[128,16,192]{0,2,1:T(8,128)(2,1)} %bitcast.5), calls=%async_computation | async-start | bytes 1572864 | tf_op jit(solution)/shard_map/all_to_all | solution.py:247
  15.4 0.2 select_reduce_fusion
  15.7 0.5 slice.78
  16.2 0.2 convert_reduce_fusion
  16.5 0.6 and_select_fusion.kseg_ref
  17.1 20.3 %all-to-all-done = bf16[128,16,192]{0,2,1:T(8,128)(2,1)S(1)} async-done(((bf16[128,16,192]{0,2,1:T(8,128)(2,1)}), bf16[128,16,192]{0,2,1:T(8,128)(2,1)S(1)}, u32[]{:S(2)}, u32[]{:S(2)}) %all-to-all-start) | async-done | bytes 786464 | tf_op jit(solution)/shard_map/all_to_all | solution.py:247
  37.4 0.5 copy.53
  37.9 0.3 reshape.97
  38.3 0.8 slice_bitcast_fusion.2
  39.1 6.9 %collective-permute-start = (bf16[1024,128]{0,1:T(8,128)(2,1)S(1)}, bf16[1024,128]{0,1:T(8,128)(2,1)S(1)}, u32[]{:S(2)}, u32[]{:S(2)}) collective-permute-start(bf16[1024,128]{0,1:T(8,128)(2,1)S(1)} %get-tuple-element.54), channel_id=1, source_target_pairs={{0,1},{1,2},{2,3},{3,4},{4,5},{5,6},{6,7},{7,8},{8,9},{9,10},{10,1... | collective-permute-start | bytes 786440 | tf_op jit(solution)/shard_map/ppermute | solution.py:18
  46.0 1.9 %collective-permute-start.1 = (bf16[1024,128]{0,1:T(8,128)(2,1)S(1)}, bf16[1024,128]{0,1:T(8,128)(2,1)S(1)}, u32[]{:S(2)}, u32[]{:S(2)}) collective-permute-start(bf16[1024,128]{0,1:T(8,128)(2,1)S(1)} %get-tuple-element.55), channel_id=1, source_target_pairs={{1,0},{2,1},{3,2},{4,3},{5,4},{6,5},{7,6},{8,7},{9,8},{10,9},{11,1... | collective-permute-start | bytes 786440 | tf_op jit(solution)/shard_map/ppermute | solution.py:21
  47.9 0.7 broadcast_minimum_fusion
  48.8 1.4 copy.56.qseg_ref
  50.1 0.6 maximum_minimum_fusion
  50.7 0.3 copy.63
  51.0 0.9 concatenate.24.clone.q_ref
  51.9 2.7 %collective-permute-done.1 = bf16[1024,128]{0,1:T(8,128)(2,1)S(1)} collective-permute-done((bf16[1024,128]{0,1:T(8,128)(2,1)S(1)}, bf16[1024,128]{0,1:T(8,128)(2,1)S(1)}, u32[]{:S(2)}, u32[]{:S(2)}) %collective-permute-start.1) | collective-permute-done | bytes 262176 | tf_op jit(solution)/shard_map/ppermute | solution.py:21
  54.7 1.3 copy.55.kv_ref
  56.0 15.3 %shard_map.102 = (bf16[64,2048]{1,0:T(8,128)(2,1)}, f32[2048,1]{1,0:T(8,128)}) custom-call(s32[4]{0:T(128)} %get-tuple-element.43.lo_ref, s32[4]{0:T(128)} %get-tuple-element.42.hi_ref, bf16[2048,128]{1,0:T(8,128)(2,1)} %concatenate.24.clone.q_ref, bf16[4096,128]{1,0:T(8,128)(2,1)} %copy.55.kv_ref, s32[2048,1]{1,0:T(8,128)} %copy.56.qseg_ref, ...), custom_call_target="tpu_custom_call" | custom-call | tf_op jit(solution)/shard_map/pallas_call | solution.py:281
  71.3 0.8 fusion.9
  72.1 1.9 %collective-permute-start.3 = (bf16[64,15]{1,0:T(8,128)(2,1)S(1)}, bf16[64,15]{1,0:T(8,128)(2,1)S(1)}, u32[]{:S(2)}, u32[]{:S(2)}) collective-permute-start(bf16[64,15]{1,0:T(8,128)(2,1)S(1)} %get-tuple-element.56), channel_id=1, source_target_pairs={{1,0},{2,1},{3,2},{4,3},{5,4},{6,5},{7,6},{8,7},{9,8},{10,9},{11,1... | collective-permute-start | bytes 5768 | tf_op jit(solution)/shard_map/ppermute | solution.py:233
  74.1 4.5 %collective-permute-start.2 = (bf16[64,15]{1,0:T(8,128)(2,1)S(1)}, bf16[64,15]{1,0:T(8,128)(2,1)S(1)}, u32[]{:S(2)}, u32[]{:S(2)}) collective-permute-start(bf16[64,15]{1,0:T(8,128)(2,1)S(1)} %get-tuple-element.57), channel_id=1, source_target_pairs={{0,1},{1,2},{2,3},{3,4},{4,5},{5,6},{6,7},{7,8},{8,9},{9,10},{10,1... | collective-permute-start | bytes 5768 | tf_op jit(solution)/shard_map/ppermute | solution.py:232
  78.6 0.6 fusion.2
  79.2 0.7 copy.57
  79.9 0.7 copy.58.gain_ref
  80.7 1.8 %concatenate.27.x_ref = f32[64,2304]{1,0:T(8,128)} concatenate(f32[64,113]{1,0:T(8,128)S(1)} %broadcast.102, bf16[64,15]{1,0:T(8,128)(2,1)S(1)} %collective-permute-done.2, bf16[64,2048]{1,0:T(8,128)(2,1)} %get-tuple-element.14.att_ref, bf16[64,15]{1,0:T(8,128)(2,1)S(1)} %collective-permute-done.3, f32[64,113]{1,0:T(8,128)S(1)} %broadcast.102), dimensions={1} | concatenate | bytes 913664 | tf_op jit(solution)/shard_map/concatenate | solution.py:235
  82.5 8.9 %shard_map.103 = (bf16[64,2048]{1,0:T(8,128)(2,1)}, f32[64,2048]{1,0:T(8,128)}) custom-call(f32[64,2304]{1,0:T(8,128)} %concatenate.27.x_ref, f32[64,31]{1,0:T(8,128)} %bitcast.30, f32[64,1]{1,0:T(8,128)} %copy.58.gain_ref, bf16[64,2048]{1,0:T(8,128)(2,1)} %cot_ref.1, s32[1,2048]{1,0:T(1,128)} %get-tuple-element.59.lo_ref, s32[1,2048]{1,0:T(1,128)} %get-tuple-element.58.hi_ref), custom_call_target="tpu_custom_call" | custom-call | tf_op jit(solution)/shard_map/pallas_call | solution.py:295
  91.4 0.8 fusion.8
  92.2 1.9 %collective-permute-start.5 = (f32[64,15]{1,0:T(8,128)S(1)}, f32[64,15]{1,0:T(8,128)S(1)}, u32[]{:S(2)}, u32[]{:S(2)}) collective-permute-start(f32[64,15]{1,0:T(8,128)S(1)} %get-tuple-element.52), channel_id=1, source_target_pairs={{1,0},{2,1},{3,2},{4,3},{5,4},{6,5},{7,6},{8,7},{9,8},{10,9},{11,1... | collective-permute-start | bytes 11528 | tf_op jit(solution)/shard_map/ppermute | solution.py:233
  94.1 4.7 %collective-permute-start.4 = (f32[64,15]{1,0:T(8,128)S(1)}, f32[64,15]{1,0:T(8,128)S(1)}, u32[]{:S(2)}, u32[]{:S(2)}) collective-permute-start(f32[64,15]{1,0:T(8,128)S(1)} %get-tuple-element.53), channel_id=1, source_target_pairs={{0,1},{1,2},{2,3},{3,4},{4,5},{5,6},{6,7},{7,8},{8,9},{9,10},{10,1... | collective-permute-start | bytes 11528 | tf_op jit(solution)/shard_map/ppermute | solution.py:232
  98.9 0.8 collective-permute-done.4
  99.7 1.9 %concatenate.28.y_ref = f32[64,2304]{1,0:T(8,128)} concatenate(f32[64,113]{1,0:T(8,128)S(1)} %broadcast.102, f32[64,15]{1,0:T(8,128)S(1)} %collective-permute-done.4, f32[64,2048]{1,0:T(8,128)} %get-tuple-element.16, f32[64,15]{1,0:T(8,128)S(1)} %collective-permute-done.5, f32[64,113]{1,0:T(8,128)S(1)} %broadcast.102), dimensions={1} | concatenate | bytes 1179648 | tf_op jit(solution)/shard_map/concatenate | solution.py:235
  101.6 8.7 %shard_map.104 = (bf16[64,2048]{1,0:T(8,128)(2,1)}, bf16[2048,128]{1,0:T(8,128)(2,1)}, f32[2048,1]{1,0:T(8,128)}) custom-call(f32[64,2304]{1,0:T(8,128)} %concatenate.28.y_ref, f32[64,31]{1,0:T(8,128)} %bitcast.31, bf16[64,2048]{1,0:T(8,128)(2,1)} %get-tuple-element.14.att_ref, s32[1,2048]{1,0:T(1,128)} %get-tuple-element.59.lo_ref, ...), custom_call_target="tpu_custom_call" | custom-call | tf_op jit(solution)/shard_map/pallas_call | solution.py:304
  110.3 17.9 %shard_map.105 = (bf16[2048,64]{1,0:T(8,128)(2,1)}, f32[64,4096]{1,0:T(8,128)}, f32[64,4096]{1,0:T(8,128)}) custom-call(s32[4]{0:T(128)} %get-tuple-element.43.lo_ref, s32[4]{0:T(128)} %get-tuple-element.42.hi_ref, bf16[2048,128]{1,0:T(8,128)(2,1)} %concatenate.24.clone.q_ref, bf16[4096,128]{1,0:T(8,128)(2,1)} %copy.55.kv_ref, ...), custom_call_target="tpu_custom_call" | custom-call | tf_op jit(solution)/shard_map/pallas_call | solution.py:316
  128.2 1.4 constant_dynamic-update-slice_fusion.1
  129.6 0.1 copy-done
  129.8 0.1 convert.9
  130.0 7.0 %collective-permute-start.6 = (bf16[128,1024]{1,0:T(8,128)(2,1)S(1)}, bf16[128,1024]{1,0:T(8,128)(2,1)S(1)}, u32[]{:S(2)}, u32[]{:S(2)}) collective-permute-start(bf16[128,1024]{1,0:T(8,128)(2,1)S(1)} %get-tuple-element.44), channel_id=1, source_target_pairs={{0,1},{1,2},{2,3},{3,4},{4,5},{5,6},{6,7},{7,8},{8,9},{9,10},{10,1... | collective-permute-start | bytes 786440 | tf_op jit(solution)/shard_map/ppermute | solution.py:29
  137.0 1.9 %collective-permute-start.7 = (bf16[128,1024]{1,0:T(8,128)(2,1)S(1)}, bf16[128,1024]{1,0:T(8,128)(2,1)}, u32[]{:S(2)}, u32[]{:S(2)}) collective-permute-start(bf16[128,1024]{1,0:T(8,128)(2,1)S(1)} %get-tuple-element.45), channel_id=1, source_target_pairs={{1,0},{2,1},{3,2},{4,3},{5,4},{6,5},{7,6},{8,7},{9,8},{10,9},{11,1... | collective-permute-start | bytes 786440 | tf_op jit(solution)/shard_map/ppermute | solution.py:29
  138.9 0.9 copy.62
  139.8 0.5 collective-permute-done.6
  140.3 5.4 %collective-permute-done.7 = bf16[128,1024]{1,0:T(8,128)(2,1)} collective-permute-done((bf16[128,1024]{1,0:T(8,128)(2,1)S(1)}, bf16[128,1024]{1,0:T(8,128)(2,1)}, u32[]{:S(2)}, u32[]{:S(2)}) %collective-permute-start.7) | collective-permute-done | bytes 262176 | tf_op jit(solution)/shard_map/ppermute | solution.py:29
  145.7 1.1 fusion
  146.7 0.8 fusion.7
  (29 shorter events, 0.8 us)
Async XLA Ops:
  4.0 11.1 %copy-start.3 = (s32[64]{0:T(128)S(1)}, s32[64]{0:T(128)}, u32[]{:S(2)}) copy-start(s32[64]{0:T(128)} %param.10) | copy-start | bytes 772
  5.1 32.3 %all-to-all-start = ((bf16[128,16,192]{0,2,1:T(8,128)(2,1)}), bf16[128,16,192]{0,2,1:T(8,128)(2,1)S(1)}, u32[]{:S(2)}, u32[]{:S(2)}) async-start(bf16[128,16,192]{0,2,1:T(8,128)(2,1)} %bitcast.5), calls=%async_computation | async-start | bytes 1572864 | tf_op jit(solution)/shard_map/all_to_all | solution.py:247
  39.1 12.8 %collective-permute-start = (bf16[1024,128]{0,1:T(8,128)(2,1)S(1)}, bf16[1024,128]{0,1:T(8,128)(2,1)S(1)}, u32[]{:S(2)}, u32[]{:S(2)}) collective-permute-start(bf16[1024,128]{0,1:T(8,128)(2,1)S(1)} %get-tuple-element.54), channel_id=1, source_target_pairs={{0,1},{1,2},{2,3},{3,4},{4,5},{5,6},{6,7},{7,8},{8,9},{9,10},{10,1... | collective-permute-start | bytes 786440 | tf_op jit(solution)/shard_map/ppermute | solution.py:18
  46.0 8.6 %collective-permute-start.1 = (bf16[1024,128]{0,1:T(8,128)(2,1)S(1)}, bf16[1024,128]{0,1:T(8,128)(2,1)S(1)}, u32[]{:S(2)}, u32[]{:S(2)}) collective-permute-start(bf16[1024,128]{0,1:T(8,128)(2,1)S(1)} %get-tuple-element.55), channel_id=1, source_target_pairs={{1,0},{2,1},{3,2},{4,3},{5,4},{6,5},{7,6},{8,7},{9,8},{10,9},{11,1... | collective-permute-start | bytes 786440 | tf_op jit(solution)/shard_map/ppermute | solution.py:21
  54.7 24.6 %copy-start.2 = (f32[31,64]{1,0:T(8,128)S(1)}, f32[31,64]{1,0:T(8,128)}, u32[]{:S(2)}) copy-start(f32[31,64]{1,0:T(8,128)} %param.11) | copy-start | bytes 23812
  54.7 25.3 %copy-start.4 = (f32[64]{0:T(128)S(1)}, f32[64]{0:T(128)}, u32[]{:S(2)}) copy-start(f32[64]{0:T(128)} %param.12) | copy-start | bytes 772
  72.1 8.5 %collective-permute-start.3 = (bf16[64,15]{1,0:T(8,128)(2,1)S(1)}, bf16[64,15]{1,0:T(8,128)(2,1)S(1)}, u32[]{:S(2)}, u32[]{:S(2)}) collective-permute-start(bf16[64,15]{1,0:T(8,128)(2,1)S(1)} %get-tuple-element.56), channel_id=1, source_target_pairs={{1,0},{2,1},{3,2},{4,3},{5,4},{6,5},{7,6},{8,7},{9,8},{10,9},{11,1... | collective-permute-start | bytes 5768 | tf_op jit(solution)/shard_map/ppermute | solution.py:233
  74.1 6.6 %collective-permute-start.2 = (bf16[64,15]{1,0:T(8,128)(2,1)S(1)}, bf16[64,15]{1,0:T(8,128)(2,1)S(1)}, u32[]{:S(2)}, u32[]{:S(2)}) collective-permute-start(bf16[64,15]{1,0:T(8,128)(2,1)S(1)} %get-tuple-element.57), channel_id=1, source_target_pairs={{0,1},{1,2},{2,3},{3,4},{4,5},{5,6},{6,7},{7,8},{8,9},{9,10},{10,1... | collective-permute-start | bytes 5768 | tf_op jit(solution)/shard_map/ppermute | solution.py:232
  92.2 6.7 %collective-permute-start.5 = (f32[64,15]{1,0:T(8,128)S(1)}, f32[64,15]{1,0:T(8,128)S(1)}, u32[]{:S(2)}, u32[]{:S(2)}) collective-permute-start(f32[64,15]{1,0:T(8,128)S(1)} %get-tuple-element.52), channel_id=1, source_target_pairs={{1,0},{2,1},{3,2},{4,3},{5,4},{6,5},{7,6},{8,7},{9,8},{10,9},{11,1... | collective-permute-start | bytes 11528 | tf_op jit(solution)/shard_map/ppermute | solution.py:233
  94.1 5.6 %collective-permute-start.4 = (f32[64,15]{1,0:T(8,128)S(1)}, f32[64,15]{1,0:T(8,128)S(1)}, u32[]{:S(2)}, u32[]{:S(2)}) collective-permute-start(f32[64,15]{1,0:T(8,128)S(1)} %get-tuple-element.53), channel_id=1, source_target_pairs={{0,1},{1,2},{2,3},{3,4},{4,5},{5,6},{6,7},{7,8},{8,9},{9,10},{10,1... | collective-permute-start | bytes 11528 | tf_op jit(solution)/shard_map/ppermute | solution.py:232
  128.2 1.5 %copy-start = (f32[64,4096]{1,0:T(8,128)S(1)}, f32[64,4096]{1,0:T(8,128)}, u32[]{:S(2)}) copy-start(f32[64,4096]{1,0:T(8,128)} %get-tuple-element.23) | copy-start | bytes 3145732
  129.8 9.1 %copy-start.1 = (bf16[2048,64]{1,0:T(8,128)(2,1)S(1)}, bf16[2048,64]{1,0:T(8,128)(2,1)}, u32[]{:S(2)}) copy-start(bf16[2048,64]{1,0:T(8,128)(2,1)} %get-tuple-element.21) | copy-start | bytes 786436
  130.0 10.3 %collective-permute-start.6 = (bf16[128,1024]{1,0:T(8,128)(2,1)S(1)}, bf16[128,1024]{1,0:T(8,128)(2,1)S(1)}, u32[]{:S(2)}, u32[]{:S(2)}) collective-permute-start(bf16[128,1024]{1,0:T(8,128)(2,1)S(1)} %get-tuple-element.44), channel_id=1, source_target_pairs={{0,1},{1,2},{2,3},{3,4},{4,5},{5,6},{6,7},{7,8},{8,9},{9,10},{10,1... | collective-permute-start | bytes 786440 | tf_op jit(solution)/shard_map/ppermute | solution.py:29
  137.0 8.7 %collective-permute-start.7 = (bf16[128,1024]{1,0:T(8,128)(2,1)S(1)}, bf16[128,1024]{1,0:T(8,128)(2,1)}, u32[]{:S(2)}, u32[]{:S(2)}) collective-permute-start(bf16[128,1024]{1,0:T(8,128)(2,1)S(1)} %get-tuple-element.45), channel_id=1, source_target_pairs={{1,0},{2,1},{3,2},{4,3},{5,4},{6,5},{7,6},{8,7},{9,8},{10,9},{11,1... | collective-permute-start | bytes 786440 | tf_op jit(solution)/shard_map/ppermute | solution.py:29

commit v19 on v17

--- a/solution.py
+++ b/solution.py
@@ -52,8 +52,8 @@
     return jnp.where(same_seg, jnp.exp(scores - row_top), 0.0) / row_total
 
 
-TILE_Q = 512
-TILE_K = 512
+TILE_Q = 256
+TILE_K = 1024
 NT = (((1,), (1,)), ((), ()))
 TN = (((0,), (0,)), ((), ()))
 

time: 147 us -> 151 us (1.027)
  the two profiles are of different devices: /device:TPU:9 before, /device:TPU:11 now
where the time goes in v19:
time: 151 us; the launch traced here: 150 us
  Pallas kernels  56.2 us (37%)
  starting transfers between devices  38.1 us (25%)
  waiting for transfers between devices  29.7 us (20%)
  local copies, waits for them, and re-layouts  20.9 us (14%)
  other arithmetic  4.53 us (3%)
    pallas_call x1, Pallas kernels, on_device(): vmem_call(backward_kernel, 2, 9, (jax.ShapeDtypeStruct((block_rows, HEAD_...  20.6 us
    all_to_all x1, waiting for transfers between devices, on_device(): lax.all_to_all(stacked, 'uly', split_axis=1, concat_axis=0, tiled=True)  20.3 us
    pallas_call x1, Pallas kernels, on_device(): vmem_call(forward_kernel, 2, 4, (jax.ShapeDtypeStruct((HEAD_DIM, block_ro...  18 us
    all_to_all x1, starting transfers between devices, on_device(): lax.all_to_all(stacked, 'uly', split_axis=1, concat_axis=0, tiled=True)  10 us
    ppermute x2, starting transfers between devices, padded_rims(): low = lax.ppermute(block[:, block.shape[1] - half:], 'blk', forward)  9.26 us
    pallas_call x1, Pallas kernels, on_device(): vmem_call(conv_forward_kernel, 0, 6, (jax.ShapeDtypeStruct((HEAD_DIM, blo...  8.86 us
    pallas_call x1, Pallas kernels, on_device(): vmem_call(conv_backward_kernel, 0, 5, (jax.ShapeDtypeStruct((HEAD_DIM, bl...  8.68 us
    ppermute x1, starting transfers between devices, extended(): lax.ppermute(lax.slice_in_dim(block, block.shape[dim] - width, None, axis...  6.87 us
  transfers between devices with their start and end apart: 9, of which 5 were waited for; matrix products, arithmetic and copies ran while one was open for 6% of the time, Pallas kernels for 0%

profile of v19, /device:TPU:11, one launch (start us, length us, event | category | flops | bytes accessed | tf_op | source)
XLA Modules:
  0.0 150.3 jit_solution(15352511238553910335)
XLA Ops:
  0.6 1.1 copy.49
  1.8 1.1 copy.50
  2.9 1.1 copy.51
  4.1 0.9 copy.52
  5.1 10.0 %all-to-all-start = ((bf16[128,16,192]{0,2,1:T(8,128)(2,1)}), bf16[128,16,192]{0,2,1:T(8,128)(2,1)S(1)}, u32[]{:S(2)}, u32[]{:S(2)}) async-start(bf16[128,16,192]{0,2,1:T(8,128)(2,1)} %bitcast.5), calls=%async_computation | async-start | bytes 1572864 | tf_op jit(solution)/shard_map/all_to_all | solution.py:246
  15.4 0.2 select_reduce_fusion
  15.7 0.5 slice.78
  16.2 0.2 convert_reduce_fusion
  16.5 0.6 and_select_fusion.kseg_ref
  17.1 20.3 %all-to-all-done = bf16[128,16,192]{0,2,1:T(8,128)(2,1)S(1)} async-done(((bf16[128,16,192]{0,2,1:T(8,128)(2,1)}), bf16[128,16,192]{0,2,1:T(8,128)(2,1)S(1)}, u32[]{:S(2)}, u32[]{:S(2)}) %all-to-all-start) | async-done | bytes 786464 | tf_op jit(solution)/shard_map/all_to_all | solution.py:246
  37.4 0.5 copy.53
  37.9 0.3 reshape.97
  38.3 0.8 slice_bitcast_fusion.2
  39.1 6.9 %collective-permute-start = (bf16[1024,128]{0,1:T(8,128)(2,1)S(1)}, bf16[1024,128]{0,1:T(8,128)(2,1)S(1)}, u32[]{:S(2)}, u32[]{:S(2)}) collective-permute-start(bf16[1024,128]{0,1:T(8,128)(2,1)S(1)} %get-tuple-element.54), channel_id=1, source_target_pairs={{0,1},{1,2},{2,3},{3,4},{4,5},{5,6},{6,7},{7,8},{8,9},{9,10},{10,1... | collective-permute-start | bytes 786440 | tf_op jit(solution)/shard_map/ppermute | solution.py:18
  46.0 1.9 %collective-permute-start.1 = (bf16[1024,128]{0,1:T(8,128)(2,1)S(1)}, bf16[1024,128]{0,1:T(8,128)(2,1)S(1)}, u32[]{:S(2)}, u32[]{:S(2)}) collective-permute-start(bf16[1024,128]{0,1:T(8,128)(2,1)S(1)} %get-tuple-element.55), channel_id=1, source_target_pairs={{1,0},{2,1},{3,2},{4,3},{5,4},{6,5},{7,6},{8,7},{9,8},{10,9},{11,1... | collective-permute-start | bytes 786440 | tf_op jit(solution)/shard_map/ppermute | solution.py:21
  47.9 0.7 broadcast_minimum_fusion
  48.8 1.4 copy.56.qseg_ref
  50.2 0.6 maximum_minimum_fusion
  50.7 0.3 copy.63
  51.0 0.9 concatenate.24.clone.q_ref
  51.9 2.7 %collective-permute-done.1 = bf16[1024,128]{0,1:T(8,128)(2,1)S(1)} collective-permute-done((bf16[1024,128]{0,1:T(8,128)(2,1)S(1)}, bf16[1024,128]{0,1:T(8,128)(2,1)S(1)}, u32[]{:S(2)}, u32[]{:S(2)}) %collective-permute-start.1) | collective-permute-done | bytes 262176 | tf_op jit(solution)/shard_map/ppermute | solution.py:21
  54.7 1.3 copy.55.kv_ref
  56.0 18.0 %shard_map.102 = (bf16[64,2048]{1,0:T(8,128)(2,1)}, f32[2048,1]{1,0:T(8,128)}) custom-call(s32[8]{0:T(128)} %get-tuple-element.43.lo_ref, s32[8]{0:T(128)} %get-tuple-element.42.hi_ref, bf16[2048,128]{1,0:T(8,128)(2,1)} %concatenate.24.clone.q_ref, bf16[4096,128]{1,0:T(8,128)(2,1)} %copy.55.kv_ref, s32[2048,1]{1,0:T(8,128)} %copy.56.qseg_ref, ...), custom_call_target="tpu_custom_call" | custom-call | tf_op jit(solution)/shard_map/pallas_call | solution.py:280
  74.0 0.8 fusion.9
  74.8 1.9 %collective-permute-start.3 = (bf16[64,15]{1,0:T(8,128)(2,1)S(1)}, bf16[64,15]{1,0:T(8,128)(2,1)S(1)}, u32[]{:S(2)}, u32[]{:S(2)}) collective-permute-start(bf16[64,15]{1,0:T(8,128)(2,1)S(1)} %get-tuple-element.56), channel_id=1, source_target_pairs={{1,0},{2,1},{3,2},{4,3},{5,4},{6,5},{7,6},{8,7},{9,8},{10,9},{11,1... | collective-permute-start | bytes 5768 | tf_op jit(solution)/shard_map/ppermute | solution.py:232
  76.8 4.5 %collective-permute-start.2 = (bf16[64,15]{1,0:T(8,128)(2,1)S(1)}, bf16[64,15]{1,0:T(8,128)(2,1)S(1)}, u32[]{:S(2)}, u32[]{:S(2)}) collective-permute-start(bf16[64,15]{1,0:T(8,128)(2,1)S(1)} %get-tuple-element.57), channel_id=1, source_target_pairs={{0,1},{1,2},{2,3},{3,4},{4,5},{5,6},{6,7},{7,8},{8,9},{9,10},{10,1... | collective-permute-start | bytes 5768 | tf_op jit(solution)/shard_map/ppermute | solution.py:231
  81.3 0.6 fusion.2
  81.9 0.7 copy.57
  82.6 0.7 copy.58.gain_ref
  83.4 1.8 %concatenate.27.x_ref = f32[64,2304]{1,0:T(8,128)} concatenate(f32[64,113]{1,0:T(8,128)S(1)} %broadcast.102, bf16[64,15]{1,0:T(8,128)(2,1)S(1)} %collective-permute-done.2, bf16[64,2048]{1,0:T(8,128)(2,1)} %get-tuple-element.14.att_ref, bf16[64,15]{1,0:T(8,128)(2,1)S(1)} %collective-permute-done.3, f32[64,113]{1,0:T(8,128)S(1)} %broadcast.102), dimensions={1} | concatenate | bytes 913664 | tf_op jit(solution)/shard_map/concatenate | solution.py:234
  85.2 8.9 %shard_map.103 = (bf16[64,2048]{1,0:T(8,128)(2,1)}, f32[64,2048]{1,0:T(8,128)}) custom-call(f32[64,2304]{1,0:T(8,128)} %concatenate.27.x_ref, f32[64,31]{1,0:T(8,128)} %bitcast.30, f32[64,1]{1,0:T(8,128)} %copy.58.gain_ref, bf16[64,2048]{1,0:T(8,128)(2,1)} %cot_ref.1, s32[1,2048]{1,0:T(1,128)} %get-tuple-element.59.lo_ref, s32[1,2048]{1,0:T(1,128)} %get-tuple-element.58.hi_ref), custom_call_target="tpu_custom_call" | custom-call | tf_op jit(solution)/shard_map/pallas_call | solution.py:294
  94.1 0.8 fusion.8
  94.9 1.9 %collective-permute-start.5 = (f32[64,15]{1,0:T(8,128)S(1)}, f32[64,15]{1,0:T(8,128)S(1)}, u32[]{:S(2)}, u32[]{:S(2)}) collective-permute-start(f32[64,15]{1,0:T(8,128)S(1)} %get-tuple-element.52), channel_id=1, source_target_pairs={{1,0},{2,1},{3,2},{4,3},{5,4},{6,5},{7,6},{8,7},{9,8},{10,9},{11,1... | collective-permute-start | bytes 11528 | tf_op jit(solution)/shard_map/ppermute | solution.py:232
  96.8 4.7 %collective-permute-start.4 = (f32[64,15]{1,0:T(8,128)S(1)}, f32[64,15]{1,0:T(8,128)S(1)}, u32[]{:S(2)}, u32[]{:S(2)}) collective-permute-start(f32[64,15]{1,0:T(8,128)S(1)} %get-tuple-element.53), channel_id=1, source_target_pairs={{0,1},{1,2},{2,3},{3,4},{4,5},{5,6},{6,7},{7,8},{8,9},{9,10},{10,1... | collective-permute-start | bytes 11528 | tf_op jit(solution)/shard_map/ppermute | solution.py:231
  101.6 0.8 collective-permute-done.4
  102.4 1.9 %concatenate.28.y_ref = f32[64,2304]{1,0:T(8,128)} concatenate(f32[64,113]{1,0:T(8,128)S(1)} %broadcast.102, f32[64,15]{1,0:T(8,128)S(1)} %collective-permute-done.4, f32[64,2048]{1,0:T(8,128)} %get-tuple-element.16, f32[64,15]{1,0:T(8,128)S(1)} %collective-permute-done.5, f32[64,113]{1,0:T(8,128)S(1)} %broadcast.102), dimensions={1} | concatenate | bytes 1179648 | tf_op jit(solution)/shard_map/concatenate | solution.py:234
  104.3 8.7 %shard_map.104 = (bf16[64,2048]{1,0:T(8,128)(2,1)}, bf16[2048,128]{1,0:T(8,128)(2,1)}, f32[2048,1]{1,0:T(8,128)}) custom-call(f32[64,2304]{1,0:T(8,128)} %concatenate.28.y_ref, f32[64,31]{1,0:T(8,128)} %bitcast.31, bf16[64,2048]{1,0:T(8,128)(2,1)} %get-tuple-element.14.att_ref, s32[1,2048]{1,0:T(1,128)} %get-tuple-element.59.lo_ref, ...), custom_call_target="tpu_custom_call" | custom-call | tf_op jit(solution)/shard_map/pallas_call | solution.py:303
  113.0 20.6 %shard_map.105 = (bf16[2048,64]{1,0:T(8,128)(2,1)}, f32[64,4096]{1,0:T(8,128)}, f32[64,4096]{1,0:T(8,128)}) custom-call(s32[8]{0:T(128)} %get-tuple-element.43.lo_ref, s32[8]{0:T(128)} %get-tuple-element.42.hi_ref, bf16[2048,128]{1,0:T(8,128)(2,1)} %concatenate.24.clone.q_ref, bf16[4096,128]{1,0:T(8,128)(2,1)} %copy.55.kv_ref, ...), custom_call_target="tpu_custom_call" | custom-call | tf_op jit(solution)/shard_map/pallas_call | solution.py:315
  133.6 1.4 constant_dynamic-update-slice_fusion.1
  135.0 0.1 copy-done
  135.3 0.1 convert.9
  135.4 4.3 %collective-permute-start.6 = (bf16[128,1024]{1,0:T(8,128)(2,1)S(1)}, bf16[128,1024]{1,0:T(8,128)(2,1)S(1)}, u32[]{:S(2)}, u32[]{:S(2)}) collective-permute-start(bf16[128,1024]{1,0:T(8,128)(2,1)S(1)} %get-tuple-element.44), channel_id=1, source_target_pairs={{0,1},{1,2},{2,3},{3,4},{4,5},{5,6},{6,7},{7,8},{8,9},{9,10},{10,1... | collective-permute-start | bytes 786440 | tf_op jit(solution)/shard_map/ppermute | solution.py:29
  139.7 1.9 %collective-permute-start.7 = (bf16[128,1024]{1,0:T(8,128)(2,1)S(1)}, bf16[128,1024]{1,0:T(8,128)(2,1)}, u32[]{:S(2)}, u32[]{:S(2)}) collective-permute-start(bf16[128,1024]{1,0:T(8,128)(2,1)S(1)} %get-tuple-element.45), channel_id=1, source_target_pairs={{1,0},{2,1},{3,2},{4,3},{5,4},{6,5},{7,6},{8,7},{9,8},{10,9},{11,1... | collective-permute-start | bytes 786440 | tf_op jit(solution)/shard_map/ppermute | solution.py:29
  141.7 0.9 copy.62
  142.6 0.5 collective-permute-done.6
  143.1 5.4 %collective-permute-done.7 = bf16[128,1024]{1,0:T(8,128)(2,1)} collective-permute-done((bf16[128,1024]{1,0:T(8,128)(2,1)S(1)}, bf16[128,1024]{1,0:T(8,128)(2,1)}, u32[]{:S(2)}, u32[]{:S(2)}) %collective-permute-start.7) | collective-permute-done | bytes 262176 | tf_op jit(solution)/shard_map/ppermute | solution.py:29
  148.4 1.1 fusion
  149.5 0.8 fusion.7
  (29 shorter events, 0.8 us)
Async XLA Ops:
  4.0 11.1 %copy-start.3 = (s32[64]{0:T(128)S(1)}, s32[64]{0:T(128)}, u32[]{:S(2)}) copy-start(s32[64]{0:T(128)} %param.10) | copy-start | bytes 772
  5.1 32.3 %all-to-all-start = ((bf16[128,16,192]{0,2,1:T(8,128)(2,1)}), bf16[128,16,192]{0,2,1:T(8,128)(2,1)S(1)}, u32[]{:S(2)}, u32[]{:S(2)}) async-start(bf16[128,16,192]{0,2,1:T(8,128)(2,1)} %bitcast.5), calls=%async_computation | async-start | bytes 1572864 | tf_op jit(solution)/shard_map/all_to_all | solution.py:246
  39.1 12.8 %collective-permute-start = (bf16[1024,128]{0,1:T(8,128)(2,1)S(1)}, bf16[1024,128]{0,1:T(8,128)(2,1)S(1)}, u32[]{:S(2)}, u32[]{:S(2)}) collective-permute-start(bf16[1024,128]{0,1:T(8,128)(2,1)S(1)} %get-tuple-element.54), channel_id=1, source_target_pairs={{0,1},{1,2},{2,3},{3,4},{4,5},{5,6},{6,7},{7,8},{8,9},{9,10},{10,1... | collective-permute-start | bytes 786440 | tf_op jit(solution)/shard_map/ppermute | solution.py:18
  46.0 8.6 %collective-permute-start.1 = (bf16[1024,128]{0,1:T(8,128)(2,1)S(1)}, bf16[1024,128]{0,1:T(8,128)(2,1)S(1)}, u32[]{:S(2)}, u32[]{:S(2)}) collective-permute-start(bf16[1024,128]{0,1:T(8,128)(2,1)S(1)} %get-tuple-element.55), channel_id=1, source_target_pairs={{1,0},{2,1},{3,2},{4,3},{5,4},{6,5},{7,6},{8,7},{9,8},{10,9},{11,1... | collective-permute-start | bytes 786440 | tf_op jit(solution)/shard_map/ppermute | solution.py:21
  54.7 27.3 %copy-start.2 = (f32[31,64]{1,0:T(8,128)S(1)}, f32[31,64]{1,0:T(8,128)}, u32[]{:S(2)}) copy-start(f32[31,64]{1,0:T(8,128)} %param.11) | copy-start | bytes 23812
  54.7 28.0 %copy-start.4 = (f32[64]{0:T(128)S(1)}, f32[64]{0:T(128)}, u32[]{:S(2)}) copy-start(f32[64]{0:T(128)} %param.12) | copy-start | bytes 772
  74.8 8.5 %collective-permute-start.3 = (bf16[64,15]{1,0:T(8,128)(2,1)S(1)}, bf16[64,15]{1,0:T(8,128)(2,1)S(1)}, u32[]{:S(2)}, u32[]{:S(2)}) collective-permute-start(bf16[64,15]{1,0:T(8,128)(2,1)S(1)} %get-tuple-element.56), channel_id=1, source_target_pairs={{1,0},{2,1},{3,2},{4,3},{5,4},{6,5},{7,6},{8,7},{9,8},{10,9},{11,1... | collective-permute-start | bytes 5768 | tf_op jit(solution)/shard_map/ppermute | solution.py:232
  76.8 6.6 %collective-permute-start.2 = (bf16[64,15]{1,0:T(8,128)(2,1)S(1)}, bf16[64,15]{1,0:T(8,128)(2,1)S(1)}, u32[]{:S(2)}, u32[]{:S(2)}) collective-permute-start(bf16[64,15]{1,0:T(8,128)(2,1)S(1)} %get-tuple-element.57), channel_id=1, source_target_pairs={{0,1},{1,2},{2,3},{3,4},{4,5},{5,6},{6,7},{7,8},{8,9},{9,10},{10,1... | collective-permute-start | bytes 5768 | tf_op jit(solution)/shard_map/ppermute | solution.py:231
  94.9 6.7 %collective-permute-start.5 = (f32[64,15]{1,0:T(8,128)S(1)}, f32[64,15]{1,0:T(8,128)S(1)}, u32[]{:S(2)}, u32[]{:S(2)}) collective-permute-start(f32[64,15]{1,0:T(8,128)S(1)} %get-tuple-element.52), channel_id=1, source_target_pairs={{1,0},{2,1},{3,2},{4,3},{5,4},{6,5},{7,6},{8,7},{9,8},{10,9},{11,1... | collective-permute-start | bytes 11528 | tf_op jit(solution)/shard_map/ppermute | solution.py:232
  96.8 5.6 %collective-permute-start.4 = (f32[64,15]{1,0:T(8,128)S(1)}, f32[64,15]{1,0:T(8,128)S(1)}, u32[]{:S(2)}, u32[]{:S(2)}) collective-permute-start(f32[64,15]{1,0:T(8,128)S(1)} %get-tuple-element.53), channel_id=1, source_target_pairs={{0,1},{1,2},{2,3},{3,4},{4,5},{5,6},{6,7},{7,8},{8,9},{9,10},{10,1... | collective-permute-start | bytes 11528 | tf_op jit(solution)/shard_map/ppermute | solution.py:231
  133.6 1.5 %copy-start = (f32[64,4096]{1,0:T(8,128)S(1)}, f32[64,4096]{1,0:T(8,128)}, u32[]{:S(2)}) copy-start(f32[64,4096]{1,0:T(8,128)} %get-tuple-element.23) | copy-start | bytes 3145732
  135.3 6.4 %copy-start.1 = (bf16[2048,64]{1,0:T(8,128)(2,1)S(1)}, bf16[2048,64]{1,0:T(8,128)(2,1)}, u32[]{:S(2)}) copy-start(bf16[2048,64]{1,0:T(8,128)(2,1)} %get-tuple-element.21) | copy-start | bytes 786436
  135.4 7.6 %collective-permute-start.6 = (bf16[128,1024]{1,0:T(8,128)(2,1)S(1)}, bf16[128,1024]{1,0:T(8,128)(2,1)S(1)}, u32[]{:S(2)}, u32[]{:S(2)}) collective-permute-start(bf16[128,1024]{1,0:T(8,128)(2,1)S(1)} %get-tuple-element.44), channel_id=1, source_target_pairs={{0,1},{1,2},{2,3},{3,4},{4,5},{5,6},{6,7},{7,8},{8,9},{9,10},{10,1... | collective-permute-start | bytes 786440 | tf_op jit(solution)/shard_map/ppermute | solution.py:29
  139.7 8.7 %collective-permute-start.7 = (bf16[128,1024]{1,0:T(8,128)(2,1)S(1)}, bf16[128,1024]{1,0:T(8,128)(2,1)}, u32[]{:S(2)}, u32[]{:S(2)}) collective-permute-start(bf16[128,1024]{1,0:T(8,128)(2,1)S(1)} %get-tuple-element.45), channel_id=1, source_target_pairs={{1,0},{2,1},{3,2},{4,3},{5,4},{6,5},{7,6},{8,7},{9,8},{10,9},{11,1... | collective-permute-start | bytes 786440 | tf_op jit(solution)/shard_map/ppermute | solution.py:29

commit v20 on v17

--- a/solution.py
+++ b/solution.py
@@ -97,11 +97,10 @@
 
 def backward_kernel(
     lo_ref, hi_ref, q_ref, kv_ref, do_ref, qt_ref, dot_ref, qseg_ref, kseg_ref, lse_ref,
-    d_ref, dq_ref, dk_ref, dv_ref,
+    d_ref, dq_ref, dkv_ref,
 ):
     scale = HEAD_DIM ** (-0.5)
-    dk_ref[...] = jnp.zeros_like(dk_ref)
-    dv_ref[...] = jnp.zeros_like(dv_ref)
+    dkv_ref[...] = jnp.zeros_like(dkv_ref)
 
     def q_body(i, carry):
         r0 = pl.multiple_of(i * TILE_Q, TILE_Q)
@@ -121,8 +120,10 @@
             p = jnp.exp(jnp.where(qs == ks, s, -1e30) - lse)
             dp = lax.dot_general(do, kv, NT, preferred_element_type=jnp.float32)
             ds = (p * (dp - dlt)).astype(jnp.bfloat16)
-            dk_ref[:, pl.ds(c0, TILE_K)] += jnp.dot(q_t, ds, preferred_element_type=jnp.float32)
-            dv_ref[:, pl.ds(c0, TILE_K)] += jnp.dot(
+            dkv_ref[:HEAD_DIM, pl.ds(c0, TILE_K)] += jnp.dot(
+                q_t, ds, preferred_element_type=jnp.float32
+            )
+            dkv_ref[HEAD_DIM:, pl.ds(c0, TILE_K)] += jnp.dot(
                 do_t, p.astype(jnp.bfloat16), preferred_element_type=jnp.float32
             )
             return dq + jnp.dot(ds, kv, preferred_element_type=jnp.float32)
@@ -134,7 +135,7 @@
         return carry
 
     lax.fori_loop(0, q_ref.shape[0] // TILE_Q, q_body, 0)
-    dk_ref[...] = scale * dk_ref[...]
+    dkv_ref[:HEAD_DIM, :] = scale * dkv_ref[:HEAD_DIM, :]
 
 
 def vmem_call(kernel, n_smem, n_vmem, out_shape):
@@ -312,14 +313,13 @@
     )(padded_rims(grad_conv_t, conv_half), weight_t, att_t, lo_off, hi_off)
 
     ext_rows = block_rows + 2 * maxlen
-    grad_q, dk_t, dv_t = vmem_call(
+    grad_q, ext_terms = vmem_call(
         backward_kernel,
         2,
         9,
         (
             jax.ShapeDtypeStruct((block_rows, HEAD_DIM), jnp.bfloat16),
-            jax.ShapeDtypeStruct((HEAD_DIM, ext_rows), jnp.float32),
-            jax.ShapeDtypeStruct((HEAD_DIM, ext_rows), jnp.float32),
+            jax.ShapeDtypeStruct((2 * HEAD_DIM, ext_rows), jnp.float32),
         ),
     )(
         lo_t,
@@ -334,7 +334,6 @@
         lse_col,
         row_delta,
     )
-    ext_terms = jnp.concatenate([dk_t, dv_t], axis=0)
     received = []
     for rim_part, direction in ((ext_terms[:, :maxlen], -1), (ext_terms[:, maxlen + block_rows :], 1)):
         received.append(

time: 147 us -> 148 us (level)
  starting transfers between devices: 38 us -> 41.7 us
  other arithmetic: 4.53 us -> 6.26 us
  Pallas kernels: 50.7 us -> 49.1 us
  local copies, waits for them, and re-layouts: 20.9 us -> 19.3 us
    ppermute x2, starting transfers between devices: 6.11 us -> 9.81 us  [passed_along(): return lax.ppermute(block, axis, route)]
    another operation x4, other arithmetic: 1.38 us -> 3.12 us
    unnamed x17 -> x16, local copies, waits for them, and re-layouts: 6.79 us -> 5.25 us
where the time goes in v20:
time: 148 us; the launch traced here: 147 us
  Pallas kernels  49.1 us (33%)
  starting transfers between devices  41.7 us (28%)
  waiting for transfers between devices  29.7 us (20%)
  local copies, waits for them, and re-layouts  19.3 us (13%)
  other arithmetic  6.26 us (4%)
    all_to_all x1, waiting for transfers between devices, on_device(): lax.all_to_all(stacked, 'uly', split_axis=1, concat_axis=0, tiled=True)  20.3 us
    pallas_call x1, Pallas kernels, on_device(): vmem_call(backward_kernel, 2, 9, (jax.ShapeDtypeStruct((block_rows, HEAD_...  17 us
    pallas_call x1, Pallas kernels, on_device(): vmem_call(forward_kernel, 2, 4, (jax.ShapeDtypeStruct((HEAD_DIM, block_ro...  14.5 us
    all_to_all x1, starting transfers between devices, on_device(): lax.all_to_all(stacked, 'uly', split_axis=1, concat_axis=0, tiled=True)  10 us
    ppermute x2, starting transfers between devices, passed_along(): return lax.ppermute(block, axis, route)  9.81 us
    ppermute x2, starting transfers between devices, padded_rims(): low = lax.ppermute(block[:, block.shape[1] - half:], 'blk', forward)  9.26 us
    pallas_call x1, Pallas kernels, on_device(): vmem_call(conv_forward_kernel, 0, 6, (jax.ShapeDtypeStruct((HEAD_DIM, blo...  8.89 us
    pallas_call x1, Pallas kernels, on_device(): vmem_call(conv_backward_kernel, 0, 5, (jax.ShapeDtypeStruct((HEAD_DIM, bl...  8.69 us
  transfers between devices with their start and end apart: 9, of which 5 were waited for; matrix products, arithmetic and copies ran while one was open for 6% of the time, Pallas kernels for 0%

profile of v20, /device:TPU:9, one launch (start us, length us, event | category | flops | bytes accessed | tf_op | source)
XLA Modules:
  0.0 146.9 jit_solution(2641405373585948717)
XLA Ops:
  0.6 1.1 copy.49
  1.8 1.1 copy.50
  2.9 1.1 copy.51
  4.1 0.9 copy.52
  5.1 10.0 %all-to-all-start = ((bf16[128,16,192]{0,2,1:T(8,128)(2,1)}), bf16[128,16,192]{0,2,1:T(8,128)(2,1)S(1)}, u32[]{:S(2)}, u32[]{:S(2)}) async-start(bf16[128,16,192]{0,2,1:T(8,128)(2,1)} %bitcast.5), calls=%async_computation | async-start | bytes 1572864 | tf_op jit(solution)/shard_map/all_to_all | solution.py:247
  15.1 0.1 copy.48
  15.3 0.1 reduce
  15.4 0.2 select_reduce_fusion
  15.7 0.5 slice.78
  16.2 0.2 convert_reduce_fusion
  16.5 0.6 and_select_fusion.kseg_ref
  17.1 20.3 %all-to-all-done = bf16[128,16,192]{0,2,1:T(8,128)(2,1)S(1)} async-done(((bf16[128,16,192]{0,2,1:T(8,128)(2,1)}), bf16[128,16,192]{0,2,1:T(8,128)(2,1)S(1)}, u32[]{:S(2)}, u32[]{:S(2)}) %all-to-all-start) | async-done | bytes 786464 | tf_op jit(solution)/shard_map/all_to_all | solution.py:247
  37.4 0.5 copy.53
  37.9 0.3 reshape.97
  38.3 0.8 slice_bitcast_fusion.2
  39.1 6.9 %collective-permute-start = (bf16[1024,128]{0,1:T(8,128)(2,1)S(1)}, bf16[1024,128]{0,1:T(8,128)(2,1)S(1)}, u32[]{:S(2)}, u32[]{:S(2)}) collective-permute-start(bf16[1024,128]{0,1:T(8,128)(2,1)S(1)} %get-tuple-element.52), channel_id=1, source_target_pairs={{0,1},{1,2},{2,3},{3,4},{4,5},{5,6},{6,7},{7,8},{8,9},{9,10},{10,1... | collective-permute-start | bytes 786440 | tf_op jit(solution)/shard_map/ppermute | solution.py:18
  46.0 1.9 %collective-permute-start.1 = (bf16[1024,128]{0,1:T(8,128)(2,1)S(1)}, bf16[1024,128]{0,1:T(8,128)(2,1)S(1)}, u32[]{:S(2)}, u32[]{:S(2)}) collective-permute-start(bf16[1024,128]{0,1:T(8,128)(2,1)S(1)} %get-tuple-element.53), channel_id=1, source_target_pairs={{1,0},{2,1},{3,2},{4,3},{5,4},{6,5},{7,6},{8,7},{9,8},{10,9},{11,1... | collective-permute-start | bytes 786440 | tf_op jit(solution)/shard_map/ppermute | solution.py:21
  47.9 0.7 broadcast_minimum_fusion
  48.8 1.4 copy.56.qseg_ref
  50.1 0.6 maximum_minimum_fusion
  50.7 0.3 copy.63
  51.0 0.9 concatenate.21.clone.q_ref
  51.9 2.7 %collective-permute-done.1 = bf16[1024,128]{0,1:T(8,128)(2,1)S(1)} collective-permute-done((bf16[1024,128]{0,1:T(8,128)(2,1)S(1)}, bf16[1024,128]{0,1:T(8,128)(2,1)S(1)}, u32[]{:S(2)}, u32[]{:S(2)}) %collective-permute-start.1) | collective-permute-done | bytes 262176 | tf_op jit(solution)/shard_map/ppermute | solution.py:21
  54.7 1.3 copy.55.kv_ref
  56.0 14.5 %shard_map.102 = (bf16[64,2048]{1,0:T(8,128)(2,1)}, f32[2048,1]{1,0:T(8,128)}) custom-call(s32[4]{0:T(128)} %get-tuple-element.41.lo_ref, s32[4]{0:T(128)} %get-tuple-element.40.hi_ref, bf16[2048,128]{1,0:T(8,128)(2,1)} %concatenate.21.clone.q_ref, bf16[4096,128]{1,0:T(8,128)(2,1)} %copy.55.kv_ref, s32[2048,1]{1,0:T(8,128)} %copy.56.qseg_ref, ...), custom_call_target="tpu_custom_call" | custom-call | tf_op jit(solution)/shard_map/pallas_call | solution.py:281
  70.5 0.8 fusion.8
  71.3 1.9 %collective-permute-start.3 = (bf16[64,15]{1,0:T(8,128)(2,1)S(1)}, bf16[64,15]{1,0:T(8,128)(2,1)S(1)}, u32[]{:S(2)}, u32[]{:S(2)}) collective-permute-start(bf16[64,15]{1,0:T(8,128)(2,1)S(1)} %get-tuple-element.54), channel_id=1, source_target_pairs={{1,0},{2,1},{3,2},{4,3},{5,4},{6,5},{7,6},{8,7},{9,8},{10,9},{11,1... | collective-permute-start | bytes 5768 | tf_op jit(solution)/shard_map/ppermute | solution.py:233
  73.3 4.5 %collective-permute-start.2 = (bf16[64,15]{1,0:T(8,128)(2,1)S(1)}, bf16[64,15]{1,0:T(8,128)(2,1)S(1)}, u32[]{:S(2)}, u32[]{:S(2)}) collective-permute-start(bf16[64,15]{1,0:T(8,128)(2,1)S(1)} %get-tuple-element.55), channel_id=1, source_target_pairs={{0,1},{1,2},{2,3},{3,4},{4,5},{5,6},{6,7},{7,8},{8,9},{9,10},{10,1... | collective-permute-start | bytes 5768 | tf_op jit(solution)/shard_map/ppermute | solution.py:232
  77.8 0.6 fusion.1
  78.4 0.7 copy.57
  79.1 0.7 copy.58.gain_ref
  79.8 1.8 %concatenate.24.x_ref = f32[64,2304]{1,0:T(8,128)} concatenate(f32[64,113]{1,0:T(8,128)S(1)} %broadcast.102, bf16[64,15]{1,0:T(8,128)(2,1)S(1)} %collective-permute-done.2, bf16[64,2048]{1,0:T(8,128)(2,1)} %get-tuple-element.13.att_ref, bf16[64,15]{1,0:T(8,128)(2,1)S(1)} %collective-permute-done.3, f32[64,113]{1,0:T(8,128)S(1)} %broadcast.102), dimensions={1} | concatenate | bytes 913664 | tf_op jit(solution)/shard_map/concatenate | solution.py:235
  81.7 8.9 %shard_map.103 = (bf16[64,2048]{1,0:T(8,128)(2,1)}, f32[64,2048]{1,0:T(8,128)}) custom-call(f32[64,2304]{1,0:T(8,128)} %concatenate.24.x_ref, f32[64,31]{1,0:T(8,128)} %bitcast.30, f32[64,1]{1,0:T(8,128)} %copy.58.gain_ref, bf16[64,2048]{1,0:T(8,128)(2,1)} %cot_ref.1, s32[1,2048]{1,0:T(1,128)} %get-tuple-element.57.lo_ref, s32[1,2048]{1,0:T(1,128)} %get-tuple-element.56.hi_ref), custom_call_target="tpu_custom_call" | custom-call | tf_op jit(solution)/shard_map/pallas_call | solution.py:295
  90.6 0.8 fusion.7
  91.4 1.9 %collective-permute-start.5 = (f32[64,15]{1,0:T(8,128)S(1)}, f32[64,15]{1,0:T(8,128)S(1)}, u32[]{:S(2)}, u32[]{:S(2)}) collective-permute-start(f32[64,15]{1,0:T(8,128)S(1)} %get-tuple-element.50), channel_id=1, source_target_pairs={{1,0},{2,1},{3,2},{4,3},{5,4},{6,5},{7,6},{8,7},{9,8},{10,9},{11,1... | collective-permute-start | bytes 11528 | tf_op jit(solution)/shard_map/ppermute | solution.py:233
  93.3 4.7 %collective-permute-start.4 = (f32[64,15]{1,0:T(8,128)S(1)}, f32[64,15]{1,0:T(8,128)S(1)}, u32[]{:S(2)}, u32[]{:S(2)}) collective-permute-start(f32[64,15]{1,0:T(8,128)S(1)} %get-tuple-element.51), channel_id=1, source_target_pairs={{0,1},{1,2},{2,3},{3,4},{4,5},{5,6},{6,7},{7,8},{8,9},{9,10},{10,1... | collective-permute-start | bytes 11528 | tf_op jit(solution)/shard_map/ppermute | solution.py:232
  98.1 0.8 collective-permute-done.4
  98.9 1.9 %concatenate.25.y_ref = f32[64,2304]{1,0:T(8,128)} concatenate(f32[64,113]{1,0:T(8,128)S(1)} %broadcast.102, f32[64,15]{1,0:T(8,128)S(1)} %collective-permute-done.4, f32[64,2048]{1,0:T(8,128)} %get-tuple-element.15, f32[64,15]{1,0:T(8,128)S(1)} %collective-permute-done.5, f32[64,113]{1,0:T(8,128)S(1)} %broadcast.102), dimensions={1} | concatenate | bytes 1179648 | tf_op jit(solution)/shard_map/concatenate | solution.py:235
  100.8 8.7 %shard_map.104 = (bf16[64,2048]{1,0:T(8,128)(2,1)}, bf16[2048,128]{1,0:T(8,128)(2,1)}, f32[2048,1]{1,0:T(8,128)}) custom-call(f32[64,2304]{1,0:T(8,128)} %concatenate.25.y_ref, f32[64,31]{1,0:T(8,128)} %bitcast.31, bf16[64,2048]{1,0:T(8,128)(2,1)} %get-tuple-element.13.att_ref, s32[1,2048]{1,0:T(1,128)} %get-tuple-element.57.lo_ref, ...), custom_call_target="tpu_custom_call" | custom-call | tf_op jit(solution)/shard_map/pallas_call | solution.py:304
  109.5 17.0 %shard_map.105 = (bf16[2048,64]{1,0:T(8,128)(2,1)}, f32[128,4096]{1,0:T(8,128)}) custom-call(s32[4]{0:T(128)} %get-tuple-element.41.lo_ref, s32[4]{0:T(128)} %get-tuple-element.40.hi_ref, bf16[2048,128]{1,0:T(8,128)(2,1)} %concatenate.21.clone.q_ref, bf16[4096,128]{1,0:T(8,128)(2,1)} %copy.55.kv_ref, bf16[2048,128]{1,0:T(8,128)(2,1)} %get-tuple-element.16.do_ref, ...), custom_call_target="tpu_custom_call" | custom-call | tf_op jit(solution)/shard_map/pallas_call | solution.py:316
  126.5 1.9 %convert.9 = bf16[128,4096]{1,0:T(8,128)(2,1)S(1)} convert(f32[128,4096]{1,0:T(8,128)} %get-tuple-element.21) | non-fusion elementwise | flops 524288 | bytes 3145728 | tf_op jit(solution)/shard_map/convert.4
  128.4 7.9 %collective-permute-start.6 = (bf16[128,1024]{1,0:T(8,128)(2,1)S(1)}, bf16[128,1024]{1,0:T(8,128)(2,1)S(1)}, u32[]{:S(2)}, u32[]{:S(2)}) collective-permute-start(bf16[128,1024]{1,0:T(8,128)(2,1)S(1)} %get-tuple-element.42), channel_id=1, source_target_pairs={{0,1},{1,2},{2,3},{3,4},{4,5},{5,6},{6,7},{7,8},{8,9},{9,10},{10,1... | collective-permute-start | bytes 786440 | tf_op jit(solution)/shard_map/ppermute | solution.py:29
  136.3 1.9 %collective-permute-start.7 = (bf16[128,1024]{1,0:T(8,128)(2,1)S(1)}, bf16[128,1024]{1,0:T(8,128)(2,1)}, u32[]{:S(2)}, u32[]{:S(2)}) collective-permute-start(bf16[128,1024]{1,0:T(8,128)(2,1)S(1)} %get-tuple-element.43), channel_id=1, source_target_pairs={{1,0},{2,1},{3,2},{4,3},{5,4},{6,5},{7,6},{8,7},{9,8},{10,9},{11,1... | collective-permute-start | bytes 786440 | tf_op jit(solution)/shard_map/ppermute | solution.py:29
  138.2 0.9 copy.62
  139.1 0.5 collective-permute-done.6
  139.6 5.4 %collective-permute-done.7 = bf16[128,1024]{1,0:T(8,128)(2,1)} collective-permute-done((bf16[128,1024]{1,0:T(8,128)(2,1)S(1)}, bf16[128,1024]{1,0:T(8,128)(2,1)}, u32[]{:S(2)}, u32[]{:S(2)}) %collective-permute-start.7) | collective-permute-done | bytes 262176 | tf_op jit(solution)/shard_map/ppermute | solution.py:29
  145.0 1.1 add_convert_fusion
  146.1 0.8 fusion.6
  (27 shorter events, 0.6 us)
Async XLA Ops:
  4.0 11.1 %copy-start.3 = (s32[64]{0:T(128)S(1)}, s32[64]{0:T(128)}, u32[]{:S(2)}) copy-start(s32[64]{0:T(128)} %param.10) | copy-start | bytes 772
  5.1 32.3 %all-to-all-start = ((bf16[128,16,192]{0,2,1:T(8,128)(2,1)}), bf16[128,16,192]{0,2,1:T(8,128)(2,1)S(1)}, u32[]{:S(2)}, u32[]{:S(2)}) async-start(bf16[128,16,192]{0,2,1:T(8,128)(2,1)} %bitcast.5), calls=%async_computation | async-start | bytes 1572864 | tf_op jit(solution)/shard_map/all_to_all | solution.py:247
  39.1 12.8 %collective-permute-start = (bf16[1024,128]{0,1:T(8,128)(2,1)S(1)}, bf16[1024,128]{0,1:T(8,128)(2,1)S(1)}, u32[]{:S(2)}, u32[]{:S(2)}) collective-permute-start(bf16[1024,128]{0,1:T(8,128)(2,1)S(1)} %get-tuple-element.52), channel_id=1, source_target_pairs={{0,1},{1,2},{2,3},{3,4},{4,5},{5,6},{6,7},{7,8},{8,9},{9,10},{10,1... | collective-permute-start | bytes 786440 | tf_op jit(solution)/shard_map/ppermute | solution.py:18
  46.0 8.6 %collective-permute-start.1 = (bf16[1024,128]{0,1:T(8,128)(2,1)S(1)}, bf16[1024,128]{0,1:T(8,128)(2,1)S(1)}, u32[]{:S(2)}, u32[]{:S(2)}) collective-permute-start(bf16[1024,128]{0,1:T(8,128)(2,1)S(1)} %get-tuple-element.53), channel_id=1, source_target_pairs={{1,0},{2,1},{3,2},{4,3},{5,4},{6,5},{7,6},{8,7},{9,8},{10,9},{11,1... | collective-permute-start | bytes 786440 | tf_op jit(solution)/shard_map/ppermute | solution.py:21
  54.7 23.8 %copy-start.2 = (f32[31,64]{1,0:T(8,128)S(1)}, f32[31,64]{1,0:T(8,128)}, u32[]{:S(2)}) copy-start(f32[31,64]{1,0:T(8,128)} %param.11) | copy-start | bytes 23812
  54.7 24.4 %copy-start.4 = (f32[64]{0:T(128)S(1)}, f32[64]{0:T(128)}, u32[]{:S(2)}) copy-start(f32[64]{0:T(128)} %param.12) | copy-start | bytes 772
  71.3 8.5 %collective-permute-start.3 = (bf16[64,15]{1,0:T(8,128)(2,1)S(1)}, bf16[64,15]{1,0:T(8,128)(2,1)S(1)}, u32[]{:S(2)}, u32[]{:S(2)}) collective-permute-start(bf16[64,15]{1,0:T(8,128)(2,1)S(1)} %get-tuple-element.54), channel_id=1, source_target_pairs={{1,0},{2,1},{3,2},{4,3},{5,4},{6,5},{7,6},{8,7},{9,8},{10,9},{11,1... | collective-permute-start | bytes 5768 | tf_op jit(solution)/shard_map/ppermute | solution.py:233
  73.3 6.6 %collective-permute-start.2 = (bf16[64,15]{1,0:T(8,128)(2,1)S(1)}, bf16[64,15]{1,0:T(8,128)(2,1)S(1)}, u32[]{:S(2)}, u32[]{:S(2)}) collective-permute-start(bf16[64,15]{1,0:T(8,128)(2,1)S(1)} %get-tuple-element.55), channel_id=1, source_target_pairs={{0,1},{1,2},{2,3},{3,4},{4,5},{5,6},{6,7},{7,8},{8,9},{9,10},{10,1... | collective-permute-start | bytes 5768 | tf_op jit(solution)/shard_map/ppermute | solution.py:232
  91.4 6.7 %collective-permute-start.5 = (f32[64,15]{1,0:T(8,128)S(1)}, f32[64,15]{1,0:T(8,128)S(1)}, u32[]{:S(2)}, u32[]{:S(2)}) collective-permute-start(f32[64,15]{1,0:T(8,128)S(1)} %get-tuple-element.50), channel_id=1, source_target_pairs={{1,0},{2,1},{3,2},{4,3},{5,4},{6,5},{7,6},{8,7},{9,8},{10,9},{11,1... | collective-permute-start | bytes 11528 | tf_op jit(solution)/shard_map/ppermute | solution.py:233
  93.3 5.6 %collective-permute-start.4 = (f32[64,15]{1,0:T(8,128)S(1)}, f32[64,15]{1,0:T(8,128)S(1)}, u32[]{:S(2)}, u32[]{:S(2)}) collective-permute-start(f32[64,15]{1,0:T(8,128)S(1)} %get-tuple-element.51), channel_id=1, source_target_pairs={{0,1},{1,2},{2,3},{3,4},{4,5},{5,6},{6,7},{7,8},{8,9},{9,10},{10,1... | collective-permute-start | bytes 11528 | tf_op jit(solution)/shard_map/ppermute | solution.py:232
  126.5 11.7 %copy-start.1 = (bf16[2048,64]{1,0:T(8,128)(2,1)S(1)}, bf16[2048,64]{1,0:T(8,128)(2,1)}, u32[]{:S(2)}) copy-start(bf16[2048,64]{1,0:T(8,128)(2,1)} %get-tuple-element.20) | copy-start | bytes 786436
  126.5 18.5 %copy-start = (f32[128,4096]{1,0:T(8,128)S(1)}, f32[128,4096]{1,0:T(8,128)}, u32[]{:S(2)}) copy-start(f32[128,4096]{1,0:T(8,128)} %get-tuple-element.21) | copy-start | bytes 6291460
  128.4 11.2 %collective-permute-start.6 = (bf16[128,1024]{1,0:T(8,128)(2,1)S(1)}, bf16[128,1024]{1,0:T(8,128)(2,1)S(1)}, u32[]{:S(2)}, u32[]{:S(2)}) collective-permute-start(bf16[128,1024]{1,0:T(8,128)(2,1)S(1)} %get-tuple-element.42), channel_id=1, source_target_pairs={{0,1},{1,2},{2,3},{3,4},{4,5},{5,6},{6,7},{7,8},{8,9},{9,10},{10,1... | collective-permute-start | bytes 786440 | tf_op jit(solution)/shard_map/ppermute | solution.py:29
  136.3 8.7 %collective-permute-start.7 = (bf16[128,1024]{1,0:T(8,128)(2,1)S(1)}, bf16[128,1024]{1,0:T(8,128)(2,1)}, u32[]{:S(2)}, u32[]{:S(2)}) collective-permute-start(bf16[128,1024]{1,0:T(8,128)(2,1)S(1)} %get-tuple-element.43), channel_id=1, source_target_pairs={{1,0},{2,1},{3,2},{4,3},{5,4},{6,5},{7,6},{8,7},{9,8},{10,9},{11,1... | collective-permute-start | bytes 786440 | tf_op jit(solution)/shard_map/ppermute | solution.py:29

commit v21 on v17

--- a/solution.py
+++ b/solution.py
@@ -62,7 +62,7 @@
     scale = HEAD_DIM ** (-0.5)
 
     def q_body(i, carry):
-        r0 = pl.multiple_of(i * TILE_Q, TILE_Q)
+        r0 = i * TILE_Q
         q = q_ref[pl.ds(r0, TILE_Q), :] * jnp.asarray(scale, q_ref.dtype)
         qs = qseg_ref[pl.ds(r0, TILE_Q), :]
 
@@ -92,7 +92,8 @@
         lse_ref[pl.ds(r0, TILE_Q), :] = m + jnp.log(l)
         return carry
 
-    lax.fori_loop(0, q_ref.shape[0] // TILE_Q, q_body, 0)
+    for tile in range(q_ref.shape[0] // TILE_Q):
+        q_body(tile, 0)
 
 
 def backward_kernel(
@@ -104,7 +105,7 @@
     dv_ref[...] = jnp.zeros_like(dv_ref)
 
     def q_body(i, carry):
-        r0 = pl.multiple_of(i * TILE_Q, TILE_Q)
+        r0 = i * TILE_Q
         q = q_ref[pl.ds(r0, TILE_Q), :] * jnp.asarray(scale, q_ref.dtype)
         do = do_ref[pl.ds(r0, TILE_Q), :]
         qs = qseg_ref[pl.ds(r0, TILE_Q), :]
@@ -133,7 +134,8 @@
         dq_ref[pl.ds(r0, TILE_Q), :] = (scale * dq[:, :HEAD_DIM]).astype(dq_ref.dtype)
         return carry
 
-    lax.fori_loop(0, q_ref.shape[0] // TILE_Q, q_body, 0)
+    for tile in range(q_ref.shape[0] // TILE_Q):
+        q_body(tile, 0)
     dk_ref[...] = scale * dk_ref[...]
 
 

time: 147 us -> 150 us (1.020); the launches traced: 145 us -> 149 us
  Pallas kernels: 50.7 us -> 54.2 us
    pallas_call x1, Pallas kernels: 17.9 us -> 19.7 us  [on_device(): vmem_call(backward_kernel, 2, 9, (jax.ShapeDtypeStruct((block_rows, HEAD_...]
    pallas_call x1, Pallas kernels: 15.3 us -> 17 us  [on_device(): vmem_call(forward_kernel, 2, 4, (jax.ShapeDtypeStruct((HEAD_DIM, block_ro...]
where the time goes in v21:
time: 150 us; the launch traced here: 149 us
  Pallas kernels  54.2 us (36%)
  starting transfers between devices  39.2 us (26%)
  waiting for transfers between devices  29.6 us (20%)
  local copies, waits for them, and re-layouts  20.9 us (14%)
  other arithmetic  4.53 us (3%)
    all_to_all x1, waiting for transfers between devices, on_device(): lax.all_to_all(stacked, 'uly', split_axis=1, concat_axis=0, tiled=True)  20.3 us
    pallas_call x1, Pallas kernels, on_device(): vmem_call(backward_kernel, 2, 9, (jax.ShapeDtypeStruct((block_rows, HEAD_...  19.7 us
    pallas_call x1, Pallas kernels, on_device(): vmem_call(forward_kernel, 2, 4, (jax.ShapeDtypeStruct((HEAD_DIM, block_ro...  17 us
    all_to_all x1, starting transfers between devices, on_device(): lax.all_to_all(stacked, 'uly', split_axis=1, concat_axis=0, tiled=True)  10 us
    ppermute x2, starting transfers between devices, padded_rims(): low = lax.ppermute(block[:, block.shape[1] - half:], 'blk', forward)  9.48 us
    pallas_call x1, Pallas kernels, on_device(): vmem_call(conv_forward_kernel, 0, 6, (jax.ShapeDtypeStruct((HEAD_DIM, blo...  8.86 us
    pallas_call x1, Pallas kernels, on_device(): vmem_call(conv_backward_kernel, 0, 5, (jax.ShapeDtypeStruct((HEAD_DIM, bl...  8.68 us
    ppermute x2, starting transfers between devices, passed_along(): return lax.ppermute(block, axis, route)  7.04 us
  transfers between devices with their start and end apart: 9, of which 5 were waited for; matrix products, arithmetic and copies ran while one was open for 6% of the time, Pallas kernels for 0%

profile of v21, /device:TPU:9, one launch (start us, length us, event | category | flops | bytes accessed | tf_op | source)
XLA Modules:
  0.0 149.3 jit_solution(9199173288231873324)
XLA Ops:
  0.6 1.1 copy.49
  1.8 1.1 copy.50
  2.9 1.1 copy.51
  4.1 0.9 copy.52
  5.1 10.0 %all-to-all-start = ((bf16[128,16,192]{0,2,1:T(8,128)(2,1)}), bf16[128,16,192]{0,2,1:T(8,128)(2,1)S(1)}, u32[]{:S(2)}, u32[]{:S(2)}) async-start(bf16[128,16,192]{0,2,1:T(8,128)(2,1)} %bitcast.5), calls=%async_computation | async-start | bytes 1572864 | tf_op jit(solution)/shard_map/all_to_all | solution.py:248
  15.4 0.2 select_reduce_fusion
  15.7 0.5 slice.78
  16.2 0.2 convert_reduce_fusion
  16.5 0.6 and_select_fusion.kseg_ref
  17.1 20.3 %all-to-all-done = bf16[128,16,192]{0,2,1:T(8,128)(2,1)S(1)} async-done(((bf16[128,16,192]{0,2,1:T(8,128)(2,1)}), bf16[128,16,192]{0,2,1:T(8,128)(2,1)S(1)}, u32[]{:S(2)}, u32[]{:S(2)}) %all-to-all-start) | async-done | bytes 786464 | tf_op jit(solution)/shard_map/all_to_all | solution.py:248
  37.4 0.5 copy.53
  37.9 0.3 reshape.97
  38.3 0.8 slice_bitcast_fusion.2
  39.1 6.9 %collective-permute-start = (bf16[1024,128]{0,1:T(8,128)(2,1)S(1)}, bf16[1024,128]{0,1:T(8,128)(2,1)S(1)}, u32[]{:S(2)}, u32[]{:S(2)}) collective-permute-start(bf16[1024,128]{0,1:T(8,128)(2,1)S(1)} %get-tuple-element.54), channel_id=1, source_target_pairs={{0,1},{1,2},{2,3},{3,4},{4,5},{5,6},{6,7},{7,8},{8,9},{9,10},{10,1... | collective-permute-start | bytes 786440 | tf_op jit(solution)/shard_map/ppermute | solution.py:18
  46.0 1.9 %collective-permute-start.1 = (bf16[1024,128]{0,1:T(8,128)(2,1)S(1)}, bf16[1024,128]{0,1:T(8,128)(2,1)S(1)}, u32[]{:S(2)}, u32[]{:S(2)}) collective-permute-start(bf16[1024,128]{0,1:T(8,128)(2,1)S(1)} %get-tuple-element.55), channel_id=1, source_target_pairs={{1,0},{2,1},{3,2},{4,3},{5,4},{6,5},{7,6},{8,7},{9,8},{10,9},{11,1... | collective-permute-start | bytes 786440 | tf_op jit(solution)/shard_map/ppermute | solution.py:21
  47.9 0.7 broadcast_minimum_fusion
  48.8 1.4 copy.56.qseg_ref
  50.1 0.6 maximum_minimum_fusion
  50.7 0.3 copy.63
  51.0 0.9 concatenate.24.clone.q_ref
  51.9 2.7 %collective-permute-done.1 = bf16[1024,128]{0,1:T(8,128)(2,1)S(1)} collective-permute-done((bf16[1024,128]{0,1:T(8,128)(2,1)S(1)}, bf16[1024,128]{0,1:T(8,128)(2,1)S(1)}, u32[]{:S(2)}, u32[]{:S(2)}) %collective-permute-start.1) | collective-permute-done | bytes 262176 | tf_op jit(solution)/shard_map/ppermute | solution.py:21
  54.7 1.3 copy.55.kv_ref
  56.0 17.0 %shard_map.102 = (bf16[64,2048]{1,0:T(8,128)(2,1)}, f32[2048,1]{1,0:T(8,128)}) custom-call(s32[4]{0:T(128)} %get-tuple-element.43.lo_ref, s32[4]{0:T(128)} %get-tuple-element.42.hi_ref, bf16[2048,128]{1,0:T(8,128)(2,1)} %concatenate.24.clone.q_ref, bf16[4096,128]{1,0:T(8,128)(2,1)} %copy.55.kv_ref, s32[2048,1]{1,0:T(8,128)} %copy.56.qseg_ref, ...), custom_call_target="tpu_custom_call" | custom-call | tf_op jit(solution)/shard_map/pallas_call | solution.py:282
  73.0 0.8 fusion.9
  73.8 1.9 %collective-permute-start.3 = (bf16[64,15]{1,0:T(8,128)(2,1)S(1)}, bf16[64,15]{1,0:T(8,128)(2,1)S(1)}, u32[]{:S(2)}, u32[]{:S(2)}) collective-permute-start(bf16[64,15]{1,0:T(8,128)(2,1)S(1)} %get-tuple-element.56), channel_id=1, source_target_pairs={{1,0},{2,1},{3,2},{4,3},{5,4},{6,5},{7,6},{8,7},{9,8},{10,9},{11,1... | collective-permute-start | bytes 5768 | tf_op jit(solution)/shard_map/ppermute | solution.py:234
  75.7 4.7 %collective-permute-start.2 = (bf16[64,15]{1,0:T(8,128)(2,1)S(1)}, bf16[64,15]{1,0:T(8,128)(2,1)S(1)}, u32[]{:S(2)}, u32[]{:S(2)}) collective-permute-start(bf16[64,15]{1,0:T(8,128)(2,1)S(1)} %get-tuple-element.57), channel_id=1, source_target_pairs={{0,1},{1,2},{2,3},{3,4},{4,5},{5,6},{6,7},{7,8},{8,9},{9,10},{10,1... | collective-permute-start | bytes 5768 | tf_op jit(solution)/shard_map/ppermute | solution.py:233
  80.4 0.6 fusion.2
  81.0 0.7 copy.57
  81.7 0.7 copy.58.gain_ref
  82.5 1.8 %concatenate.27.x_ref = f32[64,2304]{1,0:T(8,128)} concatenate(f32[64,113]{1,0:T(8,128)S(1)} %broadcast.102, bf16[64,15]{1,0:T(8,128)(2,1)S(1)} %collective-permute-done.2, bf16[64,2048]{1,0:T(8,128)(2,1)} %get-tuple-element.14.att_ref, bf16[64,15]{1,0:T(8,128)(2,1)S(1)} %collective-permute-done.3, f32[64,113]{1,0:T(8,128)S(1)} %broadcast.102), dimensions={1} | concatenate | bytes 913664 | tf_op jit(solution)/shard_map/concatenate | solution.py:236
  84.3 8.9 %shard_map.103 = (bf16[64,2048]{1,0:T(8,128)(2,1)}, f32[64,2048]{1,0:T(8,128)}) custom-call(f32[64,2304]{1,0:T(8,128)} %concatenate.27.x_ref, f32[64,31]{1,0:T(8,128)} %bitcast.30, f32[64,1]{1,0:T(8,128)} %copy.58.gain_ref, bf16[64,2048]{1,0:T(8,128)(2,1)} %cot_ref.1, s32[1,2048]{1,0:T(1,128)} %get-tuple-element.59.lo_ref, s32[1,2048]{1,0:T(1,128)} %get-tuple-element.58.hi_ref), custom_call_target="tpu_custom_call" | custom-call | tf_op jit(solution)/shard_map/pallas_call | solution.py:296
  93.2 0.8 fusion.8
  94.0 1.9 %collective-permute-start.5 = (f32[64,15]{1,0:T(8,128)S(1)}, f32[64,15]{1,0:T(8,128)S(1)}, u32[]{:S(2)}, u32[]{:S(2)}) collective-permute-start(f32[64,15]{1,0:T(8,128)S(1)} %get-tuple-element.52), channel_id=1, source_target_pairs={{1,0},{2,1},{3,2},{4,3},{5,4},{6,5},{7,6},{8,7},{9,8},{10,9},{11,1... | collective-permute-start | bytes 11528 | tf_op jit(solution)/shard_map/ppermute | solution.py:234
  95.9 4.8 %collective-permute-start.4 = (f32[64,15]{1,0:T(8,128)S(1)}, f32[64,15]{1,0:T(8,128)S(1)}, u32[]{:S(2)}, u32[]{:S(2)}) collective-permute-start(f32[64,15]{1,0:T(8,128)S(1)} %get-tuple-element.53), channel_id=1, source_target_pairs={{0,1},{1,2},{2,3},{3,4},{4,5},{5,6},{6,7},{7,8},{8,9},{9,10},{10,1... | collective-permute-start | bytes 11528 | tf_op jit(solution)/shard_map/ppermute | solution.py:233
  100.7 0.8 collective-permute-done.4
  101.5 1.9 %concatenate.28.y_ref = f32[64,2304]{1,0:T(8,128)} concatenate(f32[64,113]{1,0:T(8,128)S(1)} %broadcast.102, f32[64,15]{1,0:T(8,128)S(1)} %collective-permute-done.4, f32[64,2048]{1,0:T(8,128)} %get-tuple-element.16, f32[64,15]{1,0:T(8,128)S(1)} %collective-permute-done.5, f32[64,113]{1,0:T(8,128)S(1)} %broadcast.102), dimensions={1} | concatenate | bytes 1179648 | tf_op jit(solution)/shard_map/concatenate | solution.py:236
  103.4 8.7 %shard_map.104 = (bf16[64,2048]{1,0:T(8,128)(2,1)}, bf16[2048,128]{1,0:T(8,128)(2,1)}, f32[2048,1]{1,0:T(8,128)}) custom-call(f32[64,2304]{1,0:T(8,128)} %concatenate.28.y_ref, f32[64,31]{1,0:T(8,128)} %bitcast.31, bf16[64,2048]{1,0:T(8,128)(2,1)} %get-tuple-element.14.att_ref, s32[1,2048]{1,0:T(1,128)} %get-tuple-element.59.lo_ref, ...), custom_call_target="tpu_custom_call" | custom-call | tf_op jit(solution)/shard_map/pallas_call | solution.py:305
  112.1 19.7 %shard_map.105 = (bf16[2048,64]{1,0:T(8,128)(2,1)}, f32[64,4096]{1,0:T(8,128)}, f32[64,4096]{1,0:T(8,128)}) custom-call(s32[4]{0:T(128)} %get-tuple-element.43.lo_ref, s32[4]{0:T(128)} %get-tuple-element.42.hi_ref, bf16[2048,128]{1,0:T(8,128)(2,1)} %concatenate.24.clone.q_ref, bf16[4096,128]{1,0:T(8,128)(2,1)} %copy.55.kv_ref, ...), custom_call_target="tpu_custom_call" | custom-call | tf_op jit(solution)/shard_map/pallas_call | solution.py:317
  131.8 1.4 constant_dynamic-update-slice_fusion.1
  133.2 0.1 copy-done
  133.4 0.1 convert.9
  133.6 5.1 %collective-permute-start.6 = (bf16[128,1024]{1,0:T(8,128)(2,1)S(1)}, bf16[128,1024]{1,0:T(8,128)(2,1)S(1)}, u32[]{:S(2)}, u32[]{:S(2)}) collective-permute-start(bf16[128,1024]{1,0:T(8,128)(2,1)S(1)} %get-tuple-element.44), channel_id=1, source_target_pairs={{0,1},{1,2},{2,3},{3,4},{4,5},{5,6},{6,7},{7,8},{8,9},{9,10},{10,1... | collective-permute-start | bytes 786440 | tf_op jit(solution)/shard_map/ppermute | solution.py:29
  138.7 1.9 %collective-permute-start.7 = (bf16[128,1024]{1,0:T(8,128)(2,1)S(1)}, bf16[128,1024]{1,0:T(8,128)(2,1)}, u32[]{:S(2)}, u32[]{:S(2)}) collective-permute-start(bf16[128,1024]{1,0:T(8,128)(2,1)S(1)} %get-tuple-element.45), channel_id=1, source_target_pairs={{1,0},{2,1},{3,2},{4,3},{5,4},{6,5},{7,6},{8,7},{9,8},{10,9},{11,1... | collective-permute-start | bytes 786440 | tf_op jit(solution)/shard_map/ppermute | solution.py:29
  140.7 0.9 copy.62
  141.6 0.5 collective-permute-done.6
  142.1 5.4 %collective-permute-done.7 = bf16[128,1024]{1,0:T(8,128)(2,1)} collective-permute-done((bf16[128,1024]{1,0:T(8,128)(2,1)S(1)}, bf16[128,1024]{1,0:T(8,128)(2,1)}, u32[]{:S(2)}, u32[]{:S(2)}) %collective-permute-start.7) | collective-permute-done | bytes 262176 | tf_op jit(solution)/shard_map/ppermute | solution.py:29
  147.4 1.1 fusion
  148.5 0.8 fusion.7
  (29 shorter events, 0.8 us)
Async XLA Ops:
  4.0 11.1 %copy-start.3 = (s32[64]{0:T(128)S(1)}, s32[64]{0:T(128)}, u32[]{:S(2)}) copy-start(s32[64]{0:T(128)} %param.10) | copy-start | bytes 772
  5.1 32.3 %all-to-all-start = ((bf16[128,16,192]{0,2,1:T(8,128)(2,1)}), bf16[128,16,192]{0,2,1:T(8,128)(2,1)S(1)}, u32[]{:S(2)}, u32[]{:S(2)}) async-start(bf16[128,16,192]{0,2,1:T(8,128)(2,1)} %bitcast.5), calls=%async_computation | async-start | bytes 1572864 | tf_op jit(solution)/shard_map/all_to_all | solution.py:248
  39.1 12.8 %collective-permute-start = (bf16[1024,128]{0,1:T(8,128)(2,1)S(1)}, bf16[1024,128]{0,1:T(8,128)(2,1)S(1)}, u32[]{:S(2)}, u32[]{:S(2)}) collective-permute-start(bf16[1024,128]{0,1:T(8,128)(2,1)S(1)} %get-tuple-element.54), channel_id=1, source_target_pairs={{0,1},{1,2},{2,3},{3,4},{4,5},{5,6},{6,7},{7,8},{8,9},{9,10},{10,1... | collective-permute-start | bytes 786440 | tf_op jit(solution)/shard_map/ppermute | solution.py:18
  46.0 8.6 %collective-permute-start.1 = (bf16[1024,128]{0,1:T(8,128)(2,1)S(1)}, bf16[1024,128]{0,1:T(8,128)(2,1)S(1)}, u32[]{:S(2)}, u32[]{:S(2)}) collective-permute-start(bf16[1024,128]{0,1:T(8,128)(2,1)S(1)} %get-tuple-element.55), channel_id=1, source_target_pairs={{1,0},{2,1},{3,2},{4,3},{5,4},{6,5},{7,6},{8,7},{9,8},{10,9},{11,1... | collective-permute-start | bytes 786440 | tf_op jit(solution)/shard_map/ppermute | solution.py:21
  54.7 26.4 %copy-start.2 = (f32[31,64]{1,0:T(8,128)S(1)}, f32[31,64]{1,0:T(8,128)}, u32[]{:S(2)}) copy-start(f32[31,64]{1,0:T(8,128)} %param.11) | copy-start | bytes 23812
  54.7 27.1 %copy-start.4 = (f32[64]{0:T(128)S(1)}, f32[64]{0:T(128)}, u32[]{:S(2)}) copy-start(f32[64]{0:T(128)} %param.12) | copy-start | bytes 772
  73.8 8.7 %collective-permute-start.3 = (bf16[64,15]{1,0:T(8,128)(2,1)S(1)}, bf16[64,15]{1,0:T(8,128)(2,1)S(1)}, u32[]{:S(2)}, u32[]{:S(2)}) collective-permute-start(bf16[64,15]{1,0:T(8,128)(2,1)S(1)} %get-tuple-element.56), channel_id=1, source_target_pairs={{1,0},{2,1},{3,2},{4,3},{5,4},{6,5},{7,6},{8,7},{9,8},{10,9},{11,1... | collective-permute-start | bytes 5768 | tf_op jit(solution)/shard_map/ppermute | solution.py:234
  75.7 6.8 %collective-permute-start.2 = (bf16[64,15]{1,0:T(8,128)(2,1)S(1)}, bf16[64,15]{1,0:T(8,128)(2,1)S(1)}, u32[]{:S(2)}, u32[]{:S(2)}) collective-permute-start(bf16[64,15]{1,0:T(8,128)(2,1)S(1)} %get-tuple-element.57), channel_id=1, source_target_pairs={{0,1},{1,2},{2,3},{3,4},{4,5},{5,6},{6,7},{7,8},{8,9},{9,10},{10,1... | collective-permute-start | bytes 5768 | tf_op jit(solution)/shard_map/ppermute | solution.py:233
  94.0 6.7 %collective-permute-start.5 = (f32[64,15]{1,0:T(8,128)S(1)}, f32[64,15]{1,0:T(8,128)S(1)}, u32[]{:S(2)}, u32[]{:S(2)}) collective-permute-start(f32[64,15]{1,0:T(8,128)S(1)} %get-tuple-element.52), channel_id=1, source_target_pairs={{1,0},{2,1},{3,2},{4,3},{5,4},{6,5},{7,6},{8,7},{9,8},{10,9},{11,1... | collective-permute-start | bytes 11528 | tf_op jit(solution)/shard_map/ppermute | solution.py:234
  95.9 5.6 %collective-permute-start.4 = (f32[64,15]{1,0:T(8,128)S(1)}, f32[64,15]{1,0:T(8,128)S(1)}, u32[]{:S(2)}, u32[]{:S(2)}) collective-permute-start(f32[64,15]{1,0:T(8,128)S(1)} %get-tuple-element.53), channel_id=1, source_target_pairs={{0,1},{1,2},{2,3},{3,4},{4,5},{5,6},{6,7},{7,8},{8,9},{9,10},{10,1... | collective-permute-start | bytes 11528 | tf_op jit(solution)/shard_map/ppermute | solution.py:233
  131.8 1.5 %copy-start = (f32[64,4096]{1,0:T(8,128)S(1)}, f32[64,4096]{1,0:T(8,128)}, u32[]{:S(2)}) copy-start(f32[64,4096]{1,0:T(8,128)} %get-tuple-element.23) | copy-start | bytes 3145732
  133.4 7.2 %copy-start.1 = (bf16[2048,64]{1,0:T(8,128)(2,1)S(1)}, bf16[2048,64]{1,0:T(8,128)(2,1)}, u32[]{:S(2)}) copy-start(bf16[2048,64]{1,0:T(8,128)(2,1)} %get-tuple-element.21) | copy-start | bytes 786436
  133.6 8.5 %collective-permute-start.6 = (bf16[128,1024]{1,0:T(8,128)(2,1)S(1)}, bf16[128,1024]{1,0:T(8,128)(2,1)S(1)}, u32[]{:S(2)}, u32[]{:S(2)}) collective-permute-start(bf16[128,1024]{1,0:T(8,128)(2,1)S(1)} %get-tuple-element.44), channel_id=1, source_target_pairs={{0,1},{1,2},{2,3},{3,4},{4,5},{5,6},{6,7},{7,8},{8,9},{9,10},{10,1... | collective-permute-start | bytes 786440 | tf_op jit(solution)/shard_map/ppermute | solution.py:29
  138.7 8.7 %collective-permute-start.7 = (bf16[128,1024]{1,0:T(8,128)(2,1)S(1)}, bf16[128,1024]{1,0:T(8,128)(2,1)}, u32[]{:S(2)}, u32[]{:S(2)}) collective-permute-start(bf16[128,1024]{1,0:T(8,128)(2,1)S(1)} %get-tuple-element.45), channel_id=1, source_target_pairs={{1,0},{2,1},{3,2},{4,3},{5,4},{6,5},{7,6},{8,7},{9,8},{10,9},{11,1... | collective-permute-start | bytes 786440 | tf_op jit(solution)/shard_map/ppermute | solution.py:29

commit v22 on v17

--- a/solution.py
+++ b/solution.py
@@ -58,13 +58,14 @@
 TN = (((0,), (0,)), ((), ()))
 
 
-def forward_kernel(lo_ref, hi_ref, q_ref, kv_ref, qseg_ref, kseg_ref, o_ref, lse_ref):
+def forward_kernel(lo_ref, hi_ref, q_ref, kv_ref, kseg_ref, o_ref, lse_ref):
     scale = HEAD_DIM ** (-0.5)
 
     def q_body(i, carry):
         r0 = pl.multiple_of(i * TILE_Q, TILE_Q)
         q = q_ref[pl.ds(r0, TILE_Q), :] * jnp.asarray(scale, q_ref.dtype)
-        qs = qseg_ref[pl.ds(r0, TILE_Q), :]
+        q_off = (kseg_ref.shape[1] - q_ref.shape[0]) // 2
+        qs = jnp.broadcast_to(kseg_ref[:, pl.ds(q_off + r0, TILE_Q)], (8, TILE_Q)).T[:, :1]
 
         def k_body(j, c):
             m, l, acc = c
@@ -96,7 +97,7 @@
 
 
 def backward_kernel(
-    lo_ref, hi_ref, q_ref, kv_ref, do_ref, qt_ref, dot_ref, qseg_ref, kseg_ref, lse_ref,
+    lo_ref, hi_ref, q_ref, kv_ref, do_ref, qt_ref, dot_ref, kseg_ref, lse_ref,
     d_ref, dq_ref, dk_ref, dv_ref,
 ):
     scale = HEAD_DIM ** (-0.5)
@@ -107,7 +108,8 @@
         r0 = pl.multiple_of(i * TILE_Q, TILE_Q)
         q = q_ref[pl.ds(r0, TILE_Q), :] * jnp.asarray(scale, q_ref.dtype)
         do = do_ref[pl.ds(r0, TILE_Q), :]
-        qs = qseg_ref[pl.ds(r0, TILE_Q), :]
+        q_off = (kseg_ref.shape[1] - q_ref.shape[0]) // 2
+        qs = jnp.broadcast_to(kseg_ref[:, pl.ds(q_off + r0, TILE_Q)], (8, TILE_Q)).T[:, :1]
         lse = lse_ref[pl.ds(r0, TILE_Q), :]
         dlt = d_ref[pl.ds(r0, TILE_Q), :]
         q_t = qt_ref[:, pl.ds(r0, TILE_Q)]
@@ -280,12 +282,12 @@
     att_t, lse_col = vmem_call(
         forward_kernel,
         2,
-        4,
+        3,
         (
             jax.ShapeDtypeStruct((HEAD_DIM, block_rows), jnp.bfloat16),
             jax.ShapeDtypeStruct((block_rows, 1), jnp.float32),
         ),
-    )(lo_t, hi_t, q_wide, near_pairs, qseg_col, kseg_row)
+    )(lo_t, hi_t, q_wide, near_pairs, kseg_row)
     frame_at = first_frame + jnp.arange(block_rows, dtype=jnp.int32)
     seg_start, seg_end = segment_bounds(lengths, frame_at)
     lo_off = (seg_start - frame_at)[None, :].astype(jnp.int32)
@@ -315,7 +317,7 @@
     grad_q, dk_t, dv_t = vmem_call(
         backward_kernel,
         2,
-        9,
+        8,
         (
             jax.ShapeDtypeStruct((block_rows, HEAD_DIM), jnp.bfloat16),
             jax.ShapeDtypeStruct((HEAD_DIM, ext_rows), jnp.float32),
@@ -329,7 +331,6 @@
         grad_wide,
         local_q.T,
         grad_att_t,
-        qseg_col,
         kseg_row,
         lse_col,
         row_delta,

time: 147 us -> 149 us (1.014); the launches traced: 145 us -> 148 us
  Pallas kernels: 50.7 us -> 54.4 us
    pallas_call x2, Pallas kernels: 33.2 us -> 36.9 us  [the longest x1 19.9 us: on_device(): vmem_call(backward_kernel, 2, 8, (jax.ShapeDtypeStruct((block_rows, HEAD_...]
  transfers between devices with their start and end apart: 9 -> 9, of which waited for: 5 -> 5; matrix products, arithmetic and copies ran while one was open for 6% -> 5% of each run, Pallas kernels for 0% -> 0%
where the time goes in v22:
time: 149 us; the launch traced here: 148 us
  Pallas kernels  54.4 us (37%)
  starting transfers between devices  38 us (26%)
  waiting for transfers between devices  31 us (21%)
  local copies, waits for them, and re-layouts  19.6 us (13%)
  other arithmetic  4.53 us (3%)
    all_to_all x1, waiting for transfers between devices, on_device(): lax.all_to_all(stacked, 'uly', split_axis=1, concat_axis=0, tiled=True)  20.3 us
    pallas_call x1, Pallas kernels, on_device(): vmem_call(backward_kernel, 2, 8, (jax.ShapeDtypeStruct((block_rows, HEAD_...  19.9 us
    pallas_call x1, Pallas kernels, on_device(): vmem_call(forward_kernel, 2, 3, (jax.ShapeDtypeStruct((HEAD_DIM, block_ro...  17 us
    all_to_all x1, starting transfers between devices, on_device(): lax.all_to_all(stacked, 'uly', split_axis=1, concat_axis=0, tiled=True)  10 us
    ppermute x2, starting transfers between devices, padded_rims(): low = lax.ppermute(block[:, block.shape[1] - half:], 'blk', forward)  9.26 us
    pallas_call x1, Pallas kernels, on_device(): vmem_call(conv_forward_kernel, 0, 6, (jax.ShapeDtypeStruct((HEAD_DIM, blo...  8.85 us
    pallas_call x1, Pallas kernels, on_device(): vmem_call(conv_backward_kernel, 0, 5, (jax.ShapeDtypeStruct((HEAD_DIM, bl...  8.65 us
    ppermute x1, starting transfers between devices, extended(): lax.ppermute(lax.slice_in_dim(block, block.shape[dim] - width, None, axis...  6.87 us
  transfers between devices with their start and end apart: 9, of which 5 were waited for; matrix products, arithmetic and copies ran while one was open for 5% of the time, Pallas kernels for 0%

profile of v22, /device:TPU:9, one launch (start us, length us, event | category | flops | bytes accessed | tf_op | source)
XLA Modules:
  0.0 148.4 jit_solution(13633420163214497390)
XLA Ops:
  0.6 1.1 copy.45
  1.8 1.1 copy.46
  2.9 1.1 copy.47
  4.1 0.9 copy.48
  5.1 10.0 %all-to-all-start = ((bf16[128,16,192]{0,2,1:T(8,128)(2,1)}), bf16[128,16,192]{0,2,1:T(8,128)(2,1)S(1)}, u32[]{:S(2)}, u32[]{:S(2)}) async-start(bf16[128,16,192]{0,2,1:T(8,128)(2,1)} %bitcast.5), calls=%async_computation | async-start | bytes 1572864 | tf_op jit(solution)/shard_map/all_to_all | solution.py:248
  15.3 0.5 slice.74
  15.8 0.1 reduce
  16.0 0.2 convert_reduce_fusion
  16.2 0.2 select_reduce_fusion
  16.4 0.6 and_select_fusion.kseg_ref
  17.1 20.3 %all-to-all-done = bf16[128,16,192]{0,2,1:T(8,128)(2,1)S(1)} async-done(((bf16[128,16,192]{0,2,1:T(8,128)(2,1)}), bf16[128,16,192]{0,2,1:T(8,128)(2,1)S(1)}, u32[]{:S(2)}, u32[]{:S(2)}) %all-to-all-start) | async-done | bytes 786464 | tf_op jit(solution)/shard_map/all_to_all | solution.py:248
  37.4 0.5 copy.49
  37.9 0.3 reshape.97
  38.3 0.8 slice_bitcast_fusion.2
  39.1 6.9 %collective-permute-start = (bf16[1024,128]{0,1:T(8,128)(2,1)S(1)}, bf16[1024,128]{0,1:T(8,128)(2,1)S(1)}, u32[]{:S(2)}, u32[]{:S(2)}) collective-permute-start(bf16[1024,128]{0,1:T(8,128)(2,1)S(1)} %get-tuple-element.54), channel_id=1, source_target_pairs={{0,1},{1,2},{2,3},{3,4},{4,5},{5,6},{6,7},{7,8},{8,9},{9,10},{10,1... | collective-permute-start | bytes 786440 | tf_op jit(solution)/shard_map/ppermute | solution.py:18
  46.0 1.9 %collective-permute-start.1 = (bf16[1024,128]{0,1:T(8,128)(2,1)S(1)}, bf16[1024,128]{0,1:T(8,128)(2,1)S(1)}, u32[]{:S(2)}, u32[]{:S(2)}) collective-permute-start(bf16[1024,128]{0,1:T(8,128)(2,1)S(1)} %get-tuple-element.55), channel_id=1, source_target_pairs={{1,0},{2,1},{3,2},{4,3},{5,4},{6,5},{7,6},{8,7},{9,8},{10,9},{11,1... | collective-permute-start | bytes 786440 | tf_op jit(solution)/shard_map/ppermute | solution.py:21
  47.9 0.7 broadcast_minimum_fusion
  48.8 0.6 maximum_minimum_fusion
  49.4 0.3 copy.57
  49.7 0.9 concatenate.24.clone.q_ref
  50.6 4.0 %collective-permute-done.1 = bf16[1024,128]{0,1:T(8,128)(2,1)S(1)} collective-permute-done((bf16[1024,128]{0,1:T(8,128)(2,1)S(1)}, bf16[1024,128]{0,1:T(8,128)(2,1)S(1)}, u32[]{:S(2)}, u32[]{:S(2)}) %collective-permute-start.1) | collective-permute-done | bytes 262176 | tf_op jit(solution)/shard_map/ppermute | solution.py:21
  54.7 1.3 copy.51.kv_ref
  56.0 17.0 %shard_map.102 = (bf16[64,2048]{1,0:T(8,128)(2,1)}, f32[2048,1]{1,0:T(8,128)}) custom-call(s32[4]{0:T(128)} %get-tuple-element.43.lo_ref, s32[4]{0:T(128)} %get-tuple-element.42.hi_ref, bf16[2048,128]{1,0:T(8,128)(2,1)} %concatenate.24.clone.q_ref, bf16[4096,128]{1,0:T(8,128)(2,1)} %copy.51.kv_ref, s32[1,4096]{1,0:T(1,128)} %and_select_fusion.kseg_ref), custom_call_target="tpu_custom_call" | custom-call | tf_op jit(solution)/shard_map/pallas_call | solution.py:282
  73.0 0.8 fusion.9
  73.8 1.9 %collective-permute-start.3 = (bf16[64,15]{1,0:T(8,128)(2,1)S(1)}, bf16[64,15]{1,0:T(8,128)(2,1)S(1)}, u32[]{:S(2)}, u32[]{:S(2)}) collective-permute-start(bf16[64,15]{1,0:T(8,128)(2,1)S(1)} %get-tuple-element.56), channel_id=1, source_target_pairs={{1,0},{2,1},{3,2},{4,3},{5,4},{6,5},{7,6},{8,7},{9,8},{10,9},{11,1... | collective-permute-start | bytes 5768 | tf_op jit(solution)/shard_map/ppermute | solution.py:234
  75.7 4.5 %collective-permute-start.2 = (bf16[64,15]{1,0:T(8,128)(2,1)S(1)}, bf16[64,15]{1,0:T(8,128)(2,1)S(1)}, u32[]{:S(2)}, u32[]{:S(2)}) collective-permute-start(bf16[64,15]{1,0:T(8,128)(2,1)S(1)} %get-tuple-element.57), channel_id=1, source_target_pairs={{0,1},{1,2},{2,3},{3,4},{4,5},{5,6},{6,7},{7,8},{8,9},{9,10},{10,1... | collective-permute-start | bytes 5768 | tf_op jit(solution)/shard_map/ppermute | solution.py:233
  80.3 0.6 fusion.2
  80.9 0.7 copy.52
  81.6 0.7 copy.53.gain_ref
  82.3 1.9 %concatenate.27.x_ref = f32[64,2304]{1,0:T(8,128)} concatenate(f32[64,113]{1,0:T(8,128)S(1)} %broadcast.102, bf16[64,15]{1,0:T(8,128)(2,1)S(1)} %collective-permute-done.2, bf16[64,2048]{1,0:T(8,128)(2,1)} %get-tuple-element.14.att_ref, bf16[64,15]{1,0:T(8,128)(2,1)S(1)} %collective-permute-done.3, f32[64,113]{1,0:T(8,128)S(1)} %broadcast.102), dimensions={1} | concatenate | bytes 913664 | tf_op jit(solution)/shard_map/concatenate | solution.py:236
  84.2 8.9 %shard_map.103 = (bf16[64,2048]{1,0:T(8,128)(2,1)}, f32[64,2048]{1,0:T(8,128)}) custom-call(f32[64,2304]{1,0:T(8,128)} %concatenate.27.x_ref, f32[64,31]{1,0:T(8,128)} %bitcast.29, f32[64,1]{1,0:T(8,128)} %copy.53.gain_ref, bf16[64,2048]{1,0:T(8,128)(2,1)} %cot_ref.1, s32[1,2048]{1,0:T(1,128)} %get-tuple-element.59.lo_ref, s32[1,2048]{1,0:T(1,128)} %get-tuple-element.58.hi_ref), custom_call_target="tpu_custom_call" | custom-call | tf_op jit(solution)/shard_map/pallas_call | solution.py:296
  93.0 0.8 fusion.8
  93.9 1.9 %collective-permute-start.5 = (f32[64,15]{1,0:T(8,128)S(1)}, f32[64,15]{1,0:T(8,128)S(1)}, u32[]{:S(2)}, u32[]{:S(2)}) collective-permute-start(f32[64,15]{1,0:T(8,128)S(1)} %get-tuple-element.52), channel_id=1, source_target_pairs={{1,0},{2,1},{3,2},{4,3},{5,4},{6,5},{7,6},{8,7},{9,8},{10,9},{11,1... | collective-permute-start | bytes 11528 | tf_op jit(solution)/shard_map/ppermute | solution.py:234
  95.8 4.7 %collective-permute-start.4 = (f32[64,15]{1,0:T(8,128)S(1)}, f32[64,15]{1,0:T(8,128)S(1)}, u32[]{:S(2)}, u32[]{:S(2)}) collective-permute-start(f32[64,15]{1,0:T(8,128)S(1)} %get-tuple-element.53), channel_id=1, source_target_pairs={{0,1},{1,2},{2,3},{3,4},{4,5},{5,6},{6,7},{7,8},{8,9},{9,10},{10,1... | collective-permute-start | bytes 11528 | tf_op jit(solution)/shard_map/ppermute | solution.py:233
  100.5 0.8 collective-permute-done.4
  101.4 1.9 %concatenate.28.y_ref = f32[64,2304]{1,0:T(8,128)} concatenate(f32[64,113]{1,0:T(8,128)S(1)} %broadcast.102, f32[64,15]{1,0:T(8,128)S(1)} %collective-permute-done.4, f32[64,2048]{1,0:T(8,128)} %get-tuple-element.16, f32[64,15]{1,0:T(8,128)S(1)} %collective-permute-done.5, f32[64,113]{1,0:T(8,128)S(1)} %broadcast.102), dimensions={1} | concatenate | bytes 1179648 | tf_op jit(solution)/shard_map/concatenate | solution.py:236
  103.3 8.7 %shard_map.104 = (bf16[64,2048]{1,0:T(8,128)(2,1)}, bf16[2048,128]{1,0:T(8,128)(2,1)}, f32[2048,1]{1,0:T(8,128)}) custom-call(f32[64,2304]{1,0:T(8,128)} %concatenate.28.y_ref, f32[64,31]{1,0:T(8,128)} %bitcast.30, bf16[64,2048]{1,0:T(8,128)(2,1)} %get-tuple-element.14.att_ref, s32[1,2048]{1,0:T(1,128)} %get-tuple-element.59.lo_ref, ...), custom_call_target="tpu_custom_call" | custom-call | tf_op jit(solution)/shard_map/pallas_call | solution.py:305
  112.0 19.9 %shard_map.105 = (bf16[2048,64]{1,0:T(8,128)(2,1)}, f32[64,4096]{1,0:T(8,128)}, f32[64,4096]{1,0:T(8,128)}) custom-call(s32[4]{0:T(128)} %get-tuple-element.43.lo_ref, s32[4]{0:T(128)} %get-tuple-element.42.hi_ref, bf16[2048,128]{1,0:T(8,128)(2,1)} %concatenate.24.clone.q_ref, bf16[4096,128]{1,0:T(8,128)(2,1)} %copy.51.kv_ref, ...), custom_call_target="tpu_custom_call" | custom-call | tf_op jit(solution)/shard_map/pallas_call | solution.py:317
  131.8 1.4 constant_dynamic-update-slice_fusion.1
  133.2 0.1 copy-done
  133.4 0.1 convert.9
  133.6 4.2 %collective-permute-start.6 = (bf16[128,1024]{1,0:T(8,128)(2,1)S(1)}, bf16[128,1024]{1,0:T(8,128)(2,1)S(1)}, u32[]{:S(2)}, u32[]{:S(2)}) collective-permute-start(bf16[128,1024]{1,0:T(8,128)(2,1)S(1)} %get-tuple-element.44), channel_id=1, source_target_pairs={{0,1},{1,2},{2,3},{3,4},{4,5},{5,6},{6,7},{7,8},{8,9},{9,10},{10,1... | collective-permute-start | bytes 786440 | tf_op jit(solution)/shard_map/ppermute | solution.py:29
  137.8 1.9 %collective-permute-start.7 = (bf16[128,1024]{1,0:T(8,128)(2,1)S(1)}, bf16[128,1024]{1,0:T(8,128)(2,1)}, u32[]{:S(2)}, u32[]{:S(2)}) collective-permute-start(bf16[128,1024]{1,0:T(8,128)(2,1)S(1)} %get-tuple-element.45), channel_id=1, source_target_pairs={{1,0},{2,1},{3,2},{4,3},{5,4},{6,5},{7,6},{8,7},{9,8},{10,9},{11,1... | collective-permute-start | bytes 786440 | tf_op jit(solution)/shard_map/ppermute | solution.py:29
  139.8 0.9 copy.56
  140.7 0.5 collective-permute-done.6
  141.2 5.4 %collective-permute-done.7 = bf16[128,1024]{1,0:T(8,128)(2,1)} collective-permute-done((bf16[128,1024]{1,0:T(8,128)(2,1)S(1)}, bf16[128,1024]{1,0:T(8,128)(2,1)}, u32[]{:S(2)}, u32[]{:S(2)}) %collective-permute-start.7) | collective-permute-done | bytes 262176 | tf_op jit(solution)/shard_map/ppermute | solution.py:29
  146.5 1.1 fusion
  147.6 0.8 fusion.7
  (27 shorter events, 0.7 us)
Async XLA Ops:
  4.0 11.1 %copy-start.3 = (s32[64]{0:T(128)S(1)}, s32[64]{0:T(128)}, u32[]{:S(2)}) copy-start(s32[64]{0:T(128)} %param.10) | copy-start | bytes 772
  5.1 32.3 %all-to-all-start = ((bf16[128,16,192]{0,2,1:T(8,128)(2,1)}), bf16[128,16,192]{0,2,1:T(8,128)(2,1)S(1)}, u32[]{:S(2)}, u32[]{:S(2)}) async-start(bf16[128,16,192]{0,2,1:T(8,128)(2,1)} %bitcast.5), calls=%async_computation | async-start | bytes 1572864 | tf_op jit(solution)/shard_map/all_to_all | solution.py:248
  39.1 11.5 %collective-permute-start = (bf16[1024,128]{0,1:T(8,128)(2,1)S(1)}, bf16[1024,128]{0,1:T(8,128)(2,1)S(1)}, u32[]{:S(2)}, u32[]{:S(2)}) collective-permute-start(bf16[1024,128]{0,1:T(8,128)(2,1)S(1)} %get-tuple-element.54), channel_id=1, source_target_pairs={{0,1},{1,2},{2,3},{3,4},{4,5},{5,6},{6,7},{7,8},{8,9},{9,10},{10,1... | collective-permute-start | bytes 786440 | tf_op jit(solution)/shard_map/ppermute | solution.py:18
  46.0 8.6 %collective-permute-start.1 = (bf16[1024,128]{0,1:T(8,128)(2,1)S(1)}, bf16[1024,128]{0,1:T(8,128)(2,1)S(1)}, u32[]{:S(2)}, u32[]{:S(2)}) collective-permute-start(bf16[1024,128]{0,1:T(8,128)(2,1)S(1)} %get-tuple-element.55), channel_id=1, source_target_pairs={{1,0},{2,1},{3,2},{4,3},{5,4},{6,5},{7,6},{8,7},{9,8},{10,9},{11,1... | collective-permute-start | bytes 786440 | tf_op jit(solution)/shard_map/ppermute | solution.py:21
  54.7 26.2 %copy-start.2 = (f32[31,64]{1,0:T(8,128)S(1)}, f32[31,64]{1,0:T(8,128)}, u32[]{:S(2)}) copy-start(f32[31,64]{1,0:T(8,128)} %param.11) | copy-start | bytes 23812
  54.7 26.9 %copy-start.4 = (f32[64]{0:T(128)S(1)}, f32[64]{0:T(128)}, u32[]{:S(2)}) copy-start(f32[64]{0:T(128)} %param.12) | copy-start | bytes 772
  73.8 8.5 %collective-permute-start.3 = (bf16[64,15]{1,0:T(8,128)(2,1)S(1)}, bf16[64,15]{1,0:T(8,128)(2,1)S(1)}, u32[]{:S(2)}, u32[]{:S(2)}) collective-permute-start(bf16[64,15]{1,0:T(8,128)(2,1)S(1)} %get-tuple-element.56), channel_id=1, source_target_pairs={{1,0},{2,1},{3,2},{4,3},{5,4},{6,5},{7,6},{8,7},{9,8},{10,9},{11,1... | collective-permute-start | bytes 5768 | tf_op jit(solution)/shard_map/ppermute | solution.py:234
  75.7 6.6 %collective-permute-start.2 = (bf16[64,15]{1,0:T(8,128)(2,1)S(1)}, bf16[64,15]{1,0:T(8,128)(2,1)S(1)}, u32[]{:S(2)}, u32[]{:S(2)}) collective-permute-start(bf16[64,15]{1,0:T(8,128)(2,1)S(1)} %get-tuple-element.57), channel_id=1, source_target_pairs={{0,1},{1,2},{2,3},{3,4},{4,5},{5,6},{6,7},{7,8},{8,9},{9,10},{10,1... | collective-permute-start | bytes 5768 | tf_op jit(solution)/shard_map/ppermute | solution.py:233
  93.9 6.7 %collective-permute-start.5 = (f32[64,15]{1,0:T(8,128)S(1)}, f32[64,15]{1,0:T(8,128)S(1)}, u32[]{:S(2)}, u32[]{:S(2)}) collective-permute-start(f32[64,15]{1,0:T(8,128)S(1)} %get-tuple-element.52), channel_id=1, source_target_pairs={{1,0},{2,1},{3,2},{4,3},{5,4},{6,5},{7,6},{8,7},{9,8},{10,9},{11,1... | collective-permute-start | bytes 11528 | tf_op jit(solution)/shard_map/ppermute | solution.py:234
  95.8 5.6 %collective-permute-start.4 = (f32[64,15]{1,0:T(8,128)S(1)}, f32[64,15]{1,0:T(8,128)S(1)}, u32[]{:S(2)}, u32[]{:S(2)}) collective-permute-start(f32[64,15]{1,0:T(8,128)S(1)} %get-tuple-element.53), channel_id=1, source_target_pairs={{0,1},{1,2},{2,3},{3,4},{4,5},{5,6},{6,7},{7,8},{8,9},{9,10},{10,1... | collective-permute-start | bytes 11528 | tf_op jit(solution)/shard_map/ppermute | solution.py:233
  131.8 1.5 %copy-start = (f32[64,4096]{1,0:T(8,128)S(1)}, f32[64,4096]{1,0:T(8,128)}, u32[]{:S(2)}) copy-start(f32[64,4096]{1,0:T(8,128)} %get-tuple-element.23) | copy-start | bytes 3145732
  133.4 6.3 %copy-start.1 = (bf16[2048,64]{1,0:T(8,128)(2,1)S(1)}, bf16[2048,64]{1,0:T(8,128)(2,1)}, u32[]{:S(2)}) copy-start(bf16[2048,64]{1,0:T(8,128)(2,1)} %get-tuple-element.21) | copy-start | bytes 786436
  133.6 7.5 %collective-permute-start.6 = (bf16[128,1024]{1,0:T(8,128)(2,1)S(1)}, bf16[128,1024]{1,0:T(8,128)(2,1)S(1)}, u32[]{:S(2)}, u32[]{:S(2)}) collective-permute-start(bf16[128,1024]{1,0:T(8,128)(2,1)S(1)} %get-tuple-element.44), channel_id=1, source_target_pairs={{0,1},{1,2},{2,3},{3,4},{4,5},{5,6},{6,7},{7,8},{8,9},{9,10},{10,1... | collective-permute-start | bytes 786440 | tf_op jit(solution)/shard_map/ppermute | solution.py:29
  137.8 8.7 %collective-permute-start.7 = (bf16[128,1024]{1,0:T(8,128)(2,1)S(1)}, bf16[128,1024]{1,0:T(8,128)(2,1)}, u32[]{:S(2)}, u32[]{:S(2)}) collective-permute-start(bf16[128,1024]{1,0:T(8,128)(2,1)S(1)} %get-tuple-element.45), channel_id=1, source_target_pairs={{1,0},{2,1},{3,2},{4,3},{5,4},{6,5},{7,6},{8,7},{9,8},{10,9},{11,1... | collective-permute-start | bytes 786440 | tf_op jit(solution)/shard_map/ppermute | solution.py:29
